TPU v7x, 128 devices: a whole 4x4x4 slice. The times are simulated.
128 devices in a mesh: row: 32 (over z, x, core), col: 4 (over y).
Axes of the slice: x: 4, y: 4, z: 4, core: 2. Of those that a mesh axis runs over, the one named last changes fastest.
Arguments:
- factor_u: float32 [1, 32, 2, 4, 512, 128], P(None, 'row', None, 'col'), may hold values from -6 to 6
- factor_v: float32 [1, 32, 2, 4, 512, 128], P(None, 'row', None, 'col'), may hold values from -6 to 6
- near_field: float32 [2, 512, 512], replicated, as said below
- sketch: float32 [2, 512, 128], replicated, may hold values from -6 to 6
- tile_ranks: int32 [3, 1, 32, 2, 4], P(None, None, None, None, 'col'), may hold values from 1 to 128, as said below
Outputs:
- out_u: float32 [1, 32, 2, 4, 512, 128], P(None, 'row', None, 'col')
- out_v: float32 [1, 32, 2, 4, 512, 128], P(None, 'row', None, 'col')
Inputs may be any that keep to these rules, and one draw needn't show every extreme that they name: tile_ranks[0] is at least 16 and equals 128 on every tile (i, i); tile_ranks[1] lies between tile_ranks[0] - tile_ranks[0] // 2 and tile_ranks[0] - max(1, tile_ranks[0] // 4); tile_ranks[2] is at least 1 and at most tile_ranks[1], and when tile_ranks[1] > 1 it is at most tile_ranks[1] - max(1, tile_ranks[1] // 4). The diagonal entries of near_field[0] and near_field[1] lie between 1 and 4.
All inputs are finite; a program needn't handle non-finite values.
Results may differ from a plain program's by a relative error of at most 0.0003.
Values sent between devices are 32-bit elements; how exact they have to be, the bound alone decides.
No kernel may reach another device: no remote copies, remote signals or barrier semaphores. Data moves between devices by JAX's collectives and lax.ppermute only.
A program may use at most 64 MiB of HBM per device.

v0:
```python
import math

import jax
import jax.numpy as jnp
from jax import lax
from jax.sharding import PartitionSpec as P

NS_STEPS = 3


highest = lax.Precision.HIGHEST


def from_root(array, axis, root):
    mine = lax.axis_index(axis) == root
    return lax.psum(jnp.where(mine, array, jnp.zeros_like(array)), axis)


def padded_to(lines, peers):
    spare = -len(lines) % peers
    return jnp.pad(lines, [(0, spare)] + [(0, 0)] * (lines.ndim - 1))


def spread(array, axis, root):
    lines = jnp.where(lax.axis_index(axis) == root, array, jnp.zeros_like(array)).reshape(
        -1, *array.shape[1:][-1:]
    )
    padded = padded_to(lines, lax.axis_size(axis))
    own = lax.psum_scatter(padded, axis, scatter_dimension=0, tiled=True)
    return lax.all_gather(own, axis, axis=0, tiled=True)[: len(lines)].reshape(array.shape)


def rank_keep(ranks, width):
    return jnp.arange(width, dtype=jnp.int32) < ranks[..., None]


def orthonormal(basis, keeper):
    gram = jnp.einsum("...tk,...tl->...kl", basis, basis, precision=highest)
    unused = 1.0 - keeper.astype(basis.dtype)
    gram = gram + jnp.eye(basis.shape[-1], dtype=basis.dtype) * unused[..., None, :]
    factor = jnp.linalg.cholesky(gram)
    solved = jax.scipy.linalg.solve_triangular(factor, jnp.swapaxes(basis, -1, -2), lower=True)
    return jnp.swapaxes(solved, -1, -2)


def recompress(full_u, full_v, sketch_block, ranks):
    root_order = math.sqrt(full_u.shape[-2])
    keeper = rank_keep(ranks, sketch_block.shape[-1])
    projected = jnp.einsum("...tq,tk->...qk", full_v, sketch_block, precision=highest)
    basis = jnp.einsum("...tq,...qk->...tk", full_u, projected, precision=highest)
    basis = basis * keeper[..., None, :].astype(basis.dtype)
    ortho = orthonormal(orthonormal(basis, keeper), keeper)
    backward = jnp.einsum("...tq,...tk->...qk", full_u, ortho, precision=highest)
    new_v = jnp.einsum("...tq,...qk->...tk", full_v, backward, precision=highest) / root_order
    return (ortho * root_order, new_v)


def update_tiles(cur_u, cur_v, low_u, low_v, up_u, up_v, sketch_block, ranks):
    far_weight = 1.0 / (8.0 * cur_u.shape[-2])
    core_block = far_weight * jnp.einsum("...tk,...tl->...kl", low_v, up_u, precision=highest)
    product_u = jnp.einsum("...tk,...kl->...tl", low_u, core_block, precision=highest)
    full_u = jnp.concatenate([cur_u, -product_u], axis=-1)
    full_v = jnp.concatenate([cur_v, up_v], axis=-1)
    return (product_u, recompress(full_u, full_v, sketch_block, ranks))


def newton_inverse(pivot, start_inverse):
    inverse = jnp.diag(start_inverse)
    twice = 2.0 * jnp.eye(pivot.shape[0], dtype=pivot.dtype)
    for newton_step in range(NS_STEPS):
        inverse = jnp.dot(
            inverse, twice - jnp.dot(pivot, inverse, precision=highest), precision=highest
        )
    return inverse


def body(factor_u, factor_v, near_field, sketch, tile_ranks):
    slot_rows = factor_u.shape[0]
    slot_cols = factor_u.shape[2]
    tile_order = factor_u.shape[4]
    rank_width = factor_u.shape[5]
    row_count = lax.axis_size("row")
    col_count = lax.axis_size("col")
    row_here = lax.axis_index("row")
    col_here = lax.axis_index("col")
    cur_u = factor_u.reshape(slot_rows, slot_cols, tile_order, rank_width)
    cur_v = factor_v.reshape(slot_rows, slot_cols, tile_order, rank_width)
    own_ranks = lax.dynamic_slice_in_dim(tile_ranks, row_here, 1, 2)[:, :, 0, :, 0]
    tile_row = (jnp.arange(slot_rows, dtype=jnp.int32) * row_count + row_here)[:, None]
    tile_col = (jnp.arange(slot_cols, dtype=jnp.int32) * col_count + col_here)[None, :]
    keeper = rank_keep(own_ranks[0], rank_width).astype(jnp.float32)[..., None, :]
    cur_u = cur_u * keeper
    cur_v = cur_v * keeper
    far_weight = 1.0 / (8.0 * tile_order)
    pivot = near_field[0] + far_weight * jnp.dot(cur_u[0, 0], cur_v[0, 0].T, precision=highest)
    for panel in range(2):
        start_inverse = 1.0 / jnp.diagonal(near_field[panel])
        inverse = newton_inverse(pivot, start_inverse)
        inverse = from_root(inverse, "row", panel)
        own_lower = jnp.einsum("st,isk->itk", inverse, cur_v[:, 0], precision=highest)
        low_u, low_v = (spread(cur_u[:, 0], "col", panel), spread(own_lower, "col", panel))
        if panel == 0:
            up_u, up_v = (from_root(cur_u[0], "row", 0), from_root(cur_v[0], "row", 0))
        else:
            up_u, up_v = (from_root(cur_u[0], "row", 1), from_root(cur_v[0], "row", 1))
        product_u, fresh_pair = update_tiles(
            cur_u,
            cur_v,
            low_u[:, None],
            low_v[:, None],
            up_u[None],
            up_v[None],
            sketch[panel],
            own_ranks[panel + 1],
        )
        if panel == 0:
            pivot = near_field[1] + far_weight * (
                jnp.dot(cur_u[0, 0], cur_v[0, 0].T, precision=highest)
                - jnp.dot(product_u[0, 0], up_v[0].T, precision=highest)
            )
        chosen = (tile_row > panel) & (tile_col > panel)
        if panel == 0:
            chosen = chosen & jnp.logical_not((tile_row == 1) & (tile_col == 1))
        cur_u = jnp.where(chosen[..., None, None], fresh_pair[0], cur_u)
        cur_v = jnp.where(chosen[..., None, None], fresh_pair[1], cur_v)
        lower_here = (tile_row[:, 0] > panel) & (col_here == panel)
        cur_v = cur_v.at[:, 0].set(jnp.where(lower_here[:, None, None], own_lower, cur_v[:, 0]))
        at_pivot = ((tile_row == panel) & (tile_col == panel))[..., None, None]
        cur_u = jnp.where(at_pivot, 0.0, cur_u)
        cur_v = jnp.where(at_pivot, 0.0, cur_v)
    shape_out = (slot_rows, 1, slot_cols, 1, tile_order, rank_width)
    return (cur_u.reshape(shape_out), cur_v.reshape(shape_out))


def solution(mesh):
    return jax.shard_map(
        body,
        mesh=mesh,
        in_specs=(
            P(None, "row", None, "col", None, None),
            P(None, "row", None, "col", None, None),
            P(),
            P(),
            P(None, None, None, None, "col"),
        ),
        out_specs=(
            P(None, "row", None, "col", None, None),
            P(None, "row", None, "col", None, None),
        ),
        check_vma=False,
    )
```

profile of v0, /device:TPU:0, one launch (start us, length us, event | category | flops | bytes accessed | tf_op | source)
XLA Modules:
  0.0 545.4 jit_solution(17778307473137740390)
XLA Ops:
  8.1 1.0 fusion.70
  9.1 1.2 copy.71
  10.4 1.4 copy.69
  11.8 1.1 bitcast_multiply_fusion.3
  12.9 1.1 fusion.32
  14.0 1.2 slice_bitcast_fusion
  15.2 4.5 gather_fusion
  19.8 2.1 fusion.57
  21.8 1.9 select_subtract_fusion.5
  23.7 1.9 fusion.6
  25.6 1.9 select_subtract_fusion.4
  27.5 1.8 fusion.87
  29.3 1.9 select_subtract_fusion.3
  31.2 2.8 convolution_select_fusion.1
  34.4 1.7 fusion.58
  36.3 8.5 %gather_fusion.1 = f32[512]{0:T(512)S(1)} fusion(f32[512,512]{1,0:T(8,128)} %get-tuple-element.47, s32[512]{0:T(512)S(1)} %bitcast.273), kind=kCustom, calls=%fused_computation.1 | custom fusion | bytes 8192 | tf_op jit(solution)/shard_map/jit(diagonal)/cond/branch_0_fun/gather | solution.py:97
  44.8 99.8 %all-reduce.7.cloned.1.call-done = (f32[2,512,128]{1,2,0:T(8,128)}, f32[2,512,128]{1,2,0:T(8,128)}, f32[512,512]{1,0:T(8,128)}) async-done(((f32[2,512,128]{1,2,0:T(8,128)}, f32[2,512,128]{1,2,0:T(8,128)}, f32[512,512]{1,0:T(8,128)}), (f32[2,512,128]{1,2,0:T(8,128)}, f32[2,512,128]{1,2,0:T(8,128)}, f32[512,512]{1,0:T(8,128)})) %all-reduce.7.cloned.1.call-update) | async-done | bytes 2097168 | tf_op jit(solution)/shard_map/psum | solution.py:16
  144.6 2.0 convolution_bitcast_fusion.2
  146.7 0.7 select_bitcast_fusion.3
  147.5 14.4 %all_gather.13 = f32[512,128]{0,1:T(8,128)} all-gather(f32[128,128]{0,1:T(8,128)} %reduce-scatter.7.cloned.1.call-done), channel_id=1, replica_groups=mesh['row'=32,'col'=4] {'col'}, dimensions={0}, use_global_device_ids=true | all-gather | bytes 327680 | tf_op jit(solution)/shard_map/all_gather | solution.py:30
  162.0 3.0 fusion.23
  165.0 2.6 reduce-scatter.5.cloned.1.call-done
  167.6 12.6 %all_gather.12 = f32[512,128]{0,1:T(8,128)S(1)} all-gather(f32[128,128]{0,1:T(8,128)} %reduce-scatter.5.cloned.1.call-done), channel_id=1, replica_groups=mesh['row'=32,'col'=4] {'col'}, dimensions={0}, use_global_device_ids=true | all-gather | bytes 327680 | tf_op jit(solution)/shard_map/all_gather | solution.py:30
  180.2 1.6 fusion.20
  181.8 1.5 fusion.86
  183.4 2.1 fusion.13
  185.5 1.9 convolution_multiply_fusion.3
  187.3 1.0 convolution_add_fusion.3
  188.5 23.9 %custom-call.16 = f32[1,2,128,128]{3,2,1,0:T(8,128)S(1)} custom-call(f32[1,2,128,128]{3,2,1,0:T(8,128)S(1)} %fusion.62), custom_call_target="Cholesky" | custom-call | tf_op jit(solution)/shard_map/jit(cholesky)/cholesky | solution.py:41
  212.6 19.7 %custom-call.17 = f32[2,1,128,128]{2,3,1,0:T(8,128)S(1)} custom-call(f32[2,1,128,128]{3,2,1,0:T(8,128)S(1)} %select_bitcast_fusion.7), custom_call_target="InvertDiagBlocksLowerTriangular" | custom-call | tf_op jit(solution)/shard_map/jit(_solve_triangular)/vmap()/triangular_solve | solution.py:42
  232.3 0.6 fusion.27
  232.9 0.6 convolution_add_fusion.2
  233.7 23.5 %custom-call.18 = f32[1,2,128,128]{3,2,1,0:T(8,128)S(1)} custom-call(f32[1,2,128,128]{3,2,1,0:T(8,128)S(1)} %fusion.61), custom_call_target="Cholesky" | custom-call | tf_op jit(solution)/shard_map/jit(cholesky)/cholesky | solution.py:41
  257.4 19.8 %custom-call.19 = f32[2,1,128,128]{2,3,1,0:T(8,128)S(1)} custom-call(f32[2,1,128,128]{3,2,1,0:T(8,128)S(1)} %select_bitcast_fusion.6), custom_call_target="InvertDiagBlocksLowerTriangular" | custom-call | tf_op jit(solution)/shard_map/jit(_solve_triangular)/vmap()/triangular_solve | solution.py:42
  277.9 1.2 fusion.24
  279.2 1.8 select_subtract_fusion.2
  281.0 1.9 fusion
  282.9 1.9 select_subtract_fusion.1
  284.8 1.9 fusion.88
  286.6 1.9 select_subtract_fusion
  288.5 3.1 convolution_select_fusion
  291.6 0.7 fusion.16
  292.4 1.3 broadcast_select_fusion
  293.8 0.7 fusion.45
  294.7 106.9 %all-reduce.5.cloned.1.call-done = (f32[1,2,512,128]{2,3,1,0:T(8,128)}, f32[2,512,128]{1,2,0:T(8,128)}, f32[512,512]{1,0:T(8,128)}) async-done(((f32[1,2,512,128]{2,3,1,0:T(8,128)}, f32[2,512,128]{1,2,0:T(8,128)}, f32[512,512]{1,0:T(8,128)}), (f32[1,2,512,128]{2,3,1,0:T(8,128)}, f32[2,512,128]{1,2,0:T(8,128)}, f32[512,512]{1,0:T(8,128)})) %all-reduce.5.cloned.1.call-update) | async-done | bytes 2097168 | tf_op jit(solution)/shard_map/psum | solution.py:16
  401.6 2.0 convolution_bitcast_fusion.1
  403.6 0.7 select_bitcast_fusion.2
  404.4 12.8 %all_gather.15 = f32[512,128]{0,1:T(8,128)S(1)} all-gather(f32[128,128]{0,1:T(8,128)} %reduce-scatter.11.cloned.1.call-done), channel_id=1, replica_groups=mesh['row'=32,'col'=4] {'col'}, dimensions={0}, use_global_device_ids=true | all-gather | bytes 327680 | tf_op jit(solution)/shard_map/all_gather | solution.py:30
  417.2 1.0 fusion.21
  418.2 6.3 %reduce-scatter.9.cloned.1.call-done = f32[128,128]{0,1:T(8,128)} async-done(((f32[512,128]{0,1:T(8,128)}), f32[128,128]{0,1:T(8,128)}) %reduce-scatter.9.cloned.1.call-update) | async-done | bytes 65552 | tf_op jit(solution)/shard_map/reduce_scatter | solution.py:29
  424.5 12.5 %all_gather.14 = f32[512,128]{0,1:T(8,128)S(1)} all-gather(f32[128,128]{0,1:T(8,128)} %reduce-scatter.9.cloned.1.call-done), channel_id=1, replica_groups=mesh['row'=32,'col'=4] {'col'}, dimensions={0}, use_global_device_ids=true | all-gather | bytes 327680 | tf_op jit(solution)/shard_map/all_gather | solution.py:30
  437.0 1.6 fusion.19
  439.2 1.9 convolution_multiply_fusion.1
  441.1 1.0 convolution_add_fusion.1
  442.2 23.7 %custom-call.20 = f32[1,2,128,128]{3,2,1,0:T(8,128)S(1)} custom-call(f32[1,2,128,128]{3,2,1,0:T(8,128)S(1)} %fusion.60), custom_call_target="Cholesky" | custom-call | tf_op jit(solution)/shard_map/jit(cholesky)/cholesky | solution.py:41
  466.2 20.3 %custom-call.21 = f32[2,1,128,128]{2,3,1,0:T(8,128)} custom-call(f32[2,1,128,128]{3,2,1,0:T(8,128)S(1)} %select_bitcast_fusion.5), custom_call_target="InvertDiagBlocksLowerTriangular" | custom-call | tf_op jit(solution)/shard_map/jit(_solve_triangular)/vmap()/triangular_solve | solution.py:42
  486.5 1.5 fusion.25
  488.0 0.6 convolution_add_fusion
  488.8 23.5 %custom-call.22 = f32[1,2,128,128]{3,2,1,0:T(8,128)S(1)} custom-call(f32[1,2,128,128]{3,2,1,0:T(8,128)S(1)} %fusion.59), custom_call_target="Cholesky" | custom-call | tf_op jit(solution)/shard_map/jit(cholesky)/cholesky | solution.py:41
  512.5 20.0 %custom-call.23 = f32[2,1,128,128]{2,3,1,0:T(8,128)S(1)} custom-call(f32[2,1,128,128]{3,2,1,0:T(8,128)S(1)} %select_bitcast_fusion.4), custom_call_target="InvertDiagBlocksLowerTriangular" | custom-call | tf_op jit(solution)/shard_map/jit(_solve_triangular)/vmap()/triangular_solve | solution.py:42
  533.1 1.1 fusion.22
  534.2 0.8 fusion.18
  535.3 1.0 copy.100
  536.3 1.0 copy.99
  (81 shorter events, 4.7 us)
Async XLA Ops:
  8.0 136.7 %all-reduce.7.cloned.1.call-start = ((), (), s32[]{:S(2)}) async-start(), calls=%async_computation.9 | async-start | bytes 4194304 | tf_op jit(solution)/shard_map/psum | solution.py:16
  10.4 2.6 copy-start.4
  11.8 2.2 copy-start
  34.1 113.4 %reduce-scatter.7.cloned.1.call-start = ((), (), s32[]{:S(2)}) async-start(), calls=%async_computation.5 | async-start | bytes 327680 | tf_op jit(solution)/shard_map/reduce_scatter | solution.py:29
  36.1 131.5 %reduce-scatter.5.cloned.1.call-start = ((), (), s32[]{:S(2)}) async-start(), calls=%async_computation.4 | async-start | bytes 327680 | tf_op jit(solution)/shard_map/reduce_scatter | solution.py:29
  147.4 254.2 %all-reduce.5.cloned.1.call-start = ((), (), s32[]{:S(2)}) async-start(), calls=%async_computation.8 | async-start | bytes 4194304 | tf_op jit(solution)/shard_map/psum | solution.py:16
  167.6 15.8 %copy-start.9 = (f32[2,512,128]{1,2,0:T(8,128)S(1)}, f32[2,512,128]{1,2,0:T(8,128)}, u32[]{:S(2)}) copy-start(f32[2,512,128]{1,2,0:T(8,128)} %get-tuple-element.40) | copy-start | bytes 1572868
  183.3 4.0 copy-start.7
  183.4 2.1 copy-start.1
  183.4 2.1 copy-start.12
  232.3 45.6 %copy-start.2 = (f32[1,2,512,128]{2,3,1,0:T(8,128)S(1)}, f32[1,2,512,128]{2,3,1,0:T(8,128)}, u32[]{:S(2)}) copy-start(f32[1,2,512,128]{2,3,1,0:T(8,128)} %get-tuple-element.50) | copy-start | bytes 1572868
  232.3 45.6 %copy-start.8 = (f32[1,2,512,128]{2,3,1,0:T(8,128)S(1)}, f32[1,2,512,128]{2,3,1,0:T(8,128)}, u32[]{:S(2)}) copy-start(f32[1,2,512,128]{2,3,1,0:T(8,128)} %copy-done.7) | copy-start | bytes 1572868
  233.6 45.6 %copy-start.3 = (f32[512,512]{1,0:T(8,128)S(1)}, f32[512,512]{1,0:T(8,128)}, u32[]{:S(2)}) copy-start(f32[512,512]{1,0:T(8,128)} %fusion.13) | copy-start | bytes 3145732
  288.5 3.1 copy-start.5
  288.5 3.1 copy-start.6
  288.5 3.1 copy-start.10
  293.8 123.5 %copy-start.13 = (f32[2,512,128]{2,1,0:T(8,128)S(1)}, f32[2,512,128]{2,1,0:T(8,128)}, u32[]{:S(2)}) copy-start(f32[2,512,128]{2,1,0:T(8,128)} %param.15) | copy-start | bytes 1572868
  293.8 110.7 %reduce-scatter.11.cloned.1.call-start = ((), (), s32[]{:S(2)}) async-start(), calls=%async_computation.7 | async-start | bytes 327680 | tf_op jit(solution)/shard_map/reduce_scatter | solution.py:29
  294.6 129.9 %reduce-scatter.9.cloned.1.call-start = ((), (), s32[]{:S(2)}) async-start(), calls=%async_computation.6 | async-start | bytes 327680 | tf_op jit(solution)/shard_map/reduce_scatter | solution.py:29
  401.6 15.6 %copy-start.11 = (f32[1,2,512,128]{2,3,1,0:T(8,128)S(1)}, f32[1,2,512,128]{2,3,1,0:T(8,128)}, u32[]{:S(2)}) copy-start(f32[1,2,512,128]{2,3,1,0:T(8,128)} %get-tuple-element.37) | copy-start | bytes 1572868
Sparse Core Ops, SparseCore 0:
  34.2 110.3 all-reduce.6
  293.9 107.6 all-reduce.4
Sparse Core Ops, SparseCore 1:
  36.9 23.1 reduce-scatter.6
  147.5 20.0 reduce-scatter.4
  296.6 20.4 reduce-scatter.10
  404.5 20.0 reduce-scatter.8
where the time goes:
time: 555 us; the launch traced here: 545 us
  waiting for transfers between devices  216 us (39%)
  other arithmetic  184 us (33%)
  matrix products  56.2 us (10%)
  blocking collectives  52.3 us (9%)
  local copies, waits for them, and re-layouts  20.3 us (4%)
  between operations  16.8 us (3%)
    psum x2, waiting for transfers between devices, from_root(): return lax.psum(jnp.where(mine, array, jnp.zeros_like(array)), axis)  207 us
    another operation x13, other arithmetic, orthonormal(): factor = jnp.linalg.cholesky(gram)  95.1 us
    another operation x9, other arithmetic, orthonormal(): jax.scipy.linalg.solve_triangular(factor, jnp.swapaxes(basis, -1, -2), lo...  80.2 us
    all_gather x4, blocking collectives, spread(): lax.all_gather(own, axis, axis=0, tiled=True)[:len(lines)]  52.3 us
    dot_general x6, matrix products, newton_inverse(): jnp.dot(inverse, twice - jnp.dot(pivot, inverse, precision=highest), prec...  13.3 us
    gather x2, local copies, waits for them, and re-layouts, body(): start_inverse = 1.0 / jnp.diagonal(near_field[panel])  13 us
    dot_general x6, matrix products, newton_inverse(): jnp.dot(pivot, inverse, precision=highest)  11.2 us
  transfers between devices with their start and end apart: 6, of which 4 were waited for; matrix products, arithmetic and copies ran while one was open for 4% of the time, Pallas kernels for 0%

commit v1 on v0

v1 whole, which is shorter than its diff:
```python
import functools
import math
import jax
import jax.numpy as jnp
from jax import lax
from jax.experimental import pallas as pl
from jax.experimental.pallas import tpu as pltpu
from jax.sharding import PartitionSpec as P

F32 = jnp.float32
BF16 = jnp.bfloat16
NN = (((1,), (0,)), ((), ()))
NT = (((1,), (1,)), ((), ()))
TN = (((0,), (0,)), ((), ()))


def dot6(a, b, dims=NN):
    return lax.dot_general(a, b, dims, precision=lax.Precision.HIGHEST, preferred_element_type=F32)


def split(a):
    high = a.astype(BF16)
    return high, (a - high.astype(F32)).astype(BF16)


def dot1(a, b, dims=NN):
    return lax.dot_general(a, b, dims, preferred_element_type=F32)


def dot3(a, b, dims=NN):
    ah, al = a if isinstance(a, tuple) else split(a)
    bh, bl = b if isinstance(b, tuple) else split(b)
    return dot1(ah, bh, dims) + (dot1(ah, bl, dims) + dot1(al, bh, dims))


def iota(shape, axis):
    return lax.broadcasted_iota(jnp.int32, shape, axis)


def eliminate(grams, order):
    count = len(grams)
    lane8 = iota((8, 128), 1)
    row8 = iota((8, 128), 0)
    blocks = [[g[8 * b:8 * b + 8, :] for b in range(order // 8)] for g in grams]
    done = [[] for _ in grams]
    for step in range(order // 8):
        base = 8 * step
        panels, pivots_all = [], []
        for g in range(count):
            panel = blocks[g][step]
            cols = [jnp.broadcast_to(panel[:, base + c:base + c + 1], (8, 128)) for c in range(8)]
            inside = (lane8 >= base) & (lane8 < base + 8)
            work = jnp.where(inside, (lane8 - base == row8).astype(F32), panel)
            scale = jnp.zeros((8, 128), F32)
            for c in range(8):
                pivot = jnp.broadcast_to(cols[c][c:c + 1, :], (8, 128))
                inverse = 1.0 / pivot
                scale = jnp.where(row8 == c, inverse, scale)
                if c < 7:
                    factor = jnp.where(row8 > c, cols[c] * inverse, 0.0)
                    for d in range(c + 1, 8):
                        cols[d] = cols[d] - factor * jnp.broadcast_to(cols[d][c:c + 1, :], (8, 128))
                    work = work - factor * jnp.broadcast_to(work[c:c + 1, :], (8, 128))
            panels.append(work)
            pivots_all.append(scale)
        for g in range(count):
            work, scale = panels[g], pivots_all[g]
            done[g].append(work * jnp.sqrt(scale))
            if step + 1 < order // 8:
                update = dot6(work, work * scale, TN)
                inside = (lane8 >= base) & (lane8 < base + 8)
                for b in range(step + 1, order // 8):
                    blocks[g][b] = jnp.where(inside, 0.0, blocks[g][b]) - update[8 * b:8 * b + 8, :]
    outs = []
    for g in range(count):
        full = jnp.concatenate(done[g], axis=0)
        keep = iota((order, 128), 1) <= iota((order, 128), 0)
        outs.append(jnp.where(keep, full, 0.0))
    return outs


def panel_kernel(order, first, flags, cu, cv, lu, lowt, upu, upv, st, nu, nv, wide_out, ortho, factor):
    tile = cu.shape[1]
    width = cu.shape[2]
    weight = 1.0 / (8.0 * tile)
    root = math.sqrt(tile)
    lanes = iota((tile, width), 1)
    spare = jnp.zeros((width - order, tile), F32)
    row_g = iota((order, width), 0)
    lane_g = iota((order, width), 1)
    eye = (row_g == lane_g).astype(F32)
    full_us, full_vs, bases, grams, units = [], [], [], [], []
    low = split(lowt[...])
    lead = split(lu[...])
    sketch = st[...]
    for s in range(2):
        own_u = cu[s]
        up_u = upu[s]
        if first:
            own_u = jnp.where(lanes < flags[2 + s], own_u, 0.0)
            up_u = jnp.where(lanes < flags[4 + s], up_u, 0.0)
        core = weight * dot3(low, up_u)
        wide = dot3(lead, core)
        if s == 0 and first:
            wide_out[...] = wide
        full_u = jnp.concatenate([own_u, -wide], axis=1)
        full_v = jnp.concatenate([cv[s], upv[s]], axis=1)
        projected = dot6(sketch, full_v)
        basis = dot6(projected, full_u, NT)
        basis = jnp.where(iota((order, tile), 0) < flags[s], basis, 0.0)
        basis = jnp.concatenate([basis, spare], axis=0)
        unit = jnp.where((row_g == lane_g) & (row_g >= flags[s]), 1.0, 0.0)
        grams.append(dot6(basis[:order], basis, NT) + unit)
        full_us.append(full_u)
        full_vs.append(full_v)
        bases.append(basis)
        units.append(unit)
    inverses = eliminate(grams, order)
    twice, defect = [], jnp.zeros((), F32)
    for s in range(2):
        once = dot6(inverses[s], bases[s])
        ortho[s, :order] = once
        ortho[s, order:] = spare
        gram = dot6(once, jnp.concatenate([once, spare], axis=0), NT) + units[s]
        factor[s] = gram
        off = gram - eye
        defect = jnp.maximum(defect, jnp.sum(off * off))
    near = defect < 1e-6

    @pl.when(near)
    def _():
        for s in range(2):
            off = factor[s] - eye
            half = jnp.where(lane_g < row_g, off, jnp.where(lane_g == row_g, 0.5 * off, 0.0))
            once = ortho[s]
            ortho[s, :order] = once[:order] - dot1(half.astype(BF16), once.astype(BF16))

    @pl.when(jnp.logical_not(near))
    def _():
        again = eliminate([factor[0], factor[1]], order)
        for s in range(2):
            ortho[s, :order] = dot6(again[s], ortho[s])

    for s in range(2):
        basis = ortho[s]
        back = dot3(basis, full_us[s])
        fresh_v = dot3(full_vs[s], back, NT) * (1.0 / root)
        fresh_u = basis.T * root
        keep_u = cu[s]
        keep_v = cv[s]
        if first:
            keep_u = jnp.where(lanes < flags[2 + s], keep_u, 0.0)
            keep_v = jnp.where(lanes < flags[2 + s], keep_v, 0.0)
        if s == 0:
            keep_v = jnp.where(flags[8] == 1, lowt[...].T, keep_v)
            keep_u = jnp.where(flags[9] == 1, 0.0, keep_u)
            keep_v = jnp.where(flags[9] == 1, 0.0, keep_v)
        chosen = flags[6 + s] == 1
        nu[s] = jnp.where(chosen, fresh_u, keep_u)
        nv[s] = jnp.where(chosen, fresh_v, keep_v)


def panel_update(first, flags, cu, cv, lu, lowt, upu, upv, st):
    order = st.shape[0]
    tile, width = lu.shape
    vmem = pl.BlockSpec(memory_space=pltpu.VMEM)
    pair = jax.ShapeDtypeStruct((2, tile, width), F32)
    return pl.pallas_call(
        functools.partial(panel_kernel, order, first),
        out_shape=(pair, pair, jax.ShapeDtypeStruct((tile, width), F32)),
        in_specs=[pl.BlockSpec(memory_space=pltpu.SMEM)] + [vmem] * 7,
        out_specs=(vmem, vmem, vmem),
        scratch_shapes=[pltpu.VMEM((2, width, tile), F32), pltpu.VMEM((2, order, width), F32)],
        compiler_params=pltpu.CompilerParams(vmem_limit_bytes=40 * 1024 * 1024),
    )(flags, cu, cv, lu, lowt, upu, upv, st)


def lower_kernel(pairs, near, *refs):
    us, vs, own_v, rank, out = refs[:pairs], refs[pairs:2 * pairs], refs[2 * pairs], refs[2 * pairs + 1], refs[2 * pairs + 2]
    tile, width = own_v.shape
    weight = 1.0 / (8.0 * tile)
    eye = iota((tile, tile), 0) == iota((tile, tile), 1)
    far = near[...]
    start = 1.0 / jnp.sum(jnp.where(eye, far, 0.0), axis=0, keepdims=True)
    low_rank = dot3(us[0][...], vs[0][...], NT)
    if pairs == 2:
        low_rank = low_rank - dot3(us[1][...], vs[1][...], NT)
    pivot = far + weight * low_rank
    rest = jnp.where(eye, 1.0, 0.0) - pivot * start
    values = jnp.where(iota((tile, width), 1) < rank[0], own_v[...], 0.0).T * start
    parts = split(rest)
    square = dot3(parts, parts)
    values = values + dot3(values, parts)
    parts = split(square)
    fourth = dot3(parts, parts)
    values = values + dot3(values, parts)
    out[...] = values + dot3(values, fourth)


def lower_values(near, us, vs, own_v, rank):
    tile, width = own_v.shape
    vmem = pl.BlockSpec(memory_space=pltpu.VMEM)
    pairs = len(us)
    return pl.pallas_call(
        functools.partial(lower_kernel, pairs),
        out_shape=jax.ShapeDtypeStruct((width, tile), F32),
        in_specs=[vmem] * (2 + 2 * pairs) + [pl.BlockSpec(memory_space=pltpu.SMEM)],
        out_specs=vmem,
        compiler_params=pltpu.CompilerParams(vmem_limit_bytes=40 * 1024 * 1024),
    )(near, *us, *vs, own_v, rank)


Z_COUNT = 4
X_COUNT = 4


def row_of(z, x, core):
    return (z * X_COUNT + x) * 2 + core


def fan_out(value, axis, pair_sets):
    total = None
    for pairs in pair_sets:
        moved = lax.ppermute(value, axis, pairs)
        total = moved if total is None else total + moved
    return total


def share_column(halves, root):
    row = lax.axis_index("row")
    core = row % 2
    x = (row // 2) % X_COUNT
    z = row // (2 * X_COUNT)
    crossed = lax.ppermute(halves[1 - root], "row", [(root, 1 - root)])
    mine = jnp.where(row == root, halves[root], crossed)
    first = fan_out(
        mine,
        "row",
        [[(row_of(0, 0, 0), row_of(k, 0, 0)), (row_of(0, 0, 1), row_of(0, k, 1))] for k in (1, 3, 2)],
    )
    held = jnp.where(row < 2, mine, first)
    second = fan_out(
        held,
        "row",
        [
            [(row_of(z, 0, 0), row_of(z, k, 0)) for z in range(Z_COUNT)]
            + [(row_of(0, x, 1), row_of(k, x, 1)) for x in range(X_COUNT)]
            for k in (1, 3, 2)
        ],
    )
    holder = jnp.where(core == 0, x, z) == 0
    final = jnp.where(holder, held, second)
    other = lax.ppermute(final, "row", [(r, r ^ 1) for r in range(2 * X_COUNT * Z_COUNT)])
    return jnp.where(core == 0, final, other), jnp.where(core == 0, other, final)


def share_row(value, root):
    col = lax.axis_index("col")
    right, left, far = (root + 1) % 4, (root + 3) % 4, (root + 2) % 4
    middle = value.shape[0] // 2
    head, tail = value[:middle], value[middle:]
    head_right = lax.ppermute(head, "col", [(root, right)])
    tail_left = lax.ppermute(tail, "col", [(root, left)])
    via_right = lax.ppermute(jnp.where(col == root, tail, head_right), "col", [(root, right), (right, far)])
    via_left = lax.ppermute(jnp.where(col == root, head, tail_left), "col", [(root, left), (left, far)])
    got_head = jnp.where(col == right, head_right, jnp.where(col == far, via_right, via_left))
    got_tail = jnp.where(col == left, tail_left, jnp.where(col == far, via_left, via_right))
    return jnp.where(col == root, value, jnp.concatenate([got_head, got_tail]))


def body(factor_u, factor_v, near_field, sketch, tile_ranks):
    tile, width = factor_u.shape[4:]
    row = lax.axis_index("row")
    col = lax.axis_index("col")
    own_u = factor_u.reshape(2, tile, width)
    own_v = factor_v.reshape(2, tile, width)
    ranks = tile_ranks.reshape(3, -1, 2)
    own_ranks = lax.dynamic_slice_in_dim(ranks, row, 1, 1)[:, 0]
    order = (width - width // 4, width - width // 4 - (width - width // 4) // 4)
    sketch_t = [sketch[k, :, : order[k]].T for k in range(2)]

    def flags_of(panel):
        slots = jnp.arange(2) * 4 + col
        chosen = (row > panel) & (slots > panel)
        if panel == 0:
            chosen = chosen & jnp.logical_not((row == 1) & (slots == 1))
        lower = (row > panel) & (col == panel)
        pivot = (row == panel) & (col == panel)
        parts = [own_ranks[panel + 1], own_ranks[0], ranks[0, 0], chosen, lower[None], pivot[None]]
        return jnp.concatenate([part.astype(jnp.int32) for part in parts])

    with jax.named_scope("first_share"):
        up_a = share_column((own_u[0], own_v[0]), 0)
        up_b = share_column((own_u[1], own_v[1]), 0)
        lead = share_row(own_u[0], 0)
    with jax.named_scope("first_lower"):
        low = lower_values(near_field[0], [up_a[0]], [up_a[1]], own_v[0], own_ranks[0, :1])
        low = share_row(low, 0)
    with jax.named_scope("pivot_share"):
        corner = share_column((own_u[0], own_v[0]), 1)
    with jax.named_scope("first_update"):
        up_u, up_v = jnp.stack([up_a[0], up_b[0]]), jnp.stack([up_a[1], up_b[1]])
        cur_u, cur_v, wide = panel_update(True, flags_of(0), own_u, own_v, lead, low, up_u, up_v, sketch_t[0])
    with jax.named_scope("second_share"):
        half = tile // 2
        wide = jnp.concatenate(share_column((wide[:half], wide[half:]), 1))
        lead = share_row(cur_u[0], 1)
        fresh = jnp.concatenate([cur_u, cur_v], axis=1)
        fresh_a, fresh_b = share_column((fresh[0], fresh[1]), 1)
    with jax.named_scope("second_lower"):
        full = jnp.full((1,), width, jnp.int32)
        low = lower_values(near_field[1], [corner[0], wide], [corner[1], up_a[1]], cur_v[0], full)
        low = share_row(low, 1)
    with jax.named_scope("second_update"):
        up_u = jnp.stack([fresh_a[:tile], fresh_b[:tile]])
        up_v = jnp.stack([fresh_a[tile:], fresh_b[tile:]])
        cur_u, cur_v, _ = panel_update(False, flags_of(1), cur_u, cur_v, lead, low, up_u, up_v, sketch_t[1])
    shape_out = factor_u.shape
    return cur_u.reshape(shape_out), cur_v.reshape(shape_out)


def solution(mesh):
    tiles = P(None, "row", None, "col", None, None)
    return jax.shard_map(
        body,
        mesh=mesh,
        in_specs=(tiles, tiles, P(), P(), P(None, None, None, None, "col")),
        out_specs=(tiles, tiles),
        check_vma=False,
    )
```

time: 555 us -> 189 us (0.34); the launches traced: 545 us -> 187 us
  waiting for transfers between devices: 216 us -> 21.9 us
  other arithmetic: 184 us -> 12.9 us
  starting transfers between devices: 0.47 us -> 97.9 us
  matrix products: 56.2 us -> 0 us
  blocking collectives: 52.3 us -> 0 us
  Pallas kernels: 0 us -> 34.4 us
  between operations: 16.8 us -> 1.68 us
    psum x2 -> x0, waiting for transfers between devices: 207 us -> none  [from_root(): return lax.psum(jnp.where(mine, array, jnp.zeros_like(array)), axis)]
    another operation x22 -> x4, other arithmetic: 175 us -> 0.18 us  [the longest x2 0.11 us: body(): up_u, up_v = (jnp.stack([up_a[0], up_b[0]]), jnp.stack([up_a[1], up_b[1]]))]
    ppermute x0 -> x56, starting transfers between devices: none -> 97.9 us  [the longest x30 52.6 us: fan_out(): moved = lax.ppermute(value, axis, pairs)]
    dot_general x32 -> x0, matrix products: 52.7 us -> none  [the longest x6 13.3 us: newton_inverse(): jnp.dot(inverse, twice - jnp.dot(pivot, inverse, precision=highest), prec...]
    all_gather x4 -> x0, blocking collectives: 52.3 us -> none  [spread(): lax.all_gather(own, axis, axis=0, tiled=True)[:len(lines)]]
    pallas_call x0 -> x4, Pallas kernels: none -> 34.4 us  [the longest x2 27.3 us: panel_update(): pl.pallas_call(functools.partial(panel_kernel, order, first), out_shape=(...]
    ppermute x0 -> x56, waiting for transfers between devices: none -> 21.9 us  [the longest x4 8.41 us: share_row(): lax.ppermute(jnp.where(col == root, head, tail_left), 'col', [(root, left...]
    gather x2 -> x0, local copies, waits for them, and re-layouts: 13 us -> none  [body(): start_inverse = 1.0 / jnp.diagonal(near_field[panel])]
  transfers between devices with their start and end apart: 6 -> 56, of which waited for: 4 -> 10; matrix products, arithmetic and copies ran while one was open for 4% -> 15% of each run, Pallas kernels for 0% -> 4%
where the time goes in v1:
time: 189 us; the launch traced here: 187 us
  starting transfers between devices  97.9 us (52%)
  Pallas kernels  34.4 us (18%)
  waiting for transfers between devices  21.9 us (12%)
  local copies, waits for them, and re-layouts  18.6 us (10%)
  other arithmetic  12.9 us (7%)
    ppermute x30, starting transfers between devices, fan_out(): moved = lax.ppermute(value, axis, pairs)  52.6 us
    pallas_call x2, Pallas kernels, panel_update(): pl.pallas_call(functools.partial(panel_kernel, order, first), out_shape=(...  27.3 us
    ppermute x4, starting transfers between devices, share_row(): lax.ppermute(jnp.where(col == root, head, tail_left), 'col', [(root, left...  16.5 us
    ppermute x4, waiting for transfers between devices, share_row(): lax.ppermute(jnp.where(col == root, head, tail_left), 'col', [(root, left...  8.41 us
    ppermute x5, starting transfers between devices, share_column(): crossed = lax.ppermute(halves[1 - root], 'row', [(root, 1 - root)])  7.88 us
    pallas_call x2, Pallas kernels, lower_values(): pl.pallas_call(functools.partial(lower_kernel, pairs), out_shape=jax.Shap...  7.18 us
    ppermute x4, starting transfers between devices, share_row(): lax.ppermute(jnp.where(col == root, tail, head_right), 'col', [(root, rig...  7.04 us
    ppermute x4, starting transfers between devices, share_row(): head_right = lax.ppermute(head, 'col', [(root, right)])  6.88 us
  transfers between devices with their start and end apart: 56, of which 10 were waited for; matrix products, arithmetic and copies ran while one was open for 15% of the time, Pallas kernels for 4%

profile of v1, /device:TPU:0, one launch (start us, length us, event | category | flops | bytes accessed | tf_op | source)
XLA Modules:
  0.0 187.4 jit_solution(3180656378242039995)
XLA Ops:
  0.6 1.8 slice_bitcast_fusion.9
  2.5 2.0 %collective-permute-start.16 = (f32[512,128]{1,0:T(8,128)}, f32[512,128]{1,0:T(8,128)}, u32[]{:S(2)}, u32[]{:S(2)}) collective-permute-start(f32[512,128]{1,0:T(8,128)} %get-tuple-element.38), channel_id=1, source_target_pairs={{0,4},{1,5},{2,6},{3,7}} | collective-permute-start | bytes 786440 | tf_op jit(solution)/shard_map/first_share/ppermute | solution.py:234
  5.4 4.0 %collective-permute-start = (f32[256,128]{1,0:T(8,128)S(1)}, f32[256,128]{1,0:T(8,128)S(1)}, u32[]{:S(2)}, u32[]{:S(2)}) collective-permute-start(f32[256,128]{1,0:T(8,128)S(1)} %get-tuple-element.44), channel_id=1, source_target_pairs={{0,1},{4,5},{8,9},{12,13},{16,17},{20,21},{24,25},{28,29},{32,33},... | collective-permute-start | bytes 393224 | tf_op jit(solution)/shard_map/first_share/ppermute | solution.py:262
  9.5 2.1 %collective-permute-start.2 = (f32[256,128]{1,0:T(8,128)S(1)}, f32[256,128]{1,0:T(8,128)S(1)}, u32[]{:S(2)}, u32[]{:S(2)}) collective-permute-start(f32[256,128]{1,0:T(8,128)S(1)} %get-tuple-element.45), channel_id=1, source_target_pairs={{0,3},{4,7},{8,11},{12,15},{16,19},{20,23},{24,27},{28,31},{32,35}... | collective-permute-start | bytes 393224 | tf_op jit(solution)/shard_map/first_share/ppermute | solution.py:263
  11.6 2.0 %collective-permute-start.4 = (f32[512,128]{1,0:T(8,128)S(1)}, f32[512,128]{1,0:T(8,128)}, u32[]{:S(2)}, u32[]{:S(2)}) collective-permute-start(f32[512,128]{1,0:T(8,128)S(1)} %get-tuple-element.39.refs_2_), channel_id=1, source_target_pairs={{0,4},{1,5},{2,6},{3,7}} | collective-permute-start | bytes 786440 | tf_op jit(solution)/shard_map/first_share/ppermute | solution.py:234
  13.6 1.7 slice_bitcast_fusion.11
  17.3 1.9 %collective-permute-start.1 = (f32[256,128]{1,0:T(8,128)}, f32[256,128]{1,0:T(8,128)}, u32[]{:S(2)}, u32[]{:S(2)}) collective-permute-start(f32[256,128]{1,0:T(8,128)} %get-tuple-element.42), channel_id=1, source_target_pairs={{0,1},{1,2},{4,5},{5,6},{8,9},{9,10},{12,13},{13,14},{16,17},{17,1... | collective-permute-start | bytes 393224 | tf_op jit(solution)/shard_map/first_share/ppermute | solution.py:264
  19.3 3.1 %collective-permute-start.3 = (f32[256,128]{1,0:T(8,128)}, f32[256,128]{1,0:T(8,128)}, u32[]{:S(2)}, u32[]{:S(2)}) collective-permute-start(f32[256,128]{1,0:T(8,128)} %get-tuple-element.43), channel_id=1, source_target_pairs={{0,3},{3,2},{4,7},{7,6},{8,11},{11,10},{12,15},{15,14},{16,19},{19... | collective-permute-start | bytes 393224 | tf_op jit(solution)/shard_map/first_share/ppermute | solution.py:265
  22.3 1.7 slice_bitcast_fusion
  24.1 1.8 collective-permute-done.3
  27.8 5.3 %collective-permute-start.7 = (f32[512,128]{1,0:T(8,128)}, f32[512,128]{1,0:T(8,128)}, u32[]{:S(2)}, u32[]{:S(2)}) collective-permute-start(f32[512,128]{1,0:T(8,128)} %get-tuple-element.37), channel_id=1, source_target_pairs={{0,64},{4,20},{1,65},{5,21},{2,66},{6,22},{3,67},{7,23}} | collective-permute-start | bytes 786440 | tf_op jit(solution)/shard_map/first_share/ppermute | solution.py:224
  33.8 2.0 %collective-permute-start.5 = (f32[512,128]{1,0:T(8,128)}, f32[512,128]{1,0:T(8,128)}, u32[]{:S(2)}, u32[]{:S(2)}) collective-permute-start(f32[512,128]{1,0:T(8,128)} %get-tuple-element.37), channel_id=1, source_target_pairs={{0,32},{4,12},{1,33},{5,13},{2,34},{6,14},{3,35},{7,15}} | collective-permute-start | bytes 786440 | tf_op jit(solution)/shard_map/first_share/ppermute | solution.py:224
  35.8 2.0 %collective-permute-start.6 = (f32[512,128]{1,0:T(8,128)}, f32[512,128]{1,0:T(8,128)}, u32[]{:S(2)}, u32[]{:S(2)}) collective-permute-start(f32[512,128]{1,0:T(8,128)} %get-tuple-element.37), channel_id=1, source_target_pairs={{0,96},{4,28},{1,97},{5,29},{2,98},{6,30},{3,99},{7,31}} | collective-permute-start | bytes 786440 | tf_op jit(solution)/shard_map/first_share/ppermute | solution.py:224
  38.4 1.4 collective-permute-start.19
  39.9 1.3 collective-permute-start.17
  41.2 1.3 collective-permute-start.18
  42.5 1.7 broadcast_select_fusion.2
  44.2 2.0 %collective-permute-start.31 = (f32[512,128]{1,0:T(8,128)}, f32[512,128]{1,0:T(8,128)}, u32[]{:S(2)}, u32[]{:S(2)}) collective-permute-start(f32[512,128]{1,0:T(8,128)} %broadcast_select_fusion.2), channel_id=1, source_target_pairs={{0,64},{4,20},{1,65},{5,21},{2,66},{6,22},{3,67},{7,23}} | collective-permute-start | bytes 786440 | tf_op jit(solution)/shard_map/pivot_share/ppermute | solution.py:224
  46.2 2.0 %collective-permute-start.29 = (f32[512,128]{1,0:T(8,128)}, f32[512,128]{1,0:T(8,128)}, u32[]{:S(2)}, u32[]{:S(2)}) collective-permute-start(f32[512,128]{1,0:T(8,128)} %broadcast_select_fusion.2), channel_id=1, source_target_pairs={{0,32},{4,12},{1,33},{5,13},{2,34},{6,14},{3,35},{7,15}} | collective-permute-start | bytes 786440 | tf_op jit(solution)/shard_map/pivot_share/ppermute | solution.py:224
  48.2 2.0 %add_select_fusion.7 = f32[512,128]{1,0:T(8,128)} fusion(f32[512,128]{1,0:T(8,128)} %get-tuple-element.37, f32[512,128]{1,0:T(8,128)} %collective-permute-done.7, f32[512,128]{1,0:T(8,128)} %collective-permute-done.5, f32[512,128]{1,0:T(8,128)} %collective-permute-done.6, pred[]{:T(512)S(6)} %lt.39), kind=kLoop, calls=%fused_computation.30 | loop fusion | flops 196608 | bytes 1310721 | tf_op jit(solution)/shard_map/first_share/jit(_where)/select_n | solution.py:241
  50.2 2.0 %collective-permute-start.30 = (f32[512,128]{1,0:T(8,128)}, f32[512,128]{1,0:T(8,128)}, u32[]{:S(2)}, u32[]{:S(2)}) collective-permute-start(f32[512,128]{1,0:T(8,128)} %broadcast_select_fusion.2), channel_id=1, source_target_pairs={{0,96},{4,28},{1,97},{5,29},{2,98},{6,30},{3,99},{7,31}} | collective-permute-start | bytes 786440 | tf_op jit(solution)/shard_map/pivot_share/ppermute | solution.py:224
  52.1 2.0 %collective-permute-start.10 = (f32[512,128]{1,0:T(8,128)}, f32[512,128]{1,0:T(8,128)}, u32[]{:S(2)}, u32[]{:S(2)}) collective-permute-start(f32[512,128]{1,0:T(8,128)} %add_select_fusion.7), channel_id=1, source_target_pairs={{0,16},{32,48},{64,80},{96,112},{4,68},{12,76},{20,84},{28,92},{1,... | collective-permute-start | bytes 786440 | tf_op jit(solution)/shard_map/first_share/ppermute | solution.py:224
  54.1 2.0 %collective-permute-start.8 = (f32[512,128]{1,0:T(8,128)}, f32[512,128]{1,0:T(8,128)}, u32[]{:S(2)}, u32[]{:S(2)}) collective-permute-start(f32[512,128]{1,0:T(8,128)} %add_select_fusion.7), channel_id=1, source_target_pairs={{0,8},{32,40},{64,72},{96,104},{4,36},{12,44},{20,52},{28,60},{1,9... | collective-permute-start | bytes 786440 | tf_op jit(solution)/shard_map/first_share/ppermute | solution.py:224
  56.9 2.0 %collective-permute-start.9 = (f32[512,128]{1,0:T(8,128)}, f32[512,128]{1,0:T(8,128)}, u32[]{:S(2)}, u32[]{:S(2)}) collective-permute-start(f32[512,128]{1,0:T(8,128)} %add_select_fusion.7), channel_id=1, source_target_pairs={{0,24},{32,56},{64,88},{96,120},{4,100},{12,108},{20,116},{28,124}... | collective-permute-start | bytes 786440 | tf_op jit(solution)/shard_map/first_share/ppermute | solution.py:224
  58.9 2.0 %collective-permute-start.22 = (f32[512,128]{1,0:T(8,128)}, f32[512,128]{1,0:T(8,128)}, u32[]{:S(2)}, u32[]{:S(2)}) collective-permute-start(f32[512,128]{1,0:T(8,128)} %add_select_fusion.5), channel_id=1, source_target_pairs={{0,16},{32,48},{64,80},{96,112},{4,68},{12,76},{20,84},{28,92},{1,... | collective-permute-start | bytes 786440 | tf_op jit(solution)/shard_map/first_share/ppermute | solution.py:224
  61.5 1.7 slice.138
  63.2 1.7 slice.156
  65.5 1.7 copy.17
  68.3 1.6 dynamic-slice_reduce_fusion
  71.1 1.4 concatenate.25.flags
  72.5 1.3 collective-permute-start.20
  73.8 1.3 collective-permute-start.21
  76.4 1.3 collective-permute-start.34
  77.7 1.3 collective-permute-start.32
  79.0 1.3 collective-permute-start.33
  84.6 3.7 %first_lower.1 = f32[128,512]{1,0:T(8,128)S(1)} custom-call(f32[512,512]{1,0:T(8,128)S(1)} %get-tuple-element.20.near, f32[512,128]{1,0:T(8,128)S(1)} %get-tuple-element.41.refs_0_, f32[512,128]{1,0:T(8,128)S(1)} %get-tuple-element.40.refs_1_.refs_3_, f32[512,128]{1,0:T(8,128)S(1)} %get-tuple-element.39.refs_2_, s32[1]{0:T(128)} %bitcast.13.refs_3_), custom_call_target="tpu_custom_call" | custom-call | tf_op jit(solution)/shard_map/first_lower/pallas_call | solution.py:204
  88.2 1.3 collective-permute-start.12
  89.6 3.6 %collective-permute-done.12 = f32[64,512]{1,0:T(8,128)S(1)} collective-permute-done((f32[64,512]{1,0:T(8,128)S(1)}, f32[64,512]{1,0:T(8,128)S(1)}, u32[]{:S(2)}, u32[]{:S(2)}) %collective-permute-start.12) | collective-permute-done | bytes 131104 | tf_op jit(solution)/shard_map/first_lower/ppermute | solution.py:262
  93.2 1.4 collective-permute-start.14
  94.7 3.8 %collective-permute-start.13 = (f32[64,512]{1,0:T(8,128)S(1)}, f32[64,512]{1,0:T(8,128)S(1)}, u32[]{:S(2)}, u32[]{:S(2)}) collective-permute-start(f32[64,512]{1,0:T(8,128)S(1)} %get-tuple-element.56), channel_id=1, source_target_pairs={{0,1},{1,2},{4,5},{5,6},{8,9},{9,10},{12,13},{13,14},{16,17},{17,1... | collective-permute-start | bytes 393224 | tf_op jit(solution)/shard_map/first_lower/ppermute | solution.py:264
  98.6 5.3 %collective-permute-start.15 = (f32[64,512]{1,0:T(8,128)S(1)}, f32[64,512]{1,0:T(8,128)S(1)}, u32[]{:S(2)}, u32[]{:S(2)}) collective-permute-start(f32[64,512]{1,0:T(8,128)S(1)} %broadcast_select_fusion.10), channel_id=1, source_target_pairs={{0,3},{3,2},{4,7},{7,6},{8,11},{11,10},{12,15},{15,14},{16,19},{19... | collective-permute-start | bytes 393224 | tf_op jit(solution)/shard_map/first_lower/ppermute | solution.py:265
  103.9 2.3 %collective-permute-done.15 = f32[64,512]{1,0:T(8,128)S(1)} collective-permute-done((f32[64,512]{1,0:T(8,128)S(1)}, f32[64,512]{1,0:T(8,128)S(1)}, u32[]{:S(2)}, u32[]{:S(2)}) %collective-permute-start.15) | collective-permute-done | bytes 131104 | tf_op jit(solution)/shard_map/first_lower/ppermute | solution.py:265
  106.4 11.6 %first_update.1 = (f32[2,512,128]{2,1,0:T(8,128)S(1)}, f32[2,512,128]{2,1,0:T(8,128)S(1)}, f32[512,128]{1,0:T(8,128)S(1)}) custom-call(s32[10]{0:T(128)S(1)} %copy-done.5, f32[2,512,128]{2,1,0:T(8,128)S(1)} %bitcast.79, f32[2,512,128]{2,1,0:T(8,128)S(1)} %bitcast.81, f32[512,128]{1,0:T(8,128)S(1)} %copy-done.2, f32[128,512]{1,0:T(8,128)S(1)} %maximum_select_fusion.1.lowt, ...), custom_call_target="tpu_custom_call" | custom-call | tf_op jit(solution)/shard_map/first_update/pallas_call | solution.py:168
  118.0 1.3 collective-permute-start.36
  121.2 1.3 collective-permute-start.39
  122.6 1.3 collective-permute-start.37
  123.9 1.3 collective-permute-start.38
  125.2 1.3 collective-permute-start.48
  127.7 1.3 collective-permute-start.42
  129.0 1.3 collective-permute-start.40
  130.3 1.3 collective-permute-start.41
  131.6 1.3 collective-permute-start.26
  134.3 3.7 %collective-permute-start.51 = (f32[1024,128]{1,0:T(8,128)S(1)}, f32[1024,128]{1,0:T(8,128)S(1)}, u32[]{:S(2)}, u32[]{:S(2)}) collective-permute-start(f32[1024,128]{1,0:T(8,128)S(1)} %fusion), channel_id=1, source_target_pairs={{0,64},{4,20},{1,65},{5,21},{2,66},{6,22},{3,67},{7,23}} | collective-permute-start | bytes 1572872 | tf_op jit(solution)/shard_map/second_share/ppermute | solution.py:224
  138.1 1.3 collective-permute-start.49
  139.4 1.9 %collective-permute-start.50 = (f32[1024,128]{1,0:T(8,128)S(1)}, f32[1024,128]{1,0:T(8,128)S(1)}, u32[]{:S(2)}, u32[]{:S(2)}) collective-permute-start(f32[1024,128]{1,0:T(8,128)S(1)} %fusion), channel_id=1, source_target_pairs={{0,96},{4,28},{1,97},{5,29},{2,98},{6,30},{3,99},{7,31}} | collective-permute-start | bytes 1572872 | tf_op jit(solution)/shard_map/second_share/ppermute | solution.py:224
  142.1 6.2 %collective-permute-start.27 = (f32[256,128]{1,0:T(8,128)S(1)}, f32[256,128]{1,0:T(8,128)S(1)}, u32[]{:S(2)}, u32[]{:S(2)}) collective-permute-start(f32[256,128]{1,0:T(8,128)S(1)} %get-tuple-element.30), channel_id=1, source_target_pairs={{1,0},{0,3},{5,4},{4,7},{9,8},{8,11},{13,12},{12,15},{17,16},{16,1... | collective-permute-start | bytes 393224 | tf_op jit(solution)/shard_map/second_share/ppermute | solution.py:265
  148.4 3.5 %second_lower.1 = f32[128,512]{1,0:T(8,128)S(1)} custom-call(f32[512,512]{1,0:T(8,128)S(1)} %get-tuple-element.19.near, f32[512,128]{1,0:T(8,128)S(1)} %get-tuple-element.28.refs_0_, f32[512,128]{1,0:T(8,128)S(1)} %pad_maximum_fusion.4.refs_1_, f32[512,128]{1,0:T(8,128)S(1)} %get-tuple-element.27.refs_2_, f32[512,128]{1,0:T(8,128)S(1)} %get-tuple-element.40.refs_1_.refs_3_, ...), custom_call_target="tpu_custom_call" | custom-call | tf_op jit(solution)/shard_map/second_lower/pallas_call | solution.py:204
  152.7 1.3 collective-permute-start.54
  154.0 1.3 collective-permute-start.52
  155.4 1.3 collective-permute-start.53
  158.8 5.2 %collective-permute-done.46 = f32[64,512]{1,0:T(8,128)S(1)} collective-permute-done((f32[64,512]{1,0:T(8,128)S(1)}, f32[64,512]{1,0:T(8,128)S(1)}, u32[]{:S(2)}, u32[]{:S(2)}) %collective-permute-start.46) | collective-permute-done | bytes 131104 | tf_op jit(solution)/shard_map/second_lower/ppermute | solution.py:263
  164.0 1.9 %collective-permute-start.47 = (f32[64,512]{1,0:T(8,128)S(1)}, f32[64,512]{1,0:T(8,128)S(1)}, u32[]{:S(2)}, u32[]{:S(2)}) collective-permute-start(f32[64,512]{1,0:T(8,128)S(1)} %broadcast_select_fusion.12), channel_id=1, source_target_pairs={{1,0},{0,3},{5,4},{4,7},{9,8},{8,11},{13,12},{12,15},{17,16},{16,1... | collective-permute-start | bytes 393224 | tf_op jit(solution)/shard_map/second_lower/ppermute | solution.py:265
  166.6 4.3 %collective-permute-done.47 = f32[64,512]{1,0:T(8,128)S(1)} collective-permute-done((f32[64,512]{1,0:T(8,128)S(1)}, f32[64,512]{1,0:T(8,128)S(1)}, u32[]{:S(2)}, u32[]{:S(2)}) %collective-permute-start.47) | collective-permute-done | bytes 131104 | tf_op jit(solution)/shard_map/second_lower/ppermute | solution.py:265
  171.7 15.7 %second_update.1 = (f32[2,512,128]{2,1,0:T(8,128)}, f32[2,512,128]{2,1,0:T(8,128)}, f32[512,128]{1,0:T(8,128)}) custom-call(s32[10]{0:T(128)S(1)} %copy-done.4, f32[2,512,128]{2,1,0:T(8,128)S(1)} %get-tuple-element.7.cu, f32[2,512,128]{2,1,0:T(8,128)S(1)} %get-tuple-element.8.cv, f32[512,128]{1,0:T(8,128)S(1)} %maximum_select_fusion.2.lu, ...), custom_call_target="tpu_custom_call" | custom-call | tf_op jit(solution)/shard_map/second_update/pallas_call | solution.py:168
  (133 shorter events, 25.7 us)
Async XLA Ops:
  0.6 16.0 %copy-start = (f32[1,1,2,1,512,128]{5,4,3,2,1,0:T(8,128)S(1)}, f32[1,1,2,1,512,128]{5,4,3,2,1,0:T(8,128)}, u32[]{:S(2)}) copy-start(f32[1,1,2,1,512,128]{5,4,3,2,1,0:T(8,128)} %param.5) | copy-start | bytes 1572868
  2.5 24.4 %collective-permute-start.16 = (f32[512,128]{1,0:T(8,128)}, f32[512,128]{1,0:T(8,128)}, u32[]{:S(2)}, u32[]{:S(2)}) collective-permute-start(f32[512,128]{1,0:T(8,128)} %get-tuple-element.38), channel_id=1, source_target_pairs={{0,4},{1,5},{2,6},{3,7}} | collective-permute-start | bytes 786440 | tf_op jit(solution)/shard_map/first_share/ppermute | solution.py:234
  5.4 11.1 %collective-permute-start = (f32[256,128]{1,0:T(8,128)S(1)}, f32[256,128]{1,0:T(8,128)S(1)}, u32[]{:S(2)}, u32[]{:S(2)}) collective-permute-start(f32[256,128]{1,0:T(8,128)S(1)} %get-tuple-element.44), channel_id=1, source_target_pairs={{0,1},{4,5},{8,9},{12,13},{16,17},{20,21},{24,25},{28,29},{32,33},... | collective-permute-start | bytes 393224 | tf_op jit(solution)/shard_map/first_share/ppermute | solution.py:262
  9.5 7.1 %collective-permute-start.2 = (f32[256,128]{1,0:T(8,128)S(1)}, f32[256,128]{1,0:T(8,128)S(1)}, u32[]{:S(2)}, u32[]{:S(2)}) collective-permute-start(f32[256,128]{1,0:T(8,128)S(1)} %get-tuple-element.45), channel_id=1, source_target_pairs={{0,3},{4,7},{8,11},{12,15},{16,19},{20,23},{24,27},{28,31},{32,35}... | collective-permute-start | bytes 393224 | tf_op jit(solution)/shard_map/first_share/ppermute | solution.py:263
  11.6 15.3 %collective-permute-start.4 = (f32[512,128]{1,0:T(8,128)S(1)}, f32[512,128]{1,0:T(8,128)}, u32[]{:S(2)}, u32[]{:S(2)}) collective-permute-start(f32[512,128]{1,0:T(8,128)S(1)} %get-tuple-element.39.refs_2_), channel_id=1, source_target_pairs={{0,4},{1,5},{2,6},{3,7}} | collective-permute-start | bytes 786440 | tf_op jit(solution)/shard_map/first_share/ppermute | solution.py:234
  15.3 24.6 %collective-permute-start.28 = (f32[512,128]{1,0:T(8,128)}, f32[512,128]{1,0:T(8,128)}, u32[]{:S(2)}, u32[]{:S(2)}) collective-permute-start(f32[512,128]{1,0:T(8,128)} %slice_bitcast_fusion.11), channel_id=1, source_target_pairs={{4,0},{5,1},{6,2},{7,3}} | collective-permute-start | bytes 786440 | tf_op jit(solution)/shard_map/pivot_share/ppermute | solution.py:234
  16.6 5.7 %copy-start.7 = (f32[256,128]{1,0:T(8,128)}, f32[256,128]{1,0:T(8,128)S(1)}, u32[]{:S(2)}) copy-start(f32[256,128]{1,0:T(8,128)S(1)} %collective-permute-done.2) | copy-start | bytes 393220
  17.3 6.7 %collective-permute-start.1 = (f32[256,128]{1,0:T(8,128)}, f32[256,128]{1,0:T(8,128)}, u32[]{:S(2)}, u32[]{:S(2)}) collective-permute-start(f32[256,128]{1,0:T(8,128)} %get-tuple-element.42), channel_id=1, source_target_pairs={{0,1},{1,2},{4,5},{5,6},{8,9},{9,10},{12,13},{13,14},{16,17},{17,1... | collective-permute-start | bytes 393224 | tf_op jit(solution)/shard_map/first_share/ppermute | solution.py:264
  19.3 6.6 %collective-permute-start.3 = (f32[256,128]{1,0:T(8,128)}, f32[256,128]{1,0:T(8,128)}, u32[]{:S(2)}, u32[]{:S(2)}) collective-permute-start(f32[256,128]{1,0:T(8,128)} %get-tuple-element.43), channel_id=1, source_target_pairs={{0,3},{3,2},{4,7},{7,6},{8,11},{11,10},{12,15},{15,14},{16,19},{19... | collective-permute-start | bytes 393224 | tf_op jit(solution)/shard_map/first_share/ppermute | solution.py:265
  24.0 9.1 %copy-start.8 = (s32[3,1,32,2,1]{2,4,3,1,0:T(1,128)S(1)}, s32[3,1,32,2,1]{2,4,3,1,0:T(1,128)}, u32[]{:S(2)}) copy-start(s32[3,1,32,2,1]{2,4,3,1,0:T(1,128)} %param.9) | copy-start | bytes 2308
  24.1 18.4 %copy-start.1 = (f32[1,1,2,1,512,128]{5,4,3,2,1,0:T(8,128)S(1)}, f32[1,1,2,1,512,128]{5,4,3,2,1,0:T(8,128)}, u32[]{:S(2)}) copy-start(f32[1,1,2,1,512,128]{5,4,3,2,1,0:T(8,128)} %param.6) | copy-start | bytes 1572868
  27.8 13.4 %collective-permute-start.7 = (f32[512,128]{1,0:T(8,128)}, f32[512,128]{1,0:T(8,128)}, u32[]{:S(2)}, u32[]{:S(2)}) collective-permute-start(f32[512,128]{1,0:T(8,128)} %get-tuple-element.37), channel_id=1, source_target_pairs={{0,64},{4,20},{1,65},{5,21},{2,66},{6,22},{3,67},{7,23}} | collective-permute-start | bytes 786440 | tf_op jit(solution)/shard_map/first_share/ppermute | solution.py:224
  33.8 10.4 %collective-permute-start.5 = (f32[512,128]{1,0:T(8,128)}, f32[512,128]{1,0:T(8,128)}, u32[]{:S(2)}, u32[]{:S(2)}) collective-permute-start(f32[512,128]{1,0:T(8,128)} %get-tuple-element.37), channel_id=1, source_target_pairs={{0,32},{4,12},{1,33},{5,13},{2,34},{6,14},{3,35},{7,15}} | collective-permute-start | bytes 786440 | tf_op jit(solution)/shard_map/first_share/ppermute | solution.py:224
  35.8 10.4 %collective-permute-start.6 = (f32[512,128]{1,0:T(8,128)}, f32[512,128]{1,0:T(8,128)}, u32[]{:S(2)}, u32[]{:S(2)}) collective-permute-start(f32[512,128]{1,0:T(8,128)} %get-tuple-element.37), channel_id=1, source_target_pairs={{0,96},{4,28},{1,97},{5,29},{2,98},{6,30},{3,99},{7,31}} | collective-permute-start | bytes 786440 | tf_op jit(solution)/shard_map/first_share/ppermute | solution.py:224
  38.4 17.7 %copy-start.6 = (f32[512,128]{1,0:T(8,128)S(1)}, f32[512,128]{1,0:T(8,128)}, u32[]{:S(2)}) copy-start(f32[512,128]{1,0:T(8,128)} %get-tuple-element.35) | copy-start | bytes 786436
  38.4 11.7 %collective-permute-start.19 = (f32[512,128]{1,0:T(8,128)}, f32[512,128]{1,0:T(8,128)S(1)}, u32[]{:S(2)}, u32[]{:S(2)}) collective-permute-start(f32[512,128]{1,0:T(8,128)} %get-tuple-element.35), channel_id=1, source_target_pairs={{0,64},{4,20},{1,65},{5,21},{2,66},{6,22},{3,67},{7,23}} | collective-permute-start | bytes 786440 | tf_op jit(solution)/shard_map/first_share/ppermute | solution.py:224
  39.9 12.3 %collective-permute-start.17 = (f32[512,128]{1,0:T(8,128)}, f32[512,128]{1,0:T(8,128)S(1)}, u32[]{:S(2)}, u32[]{:S(2)}) collective-permute-start(f32[512,128]{1,0:T(8,128)} %get-tuple-element.35), channel_id=1, source_target_pairs={{0,32},{4,12},{1,33},{5,13},{2,34},{6,14},{3,35},{7,15}} | collective-permute-start | bytes 786440 | tf_op jit(solution)/shard_map/first_share/ppermute | solution.py:224
  41.2 13.0 %collective-permute-start.18 = (f32[512,128]{1,0:T(8,128)}, f32[512,128]{1,0:T(8,128)S(1)}, u32[]{:S(2)}, u32[]{:S(2)}) collective-permute-start(f32[512,128]{1,0:T(8,128)} %get-tuple-element.35), channel_id=1, source_target_pairs={{0,96},{4,28},{1,97},{5,29},{2,98},{6,30},{3,99},{7,31}} | collective-permute-start | bytes 786440 | tf_op jit(solution)/shard_map/first_share/ppermute | solution.py:224
  44.2 12.7 %collective-permute-start.31 = (f32[512,128]{1,0:T(8,128)}, f32[512,128]{1,0:T(8,128)}, u32[]{:S(2)}, u32[]{:S(2)}) collective-permute-start(f32[512,128]{1,0:T(8,128)} %broadcast_select_fusion.2), channel_id=1, source_target_pairs={{0,64},{4,20},{1,65},{5,21},{2,66},{6,22},{3,67},{7,23}} | collective-permute-start | bytes 786440 | tf_op jit(solution)/shard_map/pivot_share/ppermute | solution.py:224
  46.2 12.7 %collective-permute-start.29 = (f32[512,128]{1,0:T(8,128)}, f32[512,128]{1,0:T(8,128)}, u32[]{:S(2)}, u32[]{:S(2)}) collective-permute-start(f32[512,128]{1,0:T(8,128)} %broadcast_select_fusion.2), channel_id=1, source_target_pairs={{0,32},{4,12},{1,33},{5,13},{2,34},{6,14},{3,35},{7,15}} | collective-permute-start | bytes 786440 | tf_op jit(solution)/shard_map/pivot_share/ppermute | solution.py:224
  50.2 22.3 %collective-permute-start.30 = (f32[512,128]{1,0:T(8,128)}, f32[512,128]{1,0:T(8,128)}, u32[]{:S(2)}, u32[]{:S(2)}) collective-permute-start(f32[512,128]{1,0:T(8,128)} %broadcast_select_fusion.2), channel_id=1, source_target_pairs={{0,96},{4,28},{1,97},{5,29},{2,98},{6,30},{3,99},{7,31}} | collective-permute-start | bytes 786440 | tf_op jit(solution)/shard_map/pivot_share/ppermute | solution.py:224
  52.1 21.6 %collective-permute-start.10 = (f32[512,128]{1,0:T(8,128)}, f32[512,128]{1,0:T(8,128)}, u32[]{:S(2)}, u32[]{:S(2)}) collective-permute-start(f32[512,128]{1,0:T(8,128)} %add_select_fusion.7), channel_id=1, source_target_pairs={{0,16},{32,48},{64,80},{96,112},{4,68},{12,76},{20,84},{28,92},{1,... | collective-permute-start | bytes 786440 | tf_op jit(solution)/shard_map/first_share/ppermute | solution.py:224
  54.1 22.2 %collective-permute-start.8 = (f32[512,128]{1,0:T(8,128)}, f32[512,128]{1,0:T(8,128)}, u32[]{:S(2)}, u32[]{:S(2)}) collective-permute-start(f32[512,128]{1,0:T(8,128)} %add_select_fusion.7), channel_id=1, source_target_pairs={{0,8},{32,40},{64,72},{96,104},{4,36},{12,44},{20,52},{28,60},{1,9... | collective-permute-start | bytes 786440 | tf_op jit(solution)/shard_map/first_share/ppermute | solution.py:224
  56.9 20.8 %collective-permute-start.9 = (f32[512,128]{1,0:T(8,128)}, f32[512,128]{1,0:T(8,128)}, u32[]{:S(2)}, u32[]{:S(2)}) collective-permute-start(f32[512,128]{1,0:T(8,128)} %add_select_fusion.7), channel_id=1, source_target_pairs={{0,24},{32,56},{64,88},{96,120},{4,100},{12,108},{20,116},{28,124}... | collective-permute-start | bytes 786440 | tf_op jit(solution)/shard_map/first_share/ppermute | solution.py:224
  58.9 20.1 %collective-permute-start.22 = (f32[512,128]{1,0:T(8,128)}, f32[512,128]{1,0:T(8,128)}, u32[]{:S(2)}, u32[]{:S(2)}) collective-permute-start(f32[512,128]{1,0:T(8,128)} %add_select_fusion.5), channel_id=1, source_target_pairs={{0,16},{32,48},{64,80},{96,112},{4,68},{12,76},{20,84},{28,92},{1,... | collective-permute-start | bytes 786440 | tf_op jit(solution)/shard_map/first_share/ppermute | solution.py:224
  72.5 9.1 %collective-permute-start.20 = (f32[512,128]{1,0:T(8,128)}, f32[512,128]{1,0:T(8,128)S(1)}, u32[]{:S(2)}, u32[]{:S(2)}) collective-permute-start(f32[512,128]{1,0:T(8,128)} %add_select_fusion.5), channel_id=1, source_target_pairs={{0,8},{32,40},{64,72},{96,104},{4,36},{12,44},{20,52},{28,60},{1,9... | collective-permute-start | bytes 786440 | tf_op jit(solution)/shard_map/first_share/ppermute | solution.py:224
  73.8 7.9 %collective-permute-start.21 = (f32[512,128]{1,0:T(8,128)}, f32[512,128]{1,0:T(8,128)S(1)}, u32[]{:S(2)}, u32[]{:S(2)}) collective-permute-start(f32[512,128]{1,0:T(8,128)} %add_select_fusion.5), channel_id=1, source_target_pairs={{0,24},{32,56},{64,88},{96,120},{4,100},{12,108},{20,116},{28,124}... | collective-permute-start | bytes 786440 | tf_op jit(solution)/shard_map/first_share/ppermute | solution.py:224
  76.4 7.0 %collective-permute-start.34 = (f32[512,128]{1,0:T(8,128)S(1)}, f32[512,128]{1,0:T(8,128)S(1)}, u32[]{:S(2)}, u32[]{:S(2)}) collective-permute-start(f32[512,128]{1,0:T(8,128)S(1)} %add_select_fusion.3), channel_id=1, source_target_pairs={{0,16},{32,48},{64,80},{96,112},{4,68},{12,76},{20,84},{28,92},{1,... | collective-permute-start | bytes 786440 | tf_op jit(solution)/shard_map/pivot_share/ppermute | solution.py:224
  77.7 6.7 %collective-permute-start.32 = (f32[512,128]{1,0:T(8,128)S(1)}, f32[512,128]{1,0:T(8,128)S(1)}, u32[]{:S(2)}, u32[]{:S(2)}) collective-permute-start(f32[512,128]{1,0:T(8,128)S(1)} %add_select_fusion.3), channel_id=1, source_target_pairs={{0,8},{32,40},{64,72},{96,104},{4,36},{12,44},{20,52},{28,60},{1,9... | collective-permute-start | bytes 786440 | tf_op jit(solution)/shard_map/pivot_share/ppermute | solution.py:224
  79.0 5.3 %collective-permute-start.33 = (f32[512,128]{1,0:T(8,128)S(1)}, f32[512,128]{1,0:T(8,128)S(1)}, u32[]{:S(2)}, u32[]{:S(2)}) collective-permute-start(f32[512,128]{1,0:T(8,128)S(1)} %add_select_fusion.3), channel_id=1, source_target_pairs={{0,24},{32,56},{64,88},{96,120},{4,100},{12,108},{20,116},{28,124}... | collective-permute-start | bytes 786440 | tf_op jit(solution)/shard_map/pivot_share/ppermute | solution.py:224
  81.6 2.9 %collective-permute-start.11 = (f32[512,128]{1,0:T(8,128)S(1)}, f32[512,128]{1,0:T(8,128)S(1)}, u32[]{:S(2)}, u32[]{:S(2)}) collective-permute-start(f32[512,128]{1,0:T(8,128)S(1)} %add_select_fusion.6), channel_id=1, source_target_pairs={{0,4},{4,0},{8,12},{12,8},{16,20},{20,16},{24,28},{28,24},{32,36},... | collective-permute-start | bytes 786440 | tf_op jit(solution)/shard_map/first_share/ppermute | solution.py:253
  82.8 6.8 %collective-permute-start.23 = (f32[512,128]{1,0:T(8,128)S(1)}, f32[512,128]{1,0:T(8,128)S(1)}, u32[]{:S(2)}, u32[]{:S(2)}) collective-permute-start(f32[512,128]{1,0:T(8,128)S(1)} %add_select_fusion.4), channel_id=1, source_target_pairs={{0,4},{4,0},{8,12},{12,8},{16,20},{20,16},{24,28},{28,24},{32,36},... | collective-permute-start | bytes 786440 | tf_op jit(solution)/shard_map/first_share/ppermute | solution.py:253
  84.4 10.2 %collective-permute-start.35 = (f32[512,128]{1,0:T(8,128)S(1)}, f32[512,128]{1,0:T(8,128)S(1)}, u32[]{:S(2)}, u32[]{:S(2)}) collective-permute-start(f32[512,128]{1,0:T(8,128)S(1)} %add_select_fusion.2), channel_id=1, source_target_pairs={{0,4},{4,0},{8,12},{12,8},{16,20},{20,16},{24,28},{28,24},{32,36},... | collective-permute-start | bytes 786440 | tf_op jit(solution)/shard_map/pivot_share/ppermute | solution.py:253
  88.2 5.0 %collective-permute-start.12 = (f32[64,512]{1,0:T(8,128)S(1)}, f32[64,512]{1,0:T(8,128)S(1)}, u32[]{:S(2)}, u32[]{:S(2)}) collective-permute-start(f32[64,512]{1,0:T(8,128)S(1)} %slice.158), channel_id=1, source_target_pairs={{0,1},{4,5},{8,9},{12,13},{16,17},{20,21},{24,25},{28,29},{32,33},... | collective-permute-start | bytes 393224 | tf_op jit(solution)/shard_map/first_lower/ppermute | solution.py:262
  93.2 5.3 %collective-permute-start.14 = (f32[64,512]{1,0:T(8,128)S(1)}, f32[64,512]{1,0:T(8,128)S(1)}, u32[]{:S(2)}, u32[]{:S(2)}) collective-permute-start(f32[64,512]{1,0:T(8,128)S(1)} %get-tuple-element.57), channel_id=1, source_target_pairs={{0,3},{4,7},{8,11},{12,15},{16,19},{20,23},{24,27},{28,31},{32,35}... | collective-permute-start | bytes 393224 | tf_op jit(solution)/shard_map/first_lower/ppermute | solution.py:263
  94.7 11.6 %copy-start.2 = (f32[512,128]{1,0:T(8,128)S(1)}, f32[512,128]{1,0:T(8,128)}, u32[]{:S(2)}) copy-start(f32[512,128]{1,0:T(8,128)} %get-tuple-element.36.lu) | copy-start | bytes 786436
  94.7 11.6 %copy-start.3 = (f32[1,512,96]{1,2,0:T(8,128)S(1)}, f32[1,512,96]{1,2,0:T(8,128)}, u32[]{:S(2)}) copy-start(f32[1,512,96]{1,2,0:T(8,128)} %copy.17) | copy-start | bytes 589828
  94.7 11.6 %copy-start.5 = (s32[10]{0:T(128)S(1)}, s32[10]{0:T(128)}, u32[]{:S(2)}) copy-start(s32[10]{0:T(128)} %concatenate.25.flags) | copy-start | bytes 124
  94.7 9.2 %collective-permute-start.13 = (f32[64,512]{1,0:T(8,128)S(1)}, f32[64,512]{1,0:T(8,128)S(1)}, u32[]{:S(2)}, u32[]{:S(2)}) collective-permute-start(f32[64,512]{1,0:T(8,128)S(1)} %get-tuple-element.56), channel_id=1, source_target_pairs={{0,1},{1,2},{4,5},{5,6},{8,9},{9,10},{12,13},{13,14},{16,17},{17,1... | collective-permute-start | bytes 393224 | tf_op jit(solution)/shard_map/first_lower/ppermute | solution.py:264
  98.6 7.7 %collective-permute-start.15 = (f32[64,512]{1,0:T(8,128)S(1)}, f32[64,512]{1,0:T(8,128)S(1)}, u32[]{:S(2)}, u32[]{:S(2)}) collective-permute-start(f32[64,512]{1,0:T(8,128)S(1)} %broadcast_select_fusion.10), channel_id=1, source_target_pairs={{0,3},{3,2},{4,7},{7,6},{8,11},{11,10},{12,15},{15,14},{16,19},{19... | collective-permute-start | bytes 393224 | tf_op jit(solution)/shard_map/first_lower/ppermute | solution.py:265
  118.0 3.2 %collective-permute-start.36 = (f32[256,128]{1,0:T(8,128)S(1)}, f32[256,128]{1,0:T(8,128)S(1)}, u32[]{:S(2)}, u32[]{:S(2)}) collective-permute-start(f32[256,128]{1,0:T(8,128)S(1)} %slice.146), channel_id=1, source_target_pairs={{4,0},{5,1},{6,2},{7,3}} | collective-permute-start | bytes 393224 | tf_op jit(solution)/shard_map/second_share/ppermute | solution.py:234
  119.3 20.1 %collective-permute-start.24 = (f32[256,128]{1,0:T(8,128)S(1)}, f32[256,128]{1,0:T(8,128)S(1)}, u32[]{:S(2)}, u32[]{:S(2)}) collective-permute-start(f32[256,128]{1,0:T(8,128)S(1)} %get-tuple-element.31), channel_id=1, source_target_pairs={{1,2},{5,6},{9,10},{13,14},{17,18},{21,22},{25,26},{29,30},{33,34}... | collective-permute-start | bytes 393224 | tf_op jit(solution)/shard_map/second_share/ppermute | solution.py:262
  121.2 5.3 %collective-permute-start.39 = (f32[256,128]{1,0:T(8,128)S(1)}, f32[256,128]{1,0:T(8,128)S(1)}, u32[]{:S(2)}, u32[]{:S(2)}) collective-permute-start(f32[256,128]{1,0:T(8,128)S(1)} %slice_select_fusion), channel_id=1, source_target_pairs={{0,64},{4,20},{1,65},{5,21},{2,66},{6,22},{3,67},{7,23}} | collective-permute-start | bytes 393224 | tf_op jit(solution)/shard_map/second_share/ppermute | solution.py:224
  122.6 4.0 %collective-permute-start.37 = (f32[256,128]{1,0:T(8,128)S(1)}, f32[256,128]{1,0:T(8,128)S(1)}, u32[]{:S(2)}, u32[]{:S(2)}) collective-permute-start(f32[256,128]{1,0:T(8,128)S(1)} %slice_select_fusion), channel_id=1, source_target_pairs={{0,32},{4,12},{1,33},{5,13},{2,34},{6,14},{3,35},{7,15}} | collective-permute-start | bytes 393224 | tf_op jit(solution)/shard_map/second_share/ppermute | solution.py:224
  123.9 3.8 %collective-permute-start.38 = (f32[256,128]{1,0:T(8,128)S(1)}, f32[256,128]{1,0:T(8,128)S(1)}, u32[]{:S(2)}, u32[]{:S(2)}) collective-permute-start(f32[256,128]{1,0:T(8,128)S(1)} %slice_select_fusion), channel_id=1, source_target_pairs={{0,96},{4,28},{1,97},{5,29},{2,98},{6,30},{3,99},{7,31}} | collective-permute-start | bytes 393224 | tf_op jit(solution)/shard_map/second_share/ppermute | solution.py:224
  125.2 9.0 %collective-permute-start.48 = (f32[1024,128]{1,0:T(8,128)S(1)}, f32[1024,128]{1,0:T(8,128)S(1)}, u32[]{:S(2)}, u32[]{:S(2)}) collective-permute-start(f32[1024,128]{1,0:T(8,128)S(1)} %slice_bitcast_fusion.2), channel_id=1, source_target_pairs={{4,0},{5,1},{6,2},{7,3}} | collective-permute-start | bytes 1572872 | tf_op jit(solution)/shard_map/second_share/ppermute | solution.py:234
  127.7 3.9 %collective-permute-start.42 = (f32[256,128]{1,0:T(8,128)S(1)}, f32[256,128]{1,0:T(8,128)S(1)}, u32[]{:S(2)}, u32[]{:S(2)}) collective-permute-start(f32[256,128]{1,0:T(8,128)S(1)} %add_select_fusion.9), channel_id=1, source_target_pairs={{0,16},{32,48},{64,80},{96,112},{4,68},{12,76},{20,84},{28,92},{1,... | collective-permute-start | bytes 393224 | tf_op jit(solution)/shard_map/second_share/ppermute | solution.py:224
  129.0 4.0 %collective-permute-start.40 = (f32[256,128]{1,0:T(8,128)S(1)}, f32[256,128]{1,0:T(8,128)S(1)}, u32[]{:S(2)}, u32[]{:S(2)}) collective-permute-start(f32[256,128]{1,0:T(8,128)S(1)} %add_select_fusion.9), channel_id=1, source_target_pairs={{0,8},{32,40},{64,72},{96,104},{4,36},{12,44},{20,52},{28,60},{1,9... | collective-permute-start | bytes 393224 | tf_op jit(solution)/shard_map/second_share/ppermute | solution.py:224
  130.3 3.8 %collective-permute-start.41 = (f32[256,128]{1,0:T(8,128)S(1)}, f32[256,128]{1,0:T(8,128)S(1)}, u32[]{:S(2)}, u32[]{:S(2)}) collective-permute-start(f32[256,128]{1,0:T(8,128)S(1)} %add_select_fusion.9), channel_id=1, source_target_pairs={{0,24},{32,56},{64,88},{96,120},{4,100},{12,108},{20,116},{28,124}... | collective-permute-start | bytes 393224 | tf_op jit(solution)/shard_map/second_share/ppermute | solution.py:224
  131.6 9.7 %collective-permute-start.26 = (f32[256,128]{1,0:T(8,128)S(1)}, f32[256,128]{1,0:T(8,128)S(1)}, u32[]{:S(2)}, u32[]{:S(2)}) collective-permute-start(f32[256,128]{1,0:T(8,128)S(1)} %get-tuple-element.32), channel_id=1, source_target_pairs={{1,0},{5,4},{9,8},{13,12},{17,16},{21,20},{25,24},{29,28},{33,32},... | collective-permute-start | bytes 393224 | tf_op jit(solution)/shard_map/second_share/ppermute | solution.py:263
  134.1 7.9 %collective-permute-start.43 = (f32[256,128]{1,0:T(8,128)S(1)}, f32[256,128]{1,0:T(8,128)S(1)}, u32[]{:S(2)}, u32[]{:S(2)}) collective-permute-start(f32[256,128]{1,0:T(8,128)S(1)} %add_select_fusion.8), channel_id=1, source_target_pairs={{0,4},{4,0},{8,12},{12,8},{16,20},{20,16},{24,28},{28,24},{32,36},... | collective-permute-start | bytes 393224 | tf_op jit(solution)/shard_map/second_share/ppermute | solution.py:253
  134.3 17.6 %collective-permute-start.51 = (f32[1024,128]{1,0:T(8,128)S(1)}, f32[1024,128]{1,0:T(8,128)S(1)}, u32[]{:S(2)}, u32[]{:S(2)}) collective-permute-start(f32[1024,128]{1,0:T(8,128)S(1)} %fusion), channel_id=1, source_target_pairs={{0,64},{4,20},{1,65},{5,21},{2,66},{6,22},{3,67},{7,23}} | collective-permute-start | bytes 1572872 | tf_op jit(solution)/shard_map/second_share/ppermute | solution.py:224
  138.1 14.5 %collective-permute-start.49 = (f32[1024,128]{1,0:T(8,128)S(1)}, f32[1024,128]{1,0:T(8,128)S(1)}, u32[]{:S(2)}, u32[]{:S(2)}) collective-permute-start(f32[1024,128]{1,0:T(8,128)S(1)} %fusion), channel_id=1, source_target_pairs={{0,32},{4,12},{1,33},{5,13},{2,34},{6,14},{3,35},{7,15}} | collective-permute-start | bytes 1572872 | tf_op jit(solution)/shard_map/second_share/ppermute | solution.py:224
  139.4 13.2 %collective-permute-start.50 = (f32[1024,128]{1,0:T(8,128)S(1)}, f32[1024,128]{1,0:T(8,128)S(1)}, u32[]{:S(2)}, u32[]{:S(2)}) collective-permute-start(f32[1024,128]{1,0:T(8,128)S(1)} %fusion), channel_id=1, source_target_pairs={{0,96},{4,28},{1,97},{5,29},{2,98},{6,30},{3,99},{7,31}} | collective-permute-start | bytes 1572872 | tf_op jit(solution)/shard_map/second_share/ppermute | solution.py:224
  141.4 15.4 %collective-permute-start.25 = (f32[256,128]{1,0:T(8,128)S(1)}, f32[256,128]{1,0:T(8,128)S(1)}, u32[]{:S(2)}, u32[]{:S(2)}) collective-permute-start(f32[256,128]{1,0:T(8,128)S(1)} %get-tuple-element.29), channel_id=1, source_target_pairs={{1,2},{2,3},{5,6},{6,7},{9,10},{10,11},{13,14},{14,15},{17,18},{18... | collective-permute-start | bytes 393224 | tf_op jit(solution)/shard_map/second_share/ppermute | solution.py:264
  142.1 16.0 %collective-permute-start.27 = (f32[256,128]{1,0:T(8,128)S(1)}, f32[256,128]{1,0:T(8,128)S(1)}, u32[]{:S(2)}, u32[]{:S(2)}) collective-permute-start(f32[256,128]{1,0:T(8,128)S(1)} %get-tuple-element.30), channel_id=1, source_target_pairs={{1,0},{0,3},{5,4},{4,7},{9,8},{8,11},{13,12},{12,15},{17,16},{16,1... | collective-permute-start | bytes 393224 | tf_op jit(solution)/shard_map/second_share/ppermute | solution.py:265
  151.9 3.5 %collective-permute-start.44 = (f32[64,512]{1,0:T(8,128)S(1)}, f32[64,512]{1,0:T(8,128)S(1)}, u32[]{:S(2)}, u32[]{:S(2)}) collective-permute-start(f32[64,512]{1,0:T(8,128)S(1)} %slice.160), channel_id=1, source_target_pairs={{1,2},{5,6},{9,10},{13,14},{17,18},{21,22},{25,26},{29,30},{33,34}... | collective-permute-start | bytes 393224 | tf_op jit(solution)/shard_map/second_lower/ppermute | solution.py:262
  152.7 13.2 %collective-permute-start.54 = (f32[1024,128]{1,0:T(8,128)S(1)}, f32[1024,128]{1,0:T(8,128)S(1)}, u32[]{:S(2)}, u32[]{:S(2)}) collective-permute-start(f32[1024,128]{1,0:T(8,128)S(1)} %add_select_fusion.1), channel_id=1, source_target_pairs={{0,16},{32,48},{64,80},{96,112},{4,68},{12,76},{20,84},{28,92},{1,... | collective-permute-start | bytes 1572872 | tf_op jit(solution)/shard_map/second_share/ppermute | solution.py:224
  154.0 12.3 %collective-permute-start.52 = (f32[1024,128]{1,0:T(8,128)S(1)}, f32[1024,128]{1,0:T(8,128)S(1)}, u32[]{:S(2)}, u32[]{:S(2)}) collective-permute-start(f32[1024,128]{1,0:T(8,128)S(1)} %add_select_fusion.1), channel_id=1, source_target_pairs={{0,8},{32,40},{64,72},{96,104},{4,36},{12,44},{20,52},{28,60},{1,9... | collective-permute-start | bytes 1572872 | tf_op jit(solution)/shard_map/second_share/ppermute | solution.py:224
  155.4 10.9 %collective-permute-start.53 = (f32[1024,128]{1,0:T(8,128)S(1)}, f32[1024,128]{1,0:T(8,128)S(1)}, u32[]{:S(2)}, u32[]{:S(2)}) collective-permute-start(f32[1024,128]{1,0:T(8,128)S(1)} %add_select_fusion.1), channel_id=1, source_target_pairs={{0,24},{32,56},{64,88},{96,120},{4,100},{12,108},{20,116},{28,124}... | collective-permute-start | bytes 1572872 | tf_op jit(solution)/shard_map/second_share/ppermute | solution.py:224
  156.8 7.2 %collective-permute-start.46 = (f32[64,512]{1,0:T(8,128)S(1)}, f32[64,512]{1,0:T(8,128)S(1)}, u32[]{:S(2)}, u32[]{:S(2)}) collective-permute-start(f32[64,512]{1,0:T(8,128)S(1)} %get-tuple-element.49), channel_id=1, source_target_pairs={{1,0},{5,4},{9,8},{13,12},{17,16},{21,20},{25,24},{29,28},{33,32},... | collective-permute-start | bytes 393224 | tf_op jit(solution)/shard_map/second_lower/ppermute | solution.py:263
  158.1 8.4 %collective-permute-start.45 = (f32[64,512]{1,0:T(8,128)S(1)}, f32[64,512]{1,0:T(8,128)S(1)}, u32[]{:S(2)}, u32[]{:S(2)}) collective-permute-start(f32[64,512]{1,0:T(8,128)S(1)} %get-tuple-element.48), channel_id=1, source_target_pairs={{1,2},{2,3},{5,6},{6,7},{9,10},{10,11},{13,14},{14,15},{17,18},{18... | collective-permute-start | bytes 393224 | tf_op jit(solution)/shard_map/second_lower/ppermute | solution.py:264
  164.0 6.9 %collective-permute-start.47 = (f32[64,512]{1,0:T(8,128)S(1)}, f32[64,512]{1,0:T(8,128)S(1)}, u32[]{:S(2)}, u32[]{:S(2)}) collective-permute-start(f32[64,512]{1,0:T(8,128)S(1)} %broadcast_select_fusion.12), channel_id=1, source_target_pairs={{1,0},{0,3},{5,4},{4,7},{9,8},{8,11},{13,12},{12,15},{17,16},{16,1... | collective-permute-start | bytes 393224 | tf_op jit(solution)/shard_map/second_lower/ppermute | solution.py:265
  166.4 4.5 %collective-permute-start.55 = (f32[1024,128]{1,0:T(8,128)S(1)}, f32[1024,128]{1,0:T(8,128)S(1)}, u32[]{:S(2)}, u32[]{:S(2)}) collective-permute-start(f32[1024,128]{1,0:T(8,128)S(1)} %add_select_fusion), channel_id=1, source_target_pairs={{0,4},{4,0},{8,12},{12,8},{16,20},{20,16},{24,28},{28,24},{32,36},... | collective-permute-start | bytes 1572872 | tf_op jit(solution)/shard_map/second_share/ppermute | solution.py:253
  (1 other events, 0.6 us)

commit v2 on v1

v2 whole, which is shorter than its diff:
```python
import functools
import math
import jax
import jax.numpy as jnp
from jax import lax
from jax.experimental import pallas as pl
from jax.experimental.pallas import tpu as pltpu
from jax.sharding import PartitionSpec as P

F32 = jnp.float32
BF16 = jnp.bfloat16
NN = (((1,), (0,)), ((), ()))
NT = (((1,), (1,)), ((), ()))
TN = (((0,), (0,)), ((), ()))


def dot6(a, b, dims=NN):
    return lax.dot_general(a, b, dims, precision=lax.Precision.HIGHEST, preferred_element_type=F32)


def split(a):
    high = a.astype(BF16)
    return high, (a - high.astype(F32)).astype(BF16)


def dot1(a, b, dims=NN):
    return lax.dot_general(a, b, dims, preferred_element_type=F32)


def dot3(a, b, dims=NN):
    ah, al = a if isinstance(a, tuple) else split(a)
    bh, bl = b if isinstance(b, tuple) else split(b)
    return dot1(ah, bh, dims) + (dot1(ah, bl, dims) + dot1(al, bh, dims))


def iota(shape, axis):
    return lax.broadcasted_iota(jnp.int32, shape, axis)


def eliminate(grams, order):
    count = len(grams)
    lane8 = iota((8, 128), 1)
    row8 = iota((8, 128), 0)
    blocks = [[g[8 * b:8 * b + 8, :] for b in range(order // 8)] for g in grams]
    done = [[] for _ in grams]
    for step in range(order // 8):
        base = 8 * step
        panels, pivots_all = [], []
        for g in range(count):
            panel = blocks[g][step]
            cols = [jnp.broadcast_to(panel[:, base + c:base + c + 1], (8, 128)) for c in range(8)]
            inside = (lane8 >= base) & (lane8 < base + 8)
            work = jnp.where(inside, (lane8 - base == row8).astype(F32), panel)
            scale = jnp.zeros((8, 128), F32)
            for c in range(8):
                pivot = jnp.broadcast_to(cols[c][c:c + 1, :], (8, 128))
                inverse = 1.0 / pivot
                scale = jnp.where(row8 == c, inverse, scale)
                if c < 7:
                    factor = jnp.where(row8 > c, cols[c] * inverse, 0.0)
                    for d in range(c + 1, 8):
                        cols[d] = cols[d] - factor * jnp.broadcast_to(cols[d][c:c + 1, :], (8, 128))
                    work = work - factor * jnp.broadcast_to(work[c:c + 1, :], (8, 128))
            panels.append(work)
            pivots_all.append(scale)
        for g in range(count):
            work, scale = panels[g], pivots_all[g]
            done[g].append(work * jnp.sqrt(scale))
            if step + 1 < order // 8:
                update = dot6(work, work * scale, TN)
                inside = (lane8 >= base) & (lane8 < base + 8)
                for b in range(step + 1, order // 8):
                    blocks[g][b] = jnp.where(inside, 0.0, blocks[g][b]) - update[8 * b:8 * b + 8, :]
    outs = []
    for g in range(count):
        full = jnp.concatenate(done[g], axis=0)
        keep = iota((order, 128), 1) <= iota((order, 128), 0)
        outs.append(jnp.where(keep, full, 0.0))
    return outs


def wide_of(lead, up):
    weight = 1.0 / (8.0 * lead.shape[1])
    core = weight * dot3(lead[1], up, TN)
    return dot3(lead[0], core)


def series(pivot, start):
    eye = iota(pivot.shape, 0) == iota(pivot.shape, 1)
    rest = split(jnp.where(eye, 1.0, 0.0) - pivot * start)
    square = split(dot3(rest, rest))
    return rest, square, split(dot3(square, square))


def start_of(far, axis):
    eye = iota(far.shape, 0) == iota(far.shape, 1)
    return 1.0 / jnp.sum(jnp.where(eye, far, 0.0), axis=axis, keepdims=True)


def upper_kernel(panel, flags, near, *refs):
    if panel == 0:
        corner, own, out_a, out_b = refs
    else:
        corner, extra, own, out = refs
    tile, width = own.shape[1:]
    weight = 1.0 / (8.0 * tile)
    far = near[panel]
    low_rank = dot3(corner[0], corner[1], NT)
    if panel == 1:
        low_rank = low_rank - dot3(extra[0], extra[1], NT)
    parts = series(far + weight * low_rank, start_of(far, 0))
    lanes = iota((tile, width), 1)
    values = [own[s] for s in range(2)]
    if panel == 0:
        values = [jnp.where(lanes < flags[2 + s], values[s], 0.0) for s in range(2)]
    values = jnp.concatenate(values, axis=1)
    for part in parts[::-1]:
        values = values + dot3(part, values)
    values = values * start_of(far, 1)
    spare = corner[0] if panel == 0 else extra[0]
    first = jnp.where(flags[10] == panel, spare, values[:, :width])
    if panel == 0:
        out_a[...] = first
        out_b[...] = values[:, width:]
    else:
        out[0] = first
        out[1] = values[:, width:]


def lower_kernel(flags, near, up_a, up_b, ours, theirs, fresh_a, fresh_b, own_v, out):
    tile, width = own_v.shape[1:]
    weight = 1.0 / (8.0 * tile)
    left = flags[10] == 0
    even = flags[11] == 0
    far = jnp.where(left, near[0], near[1])
    up_u = jnp.where(even, up_a[...], up_b[...])
    up_v = jnp.where(even, ours[0], theirs[0])
    corner_u = jnp.where(even, theirs[0], ours[0])
    corner_v = jnp.where(even, theirs[1], ours[1])
    wide = jnp.where(even, fresh_a[0], fresh_b[0])
    one_u = jnp.where(left, up_u, corner_u)
    one_v = jnp.where(left, up_v, corner_v)
    two_u = jnp.where(left, 0.0, wide)
    start = start_of(far, 0)
    low_rank = dot3(one_u, one_v, NT) - dot3(two_u, up_v, NT)
    values = own_v[0].T * start
    for part in series(far + weight * low_rank, start):
        values = values + dot3(values, part)
    out[...] = values


def wide_kernel(flags, lead, up_a, up_b, ours, theirs, wide, pack):
    even = flags[11] == 0
    near_up = jnp.where(even, up_a[...], up_b[...])
    far_up = jnp.where(even, up_b[...], up_a[...])
    first = wide_of(lead, near_up)
    wide[0] = first
    wide[1] = wide_of(lead, far_up)
    pack[0] = first
    pack[1] = jnp.where(even, ours[0], theirs[0])


def panel_kernel(order, first, flags, cu, cv, *refs):
    if first:
        wide, ours, theirs, st, nu, nv, pack, ortho, factor = refs
    else:
        lead, ours, theirs, lowt, st, nu, nv, ortho, factor = refs
    tile, width = cu.shape[1:]
    root = math.sqrt(tile)
    lanes = iota((tile, width), 1)
    spare = jnp.zeros((width - order, tile), F32)
    row_g = iota((order, width), 0)
    lane_g = iota((order, width), 1)
    eye = (row_g == lane_g).astype(F32)
    even = flags[11] == 0
    full_us, full_vs, bases, grams, units = [], [], [], [], []
    sketch = st[...]
    for s in range(2):
        own_u = cu[s]
        if first:
            own_u = jnp.where(lanes < flags[2 + s], own_u, 0.0)
            side = wide[s]
            up_v = jnp.where(even, ours[s], theirs[s])
        else:
            side = wide_of(lead, jnp.where(even, ours[s], theirs[s]))
            up_v = jnp.where(even, theirs[s], ours[s])
        full_u = jnp.concatenate([own_u, -side], axis=1)
        full_v = jnp.concatenate([cv[s], up_v], axis=1)
        projected = dot6(sketch, full_v)
        basis = dot6(projected, full_u, NT)
        basis = jnp.where(iota((order, tile), 0) < flags[s], basis, 0.0)
        basis = jnp.concatenate([basis, spare], axis=0)
        unit = jnp.where((row_g == lane_g) & (row_g >= flags[s]), 1.0, 0.0)
        grams.append(dot6(basis[:order], basis, NT) + unit)
        full_us.append(full_u)
        full_vs.append(full_v)
        bases.append(basis)
        units.append(unit)
    inverses = eliminate(grams, order)
    defect = jnp.zeros((), F32)
    for s in range(2):
        once = dot6(inverses[s], bases[s])
        ortho[s, :order] = once
        ortho[s, order:] = spare
        gram = dot6(once, jnp.concatenate([once, spare], axis=0), NT) + units[s]
        factor[s] = gram
        off = gram - eye
        defect = defect + jnp.where(flags[6 + s] == 1, jnp.sum(off * off), 0.0)
    near = defect < 1e-6

    @pl.when(near)
    def _():
        for s in range(2):
            off = factor[s] - eye
            half = jnp.where(lane_g < row_g, off, jnp.where(lane_g == row_g, 0.5 * off, 0.0))
            once = ortho[s]
            ortho[s, :order] = once[:order] - dot1(half.astype(BF16), once.astype(BF16))

    @pl.when(jnp.logical_not(near))
    def _():
        again = eliminate([factor[0], factor[1]], order)
        for s in range(2):
            ortho[s, :order] = dot6(again[s], ortho[s])

    for s in range(2):
        basis = ortho[s]
        back = dot3(basis, full_us[s])
        fresh_v = dot3(full_vs[s], back, NT) * (1.0 / root)
        fresh_u = basis.T * root
        keep_u = cu[s]
        keep_v = cv[s]
        if first:
            keep_u = jnp.where(lanes < flags[2 + s], keep_u, 0.0)
            keep_v = jnp.where(lanes < flags[2 + s], keep_v, 0.0)
        elif s == 0:
            keep_v = jnp.where(flags[8] == 1, lowt[...].T, keep_v)
            keep_u = jnp.where(flags[9] == 1, 0.0, keep_u)
            keep_v = jnp.where(flags[9] == 1, 0.0, keep_v)
        chosen = flags[6 + s] == 1
        new_u = jnp.where(chosen, fresh_u, keep_u)
        new_v = jnp.where(chosen, fresh_v, keep_v)
        nu[s] = new_u
        nv[s] = new_v
        if first and s == 0:
            pack[0] = new_u
            pack[1] = new_v


def call(kernel, shapes, flags, *values, scratch=()):
    vmem = pl.BlockSpec(memory_space=pltpu.VMEM)
    shapes = tuple(jax.ShapeDtypeStruct(shape, F32) for shape in shapes)
    out = pl.pallas_call(
        kernel,
        out_shape=shapes,
        in_specs=[pl.BlockSpec(memory_space=pltpu.SMEM)] + [vmem] * len(values),
        out_specs=(vmem,) * len(shapes),
        scratch_shapes=list(scratch),
        compiler_params=pltpu.CompilerParams(vmem_limit_bytes=40 * 1024 * 1024),
    )(flags, *values)
    return out if len(out) > 1 else out[0]


Z_COUNT = 4
X_COUNT = 4
COLS = 4


def row_of(z, x, core):
    return (z * X_COUNT + x) * 2 + core


def fan_out(value, axis, pair_sets):
    total = None
    for pairs in pair_sets:
        moved = lax.ppermute(value, axis, pairs)
        total = moved if total is None else total + moved
    return total


def share_planes(mine, row):
    core = row % 2
    x = (row // 2) % X_COUNT
    z = row // (2 * X_COUNT)
    first = fan_out(
        mine,
        "row",
        [[(row_of(0, 0, 0), row_of(k, 0, 0)), (row_of(0, 0, 1), row_of(0, k, 1))] for k in (1, 3, 2)],
    )
    held = jnp.where(row < 2, mine, first)
    second = fan_out(
        held,
        "row",
        [
            [(row_of(z, 0, 0), row_of(z, k, 0)) for z in range(Z_COUNT)]
            + [(row_of(0, x, 1), row_of(k, x, 1)) for x in range(X_COUNT)]
            for k in (1, 3, 2)
        ],
    )
    holder = jnp.where(core == 0, x, z) == 0
    final = jnp.where(holder, held, second)
    other = lax.ppermute(final, "row", [(r, r ^ 1) for r in range(2 * X_COUNT * Z_COUNT)])
    return final, other


def share_row(value, root, col):
    right, left, far = (root + 1) % COLS, (root + 3) % COLS, (root + 2) % COLS
    one = lax.ppermute(value, "col", [(root, right)])
    held = jnp.where(col == root, value, one)
    two = lax.ppermute(held, "col", [(root, left), (right, far)])
    return jnp.where((col == root) | (col == right), held, two)


def share_pivots(value, roots):
    return fan_out(
        value,
        ("row", "col"),
        [[(r * COLS + c, r * COLS + (c + k) % COLS) for r, c in roots] for k in (1, 3, 2)],
    )


def body(factor_u, factor_v, near_field, sketch, tile_ranks):
    tile, width = factor_u.shape[4:]
    row = lax.axis_index("row")
    col = lax.axis_index("col")
    core = row % 2
    own_u = factor_u.reshape(2, tile, width)
    own_v = factor_v.reshape(2, tile, width)
    ranks = tile_ranks.reshape(3, -1, 2)
    own_ranks = lax.dynamic_slice_in_dim(ranks, row, 1, 1)[:, 0]
    order = (width - width // 4, width - width // 4 - (width - width // 4) // 4)
    sketch_t = [sketch[k, :, : order[k]].T for k in range(2)]

    def flags_of(panel):
        slots = jnp.arange(2) * 4 + col
        chosen = (row > panel) & (slots > panel)
        if panel == 0:
            chosen = chosen & jnp.logical_not((row == 1) & (slots == 1))
        lower = (row > col) & (col < 2)
        pivot = (row == col) & (col < 2)
        parts = [own_ranks[panel + 1], own_ranks[0], ranks[0, 0], chosen]
        parts += [lower[None], pivot[None], col[None], core[None]]
        return jnp.concatenate([part.astype(jnp.int32) for part in parts])

    flags = [flags_of(panel) for panel in range(2)]
    one, pair = (tile, width), (2, tile, width)

    with jax.named_scope("first_share"):
        keep = jnp.arange(width, dtype=jnp.int32) < own_ranks[0, 0]
        pack = jnp.where(keep, jnp.stack([own_u[0], own_v[0]]), 0.0)
        got = share_pivots(pack, [(0, 0), (1, 1)])
        corner = jnp.where(col == row, pack, got)
        ours_v, theirs_v = share_planes(jnp.where(core == 0, own_v, pack), row)
    with jax.named_scope("first_upper"):
        up_a, up_b = call(functools.partial(upper_kernel, 0), (one, one), flags[0], near_field, corner, own_u)
    with jax.named_scope("first_lead"):
        held, _ = lax.optimization_barrier((pack, got))
        lead = share_row(held, 0, col)
    with jax.named_scope("upper_share"):
        crossed = lax.ppermute(up_b, "row", [(0, 1)])
        up_a, up_b = share_planes(jnp.where(core == 0, up_a, crossed), row)
    with jax.named_scope("first_wide"):
        wide, extra = call(wide_kernel, (pair, pair), flags[0], lead, up_a, up_b, ours_v, theirs_v)
        got = share_pivots(extra, [(1, 1)])
        extra = jnp.where(col == row, extra, got)
    with jax.named_scope("first_update"):
        scratch = [[pltpu.VMEM((2, width, tile), F32), pltpu.VMEM((2, order[k], width), F32)] for k in range(2)]
        cur_u, cur_v, pack = call(
            functools.partial(panel_kernel, order[0], True),
            (pair, pair, pair),
            flags[0], own_u, own_v, wide, ours_v, theirs_v, sketch_t[0],
            scratch=scratch[0],
        )
    with jax.named_scope("second_upper"):
        fresh = call(functools.partial(upper_kernel, 1), (pair,), flags[1], near_field, corner, extra, cur_u)
    with jax.named_scope("second_share"):
        crossed = lax.ppermute(fresh, "row", [(1, 0)])
        fresh_a, fresh_b = share_planes(jnp.where(core == 1, cur_v, crossed), row)
        lead = share_row(pack, 1, col)
    with jax.named_scope("lower"):
        low = call(
            lower_kernel, ((width, tile),),
            flags[1], near_field, up_a, up_b, ours_v, theirs_v, fresh_a, fresh_b, cur_v,
        )
    with jax.named_scope("second_update"):
        cur_u, cur_v = call(
            functools.partial(panel_kernel, order[1], False),
            (pair, pair),
            flags[1], cur_u, cur_v, lead, fresh_a, fresh_b, low, sketch_t[1],
            scratch=scratch[1],
        )
    shape_out = factor_u.shape
    return cur_u.reshape(shape_out), cur_v.reshape(shape_out)


def solution(mesh):
    tiles = P(None, "row", None, "col", None, None)
    return jax.shard_map(
        body,
        mesh=mesh,
        in_specs=(tiles, tiles, P(), P(), P(None, None, None, None, "col")),
        out_specs=(tiles, tiles),
        check_vma=False,
    )
```

time: 189 us -> 189 us (level)
  starting transfers between devices: 97.9 us -> 58.2 us
  Pallas kernels: 34.4 us -> 58 us
  waiting for transfers between devices: 21.9 us -> 35.2 us
  other arithmetic: 12.9 us -> 19.1 us
  local copies, waits for them, and re-layouts: 18.6 us -> 15.7 us
    ppermute x26 -> x9, starting transfers between devices: 45.3 us -> 13 us  [the longest x2 6 us: share_row(): two = lax.ppermute(held, 'col', [(root, left), (right, far)])]
    pallas_call x4 -> x6, Pallas kernels: 34.4 us -> 58 us  [call(): pl.pallas_call(kernel, out_shape=shapes, in_specs=[pl.BlockSpec(memory_sp...]
    ppermute x30 -> x24, waiting for transfers between devices: 3.71 us -> 19.2 us  [fan_out(): moved = lax.ppermute(value, axis, pairs)]
    ppermute x30 -> x24, starting transfers between devices: 52.6 us -> 45.2 us  [fan_out(): moved = lax.ppermute(value, axis, pairs)]
    select_n x31 -> x15, other arithmetic: 11.5 us -> 18.4 us  [the longest x3 3.77 us: share_planes(): final = jnp.where(holder, held, second)]
    unnamed x21 -> x46, local copies, waits for them, and re-layouts: 3.3 us -> 9.33 us
    squeeze x5 -> x0, local copies, waits for them, and re-layouts: 5.25 us -> none  [the longest x1 1.83 us: body(): up_b = share_column((own_u[1], own_v[1]), 0)]
    concatenate x2, local copies, waits for them, and re-layouts: 2.63 us -> 0.17 us  [flags_of(): return jnp.concatenate([part.astype(jnp.int32) for part in parts])]
  transfers between devices with their start and end apart: 56 -> 33, of which waited for: 10 -> 10; matrix products, arithmetic and copies ran while one was open for 15% -> 11% of each run, Pallas kernels for 4% -> 17%
where the time goes in v2:
time: 189 us; the launch traced here: 187 us
  starting transfers between devices  58.2 us (31%)
  Pallas kernels  58 us (31%)
  waiting for transfers between devices  35.2 us (19%)
  other arithmetic  19.1 us (10%)
  local copies, waits for them, and re-layouts  15.7 us (8%)
    pallas_call x6, Pallas kernels, call(): pl.pallas_call(kernel, out_shape=shapes, in_specs=[pl.BlockSpec(memory_sp...  58 us
    ppermute x24, starting transfers between devices, fan_out(): moved = lax.ppermute(value, axis, pairs)  45.2 us
    ppermute x24, waiting for transfers between devices, fan_out(): moved = lax.ppermute(value, axis, pairs)  19.2 us
    ppermute x2, waiting for transfers between devices, share_row(): two = lax.ppermute(held, 'col', [(root, left), (right, far)])  13.2 us
    unnamed x46, local copies, waits for them, and re-layouts  9.33 us
    ppermute x2, starting transfers between devices, share_row(): two = lax.ppermute(held, 'col', [(root, left), (right, far)])  6 us
  transfers between devices with their start and end apart: 33, of which 10 were waited for; matrix products, arithmetic and copies ran while one was open for 11% of the time, Pallas kernels for 17%

profile of v2, /device:TPU:0, one launch (start us, length us, event | category | flops | bytes accessed | tf_op | source)
XLA Modules:
  0.0 187.5 jit_solution(16950835287491254861)
XLA Ops:
  2.7 1.1 slice_bitcast_fusion
  3.8 2.2 %broadcast_select_fusion.3 = (f32[2,512,128]{2,1,0:T(8,128)}, f32[2,512,128]{2,1,0:T(8,128)}) fusion(pred[]{:T(512)S(6)} %eq.54, f32[1,1,2,1,512,128]{5,4,3,2,1,0:T(8,128)} %param.6, f32[1,512,128]{2,1,0:T(8,128)S(1)} %get-tuple-element.33, f32[1,512,128]{2,1,0:T(8,128)S(1)} %get-tuple-element.34, pred[128]{0:T(512)(128)(4,1)S(1)} %iota_compare_fusion), kind=kLoop, calls=%fused_computation.14 | loop fusion | flops 393216 | bytes 2097281 | tf_op jit(solution)/shard_map/first_share/jit(_where)/select_n | solution.py:352
  6.1 3.6 %collective-permute-start = (f32[2,512,128]{2,1,0:T(8,128)}, f32[2,512,128]{2,1,0:T(8,128)S(1)}, u32[]{:S(2)}, u32[]{:S(2)}) collective-permute-start(f32[2,512,128]{2,1,0:T(8,128)} %get-tuple-element.12), channel_id=1, source_target_pairs={{0,1},{5,6}} | collective-permute-start | bytes 1572872 | tf_op jit(solution)/shard_map/first_share/ppermute | solution.py:275
  9.7 2.9 %collective-permute-start.1 = (f32[2,512,128]{2,1,0:T(8,128)}, f32[2,512,128]{2,1,0:T(8,128)}, u32[]{:S(2)}, u32[]{:S(2)}) collective-permute-start(f32[2,512,128]{2,1,0:T(8,128)} %get-tuple-element.12), channel_id=1, source_target_pairs={{0,3},{5,4}} | collective-permute-start | bytes 1572872 | tf_op jit(solution)/shard_map/first_share/ppermute | solution.py:275
  12.6 2.1 %collective-permute-start.2 = (f32[2,512,128]{2,1,0:T(8,128)}, f32[2,512,128]{2,1,0:T(8,128)}, u32[]{:S(2)}, u32[]{:S(2)}) collective-permute-start(f32[2,512,128]{2,1,0:T(8,128)} %get-tuple-element.12), channel_id=1, source_target_pairs={{0,2},{5,7}} | collective-permute-start | bytes 1572872 | tf_op jit(solution)/shard_map/first_share/ppermute | solution.py:275
  14.7 2.1 %collective-permute-start.13 = (f32[2,512,128]{2,1,0:T(8,128)}, f32[2,512,128]{2,1,0:T(8,128)}, u32[]{:S(2)}, u32[]{:S(2)}) collective-permute-start(f32[2,512,128]{2,1,0:T(8,128)} %get-tuple-element.29), channel_id=1, source_target_pairs={{0,32},{4,12},{1,33},{5,13},{2,34},{6,14},{3,35},{7,15}} | collective-permute-start | bytes 1572872 | tf_op jit(solution)/shard_map/first_share/ppermute | solution.py:275
  16.8 2.1 %collective-permute-start.14 = (f32[2,512,128]{2,1,0:T(8,128)}, f32[2,512,128]{2,1,0:T(8,128)}, u32[]{:S(2)}, u32[]{:S(2)}) collective-permute-start(f32[2,512,128]{2,1,0:T(8,128)} %get-tuple-element.29), channel_id=1, source_target_pairs={{0,96},{4,28},{1,97},{5,29},{2,98},{6,30},{3,99},{7,31}} | collective-permute-start | bytes 1572872 | tf_op jit(solution)/shard_map/first_share/ppermute | solution.py:275
  19.4 2.1 %collective-permute-start.15 = (f32[2,512,128]{2,1,0:T(8,128)}, f32[2,512,128]{2,1,0:T(8,128)}, u32[]{:S(2)}, u32[]{:S(2)}) collective-permute-start(f32[2,512,128]{2,1,0:T(8,128)} %get-tuple-element.29), channel_id=1, source_target_pairs={{0,64},{4,20},{1,65},{5,21},{2,66},{6,22},{3,67},{7,23}} | collective-permute-start | bytes 1572872 | tf_op jit(solution)/shard_map/first_share/ppermute | solution.py:275
  21.5 2.9 %collective-permute-done.1 = f32[2,512,128]{2,1,0:T(8,128)} collective-permute-done((f32[2,512,128]{2,1,0:T(8,128)}, f32[2,512,128]{2,1,0:T(8,128)}, u32[]{:S(2)}, u32[]{:S(2)}) %collective-permute-start.1) | collective-permute-done | bytes 524320 | tf_op jit(solution)/shard_map/first_share/ppermute | solution.py:275
  24.4 1.6 broadcast_select_fusion.4
  26.1 6.4 %first_upper.1 = (f32[512,128]{1,0:T(8,128)S(1)}, f32[512,128]{1,0:T(8,128)}) custom-call(s32[12]{0:T(128)S(1)} %concatenate.7.flags, f32[2,512,512]{2,1,0:T(8,128)S(1)} %copy-done, f32[2,512,128]{2,1,0:T(8,128)S(1)} %broadcast_select_fusion.4, f32[2,512,128]{2,1,0:T(8,128)S(1)} %bitcast.26), custom_call_target="tpu_custom_call" | custom-call | tf_op jit(solution)/shard_map/first_upper/pallas_call | solution.py:252
  32.4 1.3 collective-permute-start.5
  33.7 3.1 %collective-permute-start.3 = (f32[2,512,128]{2,1,0:T(8,128)}, f32[2,512,128]{2,1,0:T(8,128)}, u32[]{:S(2)}, u32[]{:S(2)}) collective-permute-start(f32[2,512,128]{2,1,0:T(8,128)} %get-tuple-element.12), channel_id=1, source_target_pairs={{0,1},{4,5},{8,9},{12,13},{16,17},{20,21},{24,25},{28,29},{32,33},... | collective-permute-start | bytes 1572872 | tf_op jit(solution)/shard_map/first_lead/ppermute | solution.py:307
  37.6 1.3 collective-permute-start.6
  38.9 2.0 %collective-permute-start.7 = (f32[512,128]{1,0:T(8,128)}, f32[512,128]{1,0:T(8,128)}, u32[]{:S(2)}, u32[]{:S(2)}) collective-permute-start(f32[512,128]{1,0:T(8,128)} %broadcast_select_fusion.7), channel_id=1, source_target_pairs={{0,96},{4,28},{1,97},{5,29},{2,98},{6,30},{3,99},{7,31}} | collective-permute-start | bytes 786440 | tf_op jit(solution)/shard_map/upper_share/ppermute | solution.py:275
  40.9 2.0 %collective-permute-start.8 = (f32[512,128]{1,0:T(8,128)}, f32[512,128]{1,0:T(8,128)}, u32[]{:S(2)}, u32[]{:S(2)}) collective-permute-start(f32[512,128]{1,0:T(8,128)} %broadcast_select_fusion.7), channel_id=1, source_target_pairs={{0,64},{4,20},{1,65},{5,21},{2,66},{6,22},{3,67},{7,23}} | collective-permute-start | bytes 786440 | tf_op jit(solution)/shard_map/upper_share/ppermute | solution.py:275
  42.9 1.6 add_select_fusion.4
  44.5 2.1 %collective-permute-start.16 = (f32[2,512,128]{2,1,0:T(8,128)S(1)}, f32[2,512,128]{2,1,0:T(8,128)}, u32[]{:S(2)}, u32[]{:S(2)}) collective-permute-start(f32[2,512,128]{2,1,0:T(8,128)S(1)} %add_select_fusion.4), channel_id=1, source_target_pairs={{0,8},{32,40},{64,72},{96,104},{4,36},{12,44},{20,52},{28,60},{1,9... | collective-permute-start | bytes 1572872 | tf_op jit(solution)/shard_map/first_share/ppermute | solution.py:275
  46.7 2.1 %collective-permute-start.17 = (f32[2,512,128]{2,1,0:T(8,128)S(1)}, f32[2,512,128]{2,1,0:T(8,128)}, u32[]{:S(2)}, u32[]{:S(2)}) collective-permute-start(f32[2,512,128]{2,1,0:T(8,128)S(1)} %add_select_fusion.4), channel_id=1, source_target_pairs={{0,24},{32,56},{64,88},{96,120},{4,100},{12,108},{20,116},{28,124}... | collective-permute-start | bytes 1572872 | tf_op jit(solution)/shard_map/first_share/ppermute | solution.py:275
  48.8 2.1 %collective-permute-start.18 = (f32[2,512,128]{2,1,0:T(8,128)S(1)}, f32[2,512,128]{2,1,0:T(8,128)}, u32[]{:S(2)}, u32[]{:S(2)}) collective-permute-start(f32[2,512,128]{2,1,0:T(8,128)S(1)} %add_select_fusion.4), channel_id=1, source_target_pairs={{0,16},{32,48},{64,80},{96,112},{4,68},{12,76},{20,84},{28,92},{1,... | collective-permute-start | bytes 1572872 | tf_op jit(solution)/shard_map/first_share/ppermute | solution.py:275
  50.9 1.2 add_select_fusion.6
  52.1 2.0 %collective-permute-start.10 = (f32[512,128]{1,0:T(8,128)S(1)}, f32[512,128]{1,0:T(8,128)}, u32[]{:S(2)}, u32[]{:S(2)}) collective-permute-start(f32[512,128]{1,0:T(8,128)S(1)} %add_select_fusion.6), channel_id=1, source_target_pairs={{0,24},{32,56},{64,88},{96,120},{4,100},{12,108},{20,116},{28,124}... | collective-permute-start | bytes 786440 | tf_op jit(solution)/shard_map/upper_share/ppermute | solution.py:275
  54.1 2.0 %collective-permute-start.11 = (f32[512,128]{1,0:T(8,128)S(1)}, f32[512,128]{1,0:T(8,128)}, u32[]{:S(2)}, u32[]{:S(2)}) collective-permute-start(f32[512,128]{1,0:T(8,128)S(1)} %add_select_fusion.6), channel_id=1, source_target_pairs={{0,16},{32,48},{64,80},{96,112},{4,68},{12,76},{20,84},{28,92},{1,... | collective-permute-start | bytes 786440 | tf_op jit(solution)/shard_map/upper_share/ppermute | solution.py:275
  56.1 1.9 %broadcast_select_fusion.5 = f32[2,512,128]{2,1,0:T(8,128)} fusion(f32[2,512,128]{2,1,0:T(8,128)} %get-tuple-element.12, f32[2,512,128]{2,1,0:T(8,128)} %collective-permute-done.3, pred[]{:T(512)S(6)} %eq.52), kind=kLoop, calls=%fused_computation.16 | loop fusion | flops 131072 | bytes 1572865 | tf_op jit(solution)/shard_map/first_lead/jit(_where)/select_n | solution.py:308
  58.0 2.0 %collective-permute-start.9 = (f32[512,128]{1,0:T(8,128)S(1)}, f32[512,128]{1,0:T(8,128)}, u32[]{:S(2)}, u32[]{:S(2)}) collective-permute-start(f32[512,128]{1,0:T(8,128)S(1)} %add_select_fusion.6), channel_id=1, source_target_pairs={{0,8},{32,40},{64,72},{96,104},{4,36},{12,44},{20,52},{28,60},{1,9... | collective-permute-start | bytes 786440 | tf_op jit(solution)/shard_map/upper_share/ppermute | solution.py:275
  60.0 4.6 %collective-permute-start.4 = (f32[2,512,128]{2,1,0:T(8,128)}, f32[2,512,128]{2,1,0:T(8,128)}, u32[]{:S(2)}, u32[]{:S(2)}) collective-permute-start(f32[2,512,128]{2,1,0:T(8,128)} %broadcast_select_fusion.5), channel_id=1, source_target_pairs={{0,3},{1,2},{4,7},{5,6},{8,11},{9,10},{12,15},{13,14},{16,19},{17,... | collective-permute-start | bytes 1572872 | tf_op jit(solution)/shard_map/first_lead/ppermute | solution.py:309
  64.6 1.6 add_select_fusion.3.ours.refs_1_
  66.4 1.2 add_select_fusion.5.up_a
  68.1 7.5 %collective-permute-done.4 = f32[2,512,128]{2,1,0:T(8,128)} collective-permute-done((f32[2,512,128]{2,1,0:T(8,128)}, f32[2,512,128]{2,1,0:T(8,128)}, u32[]{:S(2)}, u32[]{:S(2)}) %collective-permute-start.4) | collective-permute-done | bytes 524320 | tf_op jit(solution)/shard_map/first_lead/ppermute | solution.py:309
  75.7 1.1 broadcast_select_fusion.6.lead
  76.8 3.0 %first_wide.1 = (f32[2,512,128]{2,1,0:T(8,128)S(1)}, f32[2,512,128]{2,1,0:T(8,128)}) custom-call(s32[12]{0:T(128)S(1)} %concatenate.7.flags, f32[2,512,128]{2,1,0:T(8,128)S(1)} %broadcast_select_fusion.6.lead, f32[512,128]{1,0:T(8,128)S(1)} %add_select_fusion.5.up_a, f32[512,128]{1,0:T(8,128)S(1)} %collective-permute-done.12.up_b, ...), custom_call_target="tpu_custom_call" | custom-call | tf_op jit(solution)/shard_map/first_wide/pallas_call | solution.py:252
  80.6 1.5 collective-permute-start.22
  82.0 1.5 collective-permute-start.23
  83.5 1.7 collective-permute-start.24
  85.2 1.7 slice.47
  86.9 1.8 copy.17
  88.7 1.0 copy-done.4
  89.8 1.0 copy-done.5
  91.7 1.0 copy-done.14
  92.8 25.1 %first_update.1 = (f32[2,512,128]{2,1,0:T(8,128)S(1)}, f32[2,512,128]{2,1,0:T(8,128)S(1)}, f32[2,512,128]{2,1,0:T(8,128)S(1)}) custom-call(s32[12]{0:T(128)S(1)} %concatenate.7.flags, f32[2,512,128]{2,1,0:T(8,128)S(1)} %bitcast.27, f32[2,512,128]{2,1,0:T(8,128)S(1)} %bitcast.28, f32[2,512,128]{2,1,0:T(8,128)S(1)} %copy-done.14, ...), custom_call_target="tpu_custom_call" | custom-call | tf_op jit(solution)/shard_map/first_update/pallas_call | solution.py:252
  117.9 2.1 %add_select_fusion.2.refs_1_ = f32[2,512,128]{2,1,0:T(8,128)S(1)} fusion(f32[2,512,128]{2,1,0:T(8,128)} %get-tuple-element.19, f32[2,512,128]{2,1,0:T(8,128)} %collective-permute-done.24, f32[2,512,128]{2,1,0:T(8,128)} %collective-permute-done.22, f32[2,512,128]{2,1,0:T(8,128)} %collective-permute-done.23, pred[]{:T(512)S(6)} %eq.56), kind=kLoop, calls=%fused_computation.3 | loop fusion | flops 393216 | bytes 2621441 | tf_op jit(solution)/shard_map/first_wide/jit(_where)/select_n | solution.py:364
  120.1 6.8 %second_upper.1 = f32[2,512,128]{2,1,0:T(8,128)} custom-call(s32[12]{0:T(128)S(1)} %concatenate.6.flags, f32[2,512,512]{2,1,0:T(8,128)S(1)} %copy-done, f32[2,512,128]{2,1,0:T(8,128)S(1)} %broadcast_select_fusion.4, f32[2,512,128]{2,1,0:T(8,128)S(1)} %add_select_fusion.2.refs_1_, f32[2,512,128]{2,1,0:T(8,128)S(1)} %get-tuple-element.16.refs_2_.cu), custom_call_target="tpu_custom_call" | custom-call | tf_op jit(solution)/shard_map/second_upper/pallas_call | solution.py:252
  126.9 1.3 collective-permute-start.25
  128.2 2.7 %collective-permute-done.25 = f32[2,512,128]{2,1,0:T(8,128)S(1)} collective-permute-done((f32[2,512,128]{2,1,0:T(8,128)}, f32[2,512,128]{2,1,0:T(8,128)S(1)}, u32[]{:S(2)}, u32[]{:S(2)}) %collective-permute-start.25) | collective-permute-done | bytes 524320 | tf_op jit(solution)/shard_map/second_share/ppermute | solution.py:376
  131.0 1.5 collective-permute-start.26
  132.5 1.3 collective-permute-start.27
  133.8 1.3 collective-permute-start.28
  135.8 3.3 %collective-permute-done.26 = f32[2,512,128]{2,1,0:T(8,128)S(1)} collective-permute-done((f32[2,512,128]{2,1,0:T(8,128)S(1)}, f32[2,512,128]{2,1,0:T(8,128)S(1)}, u32[]{:S(2)}, u32[]{:S(2)}) %collective-permute-start.26) | collective-permute-done | bytes 524320 | tf_op jit(solution)/shard_map/second_share/ppermute | solution.py:275
  139.1 1.3 collective-permute-done.27
  140.5 4.3 %collective-permute-done.28 = f32[2,512,128]{2,1,0:T(8,128)S(1)} collective-permute-done((f32[2,512,128]{2,1,0:T(8,128)S(1)}, f32[2,512,128]{2,1,0:T(8,128)S(1)}, u32[]{:S(2)}, u32[]{:S(2)}) %collective-permute-start.28) | collective-permute-done | bytes 524320 | tf_op jit(solution)/shard_map/second_share/ppermute | solution.py:275
  144.8 1.3 collective-permute-start.29
  146.2 1.3 collective-permute-start.30
  147.5 1.3 collective-permute-start.31
  149.7 1.4 collective-permute-start.21
  151.1 1.7 collective-permute-done.29
  152.8 1.3 collective-permute-done.30
  154.2 4.3 %collective-permute-done.31 = f32[2,512,128]{2,1,0:T(8,128)S(1)} collective-permute-done((f32[2,512,128]{2,1,0:T(8,128)S(1)}, f32[2,512,128]{2,1,0:T(8,128)S(1)}, u32[]{:S(2)}, u32[]{:S(2)}) %collective-permute-start.31) | collective-permute-done | bytes 524320 | tf_op jit(solution)/shard_map/second_share/ppermute | solution.py:275
  159.4 1.7 slice.48
  161.0 1.1 copy.18
  162.1 5.7 %collective-permute-done.21 = f32[2,512,128]{2,1,0:T(8,128)} collective-permute-done((f32[2,512,128]{2,1,0:T(8,128)}, f32[2,512,128]{2,1,0:T(8,128)}, u32[]{:S(2)}, u32[]{:S(2)}) %collective-permute-start.21) | collective-permute-done | bytes 524320 | tf_op jit(solution)/shard_map/second_share/ppermute | solution.py:309
  167.8 1.1 broadcast_select_fusion.2.refs_0_
  169.0 1.0 copy-done.9
  170.6 5.1 %lower.1.refs_3_ = f32[128,512]{1,0:T(8,128)S(1)} custom-call(s32[12]{0:T(128)S(1)} %copy-done.16, f32[2,512,512]{2,1,0:T(8,128)S(1)} %copy-done, f32[512,128]{1,0:T(8,128)S(1)} %add_select_fusion.5.up_a, f32[512,128]{1,0:T(8,128)S(1)} %copy-done.9, f32[2,512,128]{2,1,0:T(8,128)S(1)} %add_select_fusion.3.ours.refs_1_, ...), custom_call_target="tpu_custom_call" | custom-call | tf_op jit(solution)/shard_map/lower/pallas_call | solution.py:252
  175.7 11.5 %second_update.1 = (f32[2,512,128]{2,1,0:T(8,128)}, f32[2,512,128]{2,1,0:T(8,128)}) custom-call(s32[12]{0:T(128)S(1)} %copy-done.16, f32[2,512,128]{2,1,0:T(8,128)S(1)} %copy-done.7, f32[2,512,128]{2,1,0:T(8,128)S(1)} %copy-done.2, f32[2,512,128]{2,1,0:T(8,128)S(1)} %broadcast_select_fusion.2.refs_0_, f32[2,512,128]{2,1,0:T(8,128)} %add_select_fusion.fresh_a.refs_1_, ...), custom_call_target="tpu_custom_call" | custom-call | tf_op jit(solution)/shard_map/second_update/pallas_call | solution.py:252
  (82 shorter events, 9.1 us)
Async XLA Ops:
  0.6 18.2 %copy-start.21 = (s32[3,1,32,2,1]{2,4,3,1,0:T(1,128)S(1)}, s32[3,1,32,2,1]{2,4,3,1,0:T(1,128)}, u32[]{:S(2)}) copy-start(s32[3,1,32,2,1]{2,4,3,1,0:T(1,128)} %param.9) | copy-start | bytes 2308
  3.8 22.2 %copy-start = (f32[2,512,512]{2,1,0:T(8,128)S(1)}, f32[2,512,512]{2,1,0:T(8,128)}, u32[]{:S(2)}) copy-start(f32[2,512,512]{2,1,0:T(8,128)} %near.5) | copy-start | bytes 6291460
  3.8 22.2 %copy-start.3 = (f32[1,1,2,1,512,128]{5,4,3,2,1,0:T(8,128)S(1)}, f32[1,1,2,1,512,128]{5,4,3,2,1,0:T(8,128)}, u32[]{:S(2)}) copy-start(f32[1,1,2,1,512,128]{5,4,3,2,1,0:T(8,128)} %param.5) | copy-start | bytes 1572868
  6.1 13.3 %collective-permute-start = (f32[2,512,128]{2,1,0:T(8,128)}, f32[2,512,128]{2,1,0:T(8,128)S(1)}, u32[]{:S(2)}, u32[]{:S(2)}) collective-permute-start(f32[2,512,128]{2,1,0:T(8,128)} %get-tuple-element.12), channel_id=1, source_target_pairs={{0,1},{5,6}} | collective-permute-start | bytes 1572872 | tf_op jit(solution)/shard_map/first_share/ppermute | solution.py:275
  9.7 14.8 %collective-permute-start.1 = (f32[2,512,128]{2,1,0:T(8,128)}, f32[2,512,128]{2,1,0:T(8,128)}, u32[]{:S(2)}, u32[]{:S(2)}) collective-permute-start(f32[2,512,128]{2,1,0:T(8,128)} %get-tuple-element.12), channel_id=1, source_target_pairs={{0,3},{5,4}} | collective-permute-start | bytes 1572872 | tf_op jit(solution)/shard_map/first_share/ppermute | solution.py:275
  12.6 11.9 %collective-permute-start.2 = (f32[2,512,128]{2,1,0:T(8,128)}, f32[2,512,128]{2,1,0:T(8,128)}, u32[]{:S(2)}, u32[]{:S(2)}) collective-permute-start(f32[2,512,128]{2,1,0:T(8,128)} %get-tuple-element.12), channel_id=1, source_target_pairs={{0,2},{5,7}} | collective-permute-start | bytes 1572872 | tf_op jit(solution)/shard_map/first_share/ppermute | solution.py:275
  14.7 24.2 %collective-permute-start.13 = (f32[2,512,128]{2,1,0:T(8,128)}, f32[2,512,128]{2,1,0:T(8,128)}, u32[]{:S(2)}, u32[]{:S(2)}) collective-permute-start(f32[2,512,128]{2,1,0:T(8,128)} %get-tuple-element.29), channel_id=1, source_target_pairs={{0,32},{4,12},{1,33},{5,13},{2,34},{6,14},{3,35},{7,15}} | collective-permute-start | bytes 1572872 | tf_op jit(solution)/shard_map/first_share/ppermute | solution.py:275
  16.8 24.2 %collective-permute-start.14 = (f32[2,512,128]{2,1,0:T(8,128)}, f32[2,512,128]{2,1,0:T(8,128)}, u32[]{:S(2)}, u32[]{:S(2)}) collective-permute-start(f32[2,512,128]{2,1,0:T(8,128)} %get-tuple-element.29), channel_id=1, source_target_pairs={{0,96},{4,28},{1,97},{5,29},{2,98},{6,30},{3,99},{7,31}} | collective-permute-start | bytes 1572872 | tf_op jit(solution)/shard_map/first_share/ppermute | solution.py:275
  19.4 5.1 %copy-start.19 = (f32[2,512,128]{2,1,0:T(8,128)}, f32[2,512,128]{2,1,0:T(8,128)S(1)}, u32[]{:S(2)}) copy-start(f32[2,512,128]{2,1,0:T(8,128)S(1)} %collective-permute-done) | copy-start | bytes 1572868
  19.4 23.5 %collective-permute-start.15 = (f32[2,512,128]{2,1,0:T(8,128)}, f32[2,512,128]{2,1,0:T(8,128)}, u32[]{:S(2)}, u32[]{:S(2)}) collective-permute-start(f32[2,512,128]{2,1,0:T(8,128)} %get-tuple-element.29), channel_id=1, source_target_pairs={{0,64},{4,20},{1,65},{5,21},{2,66},{6,22},{3,67},{7,23}} | collective-permute-start | bytes 1572872 | tf_op jit(solution)/shard_map/first_share/ppermute | solution.py:275
  32.4 4.4 %collective-permute-start.5 = (f32[512,128]{1,0:T(8,128)}, f32[512,128]{1,0:T(8,128)S(1)}, u32[]{:S(2)}, u32[]{:S(2)}) collective-permute-start(f32[512,128]{1,0:T(8,128)} %get-tuple-element.14), channel_id=1, source_target_pairs={{0,4},{1,5},{2,6},{3,7}} | collective-permute-start | bytes 786440 | tf_op jit(solution)/shard_map/upper_share/ppermute | solution.py:359
  33.7 20.4 %collective-permute-start.3 = (f32[2,512,128]{2,1,0:T(8,128)}, f32[2,512,128]{2,1,0:T(8,128)}, u32[]{:S(2)}, u32[]{:S(2)}) collective-permute-start(f32[2,512,128]{2,1,0:T(8,128)} %get-tuple-element.12), channel_id=1, source_target_pairs={{0,1},{4,5},{8,9},{12,13},{16,17},{20,21},{24,25},{28,29},{32,33},... | collective-permute-start | bytes 1572872 | tf_op jit(solution)/shard_map/first_lead/ppermute | solution.py:307
  37.6 9.1 %collective-permute-start.6 = (f32[512,128]{1,0:T(8,128)}, f32[512,128]{1,0:T(8,128)S(1)}, u32[]{:S(2)}, u32[]{:S(2)}) collective-permute-start(f32[512,128]{1,0:T(8,128)} %broadcast_select_fusion.7), channel_id=1, source_target_pairs={{0,32},{4,12},{1,33},{5,13},{2,34},{6,14},{3,35},{7,15}} | collective-permute-start | bytes 786440 | tf_op jit(solution)/shard_map/upper_share/ppermute | solution.py:275
  38.9 9.9 %collective-permute-start.7 = (f32[512,128]{1,0:T(8,128)}, f32[512,128]{1,0:T(8,128)}, u32[]{:S(2)}, u32[]{:S(2)}) collective-permute-start(f32[512,128]{1,0:T(8,128)} %broadcast_select_fusion.7), channel_id=1, source_target_pairs={{0,96},{4,28},{1,97},{5,29},{2,98},{6,30},{3,99},{7,31}} | collective-permute-start | bytes 786440 | tf_op jit(solution)/shard_map/upper_share/ppermute | solution.py:275
  40.9 9.9 %collective-permute-start.8 = (f32[512,128]{1,0:T(8,128)}, f32[512,128]{1,0:T(8,128)}, u32[]{:S(2)}, u32[]{:S(2)}) collective-permute-start(f32[512,128]{1,0:T(8,128)} %broadcast_select_fusion.7), channel_id=1, source_target_pairs={{0,64},{4,20},{1,65},{5,21},{2,66},{6,22},{3,67},{7,23}} | collective-permute-start | bytes 786440 | tf_op jit(solution)/shard_map/upper_share/ppermute | solution.py:275
  44.5 20.1 %copy-start.17 = (f32[2,512,128]{2,1,0:T(8,128)}, f32[2,512,128]{2,1,0:T(8,128)S(1)}, u32[]{:S(2)}) copy-start(f32[2,512,128]{2,1,0:T(8,128)S(1)} %add_select_fusion.4) | copy-start | bytes 1572868
  44.5 13.5 %collective-permute-start.16 = (f32[2,512,128]{2,1,0:T(8,128)S(1)}, f32[2,512,128]{2,1,0:T(8,128)}, u32[]{:S(2)}, u32[]{:S(2)}) collective-permute-start(f32[2,512,128]{2,1,0:T(8,128)S(1)} %add_select_fusion.4), channel_id=1, source_target_pairs={{0,8},{32,40},{64,72},{96,104},{4,36},{12,44},{20,52},{28,60},{1,9... | collective-permute-start | bytes 1572872 | tf_op jit(solution)/shard_map/first_share/ppermute | solution.py:275
  46.7 4.2 %copy-start.20 = (f32[512,128]{1,0:T(8,128)}, f32[512,128]{1,0:T(8,128)S(1)}, u32[]{:S(2)}) copy-start(f32[512,128]{1,0:T(8,128)S(1)} %collective-permute-done.6) | copy-start | bytes 786436
  46.7 13.3 %collective-permute-start.17 = (f32[2,512,128]{2,1,0:T(8,128)S(1)}, f32[2,512,128]{2,1,0:T(8,128)}, u32[]{:S(2)}, u32[]{:S(2)}) collective-permute-start(f32[2,512,128]{2,1,0:T(8,128)S(1)} %add_select_fusion.4), channel_id=1, source_target_pairs={{0,24},{32,56},{64,88},{96,120},{4,100},{12,108},{20,116},{28,124}... | collective-permute-start | bytes 1572872 | tf_op jit(solution)/shard_map/first_share/ppermute | solution.py:275
  48.8 15.8 %collective-permute-start.18 = (f32[2,512,128]{2,1,0:T(8,128)S(1)}, f32[2,512,128]{2,1,0:T(8,128)}, u32[]{:S(2)}, u32[]{:S(2)}) collective-permute-start(f32[2,512,128]{2,1,0:T(8,128)S(1)} %add_select_fusion.4), channel_id=1, source_target_pairs={{0,16},{32,48},{64,80},{96,112},{4,68},{12,76},{20,84},{28,92},{1,... | collective-permute-start | bytes 1572872 | tf_op jit(solution)/shard_map/first_share/ppermute | solution.py:275
  52.1 14.2 %copy-start.18 = (f32[512,128]{1,0:T(8,128)}, f32[512,128]{1,0:T(8,128)S(1)}, u32[]{:S(2)}) copy-start(f32[512,128]{1,0:T(8,128)S(1)} %add_select_fusion.6) | copy-start | bytes 786436
  52.1 14.2 %collective-permute-start.10 = (f32[512,128]{1,0:T(8,128)S(1)}, f32[512,128]{1,0:T(8,128)}, u32[]{:S(2)}, u32[]{:S(2)}) collective-permute-start(f32[512,128]{1,0:T(8,128)S(1)} %add_select_fusion.6), channel_id=1, source_target_pairs={{0,24},{32,56},{64,88},{96,120},{4,100},{12,108},{20,116},{28,124}... | collective-permute-start | bytes 786440 | tf_op jit(solution)/shard_map/upper_share/ppermute | solution.py:275
  54.1 12.2 %collective-permute-start.11 = (f32[512,128]{1,0:T(8,128)S(1)}, f32[512,128]{1,0:T(8,128)}, u32[]{:S(2)}, u32[]{:S(2)}) collective-permute-start(f32[512,128]{1,0:T(8,128)S(1)} %add_select_fusion.6), channel_id=1, source_target_pairs={{0,16},{32,48},{64,80},{96,112},{4,68},{12,76},{20,84},{28,92},{1,... | collective-permute-start | bytes 786440 | tf_op jit(solution)/shard_map/upper_share/ppermute | solution.py:275
  58.0 8.3 %collective-permute-start.9 = (f32[512,128]{1,0:T(8,128)S(1)}, f32[512,128]{1,0:T(8,128)}, u32[]{:S(2)}, u32[]{:S(2)}) collective-permute-start(f32[512,128]{1,0:T(8,128)S(1)} %add_select_fusion.6), channel_id=1, source_target_pairs={{0,8},{32,40},{64,72},{96,104},{4,36},{12,44},{20,52},{28,60},{1,9... | collective-permute-start | bytes 786440 | tf_op jit(solution)/shard_map/upper_share/ppermute | solution.py:275
  60.0 15.7 %collective-permute-start.4 = (f32[2,512,128]{2,1,0:T(8,128)}, f32[2,512,128]{2,1,0:T(8,128)}, u32[]{:S(2)}, u32[]{:S(2)}) collective-permute-start(f32[2,512,128]{2,1,0:T(8,128)} %broadcast_select_fusion.5), channel_id=1, source_target_pairs={{0,3},{1,2},{4,7},{5,6},{8,11},{9,10},{12,15},{13,14},{16,19},{17,... | collective-permute-start | bytes 1572872 | tf_op jit(solution)/shard_map/first_lead/ppermute | solution.py:309
  66.2 10.6 %collective-permute-start.19 = (f32[2,512,128]{2,1,0:T(8,128)S(1)}, f32[2,512,128]{2,1,0:T(8,128)}, u32[]{:S(2)}, u32[]{:S(2)}) collective-permute-start(f32[2,512,128]{2,1,0:T(8,128)S(1)} %add_select_fusion.3.ours.refs_1_), channel_id=1, source_target_pairs={{0,4},{4,0},{8,12},{12,8},{16,20},{20,16},{24,28},{28,24},{32,36},... | collective-permute-start | bytes 1572872 | tf_op jit(solution)/shard_map/first_share/ppermute | solution.py:301
  67.6 9.2 %collective-permute-start.12 = (f32[512,128]{1,0:T(8,128)S(1)}, f32[512,128]{1,0:T(8,128)S(1)}, u32[]{:S(2)}, u32[]{:S(2)}) collective-permute-start(f32[512,128]{1,0:T(8,128)S(1)} %add_select_fusion.5.up_a), channel_id=1, source_target_pairs={{0,4},{4,0},{8,12},{12,8},{16,20},{20,16},{24,28},{28,24},{32,36},... | collective-permute-start | bytes 786440 | tf_op jit(solution)/shard_map/upper_share/ppermute | solution.py:301
  76.8 3.0 %copy-start.8 = (f32[512,128]{1,0:T(8,128)}, f32[512,128]{1,0:T(8,128)S(1)}, u32[]{:S(2)}) copy-start(f32[512,128]{1,0:T(8,128)S(1)} %collective-permute-done.12.up_b) | copy-start | bytes 786436
  79.8 0.8 copy-start.13
  80.6 37.4 %collective-permute-start.22 = (f32[2,512,128]{2,1,0:T(8,128)}, f32[2,512,128]{2,1,0:T(8,128)}, u32[]{:S(2)}, u32[]{:S(2)}) collective-permute-start(f32[2,512,128]{2,1,0:T(8,128)} %get-tuple-element.19), channel_id=1, source_target_pairs={{5,6}} | collective-permute-start | bytes 1572872 | tf_op jit(solution)/shard_map/first_wide/ppermute | solution.py:275
  82.0 35.9 %collective-permute-start.23 = (f32[2,512,128]{2,1,0:T(8,128)}, f32[2,512,128]{2,1,0:T(8,128)}, u32[]{:S(2)}, u32[]{:S(2)}) collective-permute-start(f32[2,512,128]{2,1,0:T(8,128)} %get-tuple-element.19), channel_id=1, source_target_pairs={{5,4}} | collective-permute-start | bytes 1572872 | tf_op jit(solution)/shard_map/first_wide/ppermute | solution.py:275
  83.5 34.5 %collective-permute-start.24 = (f32[2,512,128]{2,1,0:T(8,128)}, f32[2,512,128]{2,1,0:T(8,128)}, u32[]{:S(2)}, u32[]{:S(2)}) collective-permute-start(f32[2,512,128]{2,1,0:T(8,128)} %get-tuple-element.19), channel_id=1, source_target_pairs={{5,7}} | collective-permute-start | bytes 1572872 | tf_op jit(solution)/shard_map/first_wide/ppermute | solution.py:275
  88.7 31.4 %copy-start.15 = (s32[12]{0:T(128)}, s32[12]{0:T(128)S(1)}, u32[]{:S(2)}) copy-start(s32[12]{0:T(128)S(1)} %concatenate.6.flags) | copy-start | bytes 148
  88.7 1.0 copy-start.4
  89.8 1.0 copy-start.5
  90.8 0.9 copy-start.10
  91.7 1.0 copy-start.14
  117.9 9.1 %copy-start.1 = (f32[2,512,128]{2,1,0:T(8,128)}, f32[2,512,128]{2,1,0:T(8,128)S(1)}, u32[]{:S(2)}) copy-start(f32[2,512,128]{2,1,0:T(8,128)S(1)} %get-tuple-element.17.own_v.cv) | copy-start | bytes 1572868
  117.9 9.0 %copy-start.6 = (f32[2,512,128]{2,1,0:T(8,128)}, f32[2,512,128]{2,1,0:T(8,128)S(1)}, u32[]{:S(2)}) copy-start(f32[2,512,128]{2,1,0:T(8,128)S(1)} %get-tuple-element.16.refs_2_.cu) | copy-start | bytes 1572868
  117.9 9.0 %copy-start.11 = (f32[2,512,128]{2,1,0:T(8,128)}, f32[2,512,128]{2,1,0:T(8,128)S(1)}, u32[]{:S(2)}) copy-start(f32[2,512,128]{2,1,0:T(8,128)S(1)} %get-tuple-element.18) | copy-start | bytes 1572868
  126.9 4.0 %collective-permute-start.25 = (f32[2,512,128]{2,1,0:T(8,128)}, f32[2,512,128]{2,1,0:T(8,128)S(1)}, u32[]{:S(2)}, u32[]{:S(2)}) collective-permute-start(f32[2,512,128]{2,1,0:T(8,128)} %second_upper.1), channel_id=1, source_target_pairs={{4,0},{5,1},{6,2},{7,3}} | collective-permute-start | bytes 1572872 | tf_op jit(solution)/shard_map/second_share/ppermute | solution.py:376
  131.0 17.9 %copy-start.12 = (f32[2,512,128]{2,1,0:T(8,128)S(1)}, f32[2,512,128]{2,1,0:T(8,128)}, u32[]{:S(2)}) copy-start(f32[2,512,128]{2,1,0:T(8,128)} %copy-done.11) | copy-start | bytes 1572868
  131.0 8.1 %collective-permute-start.26 = (f32[2,512,128]{2,1,0:T(8,128)S(1)}, f32[2,512,128]{2,1,0:T(8,128)S(1)}, u32[]{:S(2)}, u32[]{:S(2)}) collective-permute-start(f32[2,512,128]{2,1,0:T(8,128)S(1)} %broadcast_select_fusion), channel_id=1, source_target_pairs={{0,32},{4,12},{1,33},{5,13},{2,34},{6,14},{3,35},{7,15}} | collective-permute-start | bytes 1572872 | tf_op jit(solution)/shard_map/second_share/ppermute | solution.py:275
  132.5 8.0 %collective-permute-start.27 = (f32[2,512,128]{2,1,0:T(8,128)S(1)}, f32[2,512,128]{2,1,0:T(8,128)S(1)}, u32[]{:S(2)}, u32[]{:S(2)}) collective-permute-start(f32[2,512,128]{2,1,0:T(8,128)S(1)} %broadcast_select_fusion), channel_id=1, source_target_pairs={{0,96},{4,28},{1,97},{5,29},{2,98},{6,30},{3,99},{7,31}} | collective-permute-start | bytes 1572872 | tf_op jit(solution)/shard_map/second_share/ppermute | solution.py:275
  133.8 10.9 %collective-permute-start.28 = (f32[2,512,128]{2,1,0:T(8,128)S(1)}, f32[2,512,128]{2,1,0:T(8,128)S(1)}, u32[]{:S(2)}, u32[]{:S(2)}) collective-permute-start(f32[2,512,128]{2,1,0:T(8,128)S(1)} %broadcast_select_fusion), channel_id=1, source_target_pairs={{0,64},{4,20},{1,65},{5,21},{2,66},{6,22},{3,67},{7,23}} | collective-permute-start | bytes 1572872 | tf_op jit(solution)/shard_map/second_share/ppermute | solution.py:275
  135.1 13.7 %collective-permute-start.20 = (f32[2,512,128]{2,1,0:T(8,128)}, f32[2,512,128]{2,1,0:T(8,128)S(1)}, u32[]{:S(2)}, u32[]{:S(2)}) collective-permute-start(f32[2,512,128]{2,1,0:T(8,128)} %copy-done.11), channel_id=1, source_target_pairs={{1,2},{5,6},{9,10},{13,14},{17,18},{21,22},{25,26},{29,30},{33,34}... | collective-permute-start | bytes 1572872 | tf_op jit(solution)/shard_map/second_share/ppermute | solution.py:307
  144.8 8.0 %collective-permute-start.29 = (f32[2,512,128]{2,1,0:T(8,128)S(1)}, f32[2,512,128]{2,1,0:T(8,128)S(1)}, u32[]{:S(2)}, u32[]{:S(2)}) collective-permute-start(f32[2,512,128]{2,1,0:T(8,128)S(1)} %add_select_fusion.1), channel_id=1, source_target_pairs={{0,8},{32,40},{64,72},{96,104},{4,36},{12,44},{20,52},{28,60},{1,9... | collective-permute-start | bytes 1572872 | tf_op jit(solution)/shard_map/second_share/ppermute | solution.py:275
  146.2 8.0 %collective-permute-start.30 = (f32[2,512,128]{2,1,0:T(8,128)S(1)}, f32[2,512,128]{2,1,0:T(8,128)S(1)}, u32[]{:S(2)}, u32[]{:S(2)}) collective-permute-start(f32[2,512,128]{2,1,0:T(8,128)S(1)} %add_select_fusion.1), channel_id=1, source_target_pairs={{0,24},{32,56},{64,88},{96,120},{4,100},{12,108},{20,116},{28,124}... | collective-permute-start | bytes 1572872 | tf_op jit(solution)/shard_map/second_share/ppermute | solution.py:275
  147.5 10.9 %collective-permute-start.31 = (f32[2,512,128]{2,1,0:T(8,128)S(1)}, f32[2,512,128]{2,1,0:T(8,128)S(1)}, u32[]{:S(2)}, u32[]{:S(2)}) collective-permute-start(f32[2,512,128]{2,1,0:T(8,128)S(1)} %add_select_fusion.1), channel_id=1, source_target_pairs={{0,16},{32,48},{64,80},{96,112},{4,68},{12,76},{20,84},{28,92},{1,... | collective-permute-start | bytes 1572872 | tf_op jit(solution)/shard_map/second_share/ppermute | solution.py:275
  149.7 19.3 %copy-start.2 = (f32[2,512,128]{2,1,0:T(8,128)S(1)}, f32[2,512,128]{2,1,0:T(8,128)}, u32[]{:S(2)}) copy-start(f32[2,512,128]{2,1,0:T(8,128)} %copy-done.1) | copy-start | bytes 1572868
  149.7 18.1 %collective-permute-start.21 = (f32[2,512,128]{2,1,0:T(8,128)}, f32[2,512,128]{2,1,0:T(8,128)}, u32[]{:S(2)}, u32[]{:S(2)}) collective-permute-start(f32[2,512,128]{2,1,0:T(8,128)} %broadcast_select_fusion.1), channel_id=1, source_target_pairs={{1,0},{2,3},{5,4},{6,7},{9,8},{10,11},{13,12},{14,15},{17,16},{18,... | collective-permute-start | bytes 1572872 | tf_op jit(solution)/shard_map/second_share/ppermute | solution.py:309
  159.4 9.6 %collective-permute-start.32 = (f32[2,512,128]{2,1,0:T(8,128)}, f32[2,512,128]{2,1,0:T(8,128)}, u32[]{:S(2)}, u32[]{:S(2)}) collective-permute-start(f32[2,512,128]{2,1,0:T(8,128)} %add_select_fusion.fresh_a.refs_1_), channel_id=1, source_target_pairs={{0,4},{4,0},{8,12},{12,8},{16,20},{20,16},{24,28},{28,24},{32,36},... | collective-permute-start | bytes 1572872 | tf_op jit(solution)/shard_map/second_share/ppermute | solution.py:301
  168.9 6.8 %copy-start.7 = (f32[2,512,128]{2,1,0:T(8,128)S(1)}, f32[2,512,128]{2,1,0:T(8,128)}, u32[]{:S(2)}) copy-start(f32[2,512,128]{2,1,0:T(8,128)} %copy-done.6) | copy-start | bytes 1572868
  169.0 1.0 copy-start.9
  170.0 0.6 copy-start.16

commit v3 on v2

--- a/solution.py
+++ b/solution.py
@@ -79,10 +79,15 @@
     return outs
 
 
-def wide_of(lead, up):
+def wide_t(lead, z_t):
     weight = 1.0 / (8.0 * lead.shape[1])
-    core = weight * dot3(lead[1], up, TN)
-    return dot3(lead[0], core)
+    core_t = weight * dot3(z_t, lead[1])
+    return core_t
+
+
+def diagonal_inverse(far):
+    eye = iota(far.shape, 0) == iota(far.shape, 1)
+    return 1.0 / jnp.sum(jnp.where(eye, far, 0.0), axis=0, keepdims=True)
 
 
 def series(pivot, start):
@@ -92,80 +97,36 @@
     return rest, square, split(dot3(square, square))
 
 
-def start_of(far, axis):
-    eye = iota(far.shape, 0) == iota(far.shape, 1)
-    return 1.0 / jnp.sum(jnp.where(eye, far, 0.0), axis=axis, keepdims=True)
-
-
-def upper_kernel(panel, flags, near, *refs):
+def upper_kernel(flags, near, corner, own_u, own_v, out_a, out_b):
+    tile, width = own_u.shape[1:]
+    weight = 1.0 / (8.0 * tile)
+    far = near[0]
+    start = diagonal_inverse(far)
+    parts = series(far + weight * dot3(corner[0], corner[1], NT), start)
+    lanes = iota((tile, width), 1)
+    values = jnp.concatenate([jnp.where(lanes < flags[2 + s], own_u[s], 0.0).T for s in range(2)], axis=0)
+    for part in parts[::-1]:
+        values = values + dot3(values, part, NT)
+    values = values * start
+    out_a[:width] = jnp.where(flags[10] == 0, corner[0].T, values[:width])
+    out_a[width:] = own_v[0].T
+    out_b[:width] = values[width:]
+    out_b[width:] = own_v[1].T
+
+
+def wide_kernel(flags, lead, crossed, out):
+    width = lead.shape[2]
+    out[:width] = dot3(wide_t(lead, crossed[:width]), lead[0], NT)
+    out[width:] = crossed[width:]
+
+
+def panel_kernel(order, panel, flags, near, cu, cv, lead, ours, theirs, *refs):
     if panel == 0:
-        corner, own, out_a, out_b = refs
+        corner, extra, sketch, nu, nv, pack, out_z, out_v, ortho, factor, moved = refs
     else:
-        corner, extra, own, out = refs
-    tile, width = own.shape[1:]
+        ours_0, theirs_0, sketch, nu, nv, ortho, factor, moved = refs
+    tile, width = cu.shape[1:]
     weight = 1.0 / (8.0 * tile)
-    far = near[panel]
-    low_rank = dot3(corner[0], corner[1], NT)
-    if panel == 1:
-        low_rank = low_rank - dot3(extra[0], extra[1], NT)
-    parts = series(far + weight * low_rank, start_of(far, 0))
-    lanes = iota((tile, width), 1)
-    values = [own[s] for s in range(2)]
-    if panel == 0:
-        values = [jnp.where(lanes < flags[2 + s], values[s], 0.0) for s in range(2)]
-    values = jnp.concatenate(values, axis=1)
-    for part in parts[::-1]:
-        values = values + dot3(part, values)
-    values = values * start_of(far, 1)
-    spare = corner[0] if panel == 0 else extra[0]
-    first = jnp.where(flags[10] == panel, spare, values[:, :width])
-    if panel == 0:
-        out_a[...] = first
-        out_b[...] = values[:, width:]
-    else:
-        out[0] = first
-        out[1] = values[:, width:]
-
-
-def lower_kernel(flags, near, up_a, up_b, ours, theirs, fresh_a, fresh_b, own_v, out):
-    tile, width = own_v.shape[1:]
-    weight = 1.0 / (8.0 * tile)
-    left = flags[10] == 0
-    even = flags[11] == 0
-    far = jnp.where(left, near[0], near[1])
-    up_u = jnp.where(even, up_a[...], up_b[...])
-    up_v = jnp.where(even, ours[0], theirs[0])
-    corner_u = jnp.where(even, theirs[0], ours[0])
-    corner_v = jnp.where(even, theirs[1], ours[1])
-    wide = jnp.where(even, fresh_a[0], fresh_b[0])
-    one_u = jnp.where(left, up_u, corner_u)
-    one_v = jnp.where(left, up_v, corner_v)
-    two_u = jnp.where(left, 0.0, wide)
-    start = start_of(far, 0)
-    low_rank = dot3(one_u, one_v, NT) - dot3(two_u, up_v, NT)
-    values = own_v[0].T * start
-    for part in series(far + weight * low_rank, start):
-        values = values + dot3(values, part)
-    out[...] = values
-
-
-def wide_kernel(flags, lead, up_a, up_b, ours, theirs, wide, pack):
-    even = flags[11] == 0
-    near_up = jnp.where(even, up_a[...], up_b[...])
-    far_up = jnp.where(even, up_b[...], up_a[...])
-    first = wide_of(lead, near_up)
-    wide[0] = first
-    wide[1] = wide_of(lead, far_up)
-    pack[0] = first
-    pack[1] = jnp.where(even, ours[0], theirs[0])
-
-
-def panel_kernel(order, first, flags, cu, cv, *refs):
-    if first:
-        wide, ours, theirs, st, nu, nv, pack, ortho, factor = refs
-    else:
-        lead, ours, theirs, lowt, st, nu, nv, ortho, factor = refs
-    tile, width = cu.shape[1:]
     root = math.sqrt(tile)
     lanes = iota((tile, width), 1)
     spare = jnp.zeros((width - order, tile), F32)
@@ -174,19 +135,22 @@
     eye = (row_g == lane_g).astype(F32)
     even = flags[11] == 0
     full_us, full_vs, bases, grams, units = [], [], [], [], []
-    sketch = st[...]
+    test_t = sketch[panel].T[:order]
     for s in range(2):
         own_u = cu[s]
-        if first:
+        if panel == 0:
             own_u = jnp.where(lanes < flags[2 + s], own_u, 0.0)
-            side = wide[s]
-            up_v = jnp.where(even, ours[s], theirs[s])
+            slot = jnp.where(even, theirs[...], ours[...]) if s == 0 else jnp.where(even, ours[...], theirs[...])
+            z_t, up_v = slot[:width], slot[width:].T
         else:
-            side = wide_of(lead, jnp.where(even, ours[s], theirs[s]))
-            up_v = jnp.where(even, theirs[s], ours[s])
+            part = ours.shape[1]
+            rest = jnp.zeros((width - part, tile), F32)
+            z_t = jnp.concatenate([jnp.where(even, ours[s], theirs[s]), rest], axis=0)
+            up_v = jnp.concatenate([jnp.where(even, theirs[s], ours[s]), rest], axis=0).T
+        side = dot3(lead[0], wide_t(lead, z_t), NT)
         full_u = jnp.concatenate([own_u, -side], axis=1)
         full_v = jnp.concatenate([cv[s], up_v], axis=1)
-        projected = dot6(sketch, full_v)
+        projected = dot6(test_t, full_v)
         basis = dot6(projected, full_u, NT)
         basis = jnp.where(iota((order, tile), 0) < flags[s], basis, 0.0)
         basis = jnp.concatenate([basis, spare], axis=0)
@@ -196,6 +160,29 @@
         full_vs.append(full_v)
         bases.append(basis)
         units.append(unit)
+
+    if panel == 0:
+        far = near[1]
+        start = diagonal_inverse(far)
+        low_rank = dot3(corner[0], corner[1], NT) - dot3(extra[:width], extra[width:], TN)
+        parts = series(far + weight * low_rank, start)
+    else:
+        left = flags[10] == 0
+        slot = jnp.where(even, theirs_0[...], ours_0[...])
+        moved[:part] = jnp.where(even, ours[0], theirs[0])
+        moved[part:2 * part] = jnp.where(even, theirs[0], ours[0])
+        moved[2 * part:3 * part] = jnp.where(even, ours[2], theirs[2])
+        moved[3 * part:] = jnp.where(even, theirs[2], ours[2])
+        far = jnp.where(left, near[0], near[1])
+        start = diagonal_inverse(far)
+        one_u = jnp.where(left, slot[:width], moved[width:2 * width])
+        one_v = jnp.where(left, slot[width:], moved[2 * width:])
+        two_u = jnp.where(left, 0.0, moved[:width])
+        low_rank = dot3(one_u, one_v, TN) - dot3(two_u, slot[width:], TN)
+        low = cv[0].T * start
+        for factors in series(far + weight * low_rank, start):
+            low = low + dot3(low, factors)
+
     inverses = eliminate(grams, order)
     defect = jnp.zeros((), F32)
     for s in range(2):
@@ -206,9 +193,9 @@
         factor[s] = gram
         off = gram - eye
         defect = defect + jnp.where(flags[6 + s] == 1, jnp.sum(off * off), 0.0)
-    near = defect < 1e-6
-
-    @pl.when(near)
+    near_unit = defect < 1e-6
+
+    @pl.when(near_unit)
     def _():
         for s in range(2):
             off = factor[s] - eye
@@ -216,24 +203,26 @@
             once = ortho[s]
             ortho[s, :order] = once[:order] - dot1(half.astype(BF16), once.astype(BF16))
 
-    @pl.when(jnp.logical_not(near))
+    @pl.when(jnp.logical_not(near_unit))
     def _():
         again = eliminate([factor[0], factor[1]], order)
         for s in range(2):
             ortho[s, :order] = dot6(again[s], ortho[s])
 
+    fresh_vs = []
     for s in range(2):
         basis = ortho[s]
         back = dot3(basis, full_us[s])
         fresh_v = dot3(full_vs[s], back, NT) * (1.0 / root)
         fresh_u = basis.T * root
+        fresh_vs.append(fresh_v)
         keep_u = cu[s]
         keep_v = cv[s]
-        if first:
+        if panel == 0:
             keep_u = jnp.where(lanes < flags[2 + s], keep_u, 0.0)
             keep_v = jnp.where(lanes < flags[2 + s], keep_v, 0.0)
         elif s == 0:
-            keep_v = jnp.where(flags[8] == 1, lowt[...].T, keep_v)
+            keep_v = jnp.where(flags[8] == 1, low.T, keep_v)
             keep_u = jnp.where(flags[9] == 1, 0.0, keep_u)
             keep_v = jnp.where(flags[9] == 1, 0.0, keep_v)
         chosen = flags[6 + s] == 1
@@ -241,9 +230,24 @@
         new_v = jnp.where(chosen, fresh_v, keep_v)
         nu[s] = new_u
         nv[s] = new_v
-        if first and s == 0:
+        if panel == 0 and s == 0:
             pack[0] = new_u
             pack[1] = new_v
+    if panel == 0:
+        values = jnp.concatenate([ortho[0, :order], ortho[1, :order]], axis=0) * root
+        for factors in parts[::-1]:
+            values = values + dot3(values, factors, NT)
+        values = values * start
+        moved[:width] = extra[:width]
+        moved[width:2 * width] = corner[0].T
+        moved[2 * width:] = corner[1].T
+        middle = flags[10] == 1
+        out_z[0] = jnp.where(middle, moved[:order], values[:order])
+        out_z[1] = values[order:]
+        out_z[2] = moved[2 * order:3 * order]
+        out_v[0] = jnp.where(middle, moved[order:2 * order], fresh_vs[0].T[:order])
+        out_v[1] = fresh_vs[1].T[:order]
+        out_v[2] = moved[3 * order:]
 
 
 def call(kernel, shapes, flags, *values, scratch=()):
@@ -255,7 +259,7 @@
         in_specs=[pl.BlockSpec(memory_space=pltpu.SMEM)] + [vmem] * len(values),
         out_specs=(vmem,) * len(shapes),
         scratch_shapes=list(scratch),
-        compiler_params=pltpu.CompilerParams(vmem_limit_bytes=40 * 1024 * 1024),
+        compiler_params=pltpu.CompilerParams(vmem_limit_bytes=32 * 1024 * 1024),
     )(flags, *values)
     return out if len(out) > 1 else out[0]
 
@@ -307,7 +311,7 @@
     one = lax.ppermute(value, "col", [(root, right)])
     held = jnp.where(col == root, value, one)
     two = lax.ppermute(held, "col", [(root, left), (right, far)])
-    return jnp.where((col == root) | (col == right), held, two)
+    return held, jnp.where((col == root) | (col == right), held, two)
 
 
 def share_pivots(value, roots):
@@ -328,7 +332,6 @@
     ranks = tile_ranks.reshape(3, -1, 2)
     own_ranks = lax.dynamic_slice_in_dim(ranks, row, 1, 1)[:, 0]
     order = (width - width // 4, width - width // 4 - (width - width // 4) // 4)
-    sketch_t = [sketch[k, :, : order[k]].T for k in range(2)]
 
     def flags_of(panel):
         slots = jnp.arange(2) * 4 + col
@@ -342,50 +345,45 @@
         return jnp.concatenate([part.astype(jnp.int32) for part in parts])
 
     flags = [flags_of(panel) for panel in range(2)]
-    one, pair = (tile, width), (2, tile, width)
-
-    with jax.named_scope("first_share"):
-        keep = jnp.arange(width, dtype=jnp.int32) < own_ranks[0, 0]
-        pack = jnp.where(keep, jnp.stack([own_u[0], own_v[0]]), 0.0)
+    pair, payload = (2, tile, width), (2 * width, tile)
+    packed = (3, order[0], tile)
+    scratch = [
+        [pltpu.VMEM(pair[:1] + (width, tile), F32), pltpu.VMEM((2, order[k], width), F32), pltpu.VMEM((4 * order[0], tile), F32)]
+        for k in range(2)
+    ]
+
+    with jax.named_scope("corner_share"):
+        pack = jnp.stack([own_u[0], own_v[0]])
         got = share_pivots(pack, [(0, 0), (1, 1)])
         corner = jnp.where(col == row, pack, got)
-        ours_v, theirs_v = share_planes(jnp.where(core == 0, own_v, pack), row)
+    with jax.named_scope("first_lead"):
+        keep = jnp.arange(width, dtype=jnp.int32) < own_ranks[0, 0]
+        near_lead, lead = share_row(jnp.where(keep, pack, 0.0), 0, col)
     with jax.named_scope("first_upper"):
-        up_a, up_b = call(functools.partial(upper_kernel, 0), (one, one), flags[0], near_field, corner, own_u)
-    with jax.named_scope("first_lead"):
-        held, _ = lax.optimization_barrier((pack, got))
-        lead = share_row(held, 0, col)
+        up_a, up_b = call(upper_kernel, (payload, payload), flags[0], near_field, corner, own_u, own_v)
     with jax.named_scope("upper_share"):
-        crossed = lax.ppermute(up_b, "row", [(0, 1)])
-        up_a, up_b = share_planes(jnp.where(core == 0, up_a, crossed), row)
-    with jax.named_scope("first_wide"):
-        wide, extra = call(wide_kernel, (pair, pair), flags[0], lead, up_a, up_b, ours_v, theirs_v)
+        crossed = lax.ppermute(up_a, "row", [(0, 1)])
+        ours_0, theirs_0 = share_planes(jnp.where(core == 0, up_b, crossed), row)
+    with jax.named_scope("wide_share"):
+        extra = call(wide_kernel, (payload,), flags[0], near_lead, crossed)
         got = share_pivots(extra, [(1, 1)])
         extra = jnp.where(col == row, extra, got)
     with jax.named_scope("first_update"):
-        scratch = [[pltpu.VMEM((2, width, tile), F32), pltpu.VMEM((2, order[k], width), F32)] for k in range(2)]
-        cur_u, cur_v, pack = call(
-            functools.partial(panel_kernel, order[0], True),
-            (pair, pair, pair),
-            flags[0], own_u, own_v, wide, ours_v, theirs_v, sketch_t[0],
+        cur_u, cur_v, pack, out_z, out_v = call(
+            functools.partial(panel_kernel, order[0], 0),
+            (pair, pair, pair, packed, packed),
+            flags[0], near_field, own_u, own_v, lead, ours_0, theirs_0, corner, extra, sketch,
             scratch=scratch[0],
         )
-    with jax.named_scope("second_upper"):
-        fresh = call(functools.partial(upper_kernel, 1), (pair,), flags[1], near_field, corner, extra, cur_u)
     with jax.named_scope("second_share"):
-        crossed = lax.ppermute(fresh, "row", [(1, 0)])
-        fresh_a, fresh_b = share_planes(jnp.where(core == 1, cur_v, crossed), row)
-        lead = share_row(pack, 1, col)
-    with jax.named_scope("lower"):
-        low = call(
-            lower_kernel, ((width, tile),),
-            flags[1], near_field, up_a, up_b, ours_v, theirs_v, fresh_a, fresh_b, cur_v,
-        )
+        _, lead = share_row(pack, 1, col)
+        crossed = lax.ppermute(out_z, "row", [(1, 0)])
+        ours, theirs = share_planes(jnp.where(core == 1, out_v, crossed), row)
     with jax.named_scope("second_update"):
         cur_u, cur_v = call(
-            functools.partial(panel_kernel, order[1], False),
+            functools.partial(panel_kernel, order[1], 1),
             (pair, pair),
-            flags[1], cur_u, cur_v, lead, fresh_a, fresh_b, low, sketch_t[1],
+            flags[1], near_field, cur_u, cur_v, lead, ours, theirs, ours_0, theirs_0, sketch,
             scratch=scratch[1],
         )
     shape_out = factor_u.shape

time: 189 us -> 162 us (0.86)
  Pallas kernels: 58 us -> 38.4 us
  waiting for transfers between devices: 35.2 us -> 50.3 us
  starting transfers between devices: 58.2 us -> 44.3 us
  other arithmetic: 19.1 us -> 14.1 us
  local copies, waits for them, and re-layouts: 15.7 us -> 11.3 us
    pallas_call x6 -> x4, Pallas kernels: 58 us -> 38.4 us  [call(): pl.pallas_call(kernel, out_shape=shapes, in_specs=[pl.BlockSpec(memory_sp...]
    ppermute x24 -> x18, waiting for transfers between devices: 19.2 us -> 32.2 us  [fan_out(): moved = lax.ppermute(value, axis, pairs)]
    ppermute x24 -> x18, starting transfers between devices: 45.2 us -> 32.7 us  [fan_out(): moved = lax.ppermute(value, axis, pairs)]
    slice x3 -> x1, local copies, waits for them, and re-layouts: 4.43 us -> 1.07 us  [body(): pack = jnp.stack([own_u[0], own_v[0]])]
    ppermute x2, waiting for transfers between devices: 2.71 us -> 4.63 us  [the longest x1 2.94 us: body(): crossed = lax.ppermute(out_z, 'row', [(1, 0)])]
    select_n x1, other arithmetic: 2.13 us -> 0.22 us  [body(): extra = jnp.where(col == row, extra, got)]
    select_n x5 -> x4, other arithmetic: 5.23 us -> 3.51 us  [the longest x1 1.22 us: body(): ours, theirs = share_planes(jnp.where(core == 1, out_v, crossed), row)]
    unnamed x46 -> x40, local copies, waits for them, and re-layouts: 9.33 us -> 8.91 us
  transfers between devices with their start and end apart: 33 -> 26, of which waited for: 10 -> 14; matrix products, arithmetic and copies ran while one was open for 11% -> 6% of each run, Pallas kernels for 17% -> 1%
where the time goes in v3:
time: 162 us; the launch traced here: 159 us
  waiting for transfers between devices  50.3 us (31%)
  starting transfers between devices  44.3 us (27%)
  Pallas kernels  38.4 us (24%)
  other arithmetic  14.1 us (9%)
  local copies, waits for them, and re-layouts  11.3 us (7%)
    pallas_call x4, Pallas kernels, call(): pl.pallas_call(kernel, out_shape=shapes, in_specs=[pl.BlockSpec(memory_sp...  38.4 us
    ppermute x18, starting transfers between devices, fan_out(): moved = lax.ppermute(value, axis, pairs)  32.7 us
    ppermute x18, waiting for transfers between devices, fan_out(): moved = lax.ppermute(value, axis, pairs)  32.2 us
    ppermute x2, waiting for transfers between devices, share_row(): two = lax.ppermute(held, 'col', [(root, left), (right, far)])  13.5 us
    unnamed x40, local copies, waits for them, and re-layouts  8.91 us
    ppermute x2, starting transfers between devices, share_row(): two = lax.ppermute(held, 'col', [(root, left), (right, far)])  5.62 us
  transfers between devices with their start and end apart: 26, of which 14 were waited for; matrix products, arithmetic and copies ran while one was open for 6% of the time, Pallas kernels for 1%

profile of v3, /device:TPU:0, one launch (start us, length us, event | category | flops | bytes accessed | tf_op | source)
XLA Modules:
  0.0 159.4 jit_solution(4016942522650247650)
XLA Ops:
  0.6 1.1 slice_bitcast_fusion
  1.7 0.7 copy-done.18
  2.4 0.8 pad_maximum_fusion
  3.3 5.9 %collective-permute-start.3 = (f32[2,512,128]{2,1,0:T(8,128)}, f32[2,512,128]{2,1,0:T(8,128)}, u32[]{:S(2)}, u32[]{:S(2)}) collective-permute-start(f32[2,512,128]{2,1,0:T(8,128)} %pad_maximum_fusion), channel_id=1, source_target_pairs={{0,3},{5,4}} | collective-permute-start | bytes 1572872 | tf_op jit(solution)/shard_map/corner_share/ppermute | solution.py:279
  9.2 2.1 %collective-permute-start.2 = (f32[2,512,128]{2,1,0:T(8,128)}, f32[2,512,128]{2,1,0:T(8,128)}, u32[]{:S(2)}, u32[]{:S(2)}) collective-permute-start(f32[2,512,128]{2,1,0:T(8,128)} %pad_maximum_fusion), channel_id=1, source_target_pairs={{0,1},{5,6}} | collective-permute-start | bytes 1572872 | tf_op jit(solution)/shard_map/corner_share/ppermute | solution.py:279
  11.3 2.1 %collective-permute-start.4 = (f32[2,512,128]{2,1,0:T(8,128)}, f32[2,512,128]{2,1,0:T(8,128)}, u32[]{:S(2)}, u32[]{:S(2)}) collective-permute-start(f32[2,512,128]{2,1,0:T(8,128)} %pad_maximum_fusion), channel_id=1, source_target_pairs={{0,2},{5,7}} | collective-permute-start | bytes 1572872 | tf_op jit(solution)/shard_map/corner_share/ppermute | solution.py:279
  13.5 0.6 slice.36
  14.6 0.6 iota_compare_fusion
  15.3 5.7 %collective-permute-done.3 = f32[2,512,128]{2,1,0:T(8,128)} collective-permute-done((f32[2,512,128]{2,1,0:T(8,128)}, f32[2,512,128]{2,1,0:T(8,128)}, u32[]{:S(2)}, u32[]{:S(2)}) %collective-permute-start.3) | collective-permute-done | bytes 524320 | tf_op jit(solution)/shard_map/corner_share/ppermute | solution.py:279
  21.0 2.1 %collective-permute-done.4 = f32[2,512,128]{2,1,0:T(8,128)} collective-permute-done((f32[2,512,128]{2,1,0:T(8,128)}, f32[2,512,128]{2,1,0:T(8,128)}, u32[]{:S(2)}, u32[]{:S(2)}) %collective-permute-start.4) | collective-permute-done | bytes 524320 | tf_op jit(solution)/shard_map/corner_share/ppermute | solution.py:279
  23.1 2.3 %add_select_fusion.5 = (f32[2,512,128]{2,1,0:T(8,128)S(1)}, f32[2,512,128]{2,1,0:T(8,128)}) fusion(f32[2,512,128]{2,1,0:T(8,128)} %collective-permute-done.4, f32[2,512,128]{2,1,0:T(8,128)} %collective-permute-done.2, f32[2,512,128]{2,1,0:T(8,128)} %collective-permute-done.3, pred[]{:T(512)S(6)} %eq.51, f32[1,512,128]{2,1,0:T(8,128)S(1)} %get-tuple-element.29, ...), kind=kLoop, calls=%fused_computation.6 | loop fusion | flops 655360 | bytes 3145857 | tf_op jit(solution)/shard_map/corner_share/jit(_where)/select_n | solution.py:358
  25.4 5.2 %first_upper.1 = (f32[256,512]{1,0:T(8,128)}, f32[256,512]{1,0:T(8,128)S(1)}) custom-call(s32[12]{0:T(128)S(1)} %concatenate.7.flags, f32[2,512,512]{2,1,0:T(8,128)S(1)} %copy-done, f32[2,512,128]{2,1,0:T(8,128)S(1)} %get-tuple-element.27.corner.refs_0_, f32[2,512,128]{2,1,0:T(8,128)S(1)} %bitcast.19, f32[2,512,128]{2,1,0:T(8,128)S(1)} %bitcast.21), custom_call_target="tpu_custom_call" | custom-call | tf_op jit(solution)/shard_map/first_upper/pallas_call | solution.py:256
  30.6 0.8 copy-done.1
  31.4 0.8 copy-done.17
  32.2 1.3 collective-permute-start.5
  33.5 1.7 %collective-permute-done.5.crossed = f32[256,512]{1,0:T(8,128)S(1)} collective-permute-done((f32[256,512]{1,0:T(8,128)}, f32[256,512]{1,0:T(8,128)S(1)}, u32[]{:S(2)}, u32[]{:S(2)}) %collective-permute-start.5) | collective-permute-done | bytes 524320 | tf_op jit(solution)/shard_map/upper_share/ppermute | solution.py:365
  35.2 1.1 broadcast_select_fusion.4
  36.3 2.1 %collective-permute-start.8 = (f32[256,512]{1,0:T(8,128)S(1)}, f32[256,512]{1,0:T(8,128)}, u32[]{:S(2)}, u32[]{:S(2)}) collective-permute-start(f32[256,512]{1,0:T(8,128)S(1)} %broadcast_select_fusion.4), channel_id=1, source_target_pairs={{0,64},{4,20},{1,65},{5,21},{2,66},{6,22},{3,67},{7,23}} | collective-permute-start | bytes 1572872 | tf_op jit(solution)/shard_map/upper_share/ppermute | solution.py:279
  38.4 2.1 %collective-permute-start.7 = (f32[256,512]{1,0:T(8,128)S(1)}, f32[256,512]{1,0:T(8,128)}, u32[]{:S(2)}, u32[]{:S(2)}) collective-permute-start(f32[256,512]{1,0:T(8,128)S(1)} %broadcast_select_fusion.4), channel_id=1, source_target_pairs={{0,96},{4,28},{1,97},{5,29},{2,98},{6,30},{3,99},{7,31}} | collective-permute-start | bytes 1572872 | tf_op jit(solution)/shard_map/upper_share/ppermute | solution.py:279
  40.5 2.1 %collective-permute-start.6 = (f32[256,512]{1,0:T(8,128)S(1)}, f32[256,512]{1,0:T(8,128)}, u32[]{:S(2)}, u32[]{:S(2)}) collective-permute-start(f32[256,512]{1,0:T(8,128)S(1)} %broadcast_select_fusion.4), channel_id=1, source_target_pairs={{0,32},{4,12},{1,33},{5,13},{2,34},{6,14},{3,35},{7,15}} | collective-permute-start | bytes 1572872 | tf_op jit(solution)/shard_map/upper_share/ppermute | solution.py:279
  42.6 2.1 %collective-permute-start = (f32[2,512,128]{2,1,0:T(8,128)}, f32[2,512,128]{2,1,0:T(8,128)}, u32[]{:S(2)}, u32[]{:S(2)}) collective-permute-start(f32[2,512,128]{2,1,0:T(8,128)} %get-tuple-element.28), channel_id=1, source_target_pairs={{0,1},{4,5},{8,9},{12,13},{16,17},{20,21},{24,25},{28,29},{32,33},... | collective-permute-start | bytes 1572872 | tf_op jit(solution)/shard_map/first_lead/ppermute | solution.py:311
  44.7 1.7 %collective-permute-done.7 = f32[256,512]{1,0:T(8,128)} collective-permute-done((f32[256,512]{1,0:T(8,128)S(1)}, f32[256,512]{1,0:T(8,128)}, u32[]{:S(2)}, u32[]{:S(2)}) %collective-permute-start.7) | collective-permute-done | bytes 524320 | tf_op jit(solution)/shard_map/upper_share/ppermute | solution.py:279
  46.4 3.5 %collective-permute-done.6 = f32[256,512]{1,0:T(8,128)} collective-permute-done((f32[256,512]{1,0:T(8,128)S(1)}, f32[256,512]{1,0:T(8,128)}, u32[]{:S(2)}, u32[]{:S(2)}) %collective-permute-start.6) | collective-permute-done | bytes 524320 | tf_op jit(solution)/shard_map/upper_share/ppermute | solution.py:279
  49.9 2.4 %add_select_fusion.4 = f32[256,512]{1,0:T(8,128)} fusion(f32[256,512]{1,0:T(8,128)S(1)} %broadcast_select_fusion.4, f32[256,512]{1,0:T(8,128)} %collective-permute-done.8, f32[256,512]{1,0:T(8,128)} %collective-permute-done.6, f32[256,512]{1,0:T(8,128)} %collective-permute-done.7, pred[]{:T(512)S(6)} %lt.41), kind=kLoop, calls=%fused_computation.5 | loop fusion | flops 393216 | bytes 2621441 | tf_op jit(solution)/shard_map/upper_share/jit(_where)/select_n | solution.py:293
  52.3 2.1 %collective-permute-start.11 = (f32[256,512]{1,0:T(8,128)}, f32[256,512]{1,0:T(8,128)}, u32[]{:S(2)}, u32[]{:S(2)}) collective-permute-start(f32[256,512]{1,0:T(8,128)} %add_select_fusion.4), channel_id=1, source_target_pairs={{0,16},{32,48},{64,80},{96,112},{4,68},{12,76},{20,84},{28,92},{1,... | collective-permute-start | bytes 1572872 | tf_op jit(solution)/shard_map/upper_share/ppermute | solution.py:279
  54.4 2.1 %collective-permute-start.10 = (f32[256,512]{1,0:T(8,128)}, f32[256,512]{1,0:T(8,128)}, u32[]{:S(2)}, u32[]{:S(2)}) collective-permute-start(f32[256,512]{1,0:T(8,128)} %add_select_fusion.4), channel_id=1, source_target_pairs={{0,24},{32,56},{64,88},{96,120},{4,100},{12,108},{20,116},{28,124}... | collective-permute-start | bytes 1572872 | tf_op jit(solution)/shard_map/upper_share/ppermute | solution.py:279
  56.5 2.1 %collective-permute-start.9 = (f32[256,512]{1,0:T(8,128)}, f32[256,512]{1,0:T(8,128)}, u32[]{:S(2)}, u32[]{:S(2)}) collective-permute-start(f32[256,512]{1,0:T(8,128)} %add_select_fusion.4), channel_id=1, source_target_pairs={{0,8},{32,40},{64,72},{96,104},{4,36},{12,44},{20,52},{28,60},{1,9... | collective-permute-start | bytes 1572872 | tf_op jit(solution)/shard_map/upper_share/ppermute | solution.py:279
  58.6 1.1 broadcast_select_fusion.5.lead
  59.7 4.3 %collective-permute-start.1 = (f32[2,512,128]{2,1,0:T(8,128)S(1)}, f32[2,512,128]{2,1,0:T(8,128)}, u32[]{:S(2)}, u32[]{:S(2)}) collective-permute-start(f32[2,512,128]{2,1,0:T(8,128)S(1)} %broadcast_select_fusion.5.lead), channel_id=1, source_target_pairs={{0,3},{1,2},{4,7},{5,6},{8,11},{9,10},{12,15},{13,14},{16,19},{17,... | collective-permute-start | bytes 1572872 | tf_op jit(solution)/shard_map/first_lead/ppermute | solution.py:313
  64.0 1.0 wide_share.1
  65.0 0.7 collective-permute-start.15
  65.7 0.7 collective-permute-start.14
  66.5 0.7 collective-permute-start.13
  67.2 1.7 %add_select_fusion.3.ours.refs_0_ = f32[256,512]{1,0:T(8,128)S(1)} fusion(f32[256,512]{1,0:T(8,128)} %add_select_fusion.4, f32[256,512]{1,0:T(8,128)} %collective-permute-done.11, f32[256,512]{1,0:T(8,128)} %collective-permute-done.9, f32[256,512]{1,0:T(8,128)} %collective-permute-done.10, pred[]{:T(512)S(6)} %eq.50), kind=kLoop, calls=%fused_computation.4 | loop fusion | flops 393216 | bytes 2621441 | tf_op jit(solution)/shard_map/upper_share/jit(_where)/select_n | solution.py:304
  69.2 9.7 %collective-permute-done.1 = f32[2,512,128]{2,1,0:T(8,128)} collective-permute-done((f32[2,512,128]{2,1,0:T(8,128)S(1)}, f32[2,512,128]{2,1,0:T(8,128)}, u32[]{:S(2)}, u32[]{:S(2)}) %collective-permute-start.1) | collective-permute-done | bytes 524320 | tf_op jit(solution)/shard_map/first_lead/ppermute | solution.py:313
  79.3 17.6 %first_update.1 = (f32[2,512,128]{2,1,0:T(8,128)S(1)}, f32[2,512,128]{2,1,0:T(8,128)S(1)}, f32[2,512,128]{2,1,0:T(8,128)S(1)}, f32[3,96,512]{2,1,0:T(8,128)}, f32[3,96,512]{2,1,0:T(8,128)S(1)}) custom-call(s32[12]{0:T(128)S(1)} %concatenate.7.flags, f32[2,512,512]{2,1,0:T(8,128)S(1)} %copy-done, f32[2,512,128]{2,1,0:T(8,128)S(1)} %bitcast.20, ...), custom_call_target="tpu_custom_call" | custom-call | tf_op jit(solution)/shard_map/first_update/pallas_call | solution.py:256
  96.9 0.8 copy-done.11
  97.7 0.8 copy-done.13
  98.5 0.8 copy-done.15
  99.3 1.3 collective-permute-start.18
  100.6 2.9 %collective-permute-done.18 = f32[3,96,512]{2,1,0:T(8,128)} collective-permute-done((f32[3,96,512]{2,1,0:T(8,128)}, f32[3,96,512]{2,1,0:T(8,128)}, u32[]{:S(2)}, u32[]{:S(2)}) %collective-permute-start.18) | collective-permute-done | bytes 589856 | tf_op jit(solution)/shard_map/second_share/ppermute | solution.py:380
  103.6 1.2 broadcast_select_fusion
  104.8 1.3 collective-permute-start.21
  106.1 1.3 collective-permute-start.20
  107.4 1.3 collective-permute-start.19
  108.8 0.7 collective-permute-start.16
  109.5 4.0 %collective-permute-done.21 = f32[3,96,512]{2,1,0:T(8,128)S(1)} collective-permute-done((f32[3,96,512]{2,1,0:T(8,128)S(1)}, f32[3,96,512]{2,1,0:T(8,128)S(1)}, u32[]{:S(2)}, u32[]{:S(2)}) %collective-permute-start.21) | collective-permute-done | bytes 589856 | tf_op jit(solution)/shard_map/second_share/ppermute | solution.py:279
  113.5 1.3 collective-permute-done.20
  114.8 5.0 %collective-permute-done.19 = f32[3,96,512]{2,1,0:T(8,128)S(1)} collective-permute-done((f32[3,96,512]{2,1,0:T(8,128)S(1)}, f32[3,96,512]{2,1,0:T(8,128)S(1)}, u32[]{:S(2)}, u32[]{:S(2)}) %collective-permute-start.19) | collective-permute-done | bytes 589856 | tf_op jit(solution)/shard_map/second_share/ppermute | solution.py:279
  120.0 1.3 collective-permute-start.24
  121.4 1.3 collective-permute-start.23
  122.7 1.3 collective-permute-start.22
  124.1 0.9 broadcast_select_fusion.2
  124.9 1.3 collective-permute-start.17
  126.2 2.5 %collective-permute-done.24 = f32[3,96,512]{2,1,0:T(8,128)S(1)} collective-permute-done((f32[3,96,512]{2,1,0:T(8,128)S(1)}, f32[3,96,512]{2,1,0:T(8,128)S(1)}, u32[]{:S(2)}, u32[]{:S(2)}) %collective-permute-start.24) | collective-permute-done | bytes 589856 | tf_op jit(solution)/shard_map/second_share/ppermute | solution.py:279
  128.7 1.3 collective-permute-done.23
  130.0 5.0 %collective-permute-done.22 = f32[3,96,512]{2,1,0:T(8,128)S(1)} collective-permute-done((f32[3,96,512]{2,1,0:T(8,128)S(1)}, f32[3,96,512]{2,1,0:T(8,128)S(1)}, u32[]{:S(2)}, u32[]{:S(2)}) %collective-permute-start.22) | collective-permute-done | bytes 589856 | tf_op jit(solution)/shard_map/second_share/ppermute | solution.py:279
  135.8 3.8 %collective-permute-done.17 = f32[2,512,128]{2,1,0:T(8,128)} collective-permute-done((f32[2,512,128]{2,1,0:T(8,128)}, f32[2,512,128]{2,1,0:T(8,128)}, u32[]{:S(2)}, u32[]{:S(2)}) %collective-permute-start.17) | collective-permute-done | bytes 524320 | tf_op jit(solution)/shard_map/second_share/ppermute | solution.py:313
  139.5 1.1 broadcast_select_fusion.3.lead
  140.6 1.0 copy-done.8
  141.7 1.0 copy-done.10
  142.7 1.0 copy-done.12
  143.8 1.0 copy-done.14
  144.8 14.6 %second_update.1 = (f32[2,512,128]{2,1,0:T(8,128)}, f32[2,512,128]{2,1,0:T(8,128)}) custom-call(s32[12]{0:T(128)S(1)} %concatenate.6.flags, f32[2,512,512]{2,1,0:T(8,128)S(1)} %copy-done, f32[2,512,128]{2,1,0:T(8,128)S(1)} %copy-done.12, f32[2,512,128]{2,1,0:T(8,128)S(1)} %copy-done.14, f32[2,512,128]{2,1,0:T(8,128)S(1)} %broadcast_select_fusion.3.lead, ...), custom_call_target="tpu_custom_call" | custom-call | tf_op jit(solution)/shard_map/second_update/pallas_call | solution.py:256
  (56 shorter events, 2.2 us)
Async XLA Ops:
  0.6 12.7 %copy-start.19 = (s32[3,1,32,2,1]{2,4,3,1,0:T(1,128)S(1)}, s32[3,1,32,2,1]{2,4,3,1,0:T(1,128)}, u32[]{:S(2)}) copy-start(s32[3,1,32,2,1]{2,4,3,1,0:T(1,128)} %param.9) | copy-start | bytes 2308
  1.7 0.7 copy-start.18
  2.4 23.0 %copy-start = (f32[2,512,512]{2,1,0:T(8,128)S(1)}, f32[2,512,512]{2,1,0:T(8,128)}, u32[]{:S(2)}) copy-start(f32[2,512,512]{2,1,0:T(8,128)} %near.5) | copy-start | bytes 6291460
  2.4 23.0 %copy-start.3 = (f32[1,1,2,1,512,128]{5,4,3,2,1,0:T(8,128)S(1)}, f32[1,1,2,1,512,128]{5,4,3,2,1,0:T(8,128)}, u32[]{:S(2)}) copy-start(f32[1,1,2,1,512,128]{5,4,3,2,1,0:T(8,128)} %param.5) | copy-start | bytes 1572868
  2.4 23.0 %copy-start.5 = (f32[1,1,2,1,512,128]{5,4,3,2,1,0:T(8,128)S(1)}, f32[1,1,2,1,512,128]{5,4,3,2,1,0:T(8,128)}, u32[]{:S(2)}) copy-start(f32[1,1,2,1,512,128]{5,4,3,2,1,0:T(8,128)} %param.6) | copy-start | bytes 1572868
  3.3 17.7 %collective-permute-start.3 = (f32[2,512,128]{2,1,0:T(8,128)}, f32[2,512,128]{2,1,0:T(8,128)}, u32[]{:S(2)}, u32[]{:S(2)}) collective-permute-start(f32[2,512,128]{2,1,0:T(8,128)} %pad_maximum_fusion), channel_id=1, source_target_pairs={{0,3},{5,4}} | collective-permute-start | bytes 1572872 | tf_op jit(solution)/shard_map/corner_share/ppermute | solution.py:279
  9.2 11.8 %collective-permute-start.2 = (f32[2,512,128]{2,1,0:T(8,128)}, f32[2,512,128]{2,1,0:T(8,128)}, u32[]{:S(2)}, u32[]{:S(2)}) collective-permute-start(f32[2,512,128]{2,1,0:T(8,128)} %pad_maximum_fusion), channel_id=1, source_target_pairs={{0,1},{5,6}} | collective-permute-start | bytes 1572872 | tf_op jit(solution)/shard_map/corner_share/ppermute | solution.py:279
  11.3 11.8 %collective-permute-start.4 = (f32[2,512,128]{2,1,0:T(8,128)}, f32[2,512,128]{2,1,0:T(8,128)}, u32[]{:S(2)}, u32[]{:S(2)}) collective-permute-start(f32[2,512,128]{2,1,0:T(8,128)} %pad_maximum_fusion), channel_id=1, source_target_pairs={{0,2},{5,7}} | collective-permute-start | bytes 1572872 | tf_op jit(solution)/shard_map/corner_share/ppermute | solution.py:279
  30.6 0.8 copy-start.1
  31.4 0.8 copy-start.17
  32.2 3.0 %collective-permute-start.5 = (f32[256,512]{1,0:T(8,128)}, f32[256,512]{1,0:T(8,128)S(1)}, u32[]{:S(2)}, u32[]{:S(2)}) collective-permute-start(f32[256,512]{1,0:T(8,128)} %get-tuple-element.12), channel_id=1, source_target_pairs={{0,4},{1,5},{2,6},{3,7}} | collective-permute-start | bytes 1572872 | tf_op jit(solution)/shard_map/upper_share/ppermute | solution.py:365
  36.3 8.4 %collective-permute-start.8 = (f32[256,512]{1,0:T(8,128)S(1)}, f32[256,512]{1,0:T(8,128)}, u32[]{:S(2)}, u32[]{:S(2)}) collective-permute-start(f32[256,512]{1,0:T(8,128)S(1)} %broadcast_select_fusion.4), channel_id=1, source_target_pairs={{0,64},{4,20},{1,65},{5,21},{2,66},{6,22},{3,67},{7,23}} | collective-permute-start | bytes 1572872 | tf_op jit(solution)/shard_map/upper_share/ppermute | solution.py:279
  38.4 8.0 %collective-permute-start.7 = (f32[256,512]{1,0:T(8,128)S(1)}, f32[256,512]{1,0:T(8,128)}, u32[]{:S(2)}, u32[]{:S(2)}) collective-permute-start(f32[256,512]{1,0:T(8,128)S(1)} %broadcast_select_fusion.4), channel_id=1, source_target_pairs={{0,96},{4,28},{1,97},{5,29},{2,98},{6,30},{3,99},{7,31}} | collective-permute-start | bytes 1572872 | tf_op jit(solution)/shard_map/upper_share/ppermute | solution.py:279
  40.5 9.4 %collective-permute-start.6 = (f32[256,512]{1,0:T(8,128)S(1)}, f32[256,512]{1,0:T(8,128)}, u32[]{:S(2)}, u32[]{:S(2)}) collective-permute-start(f32[256,512]{1,0:T(8,128)S(1)} %broadcast_select_fusion.4), channel_id=1, source_target_pairs={{0,32},{4,12},{1,33},{5,13},{2,34},{6,14},{3,35},{7,15}} | collective-permute-start | bytes 1572872 | tf_op jit(solution)/shard_map/upper_share/ppermute | solution.py:279
  42.6 16.0 %collective-permute-start = (f32[2,512,128]{2,1,0:T(8,128)}, f32[2,512,128]{2,1,0:T(8,128)}, u32[]{:S(2)}, u32[]{:S(2)}) collective-permute-start(f32[2,512,128]{2,1,0:T(8,128)} %get-tuple-element.28), channel_id=1, source_target_pairs={{0,1},{4,5},{8,9},{12,13},{16,17},{20,21},{24,25},{28,29},{32,33},... | collective-permute-start | bytes 1572872 | tf_op jit(solution)/shard_map/first_lead/ppermute | solution.py:311
  52.3 13.4 %collective-permute-start.11 = (f32[256,512]{1,0:T(8,128)}, f32[256,512]{1,0:T(8,128)}, u32[]{:S(2)}, u32[]{:S(2)}) collective-permute-start(f32[256,512]{1,0:T(8,128)} %add_select_fusion.4), channel_id=1, source_target_pairs={{0,16},{32,48},{64,80},{96,112},{4,68},{12,76},{20,84},{28,92},{1,... | collective-permute-start | bytes 1572872 | tf_op jit(solution)/shard_map/upper_share/ppermute | solution.py:279
  54.4 12.1 %collective-permute-start.10 = (f32[256,512]{1,0:T(8,128)}, f32[256,512]{1,0:T(8,128)}, u32[]{:S(2)}, u32[]{:S(2)}) collective-permute-start(f32[256,512]{1,0:T(8,128)} %add_select_fusion.4), channel_id=1, source_target_pairs={{0,24},{32,56},{64,88},{96,120},{4,100},{12,108},{20,116},{28,124}... | collective-permute-start | bytes 1572872 | tf_op jit(solution)/shard_map/upper_share/ppermute | solution.py:279
  56.5 10.7 %collective-permute-start.9 = (f32[256,512]{1,0:T(8,128)}, f32[256,512]{1,0:T(8,128)}, u32[]{:S(2)}, u32[]{:S(2)}) collective-permute-start(f32[256,512]{1,0:T(8,128)} %add_select_fusion.4), channel_id=1, source_target_pairs={{0,8},{32,40},{64,72},{96,104},{4,36},{12,44},{20,52},{28,60},{1,9... | collective-permute-start | bytes 1572872 | tf_op jit(solution)/shard_map/upper_share/ppermute | solution.py:279
  59.7 19.2 %collective-permute-start.1 = (f32[2,512,128]{2,1,0:T(8,128)S(1)}, f32[2,512,128]{2,1,0:T(8,128)}, u32[]{:S(2)}, u32[]{:S(2)}) collective-permute-start(f32[2,512,128]{2,1,0:T(8,128)S(1)} %broadcast_select_fusion.5.lead), channel_id=1, source_target_pairs={{0,3},{1,2},{4,7},{5,6},{8,11},{9,10},{12,15},{13,14},{16,19},{17,... | collective-permute-start | bytes 1572872 | tf_op jit(solution)/shard_map/first_lead/ppermute | solution.py:313
  65.0 14.0 %collective-permute-start.15 = (f32[256,512]{1,0:T(8,128)S(1)}, f32[256,512]{1,0:T(8,128)S(1)}, u32[]{:S(2)}, u32[]{:S(2)}) collective-permute-start(f32[256,512]{1,0:T(8,128)S(1)} %wide_share.1), channel_id=1, source_target_pairs={{5,7}} | collective-permute-start | bytes 1572872 | tf_op jit(solution)/shard_map/wide_share/ppermute | solution.py:279
  65.7 13.3 %collective-permute-start.14 = (f32[256,512]{1,0:T(8,128)S(1)}, f32[256,512]{1,0:T(8,128)S(1)}, u32[]{:S(2)}, u32[]{:S(2)}) collective-permute-start(f32[256,512]{1,0:T(8,128)S(1)} %wide_share.1), channel_id=1, source_target_pairs={{5,4}} | collective-permute-start | bytes 1572872 | tf_op jit(solution)/shard_map/wide_share/ppermute | solution.py:279
  66.5 12.6 %collective-permute-start.13 = (f32[256,512]{1,0:T(8,128)S(1)}, f32[256,512]{1,0:T(8,128)S(1)}, u32[]{:S(2)}, u32[]{:S(2)}) collective-permute-start(f32[256,512]{1,0:T(8,128)S(1)} %wide_share.1), channel_id=1, source_target_pairs={{5,6}} | collective-permute-start | bytes 1572872 | tf_op jit(solution)/shard_map/wide_share/ppermute | solution.py:279
  68.9 10.3 %copy-start.2 = (f32[2,512,128]{2,1,0:T(8,128)S(1)}, f32[2,512,128]{2,1,0:T(8,128)}, u32[]{:S(2)}) copy-start(f32[2,512,128]{2,1,0:T(8,128)} %copy-done.1) | copy-start | bytes 1572868
  68.9 10.3 %copy-start.4 = (f32[1,1,2,1,512,128]{5,4,3,2,1,0:T(8,128)S(1)}, f32[1,1,2,1,512,128]{5,4,3,2,1,0:T(8,128)}, u32[]{:S(2)}) copy-start(f32[1,1,2,1,512,128]{5,4,3,2,1,0:T(8,128)} %param.5) | copy-start | bytes 1572868
  68.9 10.3 %copy-start.6 = (f32[1,1,2,1,512,128]{5,4,3,2,1,0:T(8,128)S(1)}, f32[1,1,2,1,512,128]{5,4,3,2,1,0:T(8,128)}, u32[]{:S(2)}) copy-start(f32[1,1,2,1,512,128]{5,4,3,2,1,0:T(8,128)} %param.6) | copy-start | bytes 1572868
  68.9 10.3 %copy-start.7 = (f32[2,512,128]{2,1,0:T(8,128)S(1)}, f32[2,512,128]{2,1,0:T(8,128)}, u32[]{:S(2)}) copy-start(f32[2,512,128]{2,1,0:T(8,128)} %refs_2_.3) | copy-start | bytes 1572868
  69.0 10.3 %collective-permute-start.12 = (f32[256,512]{1,0:T(8,128)S(1)}, f32[256,512]{1,0:T(8,128)S(1)}, u32[]{:S(2)}, u32[]{:S(2)}) collective-permute-start(f32[256,512]{1,0:T(8,128)S(1)} %add_select_fusion.3.ours.refs_0_), channel_id=1, source_target_pairs={{0,4},{4,0},{8,12},{12,8},{16,20},{20,16},{24,28},{28,24},{32,36},... | collective-permute-start | bytes 1572872 | tf_op jit(solution)/shard_map/upper_share/ppermute | solution.py:305
  79.3 17.6 %copy-start.9 = (f32[256,512]{1,0:T(8,128)}, f32[256,512]{1,0:T(8,128)S(1)}, u32[]{:S(2)}) copy-start(f32[256,512]{1,0:T(8,128)S(1)} %collective-permute-done.12.theirs.refs_1_) | copy-start | bytes 1572868
  96.9 0.8 copy-start.11
  97.7 0.8 copy-start.13
  98.5 0.8 copy-start.15
  99.3 4.2 %collective-permute-start.18 = (f32[3,96,512]{2,1,0:T(8,128)}, f32[3,96,512]{2,1,0:T(8,128)}, u32[]{:S(2)}, u32[]{:S(2)}) collective-permute-start(f32[3,96,512]{2,1,0:T(8,128)} %get-tuple-element.17), channel_id=1, source_target_pairs={{4,0},{5,1},{6,2},{7,3}} | collective-permute-start | bytes 1769480 | tf_op jit(solution)/shard_map/second_share/ppermute | solution.py:380
  103.6 20.5 %copy-start.16 = (f32[2,512,128]{2,1,0:T(8,128)S(1)}, f32[2,512,128]{2,1,0:T(8,128)}, u32[]{:S(2)}) copy-start(f32[2,512,128]{2,1,0:T(8,128)} %copy-done.15) | copy-start | bytes 1572868
  104.8 8.7 %collective-permute-start.21 = (f32[3,96,512]{2,1,0:T(8,128)S(1)}, f32[3,96,512]{2,1,0:T(8,128)S(1)}, u32[]{:S(2)}, u32[]{:S(2)}) collective-permute-start(f32[3,96,512]{2,1,0:T(8,128)S(1)} %broadcast_select_fusion), channel_id=1, source_target_pairs={{0,64},{4,20},{1,65},{5,21},{2,66},{6,22},{3,67},{7,23}} | collective-permute-start | bytes 1769480 | tf_op jit(solution)/shard_map/second_share/ppermute | solution.py:279
  106.1 8.7 %collective-permute-start.20 = (f32[3,96,512]{2,1,0:T(8,128)S(1)}, f32[3,96,512]{2,1,0:T(8,128)S(1)}, u32[]{:S(2)}, u32[]{:S(2)}) collective-permute-start(f32[3,96,512]{2,1,0:T(8,128)S(1)} %broadcast_select_fusion), channel_id=1, source_target_pairs={{0,96},{4,28},{1,97},{5,29},{2,98},{6,30},{3,99},{7,31}} | collective-permute-start | bytes 1769480 | tf_op jit(solution)/shard_map/second_share/ppermute | solution.py:279
  107.4 12.3 %collective-permute-start.19 = (f32[3,96,512]{2,1,0:T(8,128)S(1)}, f32[3,96,512]{2,1,0:T(8,128)S(1)}, u32[]{:S(2)}, u32[]{:S(2)}) collective-permute-start(f32[3,96,512]{2,1,0:T(8,128)S(1)} %broadcast_select_fusion), channel_id=1, source_target_pairs={{0,32},{4,12},{1,33},{5,13},{2,34},{6,14},{3,35},{7,15}} | collective-permute-start | bytes 1769480 | tf_op jit(solution)/shard_map/second_share/ppermute | solution.py:279
  108.8 15.3 %collective-permute-start.16 = (f32[2,512,128]{2,1,0:T(8,128)}, f32[2,512,128]{2,1,0:T(8,128)S(1)}, u32[]{:S(2)}, u32[]{:S(2)}) collective-permute-start(f32[2,512,128]{2,1,0:T(8,128)} %copy-done.15), channel_id=1, source_target_pairs={{1,2},{5,6},{9,10},{13,14},{17,18},{21,22},{25,26},{29,30},{33,34}... | collective-permute-start | bytes 1572872 | tf_op jit(solution)/shard_map/second_share/ppermute | solution.py:311
  120.0 8.7 %collective-permute-start.24 = (f32[3,96,512]{2,1,0:T(8,128)S(1)}, f32[3,96,512]{2,1,0:T(8,128)S(1)}, u32[]{:S(2)}, u32[]{:S(2)}) collective-permute-start(f32[3,96,512]{2,1,0:T(8,128)S(1)} %add_select_fusion.1), channel_id=1, source_target_pairs={{0,16},{32,48},{64,80},{96,112},{4,68},{12,76},{20,84},{28,92},{1,... | collective-permute-start | bytes 1769480 | tf_op jit(solution)/shard_map/second_share/ppermute | solution.py:279
  121.4 8.7 %collective-permute-start.23 = (f32[3,96,512]{2,1,0:T(8,128)S(1)}, f32[3,96,512]{2,1,0:T(8,128)S(1)}, u32[]{:S(2)}, u32[]{:S(2)}) collective-permute-start(f32[3,96,512]{2,1,0:T(8,128)S(1)} %add_select_fusion.1), channel_id=1, source_target_pairs={{0,24},{32,56},{64,88},{96,120},{4,100},{12,108},{20,116},{28,124}... | collective-permute-start | bytes 1769480 | tf_op jit(solution)/shard_map/second_share/ppermute | solution.py:279
  122.7 12.3 %collective-permute-start.22 = (f32[3,96,512]{2,1,0:T(8,128)S(1)}, f32[3,96,512]{2,1,0:T(8,128)S(1)}, u32[]{:S(2)}, u32[]{:S(2)}) collective-permute-start(f32[3,96,512]{2,1,0:T(8,128)S(1)} %add_select_fusion.1), channel_id=1, source_target_pairs={{0,8},{32,40},{64,72},{96,104},{4,36},{12,44},{20,52},{28,60},{1,9... | collective-permute-start | bytes 1769480 | tf_op jit(solution)/shard_map/second_share/ppermute | solution.py:279
  124.9 14.6 %collective-permute-start.17 = (f32[2,512,128]{2,1,0:T(8,128)}, f32[2,512,128]{2,1,0:T(8,128)}, u32[]{:S(2)}, u32[]{:S(2)}) collective-permute-start(f32[2,512,128]{2,1,0:T(8,128)} %broadcast_select_fusion.2), channel_id=1, source_target_pairs={{1,0},{2,3},{5,4},{6,7},{9,8},{10,11},{13,12},{14,15},{17,16},{18,... | collective-permute-start | bytes 1572872 | tf_op jit(solution)/shard_map/second_share/ppermute | solution.py:313
  135.3 5.3 %collective-permute-start.25 = (f32[3,96,512]{2,1,0:T(8,128)S(1)}, f32[3,96,512]{2,1,0:T(8,128)}, u32[]{:S(2)}, u32[]{:S(2)}) collective-permute-start(f32[3,96,512]{2,1,0:T(8,128)S(1)} %add_select_fusion.ours), channel_id=1, source_target_pairs={{0,4},{4,0},{8,12},{12,8},{16,20},{20,16},{24,28},{28,24},{32,36},... | collective-permute-start | bytes 1769480 | tf_op jit(solution)/shard_map/second_share/ppermute | solution.py:305
  140.6 1.0 copy-start.8
  141.7 1.0 copy-start.10
  142.7 1.0 copy-start.12
  143.8 1.0 copy-start.14

commit v4 on v3

--- a/solution.py
+++ b/solution.py
@@ -79,12 +79,6 @@
     return outs
 
 
-def wide_t(lead, z_t):
-    weight = 1.0 / (8.0 * lead.shape[1])
-    core_t = weight * dot3(z_t, lead[1])
-    return core_t
-
-
 def diagonal_inverse(far):
     eye = iota(far.shape, 0) == iota(far.shape, 1)
     return 1.0 / jnp.sum(jnp.where(eye, far, 0.0), axis=0, keepdims=True)
@@ -97,32 +91,26 @@
     return rest, square, split(dot3(square, square))
 
 
-def upper_kernel(flags, near, corner, own_u, own_v, out_a, out_b):
-    tile, width = own_u.shape[1:]
+def lower_kernel(flags, near, ours, theirs, own_v, out, up):
+    tile, width = ours.shape
     weight = 1.0 / (8.0 * tile)
+    even = flags[11] == 0
+    lanes = iota((tile, width), 1)
+    up_u = jnp.where(even, ours[...], theirs[...])
+    up_v = jnp.where(even, theirs[...], ours[...])
+    up[0] = jnp.where(lanes < flags[4], up_u, 0.0)
+    up[1] = up_v
     far = near[0]
     start = diagonal_inverse(far)
-    parts = series(far + weight * dot3(corner[0], corner[1], NT), start)
-    lanes = iota((tile, width), 1)
-    values = jnp.concatenate([jnp.where(lanes < flags[2 + s], own_u[s], 0.0).T for s in range(2)], axis=0)
-    for part in parts[::-1]:
-        values = values + dot3(values, part, NT)
-    values = values * start
-    out_a[:width] = jnp.where(flags[10] == 0, corner[0].T, values[:width])
-    out_a[width:] = own_v[0].T
-    out_b[:width] = values[width:]
-    out_b[width:] = own_v[1].T
-
-
-def wide_kernel(flags, lead, crossed, out):
-    width = lead.shape[2]
-    out[:width] = dot3(wide_t(lead, crossed[:width]), lead[0], NT)
-    out[width:] = crossed[width:]
+    low = jnp.where(lanes < flags[2], own_v[0], 0.0).T * start
+    for part in series(far + weight * dot3(up_u, up_v, NT), start):
+        low = low + dot3(low, part)
+    out[...] = low
 
 
 def panel_kernel(order, panel, flags, near, cu, cv, lead, ours, theirs, *refs):
     if panel == 0:
-        corner, extra, sketch, nu, nv, pack, out_z, out_v, ortho, factor, moved = refs
+        ours_1, theirs_1, low_t, corner, cross, sketch, nu, nv, pack, out_z, out_v, ortho, factor, moved = refs
     else:
         ours_0, theirs_0, sketch, nu, nv, ortho, factor, moved = refs
     tile, width = cu.shape[1:]
@@ -136,18 +124,24 @@
     even = flags[11] == 0
     full_us, full_vs, bases, grams, units = [], [], [], [], []
     test_t = sketch[panel].T[:order]
+    if panel == 1:
+        part = ours.shape[1]
+        rest = jnp.zeros((width - part, tile), F32)
+        lead_u = jnp.concatenate([lead[0], rest], axis=0)
+        lead_v = jnp.concatenate([lead[1], rest], axis=0)
     for s in range(2):
         own_u = cu[s]
         if panel == 0:
             own_u = jnp.where(lanes < flags[2 + s], own_u, 0.0)
-            slot = jnp.where(even, theirs[...], ours[...]) if s == 0 else jnp.where(even, ours[...], theirs[...])
-            z_t, up_v = slot[:width], slot[width:].T
+            mine, other = ((ours, theirs), (ours_1, theirs_1))[s]
+            up_u = jnp.where(even, mine[...], other[...])
+            up_u = jnp.where(lanes < flags[4 + s], up_u, 0.0)
+            up_v = jnp.where(even, other[...], mine[...])
+            side = dot3(lead[...], weight * dot3(low_t[...], up_u))
         else:
-            part = ours.shape[1]
-            rest = jnp.zeros((width - part, tile), F32)
             z_t = jnp.concatenate([jnp.where(even, ours[s], theirs[s]), rest], axis=0)
             up_v = jnp.concatenate([jnp.where(even, theirs[s], ours[s]), rest], axis=0).T
-        side = dot3(lead[0], wide_t(lead, z_t), NT)
+            side = dot3(weight * dot3(z_t, lead_v, NT), lead_u).T
         full_u = jnp.concatenate([own_u, -side], axis=1)
         full_v = jnp.concatenate([cv[s], up_v], axis=1)
         projected = dot6(test_t, full_v)
@@ -161,24 +155,19 @@
         bases.append(basis)
         units.append(unit)
 
+    far = near[1]
+    start = diagonal_inverse(far)
     if panel == 0:
-        far = near[1]
-        start = diagonal_inverse(far)
-        low_rank = dot3(corner[0], corner[1], NT) - dot3(extra[:width], extra[width:], TN)
+        wide = dot3(lead[...], weight * dot3(low_t[...], cross[0]))
+        low_rank = dot3(corner[0], corner[1], NT) - dot3(wide, cross[1], NT)
         parts = series(far + weight * low_rank, start)
     else:
-        left = flags[10] == 0
-        slot = jnp.where(even, theirs_0[...], ours_0[...])
         moved[:part] = jnp.where(even, ours[0], theirs[0])
         moved[part:2 * part] = jnp.where(even, theirs[0], ours[0])
         moved[2 * part:3 * part] = jnp.where(even, ours[2], theirs[2])
         moved[3 * part:] = jnp.where(even, theirs[2], ours[2])
-        far = jnp.where(left, near[0], near[1])
-        start = diagonal_inverse(far)
-        one_u = jnp.where(left, slot[:width], moved[width:2 * width])
-        one_v = jnp.where(left, slot[width:], moved[2 * width:])
-        two_u = jnp.where(left, 0.0, moved[:width])
-        low_rank = dot3(one_u, one_v, TN) - dot3(two_u, slot[width:], TN)
+        first_v = jnp.where(even, theirs_0[...], ours_0[...]).T
+        low_rank = dot3(moved[width:2 * width], moved[2 * width:], TN) - dot3(moved[:width], first_v, TN)
         low = cv[0].T * start
         for factors in series(far + weight * low_rank, start):
             low = low + dot3(low, factors)
@@ -189,7 +178,7 @@
         once = dot6(inverses[s], bases[s])
         ortho[s, :order] = once
         ortho[s, order:] = spare
-        gram = dot6(once, jnp.concatenate([once, spare], axis=0), NT) + units[s]
+        gram = dot3(once, jnp.concatenate([once, spare], axis=0), NT) + units[s]
         factor[s] = gram
         off = gram - eye
         defect = defect + jnp.where(flags[6 + s] == 1, jnp.sum(off * off), 0.0)
@@ -221,8 +210,8 @@
         if panel == 0:
             keep_u = jnp.where(lanes < flags[2 + s], keep_u, 0.0)
             keep_v = jnp.where(lanes < flags[2 + s], keep_v, 0.0)
-        elif s == 0:
-            keep_v = jnp.where(flags[8] == 1, low.T, keep_v)
+        if s == 0:
+            keep_v = jnp.where(flags[8] == 1, (low_t[...] if panel == 0 else low).T, keep_v)
             keep_u = jnp.where(flags[9] == 1, 0.0, keep_u)
             keep_v = jnp.where(flags[9] == 1, 0.0, keep_v)
         chosen = flags[6 + s] == 1
@@ -230,22 +219,22 @@
         new_v = jnp.where(chosen, fresh_v, keep_v)
         nu[s] = new_u
         nv[s] = new_v
-        if panel == 0 and s == 0:
-            pack[0] = new_u
-            pack[1] = new_v
     if panel == 0:
         values = jnp.concatenate([ortho[0, :order], ortho[1, :order]], axis=0) * root
         for factors in parts[::-1]:
             values = values + dot3(values, factors, NT)
         values = values * start
-        moved[:width] = extra[:width]
+        moved[:width] = wide.T
         moved[width:2 * width] = corner[0].T
         moved[2 * width:] = corner[1].T
         middle = flags[10] == 1
+        fresh_t = fresh_vs[0].T[:order]
+        pack[0] = ortho[0, :order] * root
+        pack[1] = fresh_t
         out_z[0] = jnp.where(middle, moved[:order], values[:order])
         out_z[1] = values[order:]
         out_z[2] = moved[2 * order:3 * order]
-        out_v[0] = jnp.where(middle, moved[order:2 * order], fresh_vs[0].T[:order])
+        out_v[0] = jnp.where(middle, moved[order:2 * order], fresh_t)
         out_v[1] = fresh_vs[1].T[:order]
         out_v[2] = moved[3 * order:]
 
@@ -259,7 +248,7 @@
         in_specs=[pl.BlockSpec(memory_space=pltpu.SMEM)] + [vmem] * len(values),
         out_specs=(vmem,) * len(shapes),
         scratch_shapes=list(scratch),
-        compiler_params=pltpu.CompilerParams(vmem_limit_bytes=32 * 1024 * 1024),
+        compiler_params=pltpu.CompilerParams(vmem_limit_bytes=24 * 1024 * 1024),
     )(flags, *values)
     return out if len(out) > 1 else out[0]
 
@@ -303,7 +292,7 @@
     holder = jnp.where(core == 0, x, z) == 0
     final = jnp.where(holder, held, second)
     other = lax.ppermute(final, "row", [(r, r ^ 1) for r in range(2 * X_COUNT * Z_COUNT)])
-    return final, other
+    return final, other, second
 
 
 def share_row(value, root, col):
@@ -311,15 +300,17 @@
     one = lax.ppermute(value, "col", [(root, right)])
     held = jnp.where(col == root, value, one)
     two = lax.ppermute(held, "col", [(root, left), (right, far)])
-    return held, jnp.where((col == root) | (col == right), held, two)
-
-
-def share_pivots(value, roots):
-    return fan_out(
-        value,
-        ("row", "col"),
-        [[(r * COLS + c, r * COLS + (c + k) % COLS) for r, c in roots] for k in (1, 3, 2)],
-    )
+    return jnp.where((col == root) | (col == right), held, two)
+
+
+def fan_row(value, root, col):
+    got = fan_out(value, "col", [[(root, (root + k) % COLS)] for k in (1, 3, 2)])
+    return jnp.where(col == root, value, got)
+
+
+def share_pivot(value, col):
+    got = fan_out(value, ("row", "col"), [[(COLS + 1, COLS + (1 + k) % COLS)] for k in (1, 3, 2)])
+    return jnp.where(col == 1, value, got)
 
 
 def body(factor_u, factor_v, near_field, sketch, tile_ranks):
@@ -338,47 +329,47 @@
         chosen = (row > panel) & (slots > panel)
         if panel == 0:
             chosen = chosen & jnp.logical_not((row == 1) & (slots == 1))
-        lower = (row > col) & (col < 2)
-        pivot = (row == col) & (col < 2)
+        lower = (row > panel) & (col == panel)
+        pivot = (row == panel) & (col == panel)
         parts = [own_ranks[panel + 1], own_ranks[0], ranks[0, 0], chosen]
         parts += [lower[None], pivot[None], col[None], core[None]]
         return jnp.concatenate([part.astype(jnp.int32) for part in parts])
 
     flags = [flags_of(panel) for panel in range(2)]
-    pair, payload = (2, tile, width), (2 * width, tile)
+    one, pair = (tile, width), (2, tile, width)
     packed = (3, order[0], tile)
     scratch = [
-        [pltpu.VMEM(pair[:1] + (width, tile), F32), pltpu.VMEM((2, order[k], width), F32), pltpu.VMEM((4 * order[0], tile), F32)]
+        [pltpu.VMEM((2, width, tile), F32), pltpu.VMEM((2, order[k], width), F32), pltpu.VMEM((4 * order[0], tile), F32)]
         for k in range(2)
     ]
 
-    with jax.named_scope("corner_share"):
-        pack = jnp.stack([own_u[0], own_v[0]])
-        got = share_pivots(pack, [(0, 0), (1, 1)])
-        corner = jnp.where(col == row, pack, got)
-    with jax.named_scope("first_lead"):
-        keep = jnp.arange(width, dtype=jnp.int32) < own_ranks[0, 0]
-        near_lead, lead = share_row(jnp.where(keep, pack, 0.0), 0, col)
-    with jax.named_scope("first_upper"):
-        up_a, up_b = call(upper_kernel, (payload, payload), flags[0], near_field, corner, own_u, own_v)
-    with jax.named_scope("upper_share"):
-        crossed = lax.ppermute(up_a, "row", [(0, 1)])
-        ours_0, theirs_0 = share_planes(jnp.where(core == 0, up_b, crossed), row)
-    with jax.named_scope("wide_share"):
-        extra = call(wide_kernel, (payload,), flags[0], near_lead, crossed)
-        got = share_pivots(extra, [(1, 1)])
-        extra = jnp.where(col == row, extra, got)
+    def first_share(slot, after):
+        value_u, value_v = own_u[slot], own_v[slot]
+        if after is not None:
+            value_u, value_v, _ = lax.optimization_barrier((value_u, value_v, after))
+        crossed = lax.ppermute(value_v, "row", [(0, 1)])
+        return share_planes(jnp.where(core == 0, value_u, crossed), row)
+
+    with jax.named_scope("first_share"):
+        ours_0, theirs_0, middle = first_share(0, None)
+        lead = share_row(own_u[0], 0, col)
+        corner = share_pivot(jnp.stack([own_u[0], own_v[0]]), col)
+    with jax.named_scope("first_lower"):
+        low_t, cross = call(lower_kernel, ((width, tile), pair), flags[0], near_field, ours_0, theirs_0, own_v)
+        low_t = fan_row(low_t, 0, col)
+        cross = share_pivot(cross, col)
+        ours_1, theirs_1, _ = first_share(1, middle)
     with jax.named_scope("first_update"):
         cur_u, cur_v, pack, out_z, out_v = call(
             functools.partial(panel_kernel, order[0], 0),
-            (pair, pair, pair, packed, packed),
-            flags[0], near_field, own_u, own_v, lead, ours_0, theirs_0, corner, extra, sketch,
+            (pair, pair, (2, order[0], tile), packed, packed),
+            flags[0], near_field, own_u, own_v, lead, ours_0, theirs_0, ours_1, theirs_1, low_t, corner, cross, sketch,
             scratch=scratch[0],
         )
     with jax.named_scope("second_share"):
-        _, lead = share_row(pack, 1, col)
+        lead = share_row(pack, 1, col)
         crossed = lax.ppermute(out_z, "row", [(1, 0)])
-        ours, theirs = share_planes(jnp.where(core == 1, out_v, crossed), row)
+        ours, theirs, _ = share_planes(jnp.where(core == 1, out_v, crossed), row)
     with jax.named_scope("second_update"):
         cur_u, cur_v = call(
             functools.partial(panel_kernel, order[1], 1),

time: 162 us -> 169 us (1.043)
  starting transfers between devices: 44.3 us -> 57.5 us
  waiting for transfers between devices: 50.3 us -> 48.4 us
  Pallas kernels: 38.4 us -> 36.6 us
    ppermute x18 -> x27, starting transfers between devices: 32.7 us -> 45.5 us  [fan_out(): moved = lax.ppermute(value, axis, pairs)]
    ppermute x2, waiting for transfers between devices: 13.5 us -> 3.01 us  [share_row(): two = lax.ppermute(held, 'col', [(root, left), (right, far)])]
    ppermute x2, waiting for transfers between devices: 0.01 us -> 5.04 us  [share_row(): one = lax.ppermute(value, 'col', [(root, right)])]
    ppermute x1, waiting for transfers between devices: 2.94 us -> 6.86 us  [body(): crossed = lax.ppermute(out_z, 'row', [(1, 0)])]
    ppermute x2, starting transfers between devices: 5.62 us -> 2.72 us  [share_row(): two = lax.ppermute(held, 'col', [(root, left), (right, far)])]
    ppermute x2, starting transfers between devices: 2.79 us -> 4.71 us  [share_row(): one = lax.ppermute(value, 'col', [(root, right)])]
    pallas_call x4 -> x3, Pallas kernels: 38.4 us -> 36.6 us  [call(): pl.pallas_call(kernel, out_shape=shapes, in_specs=[pl.BlockSpec(memory_sp...]
    ppermute x18 -> x27, waiting for transfers between devices: 32.2 us -> 30.8 us  [fan_out(): moved = lax.ppermute(value, axis, pairs)]
  transfers between devices with their start and end apart: 26 -> 37, of which waited for: 14 -> 19; matrix products, arithmetic and copies ran while one was open for 6% -> 6% of each run, Pallas kernels for 1% -> 2%
where the time goes in v4:
time: 169 us; the launch traced here: 167 us
  starting transfers between devices  57.5 us (34%)
  waiting for transfers between devices  48.4 us (29%)
  Pallas kernels  36.6 us (22%)
  other arithmetic  12.9 us (8%)
  local copies, waits for them, and re-layouts  10.8 us (6%)
    ppermute x27, starting transfers between devices, fan_out(): moved = lax.ppermute(value, axis, pairs)  45.5 us
    pallas_call x3, Pallas kernels, call(): pl.pallas_call(kernel, out_shape=shapes, in_specs=[pl.BlockSpec(memory_sp...  36.6 us
    ppermute x27, waiting for transfers between devices, fan_out(): moved = lax.ppermute(value, axis, pairs)  30.8 us
    unnamed x40, local copies, waits for them, and re-layouts  8.02 us
    ppermute x1, waiting for transfers between devices, body(): crossed = lax.ppermute(out_z, 'row', [(1, 0)])  6.86 us
    ppermute x2, waiting for transfers between devices, share_row(): one = lax.ppermute(value, 'col', [(root, right)])  5.04 us
    ppermute x2, starting transfers between devices, share_row(): one = lax.ppermute(value, 'col', [(root, right)])  4.71 us
  transfers between devices with their start and end apart: 37, of which 19 were waited for; matrix products, arithmetic and copies ran while one was open for 6% of the time, Pallas kernels for 2%

profile of v4, /device:TPU:0, one launch (start us, length us, event | category | flops | bytes accessed | tf_op | source)
XLA Modules:
  0.0 167.2 jit_solution(13470389478323564541)
XLA Ops:
  0.6 2.2 %slice_bitcast_fusion.2 = (f32[1,512,128]{2,1,0:T(8,128)}, f32[512,128]{1,0:T(8,128)}, f32[512,128]{1,0:T(8,128)S(1)}, f32[512,128]{1,0:T(8,128)S(1)}, f32[512,128]{1,0:T(8,128)}, /*index=5*/f32[1,512,128]{2,1,0:T(8,128)}) fusion(f32[1,1,2,1,512,128]{5,4,3,2,1,0:T(8,128)} %param.6, f32[1,1,2,1,512,128]{5,4,3,2,1,0:T(8,128)} %param.5), kind=kLoop, calls=%fused_computation.13 | loop fusion | bytes 2621440 | tf_op jit(solution)/shard_map/first_share/slice | solution.py:347
  2.9 1.3 collective-permute-start.2
  4.2 4.0 %collective-permute-start = (f32[512,128]{1,0:T(8,128)S(1)}, f32[512,128]{1,0:T(8,128)S(1)}, u32[]{:S(2)}, u32[]{:S(2)}) collective-permute-start(f32[512,128]{1,0:T(8,128)S(1)} %get-tuple-element.41), channel_id=1, source_target_pairs={{0,1},{4,5},{8,9},{12,13},{16,17},{20,21},{24,25},{28,29},{32,33},... | collective-permute-start | bytes 786440 | tf_op jit(solution)/shard_map/first_share/ppermute | solution.py:300
  8.2 5.0 %collective-permute-done = f32[512,128]{1,0:T(8,128)S(1)} collective-permute-done((f32[512,128]{1,0:T(8,128)S(1)}, f32[512,128]{1,0:T(8,128)S(1)}, u32[]{:S(2)}, u32[]{:S(2)}) %collective-permute-start) | collective-permute-done | bytes 262176 | tf_op jit(solution)/shard_map/first_share/ppermute | solution.py:300
  14.0 5.9 %collective-permute-start.5 = (f32[512,128]{1,0:T(8,128)S(1)}, f32[512,128]{1,0:T(8,128)}, u32[]{:S(2)}, u32[]{:S(2)}) collective-permute-start(f32[512,128]{1,0:T(8,128)S(1)} %get-tuple-element.39), channel_id=1, source_target_pairs={{0,64},{4,20},{1,65},{5,21},{2,66},{6,22},{3,67},{7,23}} | collective-permute-start | bytes 786440 | tf_op jit(solution)/shard_map/first_share/ppermute | solution.py:268
  19.9 2.0 %collective-permute-start.4 = (f32[512,128]{1,0:T(8,128)S(1)}, f32[512,128]{1,0:T(8,128)}, u32[]{:S(2)}, u32[]{:S(2)}) collective-permute-start(f32[512,128]{1,0:T(8,128)S(1)} %get-tuple-element.39), channel_id=1, source_target_pairs={{0,96},{4,28},{1,97},{5,29},{2,98},{6,30},{3,99},{7,31}} | collective-permute-start | bytes 786440 | tf_op jit(solution)/shard_map/first_share/ppermute | solution.py:268
  21.9 2.0 %collective-permute-start.3 = (f32[512,128]{1,0:T(8,128)S(1)}, f32[512,128]{1,0:T(8,128)}, u32[]{:S(2)}, u32[]{:S(2)}) collective-permute-start(f32[512,128]{1,0:T(8,128)S(1)} %get-tuple-element.39), channel_id=1, source_target_pairs={{0,32},{4,12},{1,33},{5,13},{2,34},{6,14},{3,35},{7,15}} | collective-permute-start | bytes 786440 | tf_op jit(solution)/shard_map/first_share/ppermute | solution.py:268
  23.9 1.1 collective-permute-done.4
  25.1 2.0 %collective-permute-done.3 = f32[512,128]{1,0:T(8,128)} collective-permute-done((f32[512,128]{1,0:T(8,128)S(1)}, f32[512,128]{1,0:T(8,128)}, u32[]{:S(2)}, u32[]{:S(2)}) %collective-permute-start.3) | collective-permute-done | bytes 262176 | tf_op jit(solution)/shard_map/first_share/ppermute | solution.py:268
  27.1 1.9 %add_select_fusion.7 = f32[512,128]{1,0:T(8,128)} fusion(f32[512,128]{1,0:T(8,128)S(1)} %get-tuple-element.39, f32[512,128]{1,0:T(8,128)} %collective-permute-done.5, f32[512,128]{1,0:T(8,128)} %collective-permute-done.3, f32[512,128]{1,0:T(8,128)} %collective-permute-done.4, pred[]{:T(512)S(6)} %lt.31), kind=kLoop, calls=%fused_computation.12 | loop fusion | flops 196608 | bytes 1310721 | tf_op jit(solution)/shard_map/first_share/jit(_where)/select_n | solution.py:282
  28.9 1.3 collective-permute-start.8
  30.2 2.0 %collective-permute-start.7 = (f32[512,128]{1,0:T(8,128)}, f32[512,128]{1,0:T(8,128)}, u32[]{:S(2)}, u32[]{:S(2)}) collective-permute-start(f32[512,128]{1,0:T(8,128)} %add_select_fusion.7), channel_id=1, source_target_pairs={{0,24},{32,56},{64,88},{96,120},{4,100},{12,108},{20,116},{28,124}... | collective-permute-start | bytes 786440 | tf_op jit(solution)/shard_map/first_share/ppermute | solution.py:268
  32.2 2.0 %collective-permute-start.6 = (f32[512,128]{1,0:T(8,128)}, f32[512,128]{1,0:T(8,128)}, u32[]{:S(2)}, u32[]{:S(2)}) collective-permute-start(f32[512,128]{1,0:T(8,128)} %add_select_fusion.7), channel_id=1, source_target_pairs={{0,8},{32,40},{64,72},{96,104},{4,36},{12,44},{20,52},{28,60},{1,9... | collective-permute-start | bytes 786440 | tf_op jit(solution)/shard_map/first_share/ppermute | solution.py:268
  34.4 1.3 collective-permute-done.7
  35.7 2.0 %collective-permute-done.6 = f32[512,128]{1,0:T(8,128)} collective-permute-done((f32[512,128]{1,0:T(8,128)}, f32[512,128]{1,0:T(8,128)}, u32[]{:S(2)}, u32[]{:S(2)}) %collective-permute-start.6) | collective-permute-done | bytes 262176 | tf_op jit(solution)/shard_map/first_share/ppermute | solution.py:268
  37.7 1.2 broadcast_select_fusion.5
  38.9 1.3 collective-permute-start.10
  40.3 1.2 collective-permute-done.10
  41.6 1.7 %broadcast_select_fusion.3 = f32[512,128]{1,0:T(8,128)} fusion(f32[512,128]{1,0:T(8,128)} %get-tuple-element.13, f32[512,128]{1,0:T(8,128)S(1)} %collective-permute-done.10, pred[]{:T(512)S(6)} %eq.57), kind=kLoop, calls=%fused_computation.19 | loop fusion | flops 65536 | bytes 786433 | tf_op jit(solution)/shard_map/first_lower/jit(_where)/select_n | solution.py:351
  43.3 2.0 %collective-permute-start.13 = (f32[512,128]{1,0:T(8,128)}, f32[512,128]{1,0:T(8,128)}, u32[]{:S(2)}, u32[]{:S(2)}) collective-permute-start(f32[512,128]{1,0:T(8,128)} %broadcast_select_fusion.3), channel_id=1, source_target_pairs={{0,64},{4,20},{1,65},{5,21},{2,66},{6,22},{3,67},{7,23}} | collective-permute-start | bytes 786440 | tf_op jit(solution)/shard_map/first_lower/ppermute | solution.py:268
  45.2 1.9 %pad_maximum_fusion = f32[2,512,128]{2,1,0:T(8,128)} fusion(f32[1,512,128]{2,1,0:T(8,128)} %get-tuple-element.36, f32[1,512,128]{2,1,0:T(8,128)} %get-tuple-element.43), kind=kLoop, calls=%fused_computation.2 | loop fusion | flops 131072 | bytes 1048576 | tf_op jit(solution)/shard_map/first_share/stack | solution.py:356
  47.1 1.5 collective-permute-start.23
  48.6 1.5 collective-permute-start.22
  50.0 1.5 collective-permute-start.21
  52.2 2.0 %collective-permute-start.12 = (f32[512,128]{1,0:T(8,128)}, f32[512,128]{1,0:T(8,128)}, u32[]{:S(2)}, u32[]{:S(2)}) collective-permute-start(f32[512,128]{1,0:T(8,128)} %broadcast_select_fusion.3), channel_id=1, source_target_pairs={{0,96},{4,28},{1,97},{5,29},{2,98},{6,30},{3,99},{7,31}} | collective-permute-start | bytes 786440 | tf_op jit(solution)/shard_map/first_lower/ppermute | solution.py:268
  54.2 2.1 %collective-permute-start.11 = (f32[512,128]{1,0:T(8,128)}, f32[512,128]{1,0:T(8,128)}, u32[]{:S(2)}, u32[]{:S(2)}) collective-permute-start(f32[512,128]{1,0:T(8,128)} %broadcast_select_fusion.3), channel_id=1, source_target_pairs={{0,32},{4,12},{1,33},{5,13},{2,34},{6,14},{3,35},{7,15}} | collective-permute-start | bytes 786440 | tf_op jit(solution)/shard_map/first_lower/ppermute | solution.py:268
  56.8 0.9 copy-done.4
  57.7 3.8 %first_lower.1 = (f32[128,512]{1,0:T(8,128)S(1)}, f32[2,512,128]{2,1,0:T(8,128)S(1)}) custom-call(s32[12]{0:T(128)S(1)} %concatenate.7.flags, f32[2,512,512]{2,1,0:T(8,128)S(1)} %copy-done, f32[512,128]{1,0:T(8,128)S(1)} %broadcast_select_fusion.5, f32[512,128]{1,0:T(8,128)S(1)} %copy-done.4, f32[2,512,128]{2,1,0:T(8,128)S(1)} %bitcast.31), custom_call_target="tpu_custom_call" | custom-call | tf_op jit(solution)/shard_map/first_lower/pallas_call | solution.py:245
  61.6 1.3 collective-permute-start.1
  62.9 1.3 collective-permute-start.20
  64.2 1.2 add_select_fusion.6
  65.5 1.3 collective-permute-start.19
  66.8 3.1 %collective-permute-start.18 = (f32[128,512]{1,0:T(8,128)S(1)}, f32[128,512]{1,0:T(8,128)S(1)}, u32[]{:S(2)}, u32[]{:S(2)}) collective-permute-start(f32[128,512]{1,0:T(8,128)S(1)} %get-tuple-element.15), channel_id=1, source_target_pairs={{0,1},{4,5},{8,9},{12,13},{16,17},{20,21},{24,25},{28,29},{32,33},... | collective-permute-start | bytes 786440 | tf_op jit(solution)/shard_map/first_lower/ppermute | solution.py:268
  70.0 1.3 collective-permute-start.16
  71.3 1.5 add_select_fusion.3.refs_3_
  75.0 1.4 collective-permute-done.18
  76.4 1.3 collective-permute-start.15
  77.7 1.3 collective-permute-start.14
  79.1 2.4 %collective-permute-done.15 = f32[512,128]{1,0:T(8,128)S(1)} collective-permute-done((f32[512,128]{1,0:T(8,128)S(1)}, f32[512,128]{1,0:T(8,128)S(1)}, u32[]{:S(2)}, u32[]{:S(2)}) %collective-permute-start.15) | collective-permute-done | bytes 262176 | tf_op jit(solution)/shard_map/first_lower/ppermute | solution.py:268
  81.5 1.3 collective-permute-done.14
  83.3 1.4 collective-permute-done.17.refs_1_
  84.7 17.7 %first_update.1 = (f32[2,512,128]{2,1,0:T(8,128)S(1)}, f32[2,512,128]{2,1,0:T(8,128)S(1)}, f32[2,96,512]{2,1,0:T(8,128)S(1)}, f32[3,96,512]{2,1,0:T(8,128)}, f32[3,96,512]{2,1,0:T(8,128)S(1)}) custom-call(s32[12]{0:T(128)S(1)} %concatenate.7.flags, f32[2,512,512]{2,1,0:T(8,128)S(1)} %copy-done, f32[2,512,128]{2,1,0:T(8,128)S(1)} %bitcast.33, ...), custom_call_target="tpu_custom_call" | custom-call | tf_op jit(solution)/shard_map/first_update/pallas_call | solution.py:245
  102.4 0.8 copy-done.8
  105.6 1.3 collective-permute-start.29
  106.9 6.9 %collective-permute-done.29 = f32[3,96,512]{2,1,0:T(8,128)S(1)} collective-permute-done((f32[3,96,512]{2,1,0:T(8,128)}, f32[3,96,512]{2,1,0:T(8,128)S(1)}, u32[]{:S(2)}, u32[]{:S(2)}) %collective-permute-start.29) | collective-permute-done | bytes 589856 | tf_op jit(solution)/shard_map/second_share/ppermute | solution.py:371
  113.9 1.5 collective-permute-start.32
  115.3 1.3 collective-permute-start.31
  116.7 1.3 collective-permute-start.30
  118.7 4.0 %collective-permute-done.32 = f32[3,96,512]{2,1,0:T(8,128)S(1)} collective-permute-done((f32[3,96,512]{2,1,0:T(8,128)S(1)}, f32[3,96,512]{2,1,0:T(8,128)S(1)}, u32[]{:S(2)}, u32[]{:S(2)}) %collective-permute-start.32) | collective-permute-done | bytes 589856 | tf_op jit(solution)/shard_map/second_share/ppermute | solution.py:268
  122.7 1.3 collective-permute-done.31
  124.0 5.0 %collective-permute-done.30 = f32[3,96,512]{2,1,0:T(8,128)S(1)} collective-permute-done((f32[3,96,512]{2,1,0:T(8,128)S(1)}, f32[3,96,512]{2,1,0:T(8,128)S(1)}, u32[]{:S(2)}, u32[]{:S(2)}) %collective-permute-start.30) | collective-permute-done | bytes 589856 | tf_op jit(solution)/shard_map/second_share/ppermute | solution.py:268
  129.3 1.3 collective-permute-start.35
  130.6 1.3 collective-permute-start.34
  131.9 1.3 collective-permute-start.33
  134.1 1.4 collective-permute-start.28
  135.5 2.4 %collective-permute-done.35 = f32[3,96,512]{2,1,0:T(8,128)S(1)} collective-permute-done((f32[3,96,512]{2,1,0:T(8,128)S(1)}, f32[3,96,512]{2,1,0:T(8,128)S(1)}, u32[]{:S(2)}, u32[]{:S(2)}) %collective-permute-start.35) | collective-permute-done | bytes 589856 | tf_op jit(solution)/shard_map/second_share/ppermute | solution.py:268
  137.9 1.3 collective-permute-done.34
  139.3 5.0 %collective-permute-done.33 = f32[3,96,512]{2,1,0:T(8,128)S(1)} collective-permute-done((f32[3,96,512]{2,1,0:T(8,128)S(1)}, f32[3,96,512]{2,1,0:T(8,128)S(1)}, u32[]{:S(2)}, u32[]{:S(2)}) %collective-permute-start.33) | collective-permute-done | bytes 589856 | tf_op jit(solution)/shard_map/second_share/ppermute | solution.py:268
  145.0 3.0 %collective-permute-done.28 = f32[2,96,512]{2,1,0:T(8,128)} collective-permute-done((f32[2,96,512]{2,1,0:T(8,128)}, f32[2,96,512]{2,1,0:T(8,128)}, u32[]{:S(2)}, u32[]{:S(2)}) %collective-permute-start.28) | collective-permute-done | bytes 393248 | tf_op jit(solution)/shard_map/second_share/ppermute | solution.py:302
  148.0 1.1 broadcast_select_fusion.2.lead
  149.1 1.0 copy-done.7
  150.1 1.0 copy-done.10
  151.2 1.0 copy-done.12
  152.2 15.0 %second_update.1 = (f32[2,512,128]{2,1,0:T(8,128)}, f32[2,512,128]{2,1,0:T(8,128)}) custom-call(s32[12]{0:T(128)S(1)} %concatenate.6.flags, f32[2,512,512]{2,1,0:T(8,128)S(1)} %copy-done, f32[2,512,128]{2,1,0:T(8,128)S(1)} %copy-done.10, f32[2,512,128]{2,1,0:T(8,128)S(1)} %copy-done.12, f32[2,96,512]{2,1,0:T(8,128)S(1)} %broadcast_select_fusion.2.lead, ...), custom_call_target="tpu_custom_call" | custom-call | tf_op jit(solution)/shard_map/second_update/pallas_call | solution.py:245
  (76 shorter events, 9.8 us)
Async XLA Ops:
  0.6 12.6 %copy-start.2 = (f32[1,1,2,1,512,128]{5,4,3,2,1,0:T(8,128)S(1)}, f32[1,1,2,1,512,128]{5,4,3,2,1,0:T(8,128)}, u32[]{:S(2)}) copy-start(f32[1,1,2,1,512,128]{5,4,3,2,1,0:T(8,128)} %param.5) | copy-start | bytes 1572868
  2.9 5.4 %collective-permute-start.2 = (f32[512,128]{1,0:T(8,128)S(1)}, f32[512,128]{1,0:T(8,128)S(1)}, u32[]{:S(2)}, u32[]{:S(2)}) collective-permute-start(f32[512,128]{1,0:T(8,128)S(1)} %get-tuple-element.38), channel_id=1, source_target_pairs={{0,4},{1,5},{2,6},{3,7}} | collective-permute-start | bytes 786440 | tf_op jit(solution)/shard_map/first_share/ppermute | solution.py:350
  4.2 9.1 %collective-permute-start = (f32[512,128]{1,0:T(8,128)S(1)}, f32[512,128]{1,0:T(8,128)S(1)}, u32[]{:S(2)}, u32[]{:S(2)}) collective-permute-start(f32[512,128]{1,0:T(8,128)S(1)} %get-tuple-element.41), channel_id=1, source_target_pairs={{0,1},{4,5},{8,9},{12,13},{16,17},{20,21},{24,25},{28,29},{32,33},... | collective-permute-start | bytes 786440 | tf_op jit(solution)/shard_map/first_share/ppermute | solution.py:300
  14.0 9.9 %collective-permute-start.5 = (f32[512,128]{1,0:T(8,128)S(1)}, f32[512,128]{1,0:T(8,128)}, u32[]{:S(2)}, u32[]{:S(2)}) collective-permute-start(f32[512,128]{1,0:T(8,128)S(1)} %get-tuple-element.39), channel_id=1, source_target_pairs={{0,64},{4,20},{1,65},{5,21},{2,66},{6,22},{3,67},{7,23}} | collective-permute-start | bytes 786440 | tf_op jit(solution)/shard_map/first_share/ppermute | solution.py:268
  19.9 5.2 %collective-permute-start.4 = (f32[512,128]{1,0:T(8,128)S(1)}, f32[512,128]{1,0:T(8,128)}, u32[]{:S(2)}, u32[]{:S(2)}) collective-permute-start(f32[512,128]{1,0:T(8,128)S(1)} %get-tuple-element.39), channel_id=1, source_target_pairs={{0,96},{4,28},{1,97},{5,29},{2,98},{6,30},{3,99},{7,31}} | collective-permute-start | bytes 786440 | tf_op jit(solution)/shard_map/first_share/ppermute | solution.py:268
  21.9 5.2 %collective-permute-start.3 = (f32[512,128]{1,0:T(8,128)S(1)}, f32[512,128]{1,0:T(8,128)}, u32[]{:S(2)}, u32[]{:S(2)}) collective-permute-start(f32[512,128]{1,0:T(8,128)S(1)} %get-tuple-element.39), channel_id=1, source_target_pairs={{0,32},{4,12},{1,33},{5,13},{2,34},{6,14},{3,35},{7,15}} | collective-permute-start | bytes 786440 | tf_op jit(solution)/shard_map/first_share/ppermute | solution.py:268
  23.9 32.4 %copy-start.19 = (s32[3,1,32,2,1]{2,4,3,1,0:T(1,128)S(1)}, s32[3,1,32,2,1]{2,4,3,1,0:T(1,128)}, u32[]{:S(2)}) copy-start(s32[3,1,32,2,1]{2,4,3,1,0:T(1,128)} %param.9) | copy-start | bytes 2308
  23.9 32.9 %copy-start = (f32[2,512,512]{2,1,0:T(8,128)S(1)}, f32[2,512,512]{2,1,0:T(8,128)}, u32[]{:S(2)}) copy-start(f32[2,512,512]{2,1,0:T(8,128)} %near.5) | copy-start | bytes 6291460
  23.9 32.9 %copy-start.1 = (f32[1,1,2,1,512,128]{5,4,3,2,1,0:T(8,128)S(1)}, f32[1,1,2,1,512,128]{5,4,3,2,1,0:T(8,128)}, u32[]{:S(2)}) copy-start(f32[1,1,2,1,512,128]{5,4,3,2,1,0:T(8,128)} %param.6) | copy-start | bytes 1572868
  28.9 5.5 %collective-permute-start.8 = (f32[512,128]{1,0:T(8,128)}, f32[512,128]{1,0:T(8,128)S(1)}, u32[]{:S(2)}, u32[]{:S(2)}) collective-permute-start(f32[512,128]{1,0:T(8,128)} %add_select_fusion.7), channel_id=1, source_target_pairs={{0,16},{32,48},{64,80},{96,112},{4,68},{12,76},{20,84},{28,92},{1,... | collective-permute-start | bytes 786440 | tf_op jit(solution)/shard_map/first_share/ppermute | solution.py:268
  30.2 5.5 %collective-permute-start.7 = (f32[512,128]{1,0:T(8,128)}, f32[512,128]{1,0:T(8,128)}, u32[]{:S(2)}, u32[]{:S(2)}) collective-permute-start(f32[512,128]{1,0:T(8,128)} %add_select_fusion.7), channel_id=1, source_target_pairs={{0,24},{32,56},{64,88},{96,120},{4,100},{12,108},{20,116},{28,124}... | collective-permute-start | bytes 786440 | tf_op jit(solution)/shard_map/first_share/ppermute | solution.py:268
  32.2 5.5 %collective-permute-start.6 = (f32[512,128]{1,0:T(8,128)}, f32[512,128]{1,0:T(8,128)}, u32[]{:S(2)}, u32[]{:S(2)}) collective-permute-start(f32[512,128]{1,0:T(8,128)} %add_select_fusion.7), channel_id=1, source_target_pairs={{0,8},{32,40},{64,72},{96,104},{4,36},{12,44},{20,52},{28,60},{1,9... | collective-permute-start | bytes 786440 | tf_op jit(solution)/shard_map/first_share/ppermute | solution.py:268
  34.4 1.3 copy-start.18
  38.9 2.7 %collective-permute-start.10 = (f32[512,128]{1,0:T(8,128)}, f32[512,128]{1,0:T(8,128)S(1)}, u32[]{:S(2)}, u32[]{:S(2)}) collective-permute-start(f32[512,128]{1,0:T(8,128)} %get-tuple-element.14), channel_id=1, source_target_pairs={{0,4},{1,5},{2,6},{3,7}} | collective-permute-start | bytes 786440 | tf_op jit(solution)/shard_map/first_lower/ppermute | solution.py:350
  40.2 11.3 %collective-permute-start.9 = (f32[512,128]{1,0:T(8,128)S(1)}, f32[512,128]{1,0:T(8,128)S(1)}, u32[]{:S(2)}, u32[]{:S(2)}) collective-permute-start(f32[512,128]{1,0:T(8,128)S(1)} %broadcast_select_fusion.5), channel_id=1, source_target_pairs={{0,4},{4,0},{8,12},{12,8},{16,20},{20,16},{24,28},{28,24},{32,36},... | collective-permute-start | bytes 786440 | tf_op jit(solution)/shard_map/first_share/ppermute | solution.py:294
  43.3 11.0 %collective-permute-start.13 = (f32[512,128]{1,0:T(8,128)}, f32[512,128]{1,0:T(8,128)}, u32[]{:S(2)}, u32[]{:S(2)}) collective-permute-start(f32[512,128]{1,0:T(8,128)} %broadcast_select_fusion.3), channel_id=1, source_target_pairs={{0,64},{4,20},{1,65},{5,21},{2,66},{6,22},{3,67},{7,23}} | collective-permute-start | bytes 786440 | tf_op jit(solution)/shard_map/first_lower/ppermute | solution.py:268
  47.1 18.4 %collective-permute-start.23 = (f32[2,512,128]{2,1,0:T(8,128)}, f32[2,512,128]{2,1,0:T(8,128)}, u32[]{:S(2)}, u32[]{:S(2)}) collective-permute-start(f32[2,512,128]{2,1,0:T(8,128)} %pad_maximum_fusion), channel_id=1, source_target_pairs={{5,7}} | collective-permute-start | bytes 1572872 | tf_op jit(solution)/shard_map/first_share/ppermute | solution.py:268
  48.6 18.3 %collective-permute-start.22 = (f32[2,512,128]{2,1,0:T(8,128)}, f32[2,512,128]{2,1,0:T(8,128)}, u32[]{:S(2)}, u32[]{:S(2)}) collective-permute-start(f32[2,512,128]{2,1,0:T(8,128)} %pad_maximum_fusion), channel_id=1, source_target_pairs={{5,4}} | collective-permute-start | bytes 1572872 | tf_op jit(solution)/shard_map/first_share/ppermute | solution.py:268
  50.0 19.9 %collective-permute-start.21 = (f32[2,512,128]{2,1,0:T(8,128)}, f32[2,512,128]{2,1,0:T(8,128)}, u32[]{:S(2)}, u32[]{:S(2)}) collective-permute-start(f32[2,512,128]{2,1,0:T(8,128)} %pad_maximum_fusion), channel_id=1, source_target_pairs={{5,6}} | collective-permute-start | bytes 1572872 | tf_op jit(solution)/shard_map/first_share/ppermute | solution.py:268
  51.5 0.7 copy-start.3
  52.2 9.4 %collective-permute-start.12 = (f32[512,128]{1,0:T(8,128)}, f32[512,128]{1,0:T(8,128)}, u32[]{:S(2)}, u32[]{:S(2)}) collective-permute-start(f32[512,128]{1,0:T(8,128)} %broadcast_select_fusion.3), channel_id=1, source_target_pairs={{0,96},{4,28},{1,97},{5,29},{2,98},{6,30},{3,99},{7,31}} | collective-permute-start | bytes 786440 | tf_op jit(solution)/shard_map/first_lower/ppermute | solution.py:268
  54.2 8.7 %collective-permute-start.11 = (f32[512,128]{1,0:T(8,128)}, f32[512,128]{1,0:T(8,128)}, u32[]{:S(2)}, u32[]{:S(2)}) collective-permute-start(f32[512,128]{1,0:T(8,128)} %broadcast_select_fusion.3), channel_id=1, source_target_pairs={{0,32},{4,12},{1,33},{5,13},{2,34},{6,14},{3,35},{7,15}} | collective-permute-start | bytes 786440 | tf_op jit(solution)/shard_map/first_lower/ppermute | solution.py:268
  56.8 1.0 copy-start.4
  57.7 3.9 %copy-start.17 = (f32[512,128]{1,0:T(8,128)S(1)}, f32[512,128]{1,0:T(8,128)}, u32[]{:S(2)}) copy-start(f32[512,128]{1,0:T(8,128)} %get-tuple-element.40) | copy-start | bytes 786436
  57.7 13.6 %copy-start.15 = (f32[1,512,128]{2,1,0:T(8,128)S(1)}, f32[1,512,128]{2,1,0:T(8,128)}, u32[]{:S(2)}) copy-start(f32[1,512,128]{2,1,0:T(8,128)} %get-tuple-element.36) | copy-start | bytes 786436
  57.7 13.6 %copy-start.16 = (f32[1,512,128]{2,1,0:T(8,128)S(1)}, f32[1,512,128]{2,1,0:T(8,128)}, u32[]{:S(2)}) copy-start(f32[1,512,128]{2,1,0:T(8,128)} %get-tuple-element.43) | copy-start | bytes 786436
  61.6 11.2 %collective-permute-start.1 = (f32[512,128]{1,0:T(8,128)S(1)}, f32[512,128]{1,0:T(8,128)S(1)}, u32[]{:S(2)}, u32[]{:S(2)}) collective-permute-start(f32[512,128]{1,0:T(8,128)S(1)} %copy-done.17), channel_id=1, source_target_pairs={{0,3},{1,2},{4,7},{5,6},{8,11},{9,10},{12,15},{13,14},{16,19},{17,... | collective-permute-start | bytes 786440 | tf_op jit(solution)/shard_map/first_share/ppermute | solution.py:302
  62.9 10.6 %collective-permute-start.20 = (f32[128,512]{1,0:T(8,128)S(1)}, f32[128,512]{1,0:T(8,128)S(1)}, u32[]{:S(2)}, u32[]{:S(2)}) collective-permute-start(f32[128,512]{1,0:T(8,128)S(1)} %get-tuple-element.15), channel_id=1, source_target_pairs={{0,2},{4,6},{8,10},{12,14},{16,18},{20,22},{24,26},{28,30},{32,34}... | collective-permute-start | bytes 786440 | tf_op jit(solution)/shard_map/first_lower/ppermute | solution.py:268
  65.5 8.7 %collective-permute-start.19 = (f32[128,512]{1,0:T(8,128)S(1)}, f32[128,512]{1,0:T(8,128)S(1)}, u32[]{:S(2)}, u32[]{:S(2)}) collective-permute-start(f32[128,512]{1,0:T(8,128)S(1)} %get-tuple-element.15), channel_id=1, source_target_pairs={{0,3},{4,7},{8,11},{12,15},{16,19},{20,23},{24,27},{28,31},{32,35}... | collective-permute-start | bytes 786440 | tf_op jit(solution)/shard_map/first_lower/ppermute | solution.py:268
  66.8 9.6 %collective-permute-start.18 = (f32[128,512]{1,0:T(8,128)S(1)}, f32[128,512]{1,0:T(8,128)S(1)}, u32[]{:S(2)}, u32[]{:S(2)}) collective-permute-start(f32[128,512]{1,0:T(8,128)S(1)} %get-tuple-element.15), channel_id=1, source_target_pairs={{0,1},{4,5},{8,9},{12,13},{16,17},{20,21},{24,25},{28,29},{32,33},... | collective-permute-start | bytes 786440 | tf_op jit(solution)/shard_map/first_lower/ppermute | solution.py:268
  70.0 7.7 %collective-permute-start.16 = (f32[512,128]{1,0:T(8,128)S(1)}, f32[512,128]{1,0:T(8,128)S(1)}, u32[]{:S(2)}, u32[]{:S(2)}) collective-permute-start(f32[512,128]{1,0:T(8,128)S(1)} %add_select_fusion.6), channel_id=1, source_target_pairs={{0,16},{32,48},{64,80},{96,112},{4,68},{12,76},{20,84},{28,92},{1,... | collective-permute-start | bytes 786440 | tf_op jit(solution)/shard_map/first_lower/ppermute | solution.py:268
  72.8 10.4 %collective-permute-start.26 = (f32[2,512,128]{2,1,0:T(8,128)S(1)}, f32[2,512,128]{2,1,0:T(8,128)S(1)}, u32[]{:S(2)}, u32[]{:S(2)}) collective-permute-start(f32[2,512,128]{2,1,0:T(8,128)S(1)} %get-tuple-element.16), channel_id=1, source_target_pairs={{5,7}} | collective-permute-start | bytes 1572872 | tf_op jit(solution)/shard_map/first_lower/ppermute | solution.py:268
  73.5 9.7 %collective-permute-start.25 = (f32[2,512,128]{2,1,0:T(8,128)S(1)}, f32[2,512,128]{2,1,0:T(8,128)S(1)}, u32[]{:S(2)}, u32[]{:S(2)}) collective-permute-start(f32[2,512,128]{2,1,0:T(8,128)S(1)} %get-tuple-element.16), channel_id=1, source_target_pairs={{5,4}} | collective-permute-start | bytes 1572872 | tf_op jit(solution)/shard_map/first_lower/ppermute | solution.py:268
  74.3 9.0 %collective-permute-start.24 = (f32[2,512,128]{2,1,0:T(8,128)S(1)}, f32[2,512,128]{2,1,0:T(8,128)S(1)}, u32[]{:S(2)}, u32[]{:S(2)}) collective-permute-start(f32[2,512,128]{2,1,0:T(8,128)S(1)} %get-tuple-element.16), channel_id=1, source_target_pairs={{5,6}} | collective-permute-start | bytes 1572872 | tf_op jit(solution)/shard_map/first_lower/ppermute | solution.py:268
  76.4 5.2 %collective-permute-start.15 = (f32[512,128]{1,0:T(8,128)S(1)}, f32[512,128]{1,0:T(8,128)S(1)}, u32[]{:S(2)}, u32[]{:S(2)}) collective-permute-start(f32[512,128]{1,0:T(8,128)S(1)} %add_select_fusion.6), channel_id=1, source_target_pairs={{0,24},{32,56},{64,88},{96,120},{4,100},{12,108},{20,116},{28,124}... | collective-permute-start | bytes 786440 | tf_op jit(solution)/shard_map/first_lower/ppermute | solution.py:268
  77.7 5.2 %collective-permute-start.14 = (f32[512,128]{1,0:T(8,128)S(1)}, f32[512,128]{1,0:T(8,128)S(1)}, u32[]{:S(2)}, u32[]{:S(2)}) collective-permute-start(f32[512,128]{1,0:T(8,128)S(1)} %add_select_fusion.6), channel_id=1, source_target_pairs={{0,8},{32,40},{64,72},{96,104},{4,36},{12,44},{20,52},{28,60},{1,9... | collective-permute-start | bytes 786440 | tf_op jit(solution)/shard_map/first_lower/ppermute | solution.py:268
  79.1 5.6 %copy-start.6 = (f32[2,512,128]{2,1,0:T(8,128)S(1)}, f32[2,512,128]{2,1,0:T(8,128)}, u32[]{:S(2)}) copy-start(f32[2,512,128]{2,1,0:T(8,128)} %refs_2_.1) | copy-start | bytes 1572868
  82.9 1.8 %collective-permute-start.17 = (f32[512,128]{1,0:T(8,128)S(1)}, f32[512,128]{1,0:T(8,128)S(1)}, u32[]{:S(2)}, u32[]{:S(2)}) collective-permute-start(f32[512,128]{1,0:T(8,128)S(1)} %add_select_fusion.5.refs_0_), channel_id=1, source_target_pairs={{0,4},{4,0},{8,12},{12,8},{16,20},{20,16},{24,28},{28,24},{32,36},... | collective-permute-start | bytes 786440 | tf_op jit(solution)/shard_map/first_lower/ppermute | solution.py:294
  102.4 0.8 copy-start.8
  103.2 0.8 copy-start.9
  104.0 0.8 copy-start.11
  104.8 0.8 copy-start.13
  105.6 8.2 %collective-permute-start.29 = (f32[3,96,512]{2,1,0:T(8,128)}, f32[3,96,512]{2,1,0:T(8,128)S(1)}, u32[]{:S(2)}, u32[]{:S(2)}) collective-permute-start(f32[3,96,512]{2,1,0:T(8,128)} %get-tuple-element.21), channel_id=1, source_target_pairs={{4,0},{5,1},{6,2},{7,3}} | collective-permute-start | bytes 1769480 | tf_op jit(solution)/shard_map/second_share/ppermute | solution.py:371
  113.8 19.5 %copy-start.14 = (f32[2,96,512]{2,1,0:T(8,128)S(1)}, f32[2,96,512]{2,1,0:T(8,128)}, u32[]{:S(2)}) copy-start(f32[2,96,512]{2,1,0:T(8,128)} %copy-done.13) | copy-start | bytes 1179652
  113.9 8.8 %collective-permute-start.32 = (f32[3,96,512]{2,1,0:T(8,128)S(1)}, f32[3,96,512]{2,1,0:T(8,128)S(1)}, u32[]{:S(2)}, u32[]{:S(2)}) collective-permute-start(f32[3,96,512]{2,1,0:T(8,128)S(1)} %broadcast_select_fusion), channel_id=1, source_target_pairs={{0,64},{4,20},{1,65},{5,21},{2,66},{6,22},{3,67},{7,23}} | collective-permute-start | bytes 1769480 | tf_op jit(solution)/shard_map/second_share/ppermute | solution.py:268
  115.3 8.7 %collective-permute-start.31 = (f32[3,96,512]{2,1,0:T(8,128)S(1)}, f32[3,96,512]{2,1,0:T(8,128)S(1)}, u32[]{:S(2)}, u32[]{:S(2)}) collective-permute-start(f32[3,96,512]{2,1,0:T(8,128)S(1)} %broadcast_select_fusion), channel_id=1, source_target_pairs={{0,96},{4,28},{1,97},{5,29},{2,98},{6,30},{3,99},{7,31}} | collective-permute-start | bytes 1769480 | tf_op jit(solution)/shard_map/second_share/ppermute | solution.py:268
  116.7 12.3 %collective-permute-start.30 = (f32[3,96,512]{2,1,0:T(8,128)S(1)}, f32[3,96,512]{2,1,0:T(8,128)S(1)}, u32[]{:S(2)}, u32[]{:S(2)}) collective-permute-start(f32[3,96,512]{2,1,0:T(8,128)S(1)} %broadcast_select_fusion), channel_id=1, source_target_pairs={{0,32},{4,12},{1,33},{5,13},{2,34},{6,14},{3,35},{7,15}} | collective-permute-start | bytes 1769480 | tf_op jit(solution)/shard_map/second_share/ppermute | solution.py:268
  118.0 15.3 %collective-permute-start.27 = (f32[2,96,512]{2,1,0:T(8,128)}, f32[2,96,512]{2,1,0:T(8,128)S(1)}, u32[]{:S(2)}, u32[]{:S(2)}) collective-permute-start(f32[2,96,512]{2,1,0:T(8,128)} %copy-done.13), channel_id=1, source_target_pairs={{1,2},{5,6},{9,10},{13,14},{17,18},{21,22},{25,26},{29,30},{33,34}... | collective-permute-start | bytes 1179656 | tf_op jit(solution)/shard_map/second_share/ppermute | solution.py:300
  129.3 8.7 %collective-permute-start.35 = (f32[3,96,512]{2,1,0:T(8,128)S(1)}, f32[3,96,512]{2,1,0:T(8,128)S(1)}, u32[]{:S(2)}, u32[]{:S(2)}) collective-permute-start(f32[3,96,512]{2,1,0:T(8,128)S(1)} %add_select_fusion.1), channel_id=1, source_target_pairs={{0,16},{32,48},{64,80},{96,112},{4,68},{12,76},{20,84},{28,92},{1,... | collective-permute-start | bytes 1769480 | tf_op jit(solution)/shard_map/second_share/ppermute | solution.py:268
  130.6 8.7 %collective-permute-start.34 = (f32[3,96,512]{2,1,0:T(8,128)S(1)}, f32[3,96,512]{2,1,0:T(8,128)S(1)}, u32[]{:S(2)}, u32[]{:S(2)}) collective-permute-start(f32[3,96,512]{2,1,0:T(8,128)S(1)} %add_select_fusion.1), channel_id=1, source_target_pairs={{0,24},{32,56},{64,88},{96,120},{4,100},{12,108},{20,116},{28,124}... | collective-permute-start | bytes 1769480 | tf_op jit(solution)/shard_map/second_share/ppermute | solution.py:268
  131.9 12.3 %collective-permute-start.33 = (f32[3,96,512]{2,1,0:T(8,128)S(1)}, f32[3,96,512]{2,1,0:T(8,128)S(1)}, u32[]{:S(2)}, u32[]{:S(2)}) collective-permute-start(f32[3,96,512]{2,1,0:T(8,128)S(1)} %add_select_fusion.1), channel_id=1, source_target_pairs={{0,8},{32,40},{64,72},{96,104},{4,36},{12,44},{20,52},{28,60},{1,9... | collective-permute-start | bytes 1769480 | tf_op jit(solution)/shard_map/second_share/ppermute | solution.py:268
  134.1 15.0 %copy-start.5 = (f32[512,128]{1,0:T(8,128)S(1)}, f32[512,128]{1,0:T(8,128)}, u32[]{:S(2)}) copy-start(f32[512,128]{1,0:T(8,128)} %copy-done.3) | copy-start | bytes 786436
  134.1 13.9 %collective-permute-start.28 = (f32[2,96,512]{2,1,0:T(8,128)}, f32[2,96,512]{2,1,0:T(8,128)}, u32[]{:S(2)}, u32[]{:S(2)}) collective-permute-start(f32[2,96,512]{2,1,0:T(8,128)} %broadcast_select_fusion.1), channel_id=1, source_target_pairs={{1,0},{2,3},{5,4},{6,7},{9,8},{10,11},{13,12},{14,15},{17,16},{18,... | collective-permute-start | bytes 1179656 | tf_op jit(solution)/shard_map/second_share/ppermute | solution.py:302
  144.5 4.5 %collective-permute-start.36 = (f32[3,96,512]{2,1,0:T(8,128)S(1)}, f32[3,96,512]{2,1,0:T(8,128)}, u32[]{:S(2)}, u32[]{:S(2)}) collective-permute-start(f32[3,96,512]{2,1,0:T(8,128)S(1)} %add_select_fusion.ours), channel_id=1, source_target_pairs={{0,4},{4,0},{8,12},{12,8},{16,20},{20,16},{24,28},{28,24},{32,36},... | collective-permute-start | bytes 1769480 | tf_op jit(solution)/shard_map/second_share/ppermute | solution.py:294
  149.1 1.0 copy-start.7
  150.1 1.0 copy-start.10
  151.2 1.0 copy-start.12

commit v5 on v3

--- a/solution.py
+++ b/solution.py
@@ -120,11 +120,21 @@
     out[width:] = crossed[width:]
 
 
-def panel_kernel(order, panel, flags, near, cu, cv, lead, ours, theirs, *refs):
+def panel_kernel(order, panel, flags, far_u, far_v, far_near, far_sketch, lead, ours, theirs, *refs):
     if panel == 0:
-        corner, extra, sketch, nu, nv, pack, out_z, out_v, ortho, factor, moved = refs
+        corner, extra, to_u, to_v, pack, out_z, out_v = refs[:7]
     else:
-        ours_0, theirs_0, sketch, nu, nv, ortho, factor, moved = refs
+        ours_0, theirs_0, to_u, to_v = refs[:4]
+    ortho, factor, moved, cu, cv, near, sketch, nu, nv, sems = refs[-10:]
+    near_from = far_near.at[1] if panel == 0 else far_near
+    loads = [
+        pltpu.make_async_copy(far_v, cv, sems.at[0]),
+        pltpu.make_async_copy(far_sketch.at[panel], sketch, sems.at[1]),
+        pltpu.make_async_copy(far_u, cu, sems.at[2]),
+        pltpu.make_async_copy(near_from, near, sems.at[3]),
+    ]
+    for load in loads:
+        load.start()
     tile, width = cu.shape[1:]
     weight = 1.0 / (8.0 * tile)
     root = math.sqrt(tile)
@@ -135,19 +145,25 @@
     eye = (row_g == lane_g).astype(F32)
     even = flags[11] == 0
     full_us, full_vs, bases, grams, units = [], [], [], [], []
-    test_t = sketch[panel].T[:order]
+    if panel == 1:
+        part = ours.shape[1]
+        rest = jnp.zeros((width - part, tile), F32)
+        lead_u = jnp.concatenate([lead[0], rest], axis=0)
+        lead_v = jnp.concatenate([lead[1], rest], axis=0)
+    for load in loads:
+        load.wait()
+    test_t = sketch[...].T[:order]
     for s in range(2):
         own_u = cu[s]
         if panel == 0:
             own_u = jnp.where(lanes < flags[2 + s], own_u, 0.0)
             slot = jnp.where(even, theirs[...], ours[...]) if s == 0 else jnp.where(even, ours[...], theirs[...])
-            z_t, up_v = slot[:width], slot[width:].T
+            up_v = slot[width:].T
+            side = dot3(lead[0], wide_t(lead, slot[:width]), NT)
         else:
-            part = ours.shape[1]
-            rest = jnp.zeros((width - part, tile), F32)
             z_t = jnp.concatenate([jnp.where(even, ours[s], theirs[s]), rest], axis=0)
             up_v = jnp.concatenate([jnp.where(even, theirs[s], ours[s]), rest], axis=0).T
-        side = dot3(lead[0], wide_t(lead, z_t), NT)
+            side = dot3(weight * dot3(z_t, lead_v, NT), lead_u).T
         full_u = jnp.concatenate([own_u, -side], axis=1)
         full_v = jnp.concatenate([cv[s], up_v], axis=1)
         projected = dot6(test_t, full_v)
@@ -162,7 +178,7 @@
         units.append(unit)
 
     if panel == 0:
-        far = near[1]
+        far = near[...]
         start = diagonal_inverse(far)
         low_rank = dot3(corner[0], corner[1], NT) - dot3(extra[:width], extra[width:], TN)
         parts = series(far + weight * low_rank, start)
@@ -189,7 +205,7 @@
         once = dot6(inverses[s], bases[s])
         ortho[s, :order] = once
         ortho[s, order:] = spare
-        gram = dot6(once, jnp.concatenate([once, spare], axis=0), NT) + units[s]
+        gram = dot3(once, jnp.concatenate([once, spare], axis=0), NT) + units[s]
         factor[s] = gram
         off = gram - eye
         defect = defect + jnp.where(flags[6 + s] == 1, jnp.sum(off * off), 0.0)
@@ -209,7 +225,7 @@
         for s in range(2):
             ortho[s, :order] = dot6(again[s], ortho[s])
 
-    fresh_vs = []
+    fresh_vs, pending = [], []
     for s in range(2):
         basis = ortho[s]
         back = dot3(basis, full_us[s])
@@ -230,9 +246,13 @@
         new_v = jnp.where(chosen, fresh_v, keep_v)
         nu[s] = new_u
         nv[s] = new_v
-        if panel == 0 and s == 0:
-            pack[0] = new_u
-            pack[1] = new_v
+        stores = [
+            pltpu.make_async_copy(nu.at[s], to_u.at[s], sems.at[4 + 2 * s]),
+            pltpu.make_async_copy(nv.at[s], to_v.at[s], sems.at[5 + 2 * s]),
+        ]
+        for store in stores:
+            store.start()
+        pending += stores
     if panel == 0:
         values = jnp.concatenate([ortho[0, :order], ortho[1, :order]], axis=0) * root
         for factors in parts[::-1]:
@@ -242,24 +262,29 @@
         moved[width:2 * width] = corner[0].T
         moved[2 * width:] = corner[1].T
         middle = flags[10] == 1
+        fresh_t = fresh_vs[0].T[:order]
+        pack[0] = ortho[0, :order] * root
+        pack[1] = fresh_t
         out_z[0] = jnp.where(middle, moved[:order], values[:order])
         out_z[1] = values[order:]
         out_z[2] = moved[2 * order:3 * order]
-        out_v[0] = jnp.where(middle, moved[order:2 * order], fresh_vs[0].T[:order])
+        out_v[0] = jnp.where(middle, moved[order:2 * order], fresh_t)
         out_v[1] = fresh_vs[1].T[:order]
         out_v[2] = moved[3 * order:]
-
-
-def call(kernel, shapes, flags, *values, scratch=()):
-    vmem = pl.BlockSpec(memory_space=pltpu.VMEM)
+    for store in pending:
+        store.wait()
+
+
+def call(kernel, shapes, flags, *values, scratch=(), loads=0, stores=0):
+    vmem, far = pl.BlockSpec(memory_space=pltpu.VMEM), pl.BlockSpec(memory_space=pltpu.HBM)
     shapes = tuple(jax.ShapeDtypeStruct(shape, F32) for shape in shapes)
     out = pl.pallas_call(
         kernel,
         out_shape=shapes,
-        in_specs=[pl.BlockSpec(memory_space=pltpu.SMEM)] + [vmem] * len(values),
-        out_specs=(vmem,) * len(shapes),
+        in_specs=[pl.BlockSpec(memory_space=pltpu.SMEM)] + [far] * loads + [vmem] * (len(values) - loads),
+        out_specs=(far,) * stores + (vmem,) * (len(shapes) - stores),
         scratch_shapes=list(scratch),
-        compiler_params=pltpu.CompilerParams(vmem_limit_bytes=32 * 1024 * 1024),
+        compiler_params=pltpu.CompilerParams(vmem_limit_bytes=24 * 1024 * 1024),
     )(flags, *values)
     return out if len(out) > 1 else out[0]
 
@@ -281,7 +306,7 @@
     return total
 
 
-def share_planes(mine, row):
+def share_planes(mine, row, before, beside):
     core = row % 2
     x = (row // 2) % X_COUNT
     z = row // (2 * X_COUNT)
@@ -290,7 +315,7 @@
         "row",
         [[(row_of(0, 0, 0), row_of(k, 0, 0)), (row_of(0, 0, 1), row_of(0, k, 1))] for k in (1, 3, 2)],
     )
-    held = jnp.where(row < 2, mine, first)
+    held, before = lax.optimization_barrier((jnp.where(row < 2, mine, first), before))
     second = fan_out(
         held,
         "row",
@@ -301,17 +326,26 @@
         ],
     )
     holder = jnp.where(core == 0, x, z) == 0
-    final = jnp.where(holder, held, second)
+    final, beside = lax.optimization_barrier((jnp.where(holder, held, second), beside))
     other = lax.ppermute(final, "row", [(r, r ^ 1) for r in range(2 * X_COUNT * Z_COUNT)])
-    return final, other
-
-
-def share_row(value, root, col):
+    return final, other, before, beside
+
+
+def share_row(value, root, col, lowest):
     right, left, far = (root + 1) % COLS, (root + 3) % COLS, (root + 2) % COLS
-    one = lax.ppermute(value, "col", [(root, right)])
+    count = 2 * X_COUNT * Z_COUNT
+
+    def pairs_of(pairs):
+        return [(r * COLS + a, r * COLS + b) for r in range(lowest, count) for a, b in pairs]
+
+    one = lax.ppermute(value, ("row", "col"), pairs_of([(root, right)]))
     held = jnp.where(col == root, value, one)
-    two = lax.ppermute(held, "col", [(root, left), (right, far)])
-    return held, jnp.where((col == root) | (col == right), held, two)
+
+    def finish(held):
+        two = lax.ppermute(held, ("row", "col"), pairs_of([(root, left), (right, far)]))
+        return jnp.where((col == root) | (col == right), held, two)
+
+    return held, finish
 
 
 def share_pivots(value, roots):
@@ -348,43 +382,48 @@
     pair, payload = (2, tile, width), (2 * width, tile)
     packed = (3, order[0], tile)
     scratch = [
-        [pltpu.VMEM(pair[:1] + (width, tile), F32), pltpu.VMEM((2, order[k], width), F32), pltpu.VMEM((4 * order[0], tile), F32)]
+        [pltpu.VMEM((2, width, tile), F32), pltpu.VMEM((2, order[k], width), F32), pltpu.VMEM((4 * order[0], tile), F32)]
+        + [pltpu.VMEM(shape, F32) for shape in (pair, pair, ((tile, tile), (2, tile, tile))[k], (tile, width), pair, pair)]
+        + [pltpu.SemaphoreType.DMA((8,))]
         for k in range(2)
     ]
 
     with jax.named_scope("corner_share"):
         pack = jnp.stack([own_u[0], own_v[0]])
         got = share_pivots(pack, [(0, 0), (1, 1)])
+        keep = jnp.arange(width, dtype=jnp.int32) < own_ranks[0, 0]
+        kept = jnp.where(keep, jnp.stack([own_u[0], own_v[0]]), 0.0)
+        near_lead, finish = share_row(kept, 0, col, 1)
+        got, near_lead = lax.optimization_barrier((got, near_lead))
         corner = jnp.where(col == row, pack, got)
-    with jax.named_scope("first_lead"):
-        keep = jnp.arange(width, dtype=jnp.int32) < own_ranks[0, 0]
-        near_lead, lead = share_row(jnp.where(keep, pack, 0.0), 0, col)
     with jax.named_scope("first_upper"):
         up_a, up_b = call(upper_kernel, (payload, payload), flags[0], near_field, corner, own_u, own_v)
     with jax.named_scope("upper_share"):
         crossed = lax.ppermute(up_a, "row", [(0, 1)])
-        ours_0, theirs_0 = share_planes(jnp.where(core == 0, up_b, crossed), row)
-    with jax.named_scope("wide_share"):
         extra = call(wide_kernel, (payload,), flags[0], near_lead, crossed)
+        mine, extra = lax.optimization_barrier((jnp.where(core == 0, up_b, crossed), extra))
+        lead = finish(near_lead)
         got = share_pivots(extra, [(1, 1)])
+        ours_0, theirs_0, lead, got = share_planes(mine, row, lead, got)
         extra = jnp.where(col == row, extra, got)
     with jax.named_scope("first_update"):
         cur_u, cur_v, pack, out_z, out_v = call(
             functools.partial(panel_kernel, order[0], 0),
-            (pair, pair, pair, packed, packed),
-            flags[0], near_field, own_u, own_v, lead, ours_0, theirs_0, corner, extra, sketch,
-            scratch=scratch[0],
+            (pair, pair, (2, order[0], tile), packed, packed),
+            flags[0], own_u, own_v, near_field, sketch, lead, ours_0, theirs_0, corner, extra,
+            scratch=scratch[0], loads=4, stores=2,
         )
     with jax.named_scope("second_share"):
-        _, lead = share_row(pack, 1, col)
+        near_lead, finish = share_row(pack, 1, col, 0)
         crossed = lax.ppermute(out_z, "row", [(1, 0)])
-        ours, theirs = share_planes(jnp.where(core == 1, out_v, crossed), row)
+        ours, theirs, near_lead, _ = share_planes(jnp.where(core == 1, out_v, crossed), row, near_lead, row)
+        lead = finish(near_lead)
     with jax.named_scope("second_update"):
         cur_u, cur_v = call(
             functools.partial(panel_kernel, order[1], 1),
             (pair, pair),
-            flags[1], near_field, cur_u, cur_v, lead, ours, theirs, ours_0, theirs_0, sketch,
-            scratch=scratch[1],
+            flags[1], cur_u, cur_v, near_field, sketch, lead, ours, theirs, ours_0, theirs_0,
+            scratch=scratch[1], loads=4, stores=2,
         )
     shape_out = factor_u.shape
     return cur_u.reshape(shape_out), cur_v.reshape(shape_out)

time: 162 us -> 158 us (0.975)
  the two profiles are of different devices: /device:TPU:0 before, /device:TPU:43 now
where the time goes in v5:
time: 158 us; the launch traced here: 157 us
  waiting for transfers between devices  52 us (33%)
  Pallas kernels  40.2 us (25%)
  starting transfers between devices  36.7 us (23%)
  other arithmetic  14.3 us (9%)
  local copies, waits for them, and re-layouts  12.5 us (8%)
    pallas_call x4, Pallas kernels, call(): pl.pallas_call(kernel, out_shape=shapes, in_specs=[pl.BlockSpec(memory_sp...  40.2 us
    ppermute x18, waiting for transfers between devices, fan_out(): moved = lax.ppermute(value, axis, pairs)  36.7 us
    ppermute x18, starting transfers between devices, fan_out(): moved = lax.ppermute(value, axis, pairs)  22.2 us
    ppermute x2, waiting for transfers between devices, share_row(): one = lax.ppermute(value, ('row', 'col'), pairs_of([(root, right)]))  13.3 us
    unnamed x44, local copies, waits for them, and re-layouts  9.5 us
    ppermute x2, starting transfers between devices, finish(): lax.ppermute(held, ('row', 'col'), pairs_of([(root, left), (right, far)]))  4.16 us
    ppermute x2, starting transfers between devices, share_row(): one = lax.ppermute(value, ('row', 'col'), pairs_of([(root, right)]))  4.01 us
    ppermute x2, starting transfers between devices, share_planes(): lax.ppermute(final, 'row', [(r, r ^ 1) for r in range(2 * X_COUNT * Z_COU...  3.41 us
  transfers between devices with their start and end apart: 26, of which 6 were waited for; matrix products, arithmetic and copies ran while one was open for 6% of the time, Pallas kernels for 1%

profile of v5, /device:TPU:43, one launch (start us, length us, event | category | flops | bytes accessed | tf_op | source)
XLA Modules:
  0.0 157.1 jit_solution(7339830043026431986)
XLA Ops:
  0.6 0.8 constant_dynamic-slice_fusion
  1.6 0.5 slice.42
  2.1 0.6 iota_compare_fusion
  2.7 1.1 slice_bitcast_fusion
  3.8 0.7 copy-done.18
  4.5 0.9 broadcast_select_fusion.1
  5.4 1.3 collective-permute-start.3
  6.7 1.4 collective-permute-start.2
  8.1 1.5 collective-permute-start.1
  9.6 1.5 collective-permute-start
  11.1 0.3 dynamic-slice_reduce_fusion
  11.5 8.5 %collective-permute-done.3 = f32[2,512,128]{2,1,0:T(8,128)S(1)} collective-permute-done((f32[2,512,128]{2,1,0:T(8,128)S(1)}, f32[2,512,128]{2,1,0:T(8,128)S(1)}, u32[]{:S(2)}, u32[]{:S(2)}) %collective-permute-start.3) | collective-permute-done | bytes 524320 | tf_op jit(solution)/shard_map/corner_share/ppermute | solution.py:341
  20.2 1.6 %add_add_fusion.1 = f32[2,512,128]{2,1,0:T(8,128)S(1)} fusion(f32[2,512,128]{2,1,0:T(8,128)} %collective-permute-done.2, f32[2,512,128]{2,1,0:T(8,128)} %collective-permute-done, f32[2,512,128]{2,1,0:T(8,128)} %collective-permute-done.1), kind=kLoop, calls=%fused_computation.6 | loop fusion | flops 262144 | bytes 2097152 | tf_op jit(solution)/shard_map/corner_share/add | solution.py:305
  21.8 0.3 copy-done
  22.4 5.1 %first_upper.1 = (f32[256,512]{1,0:T(8,128)}, f32[256,512]{1,0:T(8,128)S(1)}) custom-call(s32[12]{0:T(128)S(1)} %concatenate.7.flags, f32[2,512,512]{2,1,0:T(8,128)S(1)} %copy-done, f32[2,512,128]{2,1,0:T(8,128)S(1)} %broadcast_select_fusion.5.corner.refs_0_, f32[2,512,128]{2,1,0:T(8,128)S(1)} %bitcast.19, f32[2,512,128]{2,1,0:T(8,128)S(1)} %bitcast.21), custom_call_target="tpu_custom_call" | custom-call | tf_op jit(solution)/shard_map/first_upper/pallas_call | solution.py:281
  27.6 0.8 copy-done.17
  28.4 1.5 collective-permute-start.4
  29.8 2.1 %collective-permute-start.8 = (f32[2,512,128]{2,1,0:T(8,128)S(1)}, f32[2,512,128]{2,1,0:T(8,128)}, u32[]{:S(2)}, u32[]{:S(2)}) collective-permute-start(f32[2,512,128]{2,1,0:T(8,128)S(1)} %broadcast_select_fusion.4.lead), channel_id=1, source_target_pairs={{4,7},{5,6},{8,11},{9,10},{12,15},{13,14},{16,19},{17,18},{20,23},... | collective-permute-start | bytes 1572872 | tf_op jit(solution)/shard_map/upper_share/ppermute | solution.py:345
  31.9 1.5 upper_share.1
  33.5 0.8 copy-done.10
  34.2 1.9 %broadcast_select_fusion.6 = f32[256,512]{1,0:T(8,128)} fusion(f32[256,512]{1,0:T(8,128)} %copy-done.17, f32[256,512]{1,0:T(8,128)} %collective-permute-done.4.crossed, pred[]{:T(512)S(6)} %eq.47), kind=kLoop, calls=%fused_computation.15 | loop fusion | flops 131072 | bytes 1572865 | tf_op jit(solution)/shard_map/upper_share/jit(_where)/select_n | solution.py:404
  36.2 1.5 collective-permute-start.7
  37.6 1.4 collective-permute-start.6
  39.1 1.5 collective-permute-start.5
  40.5 1.5 collective-permute-start.14
  42.0 1.5 collective-permute-start.13
  43.5 0.8 broadcast_select_fusion.3.lead
  44.3 1.5 collective-permute-start.12
  45.8 1.6 %add_select_fusion.3 = f32[256,512]{1,0:T(8,128)S(1)} fusion(f32[256,512]{1,0:T(8,128)} %broadcast_select_fusion.6, f32[256,512]{1,0:T(8,128)} %collective-permute-done.7, f32[256,512]{1,0:T(8,128)} %collective-permute-done.5, f32[256,512]{1,0:T(8,128)} %collective-permute-done.6, pred[]{:T(512)S(6)} %lt.38), kind=kLoop, calls=%fused_computation.5 | loop fusion | flops 393216 | bytes 2621441 | tf_op jit(solution)/shard_map/upper_share/jit(_where)/select_n | solution.py:318
  47.4 1.5 collective-permute-start.11
  48.9 1.4 collective-permute-start.10
  50.3 1.3 collective-permute-start.9
  51.7 1.6 add_add_fusion
  53.3 18.7 %collective-permute-done.9 = f32[256,512]{1,0:T(8,128)} collective-permute-done((f32[256,512]{1,0:T(8,128)S(1)}, f32[256,512]{1,0:T(8,128)}, u32[]{:S(2)}, u32[]{:S(2)}) %collective-permute-start.9) | collective-permute-done | bytes 524320 | tf_op jit(solution)/shard_map/upper_share/ppermute | solution.py:304
  72.1 1.6 %add_select_fusion.2.ours.refs_0_ = f32[256,512]{1,0:T(8,128)S(1)} fusion(f32[256,512]{1,0:T(8,128)} %copy-done.20, f32[256,512]{1,0:T(8,128)} %collective-permute-done.11, f32[256,512]{1,0:T(8,128)} %collective-permute-done.9, f32[256,512]{1,0:T(8,128)} %collective-permute-done.10, pred[]{:T(512)S(6)} %eq.51), kind=kLoop, calls=%fused_computation.4 | loop fusion | flops 393216 | bytes 2621441 | tf_op jit(solution)/shard_map/upper_share/jit(_where)/select_n | solution.py:329
  73.7 1.6 %collective-permute-start.15 = (f32[256,512]{1,0:T(8,128)S(1)}, f32[256,512]{1,0:T(8,128)S(1)}, u32[]{:S(2)}, u32[]{:S(2)}) collective-permute-start(f32[256,512]{1,0:T(8,128)S(1)} %add_select_fusion.2.ours.refs_0_), channel_id=1, source_target_pairs={{0,4},{4,0},{8,12},{12,8},{16,20},{20,16},{24,28},{28,24},{32,36},... | collective-permute-start | bytes 1572872 | tf_op jit(solution)/shard_map/upper_share/ppermute | solution.py:330
  75.3 1.5 collective-permute-done.15.theirs.refs_1_
  76.8 18.4 %first_update.1 = (f32[2,512,128]{2,1,0:T(8,128)S(1)}, f32[2,512,128]{2,1,0:T(8,128)S(1)}, f32[2,96,512]{2,1,0:T(8,128)S(1)}, f32[3,96,512]{2,1,0:T(8,128)}, f32[3,96,512]{2,1,0:T(8,128)S(1)}) custom-call(s32[12]{0:T(128)S(1)} %concatenate.7.flags, f32[2,512,128]{2,1,0:T(8,128)S(1)} %bitcast.20, f32[2,512,128]{2,1,0:T(8,128)S(1)} %bitcast.22, ...), custom_call_target="tpu_custom_call" | custom-call | tf_op jit(solution)/shard_map/first_update/pallas_call | solution.py:281
  95.2 0.8 copy-done.12
  96.1 0.8 copy-done.13
  96.9 0.8 copy-done.15
  97.7 1.5 collective-permute-start.16
  99.2 2.7 %collective-permute-start.20 = (f32[2,96,512]{2,1,0:T(8,128)S(1)}, f32[2,96,512]{2,1,0:T(8,128)S(1)}, u32[]{:S(2)}, u32[]{:S(2)}) collective-permute-start(f32[2,96,512]{2,1,0:T(8,128)S(1)} %get-tuple-element.36), channel_id=1, source_target_pairs={{1,2},{5,6},{9,10},{13,14},{17,18},{21,22},{25,26},{29,30},{33,34}... | collective-permute-start | bytes 1179656 | tf_op jit(solution)/shard_map/second_share/ppermute | solution.py:341
  101.9 1.2 broadcast_select_fusion
  103.1 0.7 collective-permute-start.19
  103.8 0.7 collective-permute-start.18
  104.5 0.7 collective-permute-start.17
  105.2 4.8 %collective-permute-done.20 = f32[2,96,512]{2,1,0:T(8,128)S(1)} collective-permute-done((f32[2,96,512]{2,1,0:T(8,128)S(1)}, f32[2,96,512]{2,1,0:T(8,128)S(1)}, u32[]{:S(2)}, u32[]{:S(2)}) %collective-permute-start.20) | collective-permute-done | bytes 393248 | tf_op jit(solution)/shard_map/second_share/ppermute | solution.py:341
  110.0 0.8 broadcast_select_fusion.7
  110.8 0.3 add_select_fusion.1
  111.1 0.7 collective-permute-start.24
  111.8 0.7 collective-permute-start.23
  112.5 1.3 collective-permute-start.22
  113.8 2.1 %collective-permute-start.21 = (f32[2,96,512]{2,1,0:T(8,128)}, f32[2,96,512]{2,1,0:T(8,128)}, u32[]{:S(2)}, u32[]{:S(2)}) collective-permute-start(f32[2,96,512]{2,1,0:T(8,128)} %broadcast_select_fusion.7), channel_id=1, source_target_pairs={{1,0},{2,3},{5,4},{6,7},{9,8},{10,11},{13,12},{14,15},{17,16},{18,... | collective-permute-start | bytes 1179656 | tf_op jit(solution)/shard_map/second_share/ppermute | solution.py:345
  115.8 17.9 %collective-permute-done.22 = f32[3,96,512]{2,1,0:T(8,128)S(1)} collective-permute-done((f32[3,96,512]{2,1,0:T(8,128)S(1)}, f32[3,96,512]{2,1,0:T(8,128)S(1)}, u32[]{:S(2)}, u32[]{:S(2)}) %collective-permute-start.22) | collective-permute-done | bytes 589856 | tf_op jit(solution)/shard_map/second_share/ppermute | solution.py:304
  133.7 0.3 add_select_fusion.ours
  134.0 1.8 %collective-permute-start.25 = (f32[3,96,512]{2,1,0:T(8,128)S(1)}, f32[3,96,512]{2,1,0:T(8,128)}, u32[]{:S(2)}, u32[]{:S(2)}) collective-permute-start(f32[3,96,512]{2,1,0:T(8,128)S(1)} %add_select_fusion.ours), channel_id=1, source_target_pairs={{0,4},{4,0},{8,12},{12,8},{16,20},{20,16},{24,28},{28,24},{32,36},... | collective-permute-start | bytes 1769480 | tf_op jit(solution)/shard_map/second_share/ppermute | solution.py:330
  135.9 1.1 broadcast_select_fusion.8.lead
  136.9 0.6 collective-permute-done.25.theirs
  137.6 1.0 copy-done.6
  138.6 1.0 copy-done.8
  139.6 1.0 copy-done.14
  140.7 1.0 copy-done.16
  141.7 15.2 %second_update.1 = (f32[2,512,128]{2,1,0:T(8,128)}, f32[2,512,128]{2,1,0:T(8,128)}) custom-call(s32[12]{0:T(128)S(1)} %concatenate.6.flags, f32[2,512,128]{2,1,0:T(8,128)S(1)} %copy-done.14, f32[2,512,128]{2,1,0:T(8,128)S(1)} %copy-done.16, f32[2,512,512]{2,1,0:T(8,128)S(1)} %copy-done, f32[2,512,128]{2,1,0:T(8,128)S(1)} %copy-done.6, ...), custom_call_target="tpu_custom_call" | custom-call | tf_op jit(solution)/shard_map/second_update/pallas_call | solution.py:281
  (62 shorter events, 1.0 us)
Async XLA Ops:
  0.6 10.4 %copy-start.21 = (s32[3,1,32,2,1]{2,4,3,1,0:T(1,128)S(1)}, s32[3,1,32,2,1]{2,4,3,1,0:T(1,128)}, u32[]{:S(2)}) copy-start(s32[3,1,32,2,1]{2,4,3,1,0:T(1,128)} %param.9) | copy-start | bytes 2308
  3.8 0.7 copy-start.18
  5.4 14.7 %collective-permute-start.3 = (f32[2,512,128]{2,1,0:T(8,128)S(1)}, f32[2,512,128]{2,1,0:T(8,128)S(1)}, u32[]{:S(2)}, u32[]{:S(2)}) collective-permute-start(f32[2,512,128]{2,1,0:T(8,128)S(1)} %get-tuple-element.49), channel_id=1, source_target_pairs={{4,5},{8,9},{12,13},{16,17},{20,21},{24,25},{28,29},{32,33},{36,37... | collective-permute-start | bytes 1572872 | tf_op jit(solution)/shard_map/corner_share/ppermute | solution.py:341
  6.7 13.5 %collective-permute-start.2 = (f32[2,512,128]{2,1,0:T(8,128)}, f32[2,512,128]{2,1,0:T(8,128)}, u32[]{:S(2)}, u32[]{:S(2)}) collective-permute-start(f32[2,512,128]{2,1,0:T(8,128)} %get-tuple-element.50), channel_id=1, source_target_pairs={{0,2},{5,7}} | collective-permute-start | bytes 1572872 | tf_op jit(solution)/shard_map/corner_share/ppermute | solution.py:304
  8.1 12.0 %collective-permute-start.1 = (f32[2,512,128]{2,1,0:T(8,128)}, f32[2,512,128]{2,1,0:T(8,128)}, u32[]{:S(2)}, u32[]{:S(2)}) collective-permute-start(f32[2,512,128]{2,1,0:T(8,128)} %get-tuple-element.50), channel_id=1, source_target_pairs={{0,3},{5,4}} | collective-permute-start | bytes 1572872 | tf_op jit(solution)/shard_map/corner_share/ppermute | solution.py:304
  9.6 10.6 %collective-permute-start = (f32[2,512,128]{2,1,0:T(8,128)}, f32[2,512,128]{2,1,0:T(8,128)}, u32[]{:S(2)}, u32[]{:S(2)}) collective-permute-start(f32[2,512,128]{2,1,0:T(8,128)} %get-tuple-element.50), channel_id=1, source_target_pairs={{0,1},{5,6}} | collective-permute-start | bytes 1572872 | tf_op jit(solution)/shard_map/corner_share/ppermute | solution.py:304
  11.5 10.2 %copy-start.19 = (f32[1,512,128]{2,1,0:T(8,128)S(1)}, f32[1,512,128]{2,1,0:T(8,128)}, u32[]{:S(2)}) copy-start(f32[1,512,128]{2,1,0:T(8,128)} %copy-done.18) | copy-start | bytes 786436
  20.1 2.1 %copy-start = (f32[2,512,512]{2,1,0:T(8,128)S(1)}, f32[2,512,512]{2,1,0:T(8,128)}, u32[]{:S(2)}) copy-start(f32[2,512,512]{2,1,0:T(8,128)} %far_near.3) | copy-start | bytes 6291460
  20.1 2.1 %copy-start.1 = (f32[1,1,2,1,512,128]{5,4,3,2,1,0:T(8,128)S(1)}, f32[1,1,2,1,512,128]{5,4,3,2,1,0:T(8,128)}, u32[]{:S(2)}) copy-start(f32[1,1,2,1,512,128]{5,4,3,2,1,0:T(8,128)} %param.5) | copy-start | bytes 1572868
  20.1 2.3 %copy-start.3 = (f32[1,1,2,1,512,128]{5,4,3,2,1,0:T(8,128)S(1)}, f32[1,1,2,1,512,128]{5,4,3,2,1,0:T(8,128)}, u32[]{:S(2)}) copy-start(f32[1,1,2,1,512,128]{5,4,3,2,1,0:T(8,128)} %param.6) | copy-start | bytes 1572868
  27.6 0.8 copy-start.17
  28.4 3.6 %collective-permute-start.4 = (f32[256,512]{1,0:T(8,128)}, f32[256,512]{1,0:T(8,128)}, u32[]{:S(2)}, u32[]{:S(2)}) collective-permute-start(f32[256,512]{1,0:T(8,128)} %get-tuple-element.24), channel_id=1, source_target_pairs={{0,4},{1,5},{2,6},{3,7}} | collective-permute-start | bytes 1572872 | tf_op jit(solution)/shard_map/upper_share/ppermute | solution.py:402
  29.8 12.2 %collective-permute-start.8 = (f32[2,512,128]{2,1,0:T(8,128)S(1)}, f32[2,512,128]{2,1,0:T(8,128)}, u32[]{:S(2)}, u32[]{:S(2)}) collective-permute-start(f32[2,512,128]{2,1,0:T(8,128)S(1)} %broadcast_select_fusion.4.lead), channel_id=1, source_target_pairs={{4,7},{5,6},{8,11},{9,10},{12,15},{13,14},{16,19},{17,18},{20,23},... | collective-permute-start | bytes 1572872 | tf_op jit(solution)/shard_map/upper_share/ppermute | solution.py:345
  33.5 0.8 copy-start.10
  36.2 8.2 %collective-permute-start.7 = (f32[256,512]{1,0:T(8,128)}, f32[256,512]{1,0:T(8,128)}, u32[]{:S(2)}, u32[]{:S(2)}) collective-permute-start(f32[256,512]{1,0:T(8,128)} %broadcast_select_fusion.6), channel_id=1, source_target_pairs={{0,64},{4,20},{1,65},{5,21},{2,66},{6,22},{3,67},{7,23}} | collective-permute-start | bytes 1572872 | tf_op jit(solution)/shard_map/upper_share/ppermute | solution.py:304
  37.6 8.2 %collective-permute-start.6 = (f32[256,512]{1,0:T(8,128)}, f32[256,512]{1,0:T(8,128)}, u32[]{:S(2)}, u32[]{:S(2)}) collective-permute-start(f32[256,512]{1,0:T(8,128)} %broadcast_select_fusion.6), channel_id=1, source_target_pairs={{0,96},{4,28},{1,97},{5,29},{2,98},{6,30},{3,99},{7,31}} | collective-permute-start | bytes 1572872 | tf_op jit(solution)/shard_map/upper_share/ppermute | solution.py:304
  39.1 6.7 %collective-permute-start.5 = (f32[256,512]{1,0:T(8,128)}, f32[256,512]{1,0:T(8,128)}, u32[]{:S(2)}, u32[]{:S(2)}) collective-permute-start(f32[256,512]{1,0:T(8,128)} %broadcast_select_fusion.6), channel_id=1, source_target_pairs={{0,32},{4,12},{1,33},{5,13},{2,34},{6,14},{3,35},{7,15}} | collective-permute-start | bytes 1572872 | tf_op jit(solution)/shard_map/upper_share/ppermute | solution.py:304
  40.5 9.8 %collective-permute-start.14 = (f32[256,512]{1,0:T(8,128)}, f32[256,512]{1,0:T(8,128)}, u32[]{:S(2)}, u32[]{:S(2)}) collective-permute-start(f32[256,512]{1,0:T(8,128)} %copy-done.10), channel_id=1, source_target_pairs={{5,7}} | collective-permute-start | bytes 1572872 | tf_op jit(solution)/shard_map/upper_share/ppermute | solution.py:304
  42.0 9.6 %collective-permute-start.13 = (f32[256,512]{1,0:T(8,128)}, f32[256,512]{1,0:T(8,128)}, u32[]{:S(2)}, u32[]{:S(2)}) collective-permute-start(f32[256,512]{1,0:T(8,128)} %copy-done.10), channel_id=1, source_target_pairs={{5,4}} | collective-permute-start | bytes 1572872 | tf_op jit(solution)/shard_map/upper_share/ppermute | solution.py:304
  44.3 7.3 %collective-permute-start.12 = (f32[256,512]{1,0:T(8,128)}, f32[256,512]{1,0:T(8,128)}, u32[]{:S(2)}, u32[]{:S(2)}) collective-permute-start(f32[256,512]{1,0:T(8,128)} %copy-done.10), channel_id=1, source_target_pairs={{5,6}} | collective-permute-start | bytes 1572872 | tf_op jit(solution)/shard_map/upper_share/ppermute | solution.py:304
  47.4 5.9 %copy-start.20 = (f32[256,512]{1,0:T(8,128)}, f32[256,512]{1,0:T(8,128)S(1)}, u32[]{:S(2)}) copy-start(f32[256,512]{1,0:T(8,128)S(1)} %add_select_fusion.3) | copy-start | bytes 1572868
  47.4 5.9 %collective-permute-start.11 = (f32[256,512]{1,0:T(8,128)S(1)}, f32[256,512]{1,0:T(8,128)}, u32[]{:S(2)}, u32[]{:S(2)}) collective-permute-start(f32[256,512]{1,0:T(8,128)S(1)} %add_select_fusion.3), channel_id=1, source_target_pairs={{0,16},{32,48},{64,80},{96,112},{4,68},{12,76},{20,84},{28,92},{1,... | collective-permute-start | bytes 1572872 | tf_op jit(solution)/shard_map/upper_share/ppermute | solution.py:304
  48.9 4.4 %collective-permute-start.10 = (f32[256,512]{1,0:T(8,128)S(1)}, f32[256,512]{1,0:T(8,128)}, u32[]{:S(2)}, u32[]{:S(2)}) collective-permute-start(f32[256,512]{1,0:T(8,128)S(1)} %add_select_fusion.3), channel_id=1, source_target_pairs={{0,24},{32,56},{64,88},{96,120},{4,100},{12,108},{20,116},{28,124}... | collective-permute-start | bytes 1572872 | tf_op jit(solution)/shard_map/upper_share/ppermute | solution.py:304
  50.3 21.8 %collective-permute-start.9 = (f32[256,512]{1,0:T(8,128)S(1)}, f32[256,512]{1,0:T(8,128)}, u32[]{:S(2)}, u32[]{:S(2)}) collective-permute-start(f32[256,512]{1,0:T(8,128)S(1)} %add_select_fusion.3), channel_id=1, source_target_pairs={{0,8},{32,40},{64,72},{96,104},{4,36},{12,44},{20,52},{28,60},{1,9... | collective-permute-start | bytes 1572872 | tf_op jit(solution)/shard_map/upper_share/ppermute | solution.py:304
  51.7 23.6 %copy-start.11 = (f32[256,512]{1,0:T(8,128)S(1)}, f32[256,512]{1,0:T(8,128)}, u32[]{:S(2)}) copy-start(f32[256,512]{1,0:T(8,128)} %copy-done.10) | copy-start | bytes 1572868
  53.2 23.5 %copy-start.2 = (f32[1,1,2,1,512,128]{5,4,3,2,1,0:T(8,128)S(1)}, f32[1,1,2,1,512,128]{5,4,3,2,1,0:T(8,128)}, u32[]{:S(2)}) copy-start(f32[1,1,2,1,512,128]{5,4,3,2,1,0:T(8,128)} %param.5) | copy-start | bytes 1572868
  53.3 23.5 %copy-start.4 = (f32[1,1,2,1,512,128]{5,4,3,2,1,0:T(8,128)S(1)}, f32[1,1,2,1,512,128]{5,4,3,2,1,0:T(8,128)}, u32[]{:S(2)}) copy-start(f32[1,1,2,1,512,128]{5,4,3,2,1,0:T(8,128)} %param.6) | copy-start | bytes 1572868
  53.3 23.5 %copy-start.5 = (f32[2,512,128]{2,1,0:T(8,128)S(1)}, f32[2,512,128]{2,1,0:T(8,128)}, u32[]{:S(2)}) copy-start(f32[2,512,128]{2,1,0:T(8,128)} %far_sketch.3) | copy-start | bytes 1572868
  53.3 23.5 %copy-start.9 = (f32[2,512,128]{2,1,0:T(8,128)S(1)}, f32[2,512,128]{2,1,0:T(8,128)}, u32[]{:S(2)}) copy-start(f32[2,512,128]{2,1,0:T(8,128)} %broadcast_select_fusion.3.lead) | copy-start | bytes 1572868
  73.7 3.1 %collective-permute-start.15 = (f32[256,512]{1,0:T(8,128)S(1)}, f32[256,512]{1,0:T(8,128)S(1)}, u32[]{:S(2)}, u32[]{:S(2)}) collective-permute-start(f32[256,512]{1,0:T(8,128)S(1)} %add_select_fusion.2.ours.refs_0_), channel_id=1, source_target_pairs={{0,4},{4,0},{8,12},{12,8},{16,20},{20,16},{24,28},{28,24},{32,36},... | collective-permute-start | bytes 1572872 | tf_op jit(solution)/shard_map/upper_share/ppermute | solution.py:330
  76.8 18.4 %copy-start.7 = (f32[256,512]{1,0:T(8,128)}, f32[256,512]{1,0:T(8,128)S(1)}, u32[]{:S(2)}) copy-start(f32[256,512]{1,0:T(8,128)S(1)} %collective-permute-done.15.theirs.refs_1_) | copy-start | bytes 1572868
  95.2 0.9 copy-start.12
  96.1 0.8 copy-start.13
  96.9 0.8 copy-start.15
  97.7 4.2 %collective-permute-start.16 = (f32[3,96,512]{2,1,0:T(8,128)}, f32[3,96,512]{2,1,0:T(8,128)}, u32[]{:S(2)}, u32[]{:S(2)}) collective-permute-start(f32[3,96,512]{2,1,0:T(8,128)} %get-tuple-element.35), channel_id=1, source_target_pairs={{4,0},{5,1},{6,2},{7,3}} | collective-permute-start | bytes 1769480 | tf_op jit(solution)/shard_map/second_share/ppermute | solution.py:418
  99.2 10.8 %collective-permute-start.20 = (f32[2,96,512]{2,1,0:T(8,128)S(1)}, f32[2,96,512]{2,1,0:T(8,128)S(1)}, u32[]{:S(2)}, u32[]{:S(2)}) collective-permute-start(f32[2,96,512]{2,1,0:T(8,128)S(1)} %get-tuple-element.36), channel_id=1, source_target_pairs={{1,2},{5,6},{9,10},{13,14},{17,18},{21,22},{25,26},{29,30},{33,34}... | collective-permute-start | bytes 1179656 | tf_op jit(solution)/shard_map/second_share/ppermute | solution.py:341
  103.1 7.7 %collective-permute-start.19 = (f32[3,96,512]{2,1,0:T(8,128)S(1)}, f32[3,96,512]{2,1,0:T(8,128)S(1)}, u32[]{:S(2)}, u32[]{:S(2)}) collective-permute-start(f32[3,96,512]{2,1,0:T(8,128)S(1)} %broadcast_select_fusion), channel_id=1, source_target_pairs={{0,64},{4,20},{1,65},{5,21},{2,66},{6,22},{3,67},{7,23}} | collective-permute-start | bytes 1769480 | tf_op jit(solution)/shard_map/second_share/ppermute | solution.py:304
  103.8 7.0 %collective-permute-start.18 = (f32[3,96,512]{2,1,0:T(8,128)S(1)}, f32[3,96,512]{2,1,0:T(8,128)S(1)}, u32[]{:S(2)}, u32[]{:S(2)}) collective-permute-start(f32[3,96,512]{2,1,0:T(8,128)S(1)} %broadcast_select_fusion), channel_id=1, source_target_pairs={{0,96},{4,28},{1,97},{5,29},{2,98},{6,30},{3,99},{7,31}} | collective-permute-start | bytes 1769480 | tf_op jit(solution)/shard_map/second_share/ppermute | solution.py:304
  104.5 6.3 %collective-permute-start.17 = (f32[3,96,512]{2,1,0:T(8,128)S(1)}, f32[3,96,512]{2,1,0:T(8,128)S(1)}, u32[]{:S(2)}, u32[]{:S(2)}) collective-permute-start(f32[3,96,512]{2,1,0:T(8,128)S(1)} %broadcast_select_fusion), channel_id=1, source_target_pairs={{0,32},{4,12},{1,33},{5,13},{2,34},{6,14},{3,35},{7,15}} | collective-permute-start | bytes 1769480 | tf_op jit(solution)/shard_map/second_share/ppermute | solution.py:304
  111.1 4.8 %collective-permute-start.24 = (f32[3,96,512]{2,1,0:T(8,128)S(1)}, f32[3,96,512]{2,1,0:T(8,128)S(1)}, u32[]{:S(2)}, u32[]{:S(2)}) collective-permute-start(f32[3,96,512]{2,1,0:T(8,128)S(1)} %add_select_fusion.1), channel_id=1, source_target_pairs={{0,16},{32,48},{64,80},{96,112},{4,68},{12,76},{20,84},{28,92},{1,... | collective-permute-start | bytes 1769480 | tf_op jit(solution)/shard_map/second_share/ppermute | solution.py:304
  111.8 4.1 %collective-permute-start.23 = (f32[3,96,512]{2,1,0:T(8,128)S(1)}, f32[3,96,512]{2,1,0:T(8,128)S(1)}, u32[]{:S(2)}, u32[]{:S(2)}) collective-permute-start(f32[3,96,512]{2,1,0:T(8,128)S(1)} %add_select_fusion.1), channel_id=1, source_target_pairs={{0,24},{32,56},{64,88},{96,120},{4,100},{12,108},{20,116},{28,124}... | collective-permute-start | bytes 1769480 | tf_op jit(solution)/shard_map/second_share/ppermute | solution.py:304
  112.5 21.2 %collective-permute-start.22 = (f32[3,96,512]{2,1,0:T(8,128)S(1)}, f32[3,96,512]{2,1,0:T(8,128)S(1)}, u32[]{:S(2)}, u32[]{:S(2)}) collective-permute-start(f32[3,96,512]{2,1,0:T(8,128)S(1)} %add_select_fusion.1), channel_id=1, source_target_pairs={{0,8},{32,40},{64,72},{96,104},{4,36},{12,44},{20,52},{28,60},{1,9... | collective-permute-start | bytes 1769480 | tf_op jit(solution)/shard_map/second_share/ppermute | solution.py:304
  113.8 22.1 %collective-permute-start.21 = (f32[2,96,512]{2,1,0:T(8,128)}, f32[2,96,512]{2,1,0:T(8,128)}, u32[]{:S(2)}, u32[]{:S(2)}) collective-permute-start(f32[2,96,512]{2,1,0:T(8,128)} %broadcast_select_fusion.7), channel_id=1, source_target_pairs={{1,0},{2,3},{5,4},{6,7},{9,8},{10,11},{13,12},{14,15},{17,16},{18,... | collective-permute-start | bytes 1179656 | tf_op jit(solution)/shard_map/second_share/ppermute | solution.py:345
  134.0 3.6 %collective-permute-start.25 = (f32[3,96,512]{2,1,0:T(8,128)S(1)}, f32[3,96,512]{2,1,0:T(8,128)}, u32[]{:S(2)}, u32[]{:S(2)}) collective-permute-start(f32[3,96,512]{2,1,0:T(8,128)S(1)} %add_select_fusion.ours), channel_id=1, source_target_pairs={{0,4},{4,0},{8,12},{12,8},{16,20},{20,16},{24,28},{28,24},{32,36},... | collective-permute-start | bytes 1769480 | tf_op jit(solution)/shard_map/second_share/ppermute | solution.py:330
  137.5 1.0 copy-start.6
  138.6 1.0 copy-start.8
  139.6 1.0 copy-start.14
  140.7 1.0 copy-start.16

commit v6 on v5

--- a/solution.py
+++ b/solution.py
@@ -37,13 +37,16 @@
     return lax.broadcasted_iota(jnp.int32, shape, axis)
 
 
-def eliminate(grams, order):
+def eliminate(grams, order, beside=()):
     count = len(grams)
     lane8 = iota((8, 128), 1)
     row8 = iota((8, 128), 0)
     blocks = [[g[8 * b:8 * b + 8, :] for b in range(order // 8)] for g in grams]
     done = [[] for _ in grams]
-    for step in range(order // 8):
+    steps = order // 8
+    for step in range(steps):
+        for task in beside[step * len(beside) // steps:(step + 1) * len(beside) // steps]:
+            task()
         base = 8 * step
         panels, pivots_all = [], []
         for g in range(count):
@@ -95,6 +98,34 @@
     rest = split(jnp.where(eye, 1.0, 0.0) - pivot * start)
     square = split(dot3(rest, rest))
     return rest, square, split(dot3(square, square))
+
+
+def series_tasks(pivot, start, parts, values=None):
+    eye = iota(pivot.shape, 0) == iota(pivot.shape, 1)
+    parts.append(split(jnp.where(eye, 1.0, 0.0) - pivot * start))
+    half = pivot.shape[0] // 2
+    sums = {}
+
+    def block(power, side, left, right):
+        at = slice(side * half, side * half + half)
+        high = parts[power]
+        term = dot1(high[left], high[right][:, at])
+        sums[side] = term if (left, right) == (0, 0) else sums[side] + term
+        if side and (left, right) == (1, 0):
+            parts.append(split(jnp.concatenate([sums[0], sums[1]], axis=1)))
+
+    def apply(power):
+        values[0] = values[0] + dot3(values[0], parts[power])
+
+    tasks = []
+    for power in range(3):
+        if values is not None:
+            tasks.append(functools.partial(apply, power))
+        if power < 2:
+            for side in range(2):
+                for pair in ((0, 0), (0, 1), (1, 0)):
+                    tasks.append(functools.partial(block, power, side, *pair))
+    return tasks
 
 
 def upper_kernel(flags, near, corner, own_u, own_v, out_a, out_b):
@@ -166,8 +197,8 @@
             side = dot3(weight * dot3(z_t, lead_v, NT), lead_u).T
         full_u = jnp.concatenate([own_u, -side], axis=1)
         full_v = jnp.concatenate([cv[s], up_v], axis=1)
-        projected = dot6(test_t, full_v)
-        basis = dot6(projected, full_u, NT)
+        projected = dot3(test_t, full_v)
+        basis = dot3(projected, full_u, NT)
         basis = jnp.where(iota((order, tile), 0) < flags[s], basis, 0.0)
         basis = jnp.concatenate([basis, spare], axis=0)
         unit = jnp.where((row_g == lane_g) & (row_g >= flags[s]), 1.0, 0.0)
@@ -181,7 +212,8 @@
         far = near[...]
         start = diagonal_inverse(far)
         low_rank = dot3(corner[0], corner[1], NT) - dot3(extra[:width], extra[width:], TN)
-        parts = series(far + weight * low_rank, start)
+        parts = []
+        tasks = series_tasks(far + weight * low_rank, start, parts)
     else:
         left = flags[10] == 0
         slot = jnp.where(even, theirs_0[...], ours_0[...])
@@ -195,14 +227,13 @@
         one_v = jnp.where(left, slot[width:], moved[2 * width:])
         two_u = jnp.where(left, 0.0, moved[:width])
         low_rank = dot3(one_u, one_v, TN) - dot3(two_u, slot[width:], TN)
-        low = cv[0].T * start
-        for factors in series(far + weight * low_rank, start):
-            low = low + dot3(low, factors)
-
-    inverses = eliminate(grams, order)
+        low = [cv[0].T * start]
+        tasks = series_tasks(far + weight * low_rank, start, [], low)
+
+    inverses = eliminate(grams, order, tasks)
     defect = jnp.zeros((), F32)
     for s in range(2):
-        once = dot6(inverses[s], bases[s])
+        once = dot3(inverses[s], bases[s])
         ortho[s, :order] = once
         ortho[s, order:] = spare
         gram = dot3(once, jnp.concatenate([once, spare], axis=0), NT) + units[s]
@@ -238,7 +269,7 @@
             keep_u = jnp.where(lanes < flags[2 + s], keep_u, 0.0)
             keep_v = jnp.where(lanes < flags[2 + s], keep_v, 0.0)
         elif s == 0:
-            keep_v = jnp.where(flags[8] == 1, low.T, keep_v)
+            keep_v = jnp.where(flags[8] == 1, low[0].T, keep_v)
             keep_u = jnp.where(flags[9] == 1, 0.0, keep_u)
             keep_v = jnp.where(flags[9] == 1, 0.0, keep_v)
         chosen = flags[6 + s] == 1
@@ -275,6 +306,17 @@
         store.wait()
 
 
+def pack_kernel(flags, own_u, own_v, out, sems):
+    loads = [
+        pltpu.make_async_copy(own_u.at[0], out.at[0], sems.at[0]),
+        pltpu.make_async_copy(own_v.at[0], out.at[1], sems.at[1]),
+    ]
+    for load in loads:
+        load.start()
+    for load in loads:
+        load.wait()
+
+
 def call(kernel, shapes, flags, *values, scratch=(), loads=0, stores=0):
     vmem, far = pl.BlockSpec(memory_space=pltpu.VMEM), pl.BlockSpec(memory_space=pltpu.HBM)
     shapes = tuple(jax.ShapeDtypeStruct(shape, F32) for shape in shapes)
@@ -349,11 +391,11 @@
 
 
 def share_pivots(value, roots):
-    return fan_out(
-        value,
-        ("row", "col"),
-        [[(r * COLS + c, r * COLS + (c + k) % COLS) for r, c in roots] for k in (1, 3, 2)],
-    )
+    shares = [
+        lax.ppermute(value, ("row", "col"), [(r * COLS + c, r * COLS + (c + k) % COLS) for r, c in roots])
+        for k in (1, 3, 2)
+    ]
+    return shares[0], shares[1] + shares[2]
 
 
 def body(factor_u, factor_v, near_field, sketch, tile_ranks):
@@ -389,12 +431,15 @@
     ]
 
     with jax.named_scope("corner_share"):
-        pack = jnp.stack([own_u[0], own_v[0]])
-        got = share_pivots(pack, [(0, 0), (1, 1)])
+        pack = call(
+            pack_kernel, (pair,), col[None].astype(jnp.int32), own_u, own_v,
+            scratch=[pltpu.SemaphoreType.DMA((2,))], loads=2,
+        )
+        near, others = share_pivots(pack, [(0, 0), (1, 1)])
         keep = jnp.arange(width, dtype=jnp.int32) < own_ranks[0, 0]
-        kept = jnp.where(keep, jnp.stack([own_u[0], own_v[0]]), 0.0)
-        near_lead, finish = share_row(kept, 0, col, 1)
-        got, near_lead = lax.optimization_barrier((got, near_lead))
+        kept, near = lax.optimization_barrier((pack, near))
+        near_lead, finish = share_row(jnp.where(keep, kept, 0.0), 0, col, 1)
+        got = near + others
         corner = jnp.where(col == row, pack, got)
     with jax.named_scope("first_upper"):
         up_a, up_b = call(upper_kernel, (payload, payload), flags[0], near_field, corner, own_u, own_v)
@@ -403,7 +448,7 @@
         extra = call(wide_kernel, (payload,), flags[0], near_lead, crossed)
         mine, extra = lax.optimization_barrier((jnp.where(core == 0, up_b, crossed), extra))
         lead = finish(near_lead)
-        got = share_pivots(extra, [(1, 1)])
+        got = sum(share_pivots(extra, [(1, 1)]))
         ours_0, theirs_0, lead, got = share_planes(mine, row, lead, got)
         extra = jnp.where(col == row, extra, got)
     with jax.named_scope("first_update"):

time: 158 us -> 157 us (level)
  waiting for transfers between devices: 52 us -> 47.4 us
  Pallas kernels: 40.2 us -> 35.8 us
  starting transfers between devices: 36.7 us -> 40.6 us
  other arithmetic: 14.3 us -> 18 us
    ppermute x0 -> x6, starting transfers between devices: none -> 8.9 us  [share_pivots(): lax.ppermute(value, ('row', 'col'), [(r * COLS + c, r * COLS + (c + k) %...]
    ppermute x18 -> x12, starting transfers between devices: 22.2 us -> 13.4 us  [fan_out(): moved = lax.ppermute(value, axis, pairs)]
    ppermute x18 -> x12, waiting for transfers between devices: 36.7 us -> 31.8 us  [fan_out(): moved = lax.ppermute(value, axis, pairs)]
    pallas_call x4 -> x5, Pallas kernels: 40.2 us -> 35.8 us  [call(): pl.pallas_call(kernel, out_shape=shapes, in_specs=[pl.BlockSpec(memory_sp...]
    ppermute x2, waiting for transfers between devices: 0.01 us -> 3.97 us  [finish(): lax.ppermute(held, ('row', 'col'), pairs_of([(root, left), (right, far)]))]
    ppermute x2, waiting for transfers between devices: 13.3 us -> 9.53 us  [share_row(): one = lax.ppermute(value, ('row', 'col'), pairs_of([(root, right)]))]
    ppermute x2, starting transfers between devices: 3.41 us -> 5.84 us  [share_planes(): lax.ppermute(final, 'row', [(r, r ^ 1) for r in range(2 * X_COUNT * Z_COU...]
    select_n x2, other arithmetic: 0.87 us -> 2.71 us  [share_row(): held = jnp.where(col == root, value, one)]
  transfers between devices with their start and end apart: 26 -> 26, of which waited for: 6 -> 7; matrix products, arithmetic and copies ran while one was open for 6% -> 11% of each run, Pallas kernels for 1% -> 3%
where the time goes in v6:
time: 157 us; the launch traced here: 156 us
  waiting for transfers between devices  47.4 us (30%)
  starting transfers between devices  40.6 us (26%)
  Pallas kernels  35.8 us (23%)
  other arithmetic  18 us (11%)
  local copies, waits for them, and re-layouts  12.8 us (8%)
    pallas_call x5, Pallas kernels, call(): pl.pallas_call(kernel, out_shape=shapes, in_specs=[pl.BlockSpec(memory_sp...  35.8 us
    ppermute x12, waiting for transfers between devices, fan_out(): moved = lax.ppermute(value, axis, pairs)  31.8 us
    ppermute x12, starting transfers between devices, fan_out(): moved = lax.ppermute(value, axis, pairs)  13.4 us
    ppermute x2, waiting for transfers between devices, share_row(): one = lax.ppermute(value, ('row', 'col'), pairs_of([(root, right)]))  9.53 us
    unnamed x44, local copies, waits for them, and re-layouts  9.52 us
    ppermute x6, starting transfers between devices, share_pivots(): lax.ppermute(value, ('row', 'col'), [(r * COLS + c, r * COLS + (c + k) %...  8.9 us
    ppermute x2, starting transfers between devices, share_planes(): lax.ppermute(final, 'row', [(r, r ^ 1) for r in range(2 * X_COUNT * Z_COU...  5.84 us
    ppermute x2, starting transfers between devices, share_row(): one = lax.ppermute(value, ('row', 'col'), pairs_of([(root, right)]))  5.39 us
  transfers between devices with their start and end apart: 26, of which 7 were waited for; matrix products, arithmetic and copies ran while one was open for 11% of the time, Pallas kernels for 3%

profile of v6, /device:TPU:43, one launch (start us, length us, event | category | flops | bytes accessed | tf_op | source)
XLA Modules:
  0.0 156.0 jit_solution(15584058639258301183)
XLA Ops:
  0.6 1.0 copy-done.1
  1.7 1.0 copy-done.3
  2.8 1.6 %collective-permute-start = (f32[2,512,128]{2,1,0:T(8,128)S(1)}, f32[2,512,128]{2,1,0:T(8,128)}, u32[]{:S(2)}, u32[]{:S(2)}) collective-permute-start(f32[2,512,128]{2,1,0:T(8,128)S(1)} %corner_share.1), channel_id=1, source_target_pairs={{0,1},{5,6}} | collective-permute-start | bytes 1572872 | tf_op jit(solution)/shard_map/corner_share/ppermute | solution.py:395
  4.4 1.5 collective-permute-start.2
  5.9 1.5 collective-permute-start.1
  7.3 0.8 constant_dynamic-slice_fusion
  8.2 0.5 slice.24
  8.7 1.0 dynamic-slice_reduce_fusion
  9.7 0.8 slice_reduce_fusion
  10.6 0.7 iota_compare_fusion
  11.3 0.8 broadcast_select_fusion.1
  12.2 1.3 collective-permute-start.4
  13.5 1.5 add_select_fusion.4.corner.refs_0_
  15.0 5.1 %first_upper.1 = (f32[256,512]{1,0:T(8,128)}, f32[256,512]{1,0:T(8,128)S(1)}) custom-call(s32[12]{0:T(128)S(1)} %concatenate.7.flags, f32[2,512,512]{2,1,0:T(8,128)S(1)} %copy-done, f32[2,512,128]{2,1,0:T(8,128)S(1)} %add_select_fusion.4.corner.refs_0_, f32[2,512,128]{2,1,0:T(8,128)S(1)} %bitcast.16, f32[2,512,128]{2,1,0:T(8,128)S(1)} %bitcast.19), custom_call_target="tpu_custom_call" | custom-call | tf_op jit(solution)/shard_map/first_upper/pallas_call | solution.py:323
  20.1 0.8 copy-done.20
  20.9 1.5 collective-permute-start.3
  22.4 4.8 %collective-permute-done.4 = f32[2,512,128]{2,1,0:T(8,128)} collective-permute-done((f32[2,512,128]{2,1,0:T(8,128)}, f32[2,512,128]{2,1,0:T(8,128)}, u32[]{:S(2)}, u32[]{:S(2)}) %collective-permute-start.4) | collective-permute-done | bytes 524320 | tf_op jit(solution)/shard_map/corner_share/ppermute | solution.py:383
  27.1 1.9 %broadcast_select_fusion.4.lead = f32[2,512,128]{2,1,0:T(8,128)} fusion(f32[2,512,128]{2,1,0:T(8,128)} %collective-permute-done.4, pred[]{:T(512)S(6)} %eq.49, f32[2,512,128]{2,1,0:T(8,128)S(1)} %corner_share.1, pred[128]{0:T(512)(128)(4,1)S(1)} %iota_compare_fusion), kind=kLoop, calls=%fused_computation.10 | loop fusion | flops 262144 | bytes 1572993 | tf_op jit(solution)/shard_map/corner_share/jit(_where)/select_n | solution.py:384
  29.0 1.7 %upper_share.1 = f32[256,512]{1,0:T(8,128)S(1)} custom-call(s32[12]{0:T(128)S(1)} %concatenate.7.flags, f32[2,512,128]{2,1,0:T(8,128)} %broadcast_select_fusion.4.lead, f32[256,512]{1,0:T(8,128)} %collective-permute-done.3.crossed), custom_call_target="tpu_custom_call" | custom-call | tf_op jit(solution)/shard_map/upper_share/pallas_call | solution.py:323
  30.7 2.1 %broadcast_select_fusion.5 = f32[256,512]{1,0:T(8,128)} fusion(f32[256,512]{1,0:T(8,128)S(1)} %copy-done.21, f32[256,512]{1,0:T(8,128)} %collective-permute-done.3.crossed, pred[]{:T(512)S(6)} %eq.47), kind=kLoop, calls=%fused_computation.11 | loop fusion | flops 131072 | bytes 1572865 | tf_op jit(solution)/shard_map/upper_share/jit(_where)/select_n | solution.py:449
  32.8 1.4 collective-permute-start.7
  34.3 1.5 collective-permute-start.6
  35.7 1.5 collective-permute-start.5
  37.2 2.1 %collective-permute-start.8 = (f32[2,512,128]{2,1,0:T(8,128)}, f32[2,512,128]{2,1,0:T(8,128)}, u32[]{:S(2)}, u32[]{:S(2)}) collective-permute-start(f32[2,512,128]{2,1,0:T(8,128)} %broadcast_select_fusion.4.lead), channel_id=1, source_target_pairs={{4,7},{5,6},{8,11},{9,10},{12,15},{13,14},{16,19},{17,18},{20,23},... | collective-permute-start | bytes 1572872 | tf_op jit(solution)/shard_map/upper_share/ppermute | solution.py:387
  39.3 1.5 collective-permute-start.14
  40.8 1.5 collective-permute-start.13
  42.2 1.5 collective-permute-start.12
  43.7 2.4 %add_select_fusion.3 = f32[256,512]{1,0:T(8,128)} fusion(f32[256,512]{1,0:T(8,128)} %broadcast_select_fusion.5, f32[256,512]{1,0:T(8,128)} %collective-permute-done.7, f32[256,512]{1,0:T(8,128)} %collective-permute-done.5, f32[256,512]{1,0:T(8,128)} %collective-permute-done.6, pred[]{:T(512)S(6)} %lt.38), kind=kLoop, calls=%fused_computation.4 | loop fusion | flops 393216 | bytes 2621441 | tf_op jit(solution)/shard_map/upper_share/jit(_where)/select_n | solution.py:360
  46.1 4.0 %collective-permute-done.8 = f32[2,512,128]{2,1,0:T(8,128)} collective-permute-done((f32[2,512,128]{2,1,0:T(8,128)}, f32[2,512,128]{2,1,0:T(8,128)}, u32[]{:S(2)}, u32[]{:S(2)}) %collective-permute-start.8) | collective-permute-done | bytes 524320 | tf_op jit(solution)/shard_map/upper_share/ppermute | solution.py:387
  50.0 1.9 %broadcast_select_fusion.3.lead = f32[2,512,128]{2,1,0:T(8,128)} fusion(f32[2,512,128]{2,1,0:T(8,128)} %broadcast_select_fusion.4.lead, f32[2,512,128]{2,1,0:T(8,128)} %collective-permute-done.8, pred[]{:T(512)S(6)} %or.6), kind=kLoop, calls=%fused_computation.9 | loop fusion | flops 131072 | bytes 1572865 | tf_op jit(solution)/shard_map/upper_share/jit(_where)/select_n | solution.py:388
  51.9 1.5 collective-permute-start.11
  53.4 1.5 collective-permute-start.10
  54.9 1.3 collective-permute-start.9
  56.2 1.6 add_add_fusion
  57.8 12.2 %collective-permute-done.9 = f32[256,512]{1,0:T(8,128)} collective-permute-done((f32[256,512]{1,0:T(8,128)}, f32[256,512]{1,0:T(8,128)}, u32[]{:S(2)}, u32[]{:S(2)}) %collective-permute-start.9) | collective-permute-done | bytes 524320 | tf_op jit(solution)/shard_map/upper_share/ppermute | solution.py:346
  70.0 1.6 %add_select_fusion.2.ours.refs_0_ = f32[256,512]{1,0:T(8,128)S(1)} fusion(f32[256,512]{1,0:T(8,128)} %add_select_fusion.3, f32[256,512]{1,0:T(8,128)} %collective-permute-done.11, f32[256,512]{1,0:T(8,128)} %collective-permute-done.9, f32[256,512]{1,0:T(8,128)} %collective-permute-done.10, pred[]{:T(512)S(6)} %eq.51), kind=kLoop, calls=%fused_computation.3 | loop fusion | flops 393216 | bytes 2621441 | tf_op jit(solution)/shard_map/upper_share/jit(_where)/select_n | solution.py:371
  71.6 1.6 %collective-permute-start.15 = (f32[256,512]{1,0:T(8,128)S(1)}, f32[256,512]{1,0:T(8,128)S(1)}, u32[]{:S(2)}, u32[]{:S(2)}) collective-permute-start(f32[256,512]{1,0:T(8,128)S(1)} %add_select_fusion.2.ours.refs_0_), channel_id=1, source_target_pairs={{0,4},{4,0},{8,12},{12,8},{16,20},{20,16},{24,28},{28,24},{32,36},... | collective-permute-start | bytes 1572872 | tf_op jit(solution)/shard_map/upper_share/ppermute | solution.py:372
  73.3 1.5 collective-permute-done.15.theirs.refs_1_
  74.8 16.2 %first_update.1 = (f32[2,512,128]{2,1,0:T(8,128)S(1)}, f32[2,512,128]{2,1,0:T(8,128)S(1)}, f32[2,96,512]{2,1,0:T(8,128)S(1)}, f32[3,96,512]{2,1,0:T(8,128)}, f32[3,96,512]{2,1,0:T(8,128)S(1)}) custom-call(s32[12]{0:T(128)S(1)} %concatenate.7.flags, f32[2,512,128]{2,1,0:T(8,128)S(1)} %bitcast.17, f32[2,512,128]{2,1,0:T(8,128)S(1)} %bitcast.20, ...), custom_call_target="tpu_custom_call" | custom-call | tf_op jit(solution)/shard_map/first_update/pallas_call | solution.py:323
  91.0 0.8 copy-done.15
  91.8 0.8 copy-done.16
  92.6 0.8 copy-done.18
  93.4 1.5 collective-permute-start.16
  94.9 4.1 %collective-permute-start.20 = (f32[2,96,512]{2,1,0:T(8,128)S(1)}, f32[2,96,512]{2,1,0:T(8,128)S(1)}, u32[]{:S(2)}, u32[]{:S(2)}) collective-permute-start(f32[2,96,512]{2,1,0:T(8,128)S(1)} %get-tuple-element.36), channel_id=1, source_target_pairs={{1,2},{5,6},{9,10},{13,14},{17,18},{21,22},{25,26},{29,30},{33,34}... | collective-permute-start | bytes 1179656 | tf_op jit(solution)/shard_map/second_share/ppermute | solution.py:383
  99.1 1.2 broadcast_select_fusion
  100.2 0.7 collective-permute-start.19
  100.9 0.7 collective-permute-start.18
  101.6 0.7 collective-permute-start.17
  102.3 4.8 %collective-permute-done.20 = f32[2,96,512]{2,1,0:T(8,128)S(1)} collective-permute-done((f32[2,96,512]{2,1,0:T(8,128)S(1)}, f32[2,96,512]{2,1,0:T(8,128)S(1)}, u32[]{:S(2)}, u32[]{:S(2)}) %collective-permute-start.20) | collective-permute-done | bytes 393248 | tf_op jit(solution)/shard_map/second_share/ppermute | solution.py:383
  107.1 0.8 broadcast_select_fusion.6
  107.9 0.3 add_select_fusion.1
  108.2 0.7 collective-permute-start.24
  108.9 0.7 collective-permute-start.23
  109.6 1.3 collective-permute-start.22
  110.9 2.0 %collective-permute-start.21 = (f32[2,96,512]{2,1,0:T(8,128)}, f32[2,96,512]{2,1,0:T(8,128)}, u32[]{:S(2)}, u32[]{:S(2)}) collective-permute-start(f32[2,96,512]{2,1,0:T(8,128)} %broadcast_select_fusion.6), channel_id=1, source_target_pairs={{1,0},{2,3},{5,4},{6,7},{9,8},{10,11},{13,12},{14,15},{17,16},{18,... | collective-permute-start | bytes 1179656 | tf_op jit(solution)/shard_map/second_share/ppermute | solution.py:387
  113.0 19.6 %collective-permute-done.22 = f32[3,96,512]{2,1,0:T(8,128)S(1)} collective-permute-done((f32[3,96,512]{2,1,0:T(8,128)S(1)}, f32[3,96,512]{2,1,0:T(8,128)S(1)}, u32[]{:S(2)}, u32[]{:S(2)}) %collective-permute-start.22) | collective-permute-done | bytes 589856 | tf_op jit(solution)/shard_map/second_share/ppermute | solution.py:346
  132.8 4.2 %collective-permute-start.25 = (f32[3,96,512]{2,1,0:T(8,128)S(1)}, f32[3,96,512]{2,1,0:T(8,128)}, u32[]{:S(2)}, u32[]{:S(2)}) collective-permute-start(f32[3,96,512]{2,1,0:T(8,128)S(1)} %add_select_fusion.ours), channel_id=1, source_target_pairs={{0,4},{4,0},{8,12},{12,8},{16,20},{20,16},{24,28},{28,24},{32,36},... | collective-permute-start | bytes 1769480 | tf_op jit(solution)/shard_map/second_share/ppermute | solution.py:372
  137.2 1.1 broadcast_select_fusion.7.lead
  138.2 0.6 collective-permute-done.25.theirs
  138.8 1.0 copy-done.9
  139.9 1.0 copy-done.11
  140.9 1.0 copy-done.17
  142.0 1.0 copy-done.19
  143.0 12.7 %second_update.1 = (f32[2,512,128]{2,1,0:T(8,128)}, f32[2,512,128]{2,1,0:T(8,128)}) custom-call(s32[12]{0:T(128)S(1)} %concatenate.6.flags, f32[2,512,128]{2,1,0:T(8,128)S(1)} %copy-done.17, f32[2,512,128]{2,1,0:T(8,128)S(1)} %copy-done.19, f32[2,512,512]{2,1,0:T(8,128)S(1)} %copy-done, f32[2,512,128]{2,1,0:T(8,128)S(1)} %copy-done.9, ...), custom_call_target="tpu_custom_call" | custom-call | tf_op jit(solution)/shard_map/second_update/pallas_call | solution.py:323
  (61 shorter events, 0.8 us)
Async XLA Ops:
  0.6 1.0 copy-start.1
  1.7 1.0 copy-start.3
  2.8 12.1 %copy-start = (f32[2,512,512]{2,1,0:T(8,128)S(1)}, f32[2,512,512]{2,1,0:T(8,128)}, u32[]{:S(2)}) copy-start(f32[2,512,512]{2,1,0:T(8,128)} %far_near.3) | copy-start | bytes 6291460
  2.8 12.1 %copy-start.2 = (f32[1,1,2,1,512,128]{5,4,3,2,1,0:T(8,128)S(1)}, f32[1,1,2,1,512,128]{5,4,3,2,1,0:T(8,128)}, u32[]{:S(2)}) copy-start(f32[1,1,2,1,512,128]{5,4,3,2,1,0:T(8,128)} %param.5) | copy-start | bytes 1572868
  2.8 8.5 %collective-permute-start = (f32[2,512,128]{2,1,0:T(8,128)S(1)}, f32[2,512,128]{2,1,0:T(8,128)}, u32[]{:S(2)}, u32[]{:S(2)}) collective-permute-start(f32[2,512,128]{2,1,0:T(8,128)S(1)} %corner_share.1), channel_id=1, source_target_pairs={{0,1},{5,6}} | collective-permute-start | bytes 1572872 | tf_op jit(solution)/shard_map/corner_share/ppermute | solution.py:395
  4.4 9.0 %collective-permute-start.2 = (f32[2,512,128]{2,1,0:T(8,128)S(1)}, f32[2,512,128]{2,1,0:T(8,128)}, u32[]{:S(2)}, u32[]{:S(2)}) collective-permute-start(f32[2,512,128]{2,1,0:T(8,128)S(1)} %corner_share.1), channel_id=1, source_target_pairs={{0,2},{5,7}} | collective-permute-start | bytes 1572872 | tf_op jit(solution)/shard_map/corner_share/ppermute | solution.py:395
  5.9 7.6 %collective-permute-start.1 = (f32[2,512,128]{2,1,0:T(8,128)S(1)}, f32[2,512,128]{2,1,0:T(8,128)}, u32[]{:S(2)}, u32[]{:S(2)}) collective-permute-start(f32[2,512,128]{2,1,0:T(8,128)S(1)} %corner_share.1), channel_id=1, source_target_pairs={{0,3},{5,4}} | collective-permute-start | bytes 1572872 | tf_op jit(solution)/shard_map/corner_share/ppermute | solution.py:395
  10.6 4.4 %copy-start.4 = (f32[1,1,2,1,512,128]{5,4,3,2,1,0:T(8,128)S(1)}, f32[1,1,2,1,512,128]{5,4,3,2,1,0:T(8,128)}, u32[]{:S(2)}) copy-start(f32[1,1,2,1,512,128]{5,4,3,2,1,0:T(8,128)} %param.6) | copy-start | bytes 1572868
  12.2 15.0 %collective-permute-start.4 = (f32[2,512,128]{2,1,0:T(8,128)}, f32[2,512,128]{2,1,0:T(8,128)}, u32[]{:S(2)}, u32[]{:S(2)}) collective-permute-start(f32[2,512,128]{2,1,0:T(8,128)} %broadcast_select_fusion.1), channel_id=1, source_target_pairs={{4,5},{8,9},{12,13},{16,17},{20,21},{24,25},{28,29},{32,33},{36,37... | collective-permute-start | bytes 1572872 | tf_op jit(solution)/shard_map/corner_share/ppermute | solution.py:383
  15.0 5.2 %copy-start.6 = (f32[2,512,128]{2,1,0:T(8,128)}, f32[2,512,128]{2,1,0:T(8,128)S(1)}, u32[]{:S(2)}) copy-start(f32[2,512,128]{2,1,0:T(8,128)S(1)} %add_select_fusion.4.corner.refs_0_) | copy-start | bytes 1572868
  20.1 0.8 copy-start.20
  20.9 8.1 %collective-permute-start.3 = (f32[256,512]{1,0:T(8,128)}, f32[256,512]{1,0:T(8,128)}, u32[]{:S(2)}, u32[]{:S(2)}) collective-permute-start(f32[256,512]{1,0:T(8,128)} %get-tuple-element.24), channel_id=1, source_target_pairs={{0,4},{1,5},{2,6},{3,7}} | collective-permute-start | bytes 1572872 | tf_op jit(solution)/shard_map/upper_share/ppermute | solution.py:447
  22.4 8.4 %copy-start.21 = (f32[256,512]{1,0:T(8,128)S(1)}, f32[256,512]{1,0:T(8,128)}, u32[]{:S(2)}) copy-start(f32[256,512]{1,0:T(8,128)} %copy-done.20) | copy-start | bytes 1572868
  30.7 15.3 %copy-start.13 = (f32[256,512]{1,0:T(8,128)}, f32[256,512]{1,0:T(8,128)S(1)}, u32[]{:S(2)}) copy-start(f32[256,512]{1,0:T(8,128)S(1)} %upper_share.1) | copy-start | bytes 1572868
  32.8 7.9 %collective-permute-start.7 = (f32[256,512]{1,0:T(8,128)}, f32[256,512]{1,0:T(8,128)}, u32[]{:S(2)}, u32[]{:S(2)}) collective-permute-start(f32[256,512]{1,0:T(8,128)} %broadcast_select_fusion.5), channel_id=1, source_target_pairs={{0,64},{4,20},{1,65},{5,21},{2,66},{6,22},{3,67},{7,23}} | collective-permute-start | bytes 1572872 | tf_op jit(solution)/shard_map/upper_share/ppermute | solution.py:346
  34.3 7.9 %collective-permute-start.6 = (f32[256,512]{1,0:T(8,128)}, f32[256,512]{1,0:T(8,128)}, u32[]{:S(2)}, u32[]{:S(2)}) collective-permute-start(f32[256,512]{1,0:T(8,128)} %broadcast_select_fusion.5), channel_id=1, source_target_pairs={{0,96},{4,28},{1,97},{5,29},{2,98},{6,30},{3,99},{7,31}} | collective-permute-start | bytes 1572872 | tf_op jit(solution)/shard_map/upper_share/ppermute | solution.py:346
  35.7 8.0 %collective-permute-start.5 = (f32[256,512]{1,0:T(8,128)}, f32[256,512]{1,0:T(8,128)}, u32[]{:S(2)}, u32[]{:S(2)}) collective-permute-start(f32[256,512]{1,0:T(8,128)} %broadcast_select_fusion.5), channel_id=1, source_target_pairs={{0,32},{4,12},{1,33},{5,13},{2,34},{6,14},{3,35},{7,15}} | collective-permute-start | bytes 1572872 | tf_op jit(solution)/shard_map/upper_share/ppermute | solution.py:346
  37.2 12.8 %collective-permute-start.8 = (f32[2,512,128]{2,1,0:T(8,128)}, f32[2,512,128]{2,1,0:T(8,128)}, u32[]{:S(2)}, u32[]{:S(2)}) collective-permute-start(f32[2,512,128]{2,1,0:T(8,128)} %broadcast_select_fusion.4.lead), channel_id=1, source_target_pairs={{4,7},{5,6},{8,11},{9,10},{12,15},{13,14},{16,19},{17,18},{20,23},... | collective-permute-start | bytes 1572872 | tf_op jit(solution)/shard_map/upper_share/ppermute | solution.py:387
  39.3 15.6 %collective-permute-start.14 = (f32[256,512]{1,0:T(8,128)S(1)}, f32[256,512]{1,0:T(8,128)}, u32[]{:S(2)}, u32[]{:S(2)}) collective-permute-start(f32[256,512]{1,0:T(8,128)S(1)} %upper_share.1), channel_id=1, source_target_pairs={{5,7}} | collective-permute-start | bytes 1572872 | tf_op jit(solution)/shard_map/upper_share/ppermute | solution.py:395
  40.8 15.4 %collective-permute-start.13 = (f32[256,512]{1,0:T(8,128)S(1)}, f32[256,512]{1,0:T(8,128)}, u32[]{:S(2)}, u32[]{:S(2)}) collective-permute-start(f32[256,512]{1,0:T(8,128)S(1)} %upper_share.1), channel_id=1, source_target_pairs={{5,4}} | collective-permute-start | bytes 1572872 | tf_op jit(solution)/shard_map/upper_share/ppermute | solution.py:395
  42.2 14.0 %collective-permute-start.12 = (f32[256,512]{1,0:T(8,128)S(1)}, f32[256,512]{1,0:T(8,128)}, u32[]{:S(2)}, u32[]{:S(2)}) collective-permute-start(f32[256,512]{1,0:T(8,128)S(1)} %upper_share.1), channel_id=1, source_target_pairs={{5,6}} | collective-permute-start | bytes 1572872 | tf_op jit(solution)/shard_map/upper_share/ppermute | solution.py:395
  51.9 5.9 %collective-permute-start.11 = (f32[256,512]{1,0:T(8,128)}, f32[256,512]{1,0:T(8,128)}, u32[]{:S(2)}, u32[]{:S(2)}) collective-permute-start(f32[256,512]{1,0:T(8,128)} %add_select_fusion.3), channel_id=1, source_target_pairs={{0,16},{32,48},{64,80},{96,112},{4,68},{12,76},{20,84},{28,92},{1,... | collective-permute-start | bytes 1572872 | tf_op jit(solution)/shard_map/upper_share/ppermute | solution.py:346
  53.4 4.5 %collective-permute-start.10 = (f32[256,512]{1,0:T(8,128)}, f32[256,512]{1,0:T(8,128)}, u32[]{:S(2)}, u32[]{:S(2)}) collective-permute-start(f32[256,512]{1,0:T(8,128)} %add_select_fusion.3), channel_id=1, source_target_pairs={{0,24},{32,56},{64,88},{96,120},{4,100},{12,108},{20,116},{28,124}... | collective-permute-start | bytes 1572872 | tf_op jit(solution)/shard_map/upper_share/ppermute | solution.py:346
  54.9 15.2 %collective-permute-start.9 = (f32[256,512]{1,0:T(8,128)}, f32[256,512]{1,0:T(8,128)}, u32[]{:S(2)}, u32[]{:S(2)}) collective-permute-start(f32[256,512]{1,0:T(8,128)} %add_select_fusion.3), channel_id=1, source_target_pairs={{0,8},{32,40},{64,72},{96,104},{4,36},{12,44},{20,52},{28,60},{1,9... | collective-permute-start | bytes 1572872 | tf_op jit(solution)/shard_map/upper_share/ppermute | solution.py:346
  56.2 17.0 %copy-start.14 = (f32[256,512]{1,0:T(8,128)S(1)}, f32[256,512]{1,0:T(8,128)}, u32[]{:S(2)}) copy-start(f32[256,512]{1,0:T(8,128)} %copy-done.13) | copy-start | bytes 1572868
  57.8 17.0 %copy-start.5 = (f32[1,1,2,1,512,128]{5,4,3,2,1,0:T(8,128)S(1)}, f32[1,1,2,1,512,128]{5,4,3,2,1,0:T(8,128)}, u32[]{:S(2)}) copy-start(f32[1,1,2,1,512,128]{5,4,3,2,1,0:T(8,128)} %param.6) | copy-start | bytes 1572868
  57.8 17.0 %copy-start.7 = (f32[2,512,128]{2,1,0:T(8,128)S(1)}, f32[2,512,128]{2,1,0:T(8,128)}, u32[]{:S(2)}) copy-start(f32[2,512,128]{2,1,0:T(8,128)} %copy-done.6) | copy-start | bytes 1572868
  57.8 17.0 %copy-start.8 = (f32[2,512,128]{2,1,0:T(8,128)S(1)}, f32[2,512,128]{2,1,0:T(8,128)}, u32[]{:S(2)}) copy-start(f32[2,512,128]{2,1,0:T(8,128)} %far_sketch.3) | copy-start | bytes 1572868
  57.8 16.9 %copy-start.12 = (f32[2,512,128]{2,1,0:T(8,128)S(1)}, f32[2,512,128]{2,1,0:T(8,128)}, u32[]{:S(2)}) copy-start(f32[2,512,128]{2,1,0:T(8,128)} %broadcast_select_fusion.3.lead) | copy-start | bytes 1572868
  71.6 3.1 %collective-permute-start.15 = (f32[256,512]{1,0:T(8,128)S(1)}, f32[256,512]{1,0:T(8,128)S(1)}, u32[]{:S(2)}, u32[]{:S(2)}) collective-permute-start(f32[256,512]{1,0:T(8,128)S(1)} %add_select_fusion.2.ours.refs_0_), channel_id=1, source_target_pairs={{0,4},{4,0},{8,12},{12,8},{16,20},{20,16},{24,28},{28,24},{32,36},... | collective-permute-start | bytes 1572872 | tf_op jit(solution)/shard_map/upper_share/ppermute | solution.py:372
  74.8 16.2 %copy-start.10 = (f32[256,512]{1,0:T(8,128)}, f32[256,512]{1,0:T(8,128)S(1)}, u32[]{:S(2)}) copy-start(f32[256,512]{1,0:T(8,128)S(1)} %collective-permute-done.15.theirs.refs_1_) | copy-start | bytes 1572868
  91.0 0.8 copy-start.15
  91.8 0.8 copy-start.16
  92.6 0.8 copy-start.18
  93.4 5.6 %collective-permute-start.16 = (f32[3,96,512]{2,1,0:T(8,128)}, f32[3,96,512]{2,1,0:T(8,128)}, u32[]{:S(2)}, u32[]{:S(2)}) collective-permute-start(f32[3,96,512]{2,1,0:T(8,128)} %get-tuple-element.35), channel_id=1, source_target_pairs={{4,0},{5,1},{6,2},{7,3}} | collective-permute-start | bytes 1769480 | tf_op jit(solution)/shard_map/second_share/ppermute | solution.py:463
  94.9 12.2 %collective-permute-start.20 = (f32[2,96,512]{2,1,0:T(8,128)S(1)}, f32[2,96,512]{2,1,0:T(8,128)S(1)}, u32[]{:S(2)}, u32[]{:S(2)}) collective-permute-start(f32[2,96,512]{2,1,0:T(8,128)S(1)} %get-tuple-element.36), channel_id=1, source_target_pairs={{1,2},{5,6},{9,10},{13,14},{17,18},{21,22},{25,26},{29,30},{33,34}... | collective-permute-start | bytes 1179656 | tf_op jit(solution)/shard_map/second_share/ppermute | solution.py:383
  100.2 7.7 %collective-permute-start.19 = (f32[3,96,512]{2,1,0:T(8,128)S(1)}, f32[3,96,512]{2,1,0:T(8,128)S(1)}, u32[]{:S(2)}, u32[]{:S(2)}) collective-permute-start(f32[3,96,512]{2,1,0:T(8,128)S(1)} %broadcast_select_fusion), channel_id=1, source_target_pairs={{0,64},{4,20},{1,65},{5,21},{2,66},{6,22},{3,67},{7,23}} | collective-permute-start | bytes 1769480 | tf_op jit(solution)/shard_map/second_share/ppermute | solution.py:346
  100.9 7.0 %collective-permute-start.18 = (f32[3,96,512]{2,1,0:T(8,128)S(1)}, f32[3,96,512]{2,1,0:T(8,128)S(1)}, u32[]{:S(2)}, u32[]{:S(2)}) collective-permute-start(f32[3,96,512]{2,1,0:T(8,128)S(1)} %broadcast_select_fusion), channel_id=1, source_target_pairs={{0,96},{4,28},{1,97},{5,29},{2,98},{6,30},{3,99},{7,31}} | collective-permute-start | bytes 1769480 | tf_op jit(solution)/shard_map/second_share/ppermute | solution.py:346
  101.6 6.3 %collective-permute-start.17 = (f32[3,96,512]{2,1,0:T(8,128)S(1)}, f32[3,96,512]{2,1,0:T(8,128)S(1)}, u32[]{:S(2)}, u32[]{:S(2)}) collective-permute-start(f32[3,96,512]{2,1,0:T(8,128)S(1)} %broadcast_select_fusion), channel_id=1, source_target_pairs={{0,32},{4,12},{1,33},{5,13},{2,34},{6,14},{3,35},{7,15}} | collective-permute-start | bytes 1769480 | tf_op jit(solution)/shard_map/second_share/ppermute | solution.py:346
  108.2 4.8 %collective-permute-start.24 = (f32[3,96,512]{2,1,0:T(8,128)S(1)}, f32[3,96,512]{2,1,0:T(8,128)S(1)}, u32[]{:S(2)}, u32[]{:S(2)}) collective-permute-start(f32[3,96,512]{2,1,0:T(8,128)S(1)} %add_select_fusion.1), channel_id=1, source_target_pairs={{0,16},{32,48},{64,80},{96,112},{4,68},{12,76},{20,84},{28,92},{1,... | collective-permute-start | bytes 1769480 | tf_op jit(solution)/shard_map/second_share/ppermute | solution.py:346
  108.9 4.1 %collective-permute-start.23 = (f32[3,96,512]{2,1,0:T(8,128)S(1)}, f32[3,96,512]{2,1,0:T(8,128)S(1)}, u32[]{:S(2)}, u32[]{:S(2)}) collective-permute-start(f32[3,96,512]{2,1,0:T(8,128)S(1)} %add_select_fusion.1), channel_id=1, source_target_pairs={{0,24},{32,56},{64,88},{96,120},{4,100},{12,108},{20,116},{28,124}... | collective-permute-start | bytes 1769480 | tf_op jit(solution)/shard_map/second_share/ppermute | solution.py:346
  109.6 23.0 %collective-permute-start.22 = (f32[3,96,512]{2,1,0:T(8,128)S(1)}, f32[3,96,512]{2,1,0:T(8,128)S(1)}, u32[]{:S(2)}, u32[]{:S(2)}) collective-permute-start(f32[3,96,512]{2,1,0:T(8,128)S(1)} %add_select_fusion.1), channel_id=1, source_target_pairs={{0,8},{32,40},{64,72},{96,104},{4,36},{12,44},{20,52},{28,60},{1,9... | collective-permute-start | bytes 1769480 | tf_op jit(solution)/shard_map/second_share/ppermute | solution.py:346
  110.9 26.3 %collective-permute-start.21 = (f32[2,96,512]{2,1,0:T(8,128)}, f32[2,96,512]{2,1,0:T(8,128)}, u32[]{:S(2)}, u32[]{:S(2)}) collective-permute-start(f32[2,96,512]{2,1,0:T(8,128)} %broadcast_select_fusion.6), channel_id=1, source_target_pairs={{1,0},{2,3},{5,4},{6,7},{9,8},{10,11},{13,12},{14,15},{17,16},{18,... | collective-permute-start | bytes 1179656 | tf_op jit(solution)/shard_map/second_share/ppermute | solution.py:387
  132.8 6.0 %collective-permute-start.25 = (f32[3,96,512]{2,1,0:T(8,128)S(1)}, f32[3,96,512]{2,1,0:T(8,128)}, u32[]{:S(2)}, u32[]{:S(2)}) collective-permute-start(f32[3,96,512]{2,1,0:T(8,128)S(1)} %add_select_fusion.ours), channel_id=1, source_target_pairs={{0,4},{4,0},{8,12},{12,8},{16,20},{20,16},{24,28},{28,24},{32,36},... | collective-permute-start | bytes 1769480 | tf_op jit(solution)/shard_map/second_share/ppermute | solution.py:372
  138.8 1.0 copy-start.9
  139.9 1.0 copy-start.11
  140.9 1.0 copy-start.17
  142.0 1.0 copy-start.19

commit v7 on v6

--- a/solution.py
+++ b/solution.py
@@ -319,7 +319,9 @@
 
 def call(kernel, shapes, flags, *values, scratch=(), loads=0, stores=0):
     vmem, far = pl.BlockSpec(memory_space=pltpu.VMEM), pl.BlockSpec(memory_space=pltpu.HBM)
-    shapes = tuple(jax.ShapeDtypeStruct(shape, F32) for shape in shapes)
+    spaces = [pltpu.HBM] * stores + [pltpu.VMEM] * (len(shapes) - stores)
+    shapes = tuple(space(shape, F32) for space, shape in zip(spaces, shapes))
+    values = [pltpu.with_memory_space_constraint(value, pltpu.HBM) for value in values[:loads]] + list(values[loads:])
     out = pl.pallas_call(
         kernel,
         out_shape=shapes,
@@ -447,9 +449,9 @@
         crossed = lax.ppermute(up_a, "row", [(0, 1)])
         extra = call(wide_kernel, (payload,), flags[0], near_lead, crossed)
         mine, extra = lax.optimization_barrier((jnp.where(core == 0, up_b, crossed), extra))
+        got = sum(share_pivots(extra, [(1, 1)]))
+        ours_0, theirs_0, near_lead, got = share_planes(mine, row, near_lead, got)
         lead = finish(near_lead)
-        got = sum(share_pivots(extra, [(1, 1)]))
-        ours_0, theirs_0, lead, got = share_planes(mine, row, lead, got)
         extra = jnp.where(col == row, extra, got)
     with jax.named_scope("first_update"):
         cur_u, cur_v, pack, out_z, out_v = call(

time: 157 us -> 135 us (0.86)
  local copies, waits for them, and re-layouts: 12.8 us -> 4.14 us
  other arithmetic: 18 us -> 9.53 us
  starting transfers between devices: 40.6 us -> 34.5 us
    unnamed x44 -> x14, local copies, waits for them, and re-layouts: 9.52 us -> 0.83 us
    ppermute x2, waiting for transfers between devices: 3.97 us -> 0.01 us  [finish(): lax.ppermute(held, ('row', 'col'), pairs_of([(root, left), (right, far)]))]
    select_n x2, other arithmetic: 2.95 us -> 0.11 us  [finish(): return jnp.where((col == root) | (col == right), held, two)]
    ppermute x2, starting transfers between devices: 5.39 us -> 2.59 us  [share_row(): one = lax.ppermute(value, ('row', 'col'), pairs_of([(root, right)]))]
    ppermute x2, waiting for transfers between devices: 9.53 us -> 11.6 us  [share_row(): one = lax.ppermute(value, ('row', 'col'), pairs_of([(root, right)]))]
    select_n x1, other arithmetic: 2.11 us -> 0.08 us  [body(): jnp.where(core == 0, up_b, crossed)]
    ppermute x12, waiting for transfers between devices: 31.8 us -> 33.7 us  [fan_out(): moved = lax.ppermute(value, axis, pairs)]
  transfers between devices with their start and end apart: 26 -> 26, of which waited for: 7 -> 6; matrix products, arithmetic and copies ran while one was open for 11% -> 9% of each run, Pallas kernels for 3% -> 4%
where the time goes in v7:
time: 135 us; the launch traced here: 134 us
  waiting for transfers between devices  48.2 us (36%)
  Pallas kernels  36.9 us (27%)
  starting transfers between devices  34.5 us (26%)
  other arithmetic  9.53 us (7%)
  local copies, waits for them, and re-layouts  4.14 us (3%)
    pallas_call x5, Pallas kernels, call(): pl.pallas_call(kernel, out_shape=shapes, in_specs=[pl.BlockSpec(memory_sp...  36.9 us
    ppermute x12, waiting for transfers between devices, fan_out(): moved = lax.ppermute(value, axis, pairs)  33.7 us
    ppermute x12, starting transfers between devices, fan_out(): moved = lax.ppermute(value, axis, pairs)  13.4 us
    ppermute x2, waiting for transfers between devices, share_row(): one = lax.ppermute(value, ('row', 'col'), pairs_of([(root, right)]))  11.6 us
    ppermute x6, starting transfers between devices, share_pivots(): lax.ppermute(value, ('row', 'col'), [(r * COLS + c, r * COLS + (c + k) %...  8.14 us
    ppermute x2, starting transfers between devices, share_planes(): lax.ppermute(final, 'row', [(r, r ^ 1) for r in range(2 * X_COUNT * Z_COU...  6.22 us
    ppermute x2, waiting for transfers between devices, share_planes(): lax.ppermute(final, 'row', [(r, r ^ 1) for r in range(2 * X_COUNT * Z_COU...  2.85 us
  transfers between devices with their start and end apart: 26, of which 6 were waited for; matrix products, arithmetic and copies ran while one was open for 9% of the time, Pallas kernels for 4%

profile of v7, /device:TPU:43, one launch (start us, length us, event | category | flops | bytes accessed | tf_op | source)
XLA Modules:
  0.0 134.5 jit_solution(13276422535236728740)
XLA Ops:
  0.6 1.0 corner_share.1
  1.7 0.0 copy-start
  1.7 0.0 copy-start.1
  1.7 1.6 %collective-permute-start = (f32[2,512,128]{2,1,0:T(8,128)S(1)}, f32[2,512,128]{2,1,0:T(8,128)}, u32[]{:S(2)}, u32[]{:S(2)}) collective-permute-start(f32[2,512,128]{2,1,0:T(8,128)S(1)} %corner_share.1), channel_id=1, source_target_pairs={{0,1},{5,6}} | collective-permute-start | bytes 1572872 | tf_op jit(solution)/shard_map/corner_share/ppermute | solution.py:397
  3.3 1.5 %collective-permute-start.2 = (f32[2,512,128]{2,1,0:T(8,128)S(1)}, f32[2,512,128]{2,1,0:T(8,128)}, u32[]{:S(2)}, u32[]{:S(2)}) collective-permute-start(f32[2,512,128]{2,1,0:T(8,128)S(1)} %corner_share.1), channel_id=1, source_target_pairs={{0,2},{5,7}} | collective-permute-start | bytes 1572872 | tf_op jit(solution)/shard_map/corner_share/ppermute | solution.py:397
  4.8 1.5 %collective-permute-start.1 = (f32[2,512,128]{2,1,0:T(8,128)S(1)}, f32[2,512,128]{2,1,0:T(8,128)}, u32[]{:S(2)}, u32[]{:S(2)}) collective-permute-start(f32[2,512,128]{2,1,0:T(8,128)S(1)} %corner_share.1), channel_id=1, source_target_pairs={{0,3},{5,4}} | collective-permute-start | bytes 1572872 | tf_op jit(solution)/shard_map/corner_share/ppermute | solution.py:397
  6.2 0.8 constant_dynamic-slice_fusion
  7.0 0.1 copy.10
  7.1 0.5 slice.24
  7.6 1.0 dynamic-slice_reduce_fusion
  8.6 0.8 slice_reduce_fusion
  9.4 0.1 concatenate.7.flags
  9.5 0.7 iota_compare_fusion
  10.2 0.8 broadcast_select_fusion.1
  11.1 1.3 collective-permute-start.4
  12.4 0.0 collective-permute-done.1
  12.4 1.5 %add_select_fusion.4.corner.refs_0_ = f32[2,512,128]{2,1,0:T(8,128)S(1)} fusion(f32[2,512,128]{2,1,0:T(8,128)S(1)} %corner_share.1, f32[2,512,128]{2,1,0:T(8,128)} %collective-permute-done, f32[2,512,128]{2,1,0:T(8,128)} %collective-permute-done.1, f32[2,512,128]{2,1,0:T(8,128)} %collective-permute-done.2, pred[]{:T(512)S(6)} %eq.50), kind=kLoop, calls=%fused_computation.5 | loop fusion | flops 393216 | bytes 2621441 | tf_op jit(solution)/shard_map/corner_share/jit(_where)/select_n | solution.py:445
  13.9 5.1 %first_upper.1 = (f32[256,512]{1,0:T(8,128)}, f32[256,512]{1,0:T(8,128)S(1)}) custom-call(s32[12]{0:T(128)S(1)} %concatenate.7.flags, f32[2,512,512]{2,1,0:T(8,128)S(1)} %copy-done, f32[2,512,128]{2,1,0:T(8,128)S(1)} %add_select_fusion.4.corner.refs_0_, f32[2,512,128]{2,1,0:T(8,128)S(1)} %bitcast.17, f32[2,512,128]{2,1,0:T(8,128)S(1)} %bitcast.20), custom_call_target="tpu_custom_call" | custom-call | tf_op jit(solution)/shard_map/first_upper/pallas_call | solution.py:325
  19.0 0.8 copy-done.5
  19.8 0.8 collective-permute-start.3
  20.7 5.4 %collective-permute-done.4 = f32[2,512,128]{2,1,0:T(8,128)} collective-permute-done((f32[2,512,128]{2,1,0:T(8,128)}, f32[2,512,128]{2,1,0:T(8,128)}, u32[]{:S(2)}, u32[]{:S(2)}) %collective-permute-start.4) | collective-permute-done | bytes 524320 | tf_op jit(solution)/shard_map/corner_share/ppermute | solution.py:385
  26.1 1.1 broadcast_select_fusion.3.lead
  27.2 1.0 upper_share.1
  28.2 0.1 broadcast_select_fusion.4
  28.3 1.5 %collective-permute-start.7 = (f32[256,512]{1,0:T(8,128)S(1)}, f32[256,512]{1,0:T(8,128)}, u32[]{:S(2)}, u32[]{:S(2)}) collective-permute-start(f32[256,512]{1,0:T(8,128)S(1)} %broadcast_select_fusion.4), channel_id=1, source_target_pairs={{0,64},{4,20},{1,65},{5,21},{2,66},{6,22},{3,67},{7,23}} | collective-permute-start | bytes 1572872 | tf_op jit(solution)/shard_map/upper_share/ppermute | solution.py:348
  29.8 1.5 %collective-permute-start.6 = (f32[256,512]{1,0:T(8,128)S(1)}, f32[256,512]{1,0:T(8,128)}, u32[]{:S(2)}, u32[]{:S(2)}) collective-permute-start(f32[256,512]{1,0:T(8,128)S(1)} %broadcast_select_fusion.4), channel_id=1, source_target_pairs={{0,96},{4,28},{1,97},{5,29},{2,98},{6,30},{3,99},{7,31}} | collective-permute-start | bytes 1572872 | tf_op jit(solution)/shard_map/upper_share/ppermute | solution.py:348
  31.2 1.4 %collective-permute-start.5 = (f32[256,512]{1,0:T(8,128)S(1)}, f32[256,512]{1,0:T(8,128)}, u32[]{:S(2)}, u32[]{:S(2)}) collective-permute-start(f32[256,512]{1,0:T(8,128)S(1)} %broadcast_select_fusion.4), channel_id=1, source_target_pairs={{0,32},{4,12},{1,33},{5,13},{2,34},{6,14},{3,35},{7,15}} | collective-permute-start | bytes 1572872 | tf_op jit(solution)/shard_map/upper_share/ppermute | solution.py:348
  32.7 0.7 collective-permute-start.14
  33.4 1.5 %collective-permute-start.13 = (f32[256,512]{1,0:T(8,128)S(1)}, f32[256,512]{1,0:T(8,128)}, u32[]{:S(2)}, u32[]{:S(2)}) collective-permute-start(f32[256,512]{1,0:T(8,128)S(1)} %upper_share.1), channel_id=1, source_target_pairs={{5,4}} | collective-permute-start | bytes 1572872 | tf_op jit(solution)/shard_map/upper_share/ppermute | solution.py:397
  34.8 1.5 %collective-permute-start.12 = (f32[256,512]{1,0:T(8,128)S(1)}, f32[256,512]{1,0:T(8,128)}, u32[]{:S(2)}, u32[]{:S(2)}) collective-permute-start(f32[256,512]{1,0:T(8,128)S(1)} %upper_share.1), channel_id=1, source_target_pairs={{5,6}} | collective-permute-start | bytes 1572872 | tf_op jit(solution)/shard_map/upper_share/ppermute | solution.py:397
  36.3 0.0 collective-permute-done.6
  36.3 1.6 %add_select_fusion.3 = f32[256,512]{1,0:T(8,128)S(1)} fusion(f32[256,512]{1,0:T(8,128)S(1)} %broadcast_select_fusion.4, f32[256,512]{1,0:T(8,128)} %collective-permute-done.7, f32[256,512]{1,0:T(8,128)} %collective-permute-done.5, f32[256,512]{1,0:T(8,128)} %collective-permute-done.6, pred[]{:T(512)S(6)} %lt.38), kind=kLoop, calls=%fused_computation.4 | loop fusion | flops 393216 | bytes 2621441 | tf_op jit(solution)/shard_map/upper_share/jit(_where)/select_n | solution.py:362
  37.9 1.5 %collective-permute-start.11 = (f32[256,512]{1,0:T(8,128)S(1)}, f32[256,512]{1,0:T(8,128)}, u32[]{:S(2)}, u32[]{:S(2)}) collective-permute-start(f32[256,512]{1,0:T(8,128)S(1)} %add_select_fusion.3), channel_id=1, source_target_pairs={{0,16},{32,48},{64,80},{96,112},{4,68},{12,76},{20,84},{28,92},{1,... | collective-permute-start | bytes 1572872 | tf_op jit(solution)/shard_map/upper_share/ppermute | solution.py:348
  39.3 1.5 %collective-permute-start.10 = (f32[256,512]{1,0:T(8,128)S(1)}, f32[256,512]{1,0:T(8,128)}, u32[]{:S(2)}, u32[]{:S(2)}) collective-permute-start(f32[256,512]{1,0:T(8,128)S(1)} %add_select_fusion.3), channel_id=1, source_target_pairs={{0,24},{32,56},{64,88},{96,120},{4,100},{12,108},{20,116},{28,124}... | collective-permute-start | bytes 1572872 | tf_op jit(solution)/shard_map/upper_share/ppermute | solution.py:348
  40.8 1.3 collective-permute-start.9
  42.1 1.3 collective-permute-start.8
  43.5 1.3 %add_add_fusion = f32[256,512]{1,0:T(8,128)S(1)} fusion(f32[256,512]{1,0:T(8,128)} %collective-permute-done.12, f32[256,512]{1,0:T(8,128)} %collective-permute-done.13, f32[256,512]{1,0:T(8,128)S(1)} %collective-permute-done.14), kind=kLoop, calls=%fused_computation.2 | loop fusion | flops 262144 | bytes 2097152 | tf_op jit(solution)/shard_map/upper_share/add | solution.py:452
  44.9 15.9 %collective-permute-done.9 = f32[256,512]{1,0:T(8,128)} collective-permute-done((f32[256,512]{1,0:T(8,128)S(1)}, f32[256,512]{1,0:T(8,128)}, u32[]{:S(2)}, u32[]{:S(2)}) %collective-permute-start.9) | collective-permute-done | bytes 524320 | tf_op jit(solution)/shard_map/upper_share/ppermute | solution.py:348
  60.8 1.6 %add_select_fusion.2.ours.refs_0_ = f32[256,512]{1,0:T(8,128)S(1)} fusion(f32[256,512]{1,0:T(8,128)S(1)} %add_select_fusion.3, f32[256,512]{1,0:T(8,128)} %collective-permute-done.11, f32[256,512]{1,0:T(8,128)} %collective-permute-done.9, f32[256,512]{1,0:T(8,128)} %collective-permute-done.10, pred[]{:T(512)S(6)} %eq.51), kind=kLoop, calls=%fused_computation.3 | loop fusion | flops 393216 | bytes 2621441 | tf_op jit(solution)/shard_map/upper_share/jit(_where)/select_n | solution.py:373
  62.4 4.3 %collective-permute-start.15 = (f32[256,512]{1,0:T(8,128)S(1)}, f32[256,512]{1,0:T(8,128)S(1)}, u32[]{:S(2)}, u32[]{:S(2)}) collective-permute-start(f32[256,512]{1,0:T(8,128)S(1)} %add_select_fusion.2.ours.refs_0_), channel_id=1, source_target_pairs={{0,4},{4,0},{8,12},{12,8},{16,20},{20,16},{24,28},{28,24},{32,36},... | collective-permute-start | bytes 1572872 | tf_op jit(solution)/shard_map/upper_share/ppermute | solution.py:374
  66.7 0.1 broadcast_select_fusion.2.refs_1_
  66.8 0.1 broadcast_select_fusion.5.lead
  66.9 1.4 %collective-permute-done.15.theirs.refs_1_ = f32[256,512]{1,0:T(8,128)S(1)} collective-permute-done((f32[256,512]{1,0:T(8,128)S(1)}, f32[256,512]{1,0:T(8,128)S(1)}, u32[]{:S(2)}, u32[]{:S(2)}) %collective-permute-start.15) | collective-permute-done | bytes 524320 | tf_op jit(solution)/shard_map/upper_share/ppermute | solution.py:374
  68.2 15.7 %first_update.1 = (f32[2,512,128]{2,1,0:T(8,128)}, f32[2,512,128]{2,1,0:T(8,128)}, f32[2,96,512]{2,1,0:T(8,128)S(1)}, f32[3,96,512]{2,1,0:T(8,128)S(1)}, f32[3,96,512]{2,1,0:T(8,128)S(1)}) custom-call(s32[12]{0:T(128)S(1)} %concatenate.7.flags, f32[2,512,128]{2,1,0:T(8,128)} %bitcast.16, f32[2,512,128]{2,1,0:T(8,128)} %bitcast.19, f32[2,512,512]{2,1,0:T(8,128)} %far_near.3, ...), custom_call_target="tpu_custom_call" | custom-call | tf_op jit(solution)/shard_map/first_update/pallas_call | solution.py:325
  84.0 0.7 collective-permute-start.16
  84.7 1.3 collective-permute-start.20
  86.0 0.1 broadcast_select_fusion
  86.1 0.7 collective-permute-start.19
  86.8 0.7 collective-permute-start.18
  87.5 0.7 collective-permute-start.17
  88.2 6.2 %collective-permute-done.20 = f32[2,96,512]{2,1,0:T(8,128)S(1)} collective-permute-done((f32[2,96,512]{2,1,0:T(8,128)S(1)}, f32[2,96,512]{2,1,0:T(8,128)S(1)}, u32[]{:S(2)}, u32[]{:S(2)}) %collective-permute-start.20) | collective-permute-done | bytes 393248 | tf_op jit(solution)/shard_map/second_share/ppermute | solution.py:385
  94.4 0.1 broadcast_select_fusion.6
  94.5 0.3 add_select_fusion.1
  94.7 0.7 collective-permute-start.24
  95.4 0.7 collective-permute-start.23
  96.2 1.3 collective-permute-start.22
  97.5 1.3 collective-permute-start.21
  98.8 17.8 %collective-permute-done.22 = f32[3,96,512]{2,1,0:T(8,128)S(1)} collective-permute-done((f32[3,96,512]{2,1,0:T(8,128)S(1)}, f32[3,96,512]{2,1,0:T(8,128)S(1)}, u32[]{:S(2)}, u32[]{:S(2)}) %collective-permute-start.22) | collective-permute-done | bytes 589856 | tf_op jit(solution)/shard_map/second_share/ppermute | solution.py:348
  116.6 0.3 add_select_fusion.ours
  116.8 1.9 %collective-permute-start.25 = (f32[3,96,512]{2,1,0:T(8,128)S(1)}, f32[3,96,512]{2,1,0:T(8,128)S(1)}, u32[]{:S(2)}, u32[]{:S(2)}) collective-permute-start(f32[3,96,512]{2,1,0:T(8,128)S(1)} %add_select_fusion.ours), channel_id=1, source_target_pairs={{0,4},{4,0},{8,12},{12,8},{16,20},{20,16},{24,28},{28,24},{32,36},... | collective-permute-start | bytes 1769480 | tf_op jit(solution)/shard_map/second_share/ppermute | solution.py:374
  118.7 0.1 concatenate.6.flags
  118.8 0.1 broadcast_select_fusion.7.lead
  118.9 1.5 %collective-permute-done.25.theirs = f32[3,96,512]{2,1,0:T(8,128)S(1)} collective-permute-done((f32[3,96,512]{2,1,0:T(8,128)S(1)}, f32[3,96,512]{2,1,0:T(8,128)S(1)}, u32[]{:S(2)}, u32[]{:S(2)}) %collective-permute-start.25) | collective-permute-done | bytes 589856 | tf_op jit(solution)/shard_map/second_share/ppermute | solution.py:374
  120.3 13.9 %second_update.1 = (f32[2,512,128]{2,1,0:T(8,128)}, f32[2,512,128]{2,1,0:T(8,128)}) custom-call(s32[12]{0:T(128)S(1)} %concatenate.6.flags, f32[2,512,128]{2,1,0:T(8,128)} %get-tuple-element.32.far_u, f32[2,512,128]{2,1,0:T(8,128)} %get-tuple-element.33.far_v, f32[2,512,512]{2,1,0:T(8,128)} %far_near.3, f32[2,512,128]{2,1,0:T(8,128)} %far_sketch.3, ...), custom_call_target="tpu_custom_call" | custom-call | tf_op jit(solution)/shard_map/second_update/pallas_call | solution.py:325
  (31 shorter events, 0.1 us)
Async XLA Ops:
  1.7 12.1 %copy-start = (f32[2,512,512]{2,1,0:T(8,128)S(1)}, f32[2,512,512]{2,1,0:T(8,128)}, u32[]{:S(2)}) copy-start(f32[2,512,512]{2,1,0:T(8,128)} %far_near.3) | copy-start | bytes 6291460
  1.7 12.1 %copy-start.1 = (f32[1,1,2,1,512,128]{5,4,3,2,1,0:T(8,128)S(1)}, f32[1,1,2,1,512,128]{5,4,3,2,1,0:T(8,128)}, u32[]{:S(2)}) copy-start(f32[1,1,2,1,512,128]{5,4,3,2,1,0:T(8,128)} %param.5) | copy-start | bytes 1572868
  1.7 8.5 %collective-permute-start = (f32[2,512,128]{2,1,0:T(8,128)S(1)}, f32[2,512,128]{2,1,0:T(8,128)}, u32[]{:S(2)}, u32[]{:S(2)}) collective-permute-start(f32[2,512,128]{2,1,0:T(8,128)S(1)} %corner_share.1), channel_id=1, source_target_pairs={{0,1},{5,6}} | collective-permute-start | bytes 1572872 | tf_op jit(solution)/shard_map/corner_share/ppermute | solution.py:397
  3.3 9.0 %collective-permute-start.2 = (f32[2,512,128]{2,1,0:T(8,128)S(1)}, f32[2,512,128]{2,1,0:T(8,128)}, u32[]{:S(2)}, u32[]{:S(2)}) collective-permute-start(f32[2,512,128]{2,1,0:T(8,128)S(1)} %corner_share.1), channel_id=1, source_target_pairs={{0,2},{5,7}} | collective-permute-start | bytes 1572872 | tf_op jit(solution)/shard_map/corner_share/ppermute | solution.py:397
  4.8 7.6 %collective-permute-start.1 = (f32[2,512,128]{2,1,0:T(8,128)S(1)}, f32[2,512,128]{2,1,0:T(8,128)}, u32[]{:S(2)}, u32[]{:S(2)}) collective-permute-start(f32[2,512,128]{2,1,0:T(8,128)S(1)} %corner_share.1), channel_id=1, source_target_pairs={{0,3},{5,4}} | collective-permute-start | bytes 1572872 | tf_op jit(solution)/shard_map/corner_share/ppermute | solution.py:397
  9.5 4.4 %copy-start.2 = (f32[1,1,2,1,512,128]{5,4,3,2,1,0:T(8,128)S(1)}, f32[1,1,2,1,512,128]{5,4,3,2,1,0:T(8,128)}, u32[]{:S(2)}) copy-start(f32[1,1,2,1,512,128]{5,4,3,2,1,0:T(8,128)} %param.6) | copy-start | bytes 1572868
  11.1 15.0 %collective-permute-start.4 = (f32[2,512,128]{2,1,0:T(8,128)}, f32[2,512,128]{2,1,0:T(8,128)}, u32[]{:S(2)}, u32[]{:S(2)}) collective-permute-start(f32[2,512,128]{2,1,0:T(8,128)} %broadcast_select_fusion.1), channel_id=1, source_target_pairs={{4,5},{8,9},{12,13},{16,17},{20,21},{24,25},{28,29},{32,33},{36,37... | collective-permute-start | bytes 1572872 | tf_op jit(solution)/shard_map/corner_share/ppermute | solution.py:385
  13.9 5.2 %copy-start.3 = (f32[2,512,128]{2,1,0:T(8,128)}, f32[2,512,128]{2,1,0:T(8,128)S(1)}, u32[]{:S(2)}) copy-start(f32[2,512,128]{2,1,0:T(8,128)S(1)} %add_select_fusion.4.corner.refs_0_) | copy-start | bytes 1572868
  19.0 0.8 copy-start.5
  19.8 8.4 %copy-start.6 = (f32[256,512]{1,0:T(8,128)S(1)}, f32[256,512]{1,0:T(8,128)}, u32[]{:S(2)}) copy-start(f32[256,512]{1,0:T(8,128)} %copy-done.5) | copy-start | bytes 1572868
  19.8 7.3 %collective-permute-start.3 = (f32[256,512]{1,0:T(8,128)}, f32[256,512]{1,0:T(8,128)S(1)}, u32[]{:S(2)}, u32[]{:S(2)}) collective-permute-start(f32[256,512]{1,0:T(8,128)} %get-tuple-element.24), channel_id=1, source_target_pairs={{0,4},{1,5},{2,6},{3,7}} | collective-permute-start | bytes 1572872 | tf_op jit(solution)/shard_map/upper_share/ppermute | solution.py:449
  28.3 6.5 %collective-permute-start.7 = (f32[256,512]{1,0:T(8,128)S(1)}, f32[256,512]{1,0:T(8,128)}, u32[]{:S(2)}, u32[]{:S(2)}) collective-permute-start(f32[256,512]{1,0:T(8,128)S(1)} %broadcast_select_fusion.4), channel_id=1, source_target_pairs={{0,64},{4,20},{1,65},{5,21},{2,66},{6,22},{3,67},{7,23}} | collective-permute-start | bytes 1572872 | tf_op jit(solution)/shard_map/upper_share/ppermute | solution.py:348
  29.8 6.5 %collective-permute-start.6 = (f32[256,512]{1,0:T(8,128)S(1)}, f32[256,512]{1,0:T(8,128)}, u32[]{:S(2)}, u32[]{:S(2)}) collective-permute-start(f32[256,512]{1,0:T(8,128)S(1)} %broadcast_select_fusion.4), channel_id=1, source_target_pairs={{0,96},{4,28},{1,97},{5,29},{2,98},{6,30},{3,99},{7,31}} | collective-permute-start | bytes 1572872 | tf_op jit(solution)/shard_map/upper_share/ppermute | solution.py:348
  31.2 5.1 %collective-permute-start.5 = (f32[256,512]{1,0:T(8,128)S(1)}, f32[256,512]{1,0:T(8,128)}, u32[]{:S(2)}, u32[]{:S(2)}) collective-permute-start(f32[256,512]{1,0:T(8,128)S(1)} %broadcast_select_fusion.4), channel_id=1, source_target_pairs={{0,32},{4,12},{1,33},{5,13},{2,34},{6,14},{3,35},{7,15}} | collective-permute-start | bytes 1572872 | tf_op jit(solution)/shard_map/upper_share/ppermute | solution.py:348
  32.7 8.1 %collective-permute-start.14 = (f32[256,512]{1,0:T(8,128)S(1)}, f32[256,512]{1,0:T(8,128)S(1)}, u32[]{:S(2)}, u32[]{:S(2)}) collective-permute-start(f32[256,512]{1,0:T(8,128)S(1)} %upper_share.1), channel_id=1, source_target_pairs={{5,7}} | collective-permute-start | bytes 1572872 | tf_op jit(solution)/shard_map/upper_share/ppermute | solution.py:397
  33.4 8.8 %collective-permute-start.13 = (f32[256,512]{1,0:T(8,128)S(1)}, f32[256,512]{1,0:T(8,128)}, u32[]{:S(2)}, u32[]{:S(2)}) collective-permute-start(f32[256,512]{1,0:T(8,128)S(1)} %upper_share.1), channel_id=1, source_target_pairs={{5,4}} | collective-permute-start | bytes 1572872 | tf_op jit(solution)/shard_map/upper_share/ppermute | solution.py:397
  34.8 8.7 %collective-permute-start.12 = (f32[256,512]{1,0:T(8,128)S(1)}, f32[256,512]{1,0:T(8,128)}, u32[]{:S(2)}, u32[]{:S(2)}) collective-permute-start(f32[256,512]{1,0:T(8,128)S(1)} %upper_share.1), channel_id=1, source_target_pairs={{5,6}} | collective-permute-start | bytes 1572872 | tf_op jit(solution)/shard_map/upper_share/ppermute | solution.py:397
  37.9 7.0 %collective-permute-start.11 = (f32[256,512]{1,0:T(8,128)S(1)}, f32[256,512]{1,0:T(8,128)}, u32[]{:S(2)}, u32[]{:S(2)}) collective-permute-start(f32[256,512]{1,0:T(8,128)S(1)} %add_select_fusion.3), channel_id=1, source_target_pairs={{0,16},{32,48},{64,80},{96,112},{4,68},{12,76},{20,84},{28,92},{1,... | collective-permute-start | bytes 1572872 | tf_op jit(solution)/shard_map/upper_share/ppermute | solution.py:348
  39.3 5.5 %collective-permute-start.10 = (f32[256,512]{1,0:T(8,128)S(1)}, f32[256,512]{1,0:T(8,128)}, u32[]{:S(2)}, u32[]{:S(2)}) collective-permute-start(f32[256,512]{1,0:T(8,128)S(1)} %add_select_fusion.3), channel_id=1, source_target_pairs={{0,24},{32,56},{64,88},{96,120},{4,100},{12,108},{20,116},{28,124}... | collective-permute-start | bytes 1572872 | tf_op jit(solution)/shard_map/upper_share/ppermute | solution.py:348
  40.8 20.0 %collective-permute-start.9 = (f32[256,512]{1,0:T(8,128)S(1)}, f32[256,512]{1,0:T(8,128)}, u32[]{:S(2)}, u32[]{:S(2)}) collective-permute-start(f32[256,512]{1,0:T(8,128)S(1)} %add_select_fusion.3), channel_id=1, source_target_pairs={{0,8},{32,40},{64,72},{96,104},{4,36},{12,44},{20,52},{28,60},{1,9... | collective-permute-start | bytes 1572872 | tf_op jit(solution)/shard_map/upper_share/ppermute | solution.py:348
  42.1 24.6 %collective-permute-start.8 = (f32[2,512,128]{2,1,0:T(8,128)S(1)}, f32[2,512,128]{2,1,0:T(8,128)S(1)}, u32[]{:S(2)}, u32[]{:S(2)}) collective-permute-start(f32[2,512,128]{2,1,0:T(8,128)S(1)} %broadcast_select_fusion.3.lead), channel_id=1, source_target_pairs={{4,7},{5,6},{8,11},{9,10},{12,15},{13,14},{16,19},{17,18},{20,23},... | collective-permute-start | bytes 1572872 | tf_op jit(solution)/shard_map/upper_share/ppermute | solution.py:389
  62.4 5.9 %copy-start.4 = (f32[2,512,128]{2,1,0:T(8,128)S(1)}, f32[2,512,128]{2,1,0:T(8,128)}, u32[]{:S(2)}) copy-start(f32[2,512,128]{2,1,0:T(8,128)} %copy-done.3) | copy-start | bytes 1572868
  62.4 5.9 %collective-permute-start.15 = (f32[256,512]{1,0:T(8,128)S(1)}, f32[256,512]{1,0:T(8,128)S(1)}, u32[]{:S(2)}, u32[]{:S(2)}) collective-permute-start(f32[256,512]{1,0:T(8,128)S(1)} %add_select_fusion.2.ours.refs_0_), channel_id=1, source_target_pairs={{0,4},{4,0},{8,12},{12,8},{16,20},{20,16},{24,28},{28,24},{32,36},... | collective-permute-start | bytes 1572872 | tf_op jit(solution)/shard_map/upper_share/ppermute | solution.py:374
  84.0 2.0 %collective-permute-start.16 = (f32[3,96,512]{2,1,0:T(8,128)S(1)}, f32[3,96,512]{2,1,0:T(8,128)S(1)}, u32[]{:S(2)}, u32[]{:S(2)}) collective-permute-start(f32[3,96,512]{2,1,0:T(8,128)S(1)} %get-tuple-element.35), channel_id=1, source_target_pairs={{4,0},{5,1},{6,2},{7,3}} | collective-permute-start | bytes 1769480 | tf_op jit(solution)/shard_map/second_share/ppermute | solution.py:465
  84.7 9.7 %collective-permute-start.20 = (f32[2,96,512]{2,1,0:T(8,128)S(1)}, f32[2,96,512]{2,1,0:T(8,128)S(1)}, u32[]{:S(2)}, u32[]{:S(2)}) collective-permute-start(f32[2,96,512]{2,1,0:T(8,128)S(1)} %get-tuple-element.36), channel_id=1, source_target_pairs={{1,2},{5,6},{9,10},{13,14},{17,18},{21,22},{25,26},{29,30},{33,34}... | collective-permute-start | bytes 1179656 | tf_op jit(solution)/shard_map/second_share/ppermute | solution.py:385
  86.1 8.3 %collective-permute-start.19 = (f32[3,96,512]{2,1,0:T(8,128)S(1)}, f32[3,96,512]{2,1,0:T(8,128)S(1)}, u32[]{:S(2)}, u32[]{:S(2)}) collective-permute-start(f32[3,96,512]{2,1,0:T(8,128)S(1)} %broadcast_select_fusion), channel_id=1, source_target_pairs={{0,64},{4,20},{1,65},{5,21},{2,66},{6,22},{3,67},{7,23}} | collective-permute-start | bytes 1769480 | tf_op jit(solution)/shard_map/second_share/ppermute | solution.py:348
  86.8 7.6 %collective-permute-start.18 = (f32[3,96,512]{2,1,0:T(8,128)S(1)}, f32[3,96,512]{2,1,0:T(8,128)S(1)}, u32[]{:S(2)}, u32[]{:S(2)}) collective-permute-start(f32[3,96,512]{2,1,0:T(8,128)S(1)} %broadcast_select_fusion), channel_id=1, source_target_pairs={{0,96},{4,28},{1,97},{5,29},{2,98},{6,30},{3,99},{7,31}} | collective-permute-start | bytes 1769480 | tf_op jit(solution)/shard_map/second_share/ppermute | solution.py:348
  87.5 7.0 %collective-permute-start.17 = (f32[3,96,512]{2,1,0:T(8,128)S(1)}, f32[3,96,512]{2,1,0:T(8,128)S(1)}, u32[]{:S(2)}, u32[]{:S(2)}) collective-permute-start(f32[3,96,512]{2,1,0:T(8,128)S(1)} %broadcast_select_fusion), channel_id=1, source_target_pairs={{0,32},{4,12},{1,33},{5,13},{2,34},{6,14},{3,35},{7,15}} | collective-permute-start | bytes 1769480 | tf_op jit(solution)/shard_map/second_share/ppermute | solution.py:348
  94.7 4.0 %collective-permute-start.24 = (f32[3,96,512]{2,1,0:T(8,128)S(1)}, f32[3,96,512]{2,1,0:T(8,128)S(1)}, u32[]{:S(2)}, u32[]{:S(2)}) collective-permute-start(f32[3,96,512]{2,1,0:T(8,128)S(1)} %add_select_fusion.1), channel_id=1, source_target_pairs={{0,16},{32,48},{64,80},{96,112},{4,68},{12,76},{20,84},{28,92},{1,... | collective-permute-start | bytes 1769480 | tf_op jit(solution)/shard_map/second_share/ppermute | solution.py:348
  95.4 3.3 %collective-permute-start.23 = (f32[3,96,512]{2,1,0:T(8,128)S(1)}, f32[3,96,512]{2,1,0:T(8,128)S(1)}, u32[]{:S(2)}, u32[]{:S(2)}) collective-permute-start(f32[3,96,512]{2,1,0:T(8,128)S(1)} %add_select_fusion.1), channel_id=1, source_target_pairs={{0,24},{32,56},{64,88},{96,120},{4,100},{12,108},{20,116},{28,124}... | collective-permute-start | bytes 1769480 | tf_op jit(solution)/shard_map/second_share/ppermute | solution.py:348
  96.2 20.4 %collective-permute-start.22 = (f32[3,96,512]{2,1,0:T(8,128)S(1)}, f32[3,96,512]{2,1,0:T(8,128)S(1)}, u32[]{:S(2)}, u32[]{:S(2)}) collective-permute-start(f32[3,96,512]{2,1,0:T(8,128)S(1)} %add_select_fusion.1), channel_id=1, source_target_pairs={{0,8},{32,40},{64,72},{96,104},{4,36},{12,44},{20,52},{28,60},{1,9... | collective-permute-start | bytes 1769480 | tf_op jit(solution)/shard_map/second_share/ppermute | solution.py:348
  97.5 21.3 %collective-permute-start.21 = (f32[2,96,512]{2,1,0:T(8,128)S(1)}, f32[2,96,512]{2,1,0:T(8,128)S(1)}, u32[]{:S(2)}, u32[]{:S(2)}) collective-permute-start(f32[2,96,512]{2,1,0:T(8,128)S(1)} %broadcast_select_fusion.6), channel_id=1, source_target_pairs={{1,0},{2,3},{5,4},{6,7},{9,8},{10,11},{13,12},{14,15},{17,16},{18,... | collective-permute-start | bytes 1179656 | tf_op jit(solution)/shard_map/second_share/ppermute | solution.py:389
  116.8 3.5 %collective-permute-start.25 = (f32[3,96,512]{2,1,0:T(8,128)S(1)}, f32[3,96,512]{2,1,0:T(8,128)S(1)}, u32[]{:S(2)}, u32[]{:S(2)}) collective-permute-start(f32[3,96,512]{2,1,0:T(8,128)S(1)} %add_select_fusion.ours), channel_id=1, source_target_pairs={{0,4},{4,0},{8,12},{12,8},{16,20},{20,16},{24,28},{28,24},{32,36},... | collective-permute-start | bytes 1769480 | tf_op jit(solution)/shard_map/second_share/ppermute | solution.py:374

commit v8 on v7

--- a/solution.py
+++ b/solution.py
@@ -128,7 +128,7 @@
     return tasks
 
 
-def upper_kernel(flags, near, corner, own_u, own_v, out_a, out_b):
+def upper_kernel(flags, near, corner, own_u, own_v, *outs):
     tile, width = own_u.shape[1:]
     weight = 1.0 / (8.0 * tile)
     far = near[0]
@@ -139,23 +139,25 @@
     for part in parts[::-1]:
         values = values + dot3(values, part, NT)
     values = values * start
-    out_a[:width] = jnp.where(flags[10] == 0, corner[0].T, values[:width])
-    out_a[width:] = own_v[0].T
-    out_b[:width] = values[width:]
-    out_b[width:] = own_v[1].T
-
-
-def wide_kernel(flags, lead, crossed, out):
+    outs[0][...] = jnp.where(flags[10] == 0, corner[0].T, values[:width])
+    outs[1][...] = own_v[0].T
+    outs[2][...] = values[width:]
+    outs[3][...] = own_v[1].T
+
+
+def wide_kernel(flags, lead, z_t, v_t, out):
     width = lead.shape[2]
-    out[:width] = dot3(wide_t(lead, crossed[:width]), lead[0], NT)
-    out[width:] = crossed[width:]
-
-
-def panel_kernel(order, panel, flags, far_u, far_v, far_near, far_sketch, lead, ours, theirs, *refs):
+    out[:width] = dot3(wide_t(lead, z_t[...]), lead[0], NT)
+    out[width:] = v_t[...]
+
+
+def panel_kernel(order, panel, flags, far_u, far_v, far_near, far_sketch, lead, *refs):
+    ours, theirs, refs = refs[:2], refs[2:4], refs[4:]
     if panel == 0:
-        corner, extra, to_u, to_v, pack, out_z, out_v = refs[:7]
+        corner, extra, to_u, to_v, pack = refs[:5]
+        out_z, out_v = refs[5:7], refs[7:9]
     else:
-        ours_0, theirs_0, to_u, to_v = refs[:4]
+        ours_0, theirs_0, to_u, to_v = refs[:2], refs[2:4], refs[4], refs[5]
     ortho, factor, moved, cu, cv, near, sketch, nu, nv, sems = refs[-10:]
     near_from = far_near.at[1] if panel == 0 else far_near
     loads = [
@@ -167,6 +169,7 @@
     for load in loads:
         load.start()
     tile, width = cu.shape[1:]
+    even = flags[11] == 0
     weight = 1.0 / (8.0 * tile)
     root = math.sqrt(tile)
     lanes = iota((tile, width), 1)
@@ -174,13 +177,18 @@
     row_g = iota((order, width), 0)
     lane_g = iota((order, width), 1)
     eye = (row_g == lane_g).astype(F32)
-    even = flags[11] == 0
     full_us, full_vs, bases, grams, units = [], [], [], [], []
     if panel == 1:
-        part = ours.shape[1]
+        part = 2 * ours[0].shape[0] // 3
         rest = jnp.zeros((width - part, tile), F32)
         lead_u = jnp.concatenate([lead[0], rest], axis=0)
         lead_v = jnp.concatenate([lead[1], rest], axis=0)
+        cut = part // 2
+        planes = []
+        for one, two in ((ours, theirs), (theirs, ours)):
+            head, tail = [jnp.where(even, one[at][...], two[at][...]) for at in range(2)]
+            planes.append([head[:part], jnp.concatenate([head[part:], tail[:cut]], axis=0), tail[cut:]])
+        z_rows, v_rows = planes
     for load in loads:
         load.wait()
     test_t = sketch[...].T[:order]
@@ -188,12 +196,12 @@
         own_u = cu[s]
         if panel == 0:
             own_u = jnp.where(lanes < flags[2 + s], own_u, 0.0)
-            slot = jnp.where(even, theirs[...], ours[...]) if s == 0 else jnp.where(even, ours[...], theirs[...])
-            up_v = slot[width:].T
-            side = dot3(lead[0], wide_t(lead, slot[:width]), NT)
+            one, two = (theirs, ours) if s == 0 else (ours, theirs)
+            up_v = jnp.where(even, one[1][...], two[1][...]).T
+            side = dot3(lead[0], wide_t(lead, jnp.where(even, one[0][...], two[0][...])), NT)
         else:
-            z_t = jnp.concatenate([jnp.where(even, ours[s], theirs[s]), rest], axis=0)
-            up_v = jnp.concatenate([jnp.where(even, theirs[s], ours[s]), rest], axis=0).T
+            z_t = jnp.concatenate([z_rows[s], rest], axis=0)
+            up_v = jnp.concatenate([v_rows[s], rest], axis=0).T
             side = dot3(weight * dot3(z_t, lead_v, NT), lead_u).T
         full_u = jnp.concatenate([own_u, -side], axis=1)
         full_v = jnp.concatenate([cv[s], up_v], axis=1)
@@ -216,17 +224,17 @@
         tasks = series_tasks(far + weight * low_rank, start, parts)
     else:
         left = flags[10] == 0
-        slot = jnp.where(even, theirs_0[...], ours_0[...])
-        moved[:part] = jnp.where(even, ours[0], theirs[0])
-        moved[part:2 * part] = jnp.where(even, theirs[0], ours[0])
-        moved[2 * part:3 * part] = jnp.where(even, ours[2], theirs[2])
-        moved[3 * part:] = jnp.where(even, theirs[2], ours[2])
+        first_u, first_v = [jnp.where(even, theirs_0[at][...], ours_0[at][...]) for at in range(2)]
+        moved[:part] = z_rows[0]
+        moved[part:2 * part] = v_rows[0]
+        moved[2 * part:3 * part] = z_rows[2]
+        moved[3 * part:] = v_rows[2]
         far = jnp.where(left, near[0], near[1])
         start = diagonal_inverse(far)
-        one_u = jnp.where(left, slot[:width], moved[width:2 * width])
-        one_v = jnp.where(left, slot[width:], moved[2 * width:])
+        one_u = jnp.where(left, first_u, moved[width:2 * width])
+        one_v = jnp.where(left, first_v, moved[2 * width:])
         two_u = jnp.where(left, 0.0, moved[:width])
-        low_rank = dot3(one_u, one_v, TN) - dot3(two_u, slot[width:], TN)
+        low_rank = dot3(one_u, one_v, TN) - dot3(two_u, first_v, TN)
         low = [cv[0].T * start]
         tasks = series_tasks(far + weight * low_rank, start, [], low)
 
@@ -296,12 +304,14 @@
         fresh_t = fresh_vs[0].T[:order]
         pack[0] = ortho[0, :order] * root
         pack[1] = fresh_t
-        out_z[0] = jnp.where(middle, moved[:order], values[:order])
-        out_z[1] = values[order:]
-        out_z[2] = moved[2 * order:3 * order]
-        out_v[0] = jnp.where(middle, moved[order:2 * order], fresh_t)
-        out_v[1] = fresh_vs[1].T[:order]
-        out_v[2] = moved[3 * order:]
+        cut = order // 2
+        z_rows = [jnp.where(middle, moved[:order], values[:order]), values[order:], moved[2 * order:3 * order]]
+        v_rows = [jnp.where(middle, moved[order:2 * order], fresh_t), fresh_vs[1].T[:order], moved[3 * order:]]
+        for (head, tail), rows in ((out_z, z_rows), (out_v, v_rows)):
+            head[:order] = rows[0]
+            head[order:] = rows[1][:cut]
+            tail[:cut] = rows[1][cut:]
+            tail[cut:] = rows[2]
     for store in pending:
         store.wait()
 
@@ -350,29 +360,28 @@
     return total
 
 
-def share_planes(mine, row, before, beside):
+def share_planes(pieces, row, before, beside):
     core = row % 2
     x = (row // 2) % X_COUNT
     z = row // (2 * X_COUNT)
-    first = fan_out(
-        mine,
-        "row",
-        [[(row_of(0, 0, 0), row_of(k, 0, 0)), (row_of(0, 0, 1), row_of(0, k, 1))] for k in (1, 3, 2)],
-    )
-    held, before = lax.optimization_barrier((jnp.where(row < 2, mine, first), before))
-    second = fan_out(
-        held,
-        "row",
-        [
-            [(row_of(z, 0, 0), row_of(z, k, 0)) for z in range(Z_COUNT)]
-            + [(row_of(0, x, 1), row_of(k, x, 1)) for x in range(X_COUNT)]
-            for k in (1, 3, 2)
-        ],
-    )
+    first_sets = [[(row_of(0, 0, 0), row_of(k, 0, 0)), (row_of(0, 0, 1), row_of(0, k, 1))] for k in (1, 3, 2)]
+    second_sets = [
+        [(row_of(z, 0, 0), row_of(z, k, 0)) for z in range(Z_COUNT)]
+        + [(row_of(0, x, 1), row_of(k, x, 1)) for x in range(X_COUNT)]
+        for k in (1, 3, 2)
+    ]
     holder = jnp.where(core == 0, x, z) == 0
-    final, beside = lax.optimization_barrier((jnp.where(holder, held, second), beside))
-    other = lax.ppermute(final, "row", [(r, r ^ 1) for r in range(2 * X_COUNT * Z_COUNT)])
-    return final, other, before, beside
+    ours, theirs = [], []
+    for at, mine in enumerate(pieces):
+        held = jnp.where(row < 2, mine, fan_out(mine, "row", first_sets))
+        if at == 1:
+            held, before = lax.optimization_barrier((held, before))
+        final = jnp.where(holder, held, fan_out(held, "row", second_sets))
+        if at == 1:
+            final, beside = lax.optimization_barrier((final, beside))
+        ours.append(final)
+        theirs.append(lax.ppermute(final, "row", [(r, r ^ 1) for r in range(2 * X_COUNT * Z_COUNT)]))
+    return ours, theirs, before, beside
 
 
 def share_row(value, root, col, lowest):
@@ -424,7 +433,7 @@
 
     flags = [flags_of(panel) for panel in range(2)]
     pair, payload = (2, tile, width), (2 * width, tile)
-    packed = (3, order[0], tile)
+    packed = (3 * order[0] // 2, tile)
     scratch = [
         [pltpu.VMEM((2, width, tile), F32), pltpu.VMEM((2, order[k], width), F32), pltpu.VMEM((4 * order[0], tile), F32)]
         + [pltpu.VMEM(shape, F32) for shape in (pair, pair, ((tile, tile), (2, tile, tile))[k], (tile, width), pair, pair)]
@@ -444,32 +453,35 @@
         got = near + others
         corner = jnp.where(col == row, pack, got)
     with jax.named_scope("first_upper"):
-        up_a, up_b = call(upper_kernel, (payload, payload), flags[0], near_field, corner, own_u, own_v)
+        ups = call(upper_kernel, ((width, tile),) * 4, flags[0], near_field, corner, own_u, own_v)
     with jax.named_scope("upper_share"):
-        crossed = lax.ppermute(up_a, "row", [(0, 1)])
-        extra = call(wide_kernel, (payload,), flags[0], near_lead, crossed)
-        mine, extra = lax.optimization_barrier((jnp.where(core == 0, up_b, crossed), extra))
+        *sent, near_lead = lax.optimization_barrier((*ups[:2], near_lead))
+        crossed = [lax.ppermute(up, "row", [(0, 1)]) for up in sent]
+        extra = call(wide_kernel, (payload,), flags[0], near_lead, *crossed)
+        pieces = [jnp.where(core == 0, up, other) for up, other in zip(ups[2:], crossed)]
+        *pieces, extra = lax.optimization_barrier((*pieces, extra))
         got = sum(share_pivots(extra, [(1, 1)]))
-        ours_0, theirs_0, near_lead, got = share_planes(mine, row, near_lead, got)
+        ours_0, theirs_0, near_lead, got = share_planes(pieces, row, near_lead, got)
         lead = finish(near_lead)
         extra = jnp.where(col == row, extra, got)
     with jax.named_scope("first_update"):
-        cur_u, cur_v, pack, out_z, out_v = call(
+        cur_u, cur_v, pack, *outs = call(
             functools.partial(panel_kernel, order[0], 0),
-            (pair, pair, (2, order[0], tile), packed, packed),
-            flags[0], own_u, own_v, near_field, sketch, lead, ours_0, theirs_0, corner, extra,
+            (pair, pair, (2, order[0], tile), packed, packed, packed, packed),
+            flags[0], own_u, own_v, near_field, sketch, lead, *ours_0, *theirs_0, corner, extra,
             scratch=scratch[0], loads=4, stores=2,
         )
     with jax.named_scope("second_share"):
         near_lead, finish = share_row(pack, 1, col, 0)
-        crossed = lax.ppermute(out_z, "row", [(1, 0)])
-        ours, theirs, near_lead, _ = share_planes(jnp.where(core == 1, out_v, crossed), row, near_lead, row)
+        crossed = [lax.ppermute(out, "row", [(1, 0)]) for out in outs[:2]]
+        pieces = [jnp.where(core == 1, out, other) for out, other in zip(outs[2:], crossed)]
+        ours, theirs, near_lead, _ = share_planes(pieces, row, near_lead, row)
         lead = finish(near_lead)
     with jax.named_scope("second_update"):
         cur_u, cur_v = call(
             functools.partial(panel_kernel, order[1], 1),
             (pair, pair),
-            flags[1], cur_u, cur_v, near_field, sketch, lead, ours, theirs, ours_0, theirs_0,
+            flags[1], cur_u, cur_v, near_field, sketch, lead, *ours, *theirs, *ours_0, *theirs_0,
             scratch=scratch[1], loads=4, stores=2,
         )
     shape_out = factor_u.shape

time: 135 us -> 149 us (1.10)
  the two profiles are of different devices: /device:TPU:43 before, /device:TPU:0 now
where the time goes in v8:
time: 149 us; the launch traced here: 148 us
  starting transfers between devices  69.4 us (47%)
  Pallas kernels  37.5 us (25%)
  waiting for transfers between devices  26.2 us (18%)
  other arithmetic  10.6 us (7%)
  local copies, waits for them, and re-layouts  2.56 us (2%)
    ppermute x24, starting transfers between devices, fan_out(): moved = lax.ppermute(value, axis, pairs)  42.4 us
    pallas_call x5, Pallas kernels, call(): pl.pallas_call(kernel, out_shape=shapes, in_specs=[pl.BlockSpec(memory_sp...  37.5 us
    ppermute x6, starting transfers between devices, share_pivots(): lax.ppermute(value, ('row', 'col'), [(r * COLS + c, r * COLS + (c + k) %...  13.3 us
    ppermute x24, waiting for transfers between devices, fan_out(): moved = lax.ppermute(value, axis, pairs)  11.7 us
    ppermute x2, waiting for transfers between devices, finish(): lax.ppermute(held, ('row', 'col'), pairs_of([(root, left), (right, far)]))  6.61 us
    ppermute x2, starting transfers between devices, body(): crossed = [lax.ppermute(up, 'row', [(0, 1)]) for up in sent]  4.2 us
    ppermute x6, waiting for transfers between devices, share_pivots(): lax.ppermute(value, ('row', 'col'), [(r * COLS + c, r * COLS + (c + k) %...  3.61 us
    select_n x4, other arithmetic, share_planes(): final = jnp.where(holder, held, fan_out(held, 'row', second_sets))  3.48 us
  transfers between devices with their start and end apart: 42, of which 13 were waited for; matrix products, arithmetic and copies ran while one was open for 8% of the time, Pallas kernels for 4%

profile of v8, /device:TPU:0, one launch (start us, length us, event | category | flops | bytes accessed | tf_op | source)
XLA Modules:
  0.0 147.8 jit_solution(8182298485589420027)
XLA Ops:
  0.6 1.0 corner_share.1
  1.7 4.5 %collective-permute-start = (f32[2,512,128]{2,1,0:T(8,128)S(1)}, f32[2,512,128]{2,1,0:T(8,128)}, u32[]{:S(2)}, u32[]{:S(2)}) collective-permute-start(f32[2,512,128]{2,1,0:T(8,128)S(1)} %corner_share.1), channel_id=1, source_target_pairs={{0,1},{5,6}} | collective-permute-start | bytes 1572872 | tf_op jit(solution)/shard_map/corner_share/ppermute | solution.py:406
  6.3 3.1 %collective-permute-start.2 = (f32[2,512,128]{2,1,0:T(8,128)S(1)}, f32[2,512,128]{2,1,0:T(8,128)}, u32[]{:S(2)}, u32[]{:S(2)}) collective-permute-start(f32[2,512,128]{2,1,0:T(8,128)S(1)} %corner_share.1), channel_id=1, source_target_pairs={{0,2},{5,7}} | collective-permute-start | bytes 1572872 | tf_op jit(solution)/shard_map/corner_share/ppermute | solution.py:406
  9.3 2.1 %collective-permute-start.1 = (f32[2,512,128]{2,1,0:T(8,128)S(1)}, f32[2,512,128]{2,1,0:T(8,128)}, u32[]{:S(2)}, u32[]{:S(2)}) collective-permute-start(f32[2,512,128]{2,1,0:T(8,128)S(1)} %corner_share.1), channel_id=1, source_target_pairs={{0,3},{5,4}} | collective-permute-start | bytes 1572872 | tf_op jit(solution)/shard_map/corner_share/ppermute | solution.py:406
  11.4 0.8 constant_dynamic-slice_fusion
  13.5 0.8 broadcast_select_fusion
  14.3 1.4 collective-permute-start.3
  16.2 2.5 %collective-permute-done.2 = f32[2,512,128]{2,1,0:T(8,128)} collective-permute-done((f32[2,512,128]{2,1,0:T(8,128)S(1)}, f32[2,512,128]{2,1,0:T(8,128)}, u32[]{:S(2)}, u32[]{:S(2)}) %collective-permute-start.2) | collective-permute-done | bytes 524320 | tf_op jit(solution)/shard_map/corner_share/ppermute | solution.py:406
  18.7 1.1 collective-permute-done.1
  19.8 1.5 %add_select_fusion.corner.refs_4_ = f32[2,512,128]{2,1,0:T(8,128)S(1)} fusion(f32[2,512,128]{2,1,0:T(8,128)S(1)} %corner_share.1, f32[2,512,128]{2,1,0:T(8,128)} %collective-permute-done, f32[2,512,128]{2,1,0:T(8,128)} %collective-permute-done.1, f32[2,512,128]{2,1,0:T(8,128)} %collective-permute-done.2, pred[]{:T(512)S(6)} %eq.52), kind=kLoop, calls=%fused_computation.1 | loop fusion | flops 393216 | bytes 2621441 | tf_op jit(solution)/shard_map/corner_share/jit(_where)/select_n | solution.py:454
  21.4 5.2 %first_upper.1 = (f32[128,512]{1,0:T(8,128)}, f32[128,512]{1,0:T(8,128)}, f32[128,512]{1,0:T(8,128)S(1)}, f32[128,512]{1,0:T(8,128)S(1)}) custom-call(s32[12]{0:T(128)S(1)} %concatenate.7.flags, f32[2,512,512]{2,1,0:T(8,128)S(1)} %copy-done, f32[2,512,128]{2,1,0:T(8,128)S(1)} %add_select_fusion.corner.refs_4_, f32[2,512,128]{2,1,0:T(8,128)S(1)} %bitcast.17, ...), custom_call_target="tpu_custom_call" | custom-call | tf_op jit(solution)/shard_map/first_upper/pallas_call | solution.py:335
  27.2 2.9 %collective-permute-start.4 = (f32[128,512]{1,0:T(8,128)}, f32[128,512]{1,0:T(8,128)S(1)}, u32[]{:S(2)}, u32[]{:S(2)}) collective-permute-start(f32[128,512]{1,0:T(8,128)} %get-tuple-element.35), channel_id=1, source_target_pairs={{0,4},{1,5},{2,6},{3,7}} | collective-permute-start | bytes 786440 | tf_op jit(solution)/shard_map/upper_share/ppermute | solution.py:459
  30.1 1.3 collective-permute-start.5
  31.5 1.0 broadcast_select_fusion.9
  32.8 1.0 upper_share.1
  33.8 1.3 collective-permute-start.12
  35.2 1.3 collective-permute-start.11
  36.5 1.3 collective-permute-start.10
  37.8 1.3 collective-permute-start.8
  39.1 1.3 collective-permute-start.7
  40.4 1.3 collective-permute-start.6
  41.9 1.3 collective-permute-start.15
  43.2 0.7 collective-permute-start.21
  43.9 1.4 collective-permute-done.8
  45.3 1.5 %collective-permute-start.20 = (f32[256,512]{1,0:T(8,128)S(1)}, f32[256,512]{1,0:T(8,128)}, u32[]{:S(2)}, u32[]{:S(2)}) collective-permute-start(f32[256,512]{1,0:T(8,128)S(1)} %upper_share.1), channel_id=1, source_target_pairs={{5,4}} | collective-permute-start | bytes 1572872 | tf_op jit(solution)/shard_map/upper_share/ppermute | solution.py:406
  46.8 1.4 collective-permute-start.19
  48.2 2.0 %collective-permute-done.6 = f32[128,512]{1,0:T(8,128)S(1)} collective-permute-done((f32[128,512]{1,0:T(8,128)S(1)}, f32[128,512]{1,0:T(8,128)S(1)}, u32[]{:S(2)}, u32[]{:S(2)}) %collective-permute-start.6) | collective-permute-done | bytes 262176 | tf_op jit(solution)/shard_map/upper_share/ppermute | solution.py:358
  50.3 1.3 collective-permute-start.14
  51.6 2.0 %collective-permute-start.13 = (f32[128,512]{1,0:T(8,128)S(1)}, f32[128,512]{1,0:T(8,128)}, u32[]{:S(2)}, u32[]{:S(2)}) collective-permute-start(f32[128,512]{1,0:T(8,128)S(1)} %add_select_fusion.7), channel_id=1, source_target_pairs={{0,8},{32,40},{64,72},{96,104},{4,36},{12,44},{20,52},{28,60},{1,9... | collective-permute-start | bytes 786440 | tf_op jit(solution)/shard_map/upper_share/ppermute | solution.py:358
  53.6 1.8 %collective-permute-done.14 = f32[128,512]{1,0:T(8,128)S(1)} collective-permute-done((f32[128,512]{1,0:T(8,128)S(1)}, f32[128,512]{1,0:T(8,128)S(1)}, u32[]{:S(2)}, u32[]{:S(2)}) %collective-permute-start.14) | collective-permute-done | bytes 262176 | tf_op jit(solution)/shard_map/upper_share/ppermute | solution.py:358
  55.4 1.9 %collective-permute-start.18 = (f32[128,512]{1,0:T(8,128)S(1)}, f32[128,512]{1,0:T(8,128)S(1)}, u32[]{:S(2)}, u32[]{:S(2)}) collective-permute-start(f32[128,512]{1,0:T(8,128)S(1)} %add_select_fusion.8), channel_id=1, source_target_pairs={{0,16},{32,48},{64,80},{96,112},{4,68},{12,76},{20,84},{28,92},{1,... | collective-permute-start | bytes 786440 | tf_op jit(solution)/shard_map/upper_share/ppermute | solution.py:358
  57.3 4.4 %collective-permute-start.17 = (f32[128,512]{1,0:T(8,128)S(1)}, f32[128,512]{1,0:T(8,128)S(1)}, u32[]{:S(2)}, u32[]{:S(2)}) collective-permute-start(f32[128,512]{1,0:T(8,128)S(1)} %add_select_fusion.8), channel_id=1, source_target_pairs={{0,24},{32,56},{64,88},{96,120},{4,100},{12,108},{20,116},{28,124}... | collective-permute-start | bytes 786440 | tf_op jit(solution)/shard_map/upper_share/ppermute | solution.py:358
  61.7 1.0 add_select_fusion.6.refs_0_.refs_4_
  62.8 1.3 collective-permute-start.16
  64.1 0.7 collective-permute-start.9
  64.8 2.4 %collective-permute-start.22 = (f32[128,512]{1,0:T(8,128)S(1)}, f32[128,512]{1,0:T(8,128)S(1)}, u32[]{:S(2)}, u32[]{:S(2)}) collective-permute-start(f32[128,512]{1,0:T(8,128)S(1)} %add_select_fusion.6.refs_0_.refs_4_), channel_id=1, source_target_pairs={{0,4},{4,0},{8,12},{12,8},{16,20},{20,16},{24,28},{28,24},{32,36},... | collective-permute-start | bytes 786440 | tf_op jit(solution)/shard_map/upper_share/ppermute | solution.py:383
  67.2 1.3 add_add_fusion
  69.2 1.3 collective-permute-done.23.refs_3_.refs_7_
  70.5 16.3 %first_update.1 = (f32[2,512,128]{2,1,0:T(8,128)}, f32[2,512,128]{2,1,0:T(8,128)}, f32[2,96,512]{2,1,0:T(8,128)S(1)}, f32[144,512]{1,0:T(8,128)S(1)}, f32[144,51...) custom-call(s32[12]{0:T(128)S(1)} %concatenate.7.flags, f32[2,512,128]{2,1,0:T(8,128)} %bitcast.16, ...), custom_call_target="tpu_custom_call" | custom-call | tf_op jit(solution)/shard_map/first_update/pallas_call | solution.py:335
  86.8 1.3 collective-permute-start.30
  88.1 1.3 collective-permute-start.24
  89.4 2.6 %collective-permute-done.30 = f32[144,512]{1,0:T(8,128)S(1)} collective-permute-done((f32[144,512]{1,0:T(8,128)S(1)}, f32[144,512]{1,0:T(8,128)S(1)}, u32[]{:S(2)}, u32[]{:S(2)}) %collective-permute-start.30) | collective-permute-done | bytes 294944 | tf_op jit(solution)/shard_map/second_share/ppermute | solution.py:476
  92.0 5.1 %collective-permute-start.33 = (f32[144,512]{1,0:T(8,128)S(1)}, f32[144,512]{1,0:T(8,128)S(1)}, u32[]{:S(2)}, u32[]{:S(2)}) collective-permute-start(f32[144,512]{1,0:T(8,128)S(1)} %broadcast_select_fusion.6), channel_id=1, source_target_pairs={{0,64},{4,20},{1,65},{5,21},{2,66},{6,22},{3,67},{7,23}} | collective-permute-start | bytes 884744 | tf_op jit(solution)/shard_map/second_share/ppermute | solution.py:358
  97.2 1.3 collective-permute-start.32
  98.5 1.3 collective-permute-start.31
  99.8 0.7 collective-permute-start.28
  100.6 1.3 collective-permute-start.27
  101.9 1.3 collective-permute-start.26
  103.2 1.3 collective-permute-start.25
  104.6 1.3 collective-permute-start.36
  106.0 1.3 collective-permute-start.35
  107.3 1.1 collective-permute-done.27
  108.5 2.0 %collective-permute-start.34 = (f32[144,512]{1,0:T(8,128)S(1)}, f32[144,512]{1,0:T(8,128)}, u32[]{:S(2)}, u32[]{:S(2)}) collective-permute-start(f32[144,512]{1,0:T(8,128)S(1)} %add_select_fusion.3), channel_id=1, source_target_pairs={{0,8},{32,40},{64,72},{96,104},{4,36},{12,44},{20,52},{28,60},{1,9... | collective-permute-start | bytes 884744 | tf_op jit(solution)/shard_map/second_share/ppermute | solution.py:358
  110.5 4.3 %collective-permute-done.25 = f32[144,512]{1,0:T(8,128)S(1)} collective-permute-done((f32[144,512]{1,0:T(8,128)S(1)}, f32[144,512]{1,0:T(8,128)S(1)}, u32[]{:S(2)}, u32[]{:S(2)}) %collective-permute-start.25) | collective-permute-done | bytes 294944 | tf_op jit(solution)/shard_map/second_share/ppermute | solution.py:358
  114.9 2.0 %collective-permute-start.39 = (f32[144,512]{1,0:T(8,128)S(1)}, f32[144,512]{1,0:T(8,128)}, u32[]{:S(2)}, u32[]{:S(2)}) collective-permute-start(f32[144,512]{1,0:T(8,128)S(1)} %add_select_fusion.4), channel_id=1, source_target_pairs={{0,16},{32,48},{64,80},{96,112},{4,68},{12,76},{20,84},{28,92},{1,... | collective-permute-start | bytes 884744 | tf_op jit(solution)/shard_map/second_share/ppermute | solution.py:358
  116.9 2.0 %collective-permute-start.38 = (f32[144,512]{1,0:T(8,128)S(1)}, f32[144,512]{1,0:T(8,128)}, u32[]{:S(2)}, u32[]{:S(2)}) collective-permute-start(f32[144,512]{1,0:T(8,128)S(1)} %add_select_fusion.4), channel_id=1, source_target_pairs={{0,24},{32,56},{64,88},{96,120},{4,100},{12,108},{20,116},{28,124}... | collective-permute-start | bytes 884744 | tf_op jit(solution)/shard_map/second_share/ppermute | solution.py:358
  118.9 2.0 %collective-permute-start.37 = (f32[144,512]{1,0:T(8,128)S(1)}, f32[144,512]{1,0:T(8,128)}, u32[]{:S(2)}, u32[]{:S(2)}) collective-permute-start(f32[144,512]{1,0:T(8,128)S(1)} %add_select_fusion.4), channel_id=1, source_target_pairs={{0,8},{32,40},{64,72},{96,104},{4,36},{12,44},{20,52},{28,60},{1,9... | collective-permute-start | bytes 884744 | tf_op jit(solution)/shard_map/second_share/ppermute | solution.py:358
  121.0 1.3 collective-permute-start.29
  122.3 1.1 add_select_fusion.2.refs_0_
  123.4 1.0 collective-permute-done.37
  124.5 1.3 add_select_fusion.1.refs_1_
  125.9 6.6 %collective-permute-done.29 = f32[2,96,512]{2,1,0:T(8,128)} collective-permute-done((f32[2,96,512]{2,1,0:T(8,128)S(1)}, f32[2,96,512]{2,1,0:T(8,128)}, u32[]{:S(2)}, u32[]{:S(2)}) %collective-permute-start.29) | collective-permute-done | bytes 393248 | tf_op jit(solution)/shard_map/second_share/ppermute | solution.py:398
  132.5 1.1 broadcast_select_fusion.5.lead
  133.6 14.0 %second_update.1 = (f32[2,512,128]{2,1,0:T(8,128)}, f32[2,512,128]{2,1,0:T(8,128)}) custom-call(s32[12]{0:T(128)S(1)} %concatenate.6.flags, f32[2,512,128]{2,1,0:T(8,128)} %get-tuple-element.46.far_u, f32[2,512,128]{2,1,0:T(8,128)} %get-tuple-element.47.far_v, f32[2,512,512]{2,1,0:T(8,128)} %far_near.3, f32[2,512,128]{2,1,0:T(8,128)} %far_sketch.3, ...), custom_call_target="tpu_custom_call" | custom-call | tf_op jit(solution)/shard_map/second_update/pallas_call | solution.py:335
  (69 shorter events, 4.3 us)
Async XLA Ops:
  0.6 15.1 %copy-start.6 = (s32[3,1,32,2,1]{2,4,3,1,0:T(1,128)S(1)}, s32[3,1,32,2,1]{2,4,3,1,0:T(1,128)}, u32[]{:S(2)}) copy-start(s32[3,1,32,2,1]{2,4,3,1,0:T(1,128)} %param.9) | copy-start | bytes 2308
  1.7 19.6 %copy-start = (f32[2,512,512]{2,1,0:T(8,128)S(1)}, f32[2,512,512]{2,1,0:T(8,128)}, u32[]{:S(2)}) copy-start(f32[2,512,512]{2,1,0:T(8,128)} %far_near.3) | copy-start | bytes 6291460
  1.7 19.6 %copy-start.1 = (f32[1,1,2,1,512,128]{5,4,3,2,1,0:T(8,128)S(1)}, f32[1,1,2,1,512,128]{5,4,3,2,1,0:T(8,128)}, u32[]{:S(2)}) copy-start(f32[1,1,2,1,512,128]{5,4,3,2,1,0:T(8,128)} %param.5) | copy-start | bytes 1572868
  1.7 11.7 %collective-permute-start = (f32[2,512,128]{2,1,0:T(8,128)S(1)}, f32[2,512,128]{2,1,0:T(8,128)}, u32[]{:S(2)}, u32[]{:S(2)}) collective-permute-start(f32[2,512,128]{2,1,0:T(8,128)S(1)} %corner_share.1), channel_id=1, source_target_pairs={{0,1},{5,6}} | collective-permute-start | bytes 1572872 | tf_op jit(solution)/shard_map/corner_share/ppermute | solution.py:406
  6.3 12.4 %collective-permute-start.2 = (f32[2,512,128]{2,1,0:T(8,128)S(1)}, f32[2,512,128]{2,1,0:T(8,128)}, u32[]{:S(2)}, u32[]{:S(2)}) collective-permute-start(f32[2,512,128]{2,1,0:T(8,128)S(1)} %corner_share.1), channel_id=1, source_target_pairs={{0,2},{5,7}} | collective-permute-start | bytes 1572872 | tf_op jit(solution)/shard_map/corner_share/ppermute | solution.py:406
  9.3 10.5 %collective-permute-start.1 = (f32[2,512,128]{2,1,0:T(8,128)S(1)}, f32[2,512,128]{2,1,0:T(8,128)}, u32[]{:S(2)}, u32[]{:S(2)}) collective-permute-start(f32[2,512,128]{2,1,0:T(8,128)S(1)} %corner_share.1), channel_id=1, source_target_pairs={{0,3},{5,4}} | collective-permute-start | bytes 1572872 | tf_op jit(solution)/shard_map/corner_share/ppermute | solution.py:406
  14.3 12.3 %collective-permute-start.3 = (f32[2,512,128]{2,1,0:T(8,128)}, f32[2,512,128]{2,1,0:T(8,128)}, u32[]{:S(2)}, u32[]{:S(2)}) collective-permute-start(f32[2,512,128]{2,1,0:T(8,128)} %broadcast_select_fusion), channel_id=1, source_target_pairs={{4,5},{8,9},{12,13},{16,17},{20,21},{24,25},{28,29},{32,33},{36,37... | collective-permute-start | bytes 1572872 | tf_op jit(solution)/shard_map/corner_share/ppermute | solution.py:394
  16.2 5.1 %copy-start.2 = (f32[1,1,2,1,512,128]{5,4,3,2,1,0:T(8,128)S(1)}, f32[1,1,2,1,512,128]{5,4,3,2,1,0:T(8,128)}, u32[]{:S(2)}) copy-start(f32[1,1,2,1,512,128]{5,4,3,2,1,0:T(8,128)} %param.6) | copy-start | bytes 1572868
  21.3 5.3 %copy-start.3 = (f32[2,512,128]{2,1,0:T(8,128)}, f32[2,512,128]{2,1,0:T(8,128)S(1)}, u32[]{:S(2)}) copy-start(f32[2,512,128]{2,1,0:T(8,128)S(1)} %add_select_fusion.corner.refs_4_) | copy-start | bytes 1572868
  26.5 0.7 copy-start.5
  27.2 4.2 %collective-permute-start.4 = (f32[128,512]{1,0:T(8,128)}, f32[128,512]{1,0:T(8,128)S(1)}, u32[]{:S(2)}, u32[]{:S(2)}) collective-permute-start(f32[128,512]{1,0:T(8,128)} %get-tuple-element.35), channel_id=1, source_target_pairs={{0,4},{1,5},{2,6},{3,7}} | collective-permute-start | bytes 786440 | tf_op jit(solution)/shard_map/upper_share/ppermute | solution.py:459
  30.1 2.7 %collective-permute-start.5 = (f32[128,512]{1,0:T(8,128)}, f32[128,512]{1,0:T(8,128)S(1)}, u32[]{:S(2)}, u32[]{:S(2)}) collective-permute-start(f32[128,512]{1,0:T(8,128)} %get-tuple-element.37), channel_id=1, source_target_pairs={{0,4},{1,5},{2,6},{3,7}} | collective-permute-start | bytes 786440 | tf_op jit(solution)/shard_map/upper_share/ppermute | solution.py:459
  33.8 6.6 %collective-permute-start.12 = (f32[128,512]{1,0:T(8,128)S(1)}, f32[128,512]{1,0:T(8,128)S(1)}, u32[]{:S(2)}, u32[]{:S(2)}) collective-permute-start(f32[128,512]{1,0:T(8,128)S(1)} %broadcast_select_fusion.9), channel_id=1, source_target_pairs={{0,64},{4,20},{1,65},{5,21},{2,66},{6,22},{3,67},{7,23}} | collective-permute-start | bytes 786440 | tf_op jit(solution)/shard_map/upper_share/ppermute | solution.py:358
  35.2 6.6 %collective-permute-start.11 = (f32[128,512]{1,0:T(8,128)S(1)}, f32[128,512]{1,0:T(8,128)S(1)}, u32[]{:S(2)}, u32[]{:S(2)}) collective-permute-start(f32[128,512]{1,0:T(8,128)S(1)} %broadcast_select_fusion.9), channel_id=1, source_target_pairs={{0,96},{4,28},{1,97},{5,29},{2,98},{6,30},{3,99},{7,31}} | collective-permute-start | bytes 786440 | tf_op jit(solution)/shard_map/upper_share/ppermute | solution.py:358
  36.5 5.4 %collective-permute-start.10 = (f32[128,512]{1,0:T(8,128)S(1)}, f32[128,512]{1,0:T(8,128)S(1)}, u32[]{:S(2)}, u32[]{:S(2)}) collective-permute-start(f32[128,512]{1,0:T(8,128)S(1)} %broadcast_select_fusion.9), channel_id=1, source_target_pairs={{0,32},{4,12},{1,33},{5,13},{2,34},{6,14},{3,35},{7,15}} | collective-permute-start | bytes 786440 | tf_op jit(solution)/shard_map/upper_share/ppermute | solution.py:358
  37.8 7.5 %collective-permute-start.8 = (f32[128,512]{1,0:T(8,128)S(1)}, f32[128,512]{1,0:T(8,128)S(1)}, u32[]{:S(2)}, u32[]{:S(2)}) collective-permute-start(f32[128,512]{1,0:T(8,128)S(1)} %broadcast_select_fusion.8), channel_id=1, source_target_pairs={{0,64},{4,20},{1,65},{5,21},{2,66},{6,22},{3,67},{7,23}} | collective-permute-start | bytes 786440 | tf_op jit(solution)/shard_map/upper_share/ppermute | solution.py:358
  39.1 7.7 %collective-permute-start.7 = (f32[128,512]{1,0:T(8,128)S(1)}, f32[128,512]{1,0:T(8,128)S(1)}, u32[]{:S(2)}, u32[]{:S(2)}) collective-permute-start(f32[128,512]{1,0:T(8,128)S(1)} %broadcast_select_fusion.8), channel_id=1, source_target_pairs={{0,96},{4,28},{1,97},{5,29},{2,98},{6,30},{3,99},{7,31}} | collective-permute-start | bytes 786440 | tf_op jit(solution)/shard_map/upper_share/ppermute | solution.py:358
  40.4 9.8 %collective-permute-start.6 = (f32[128,512]{1,0:T(8,128)S(1)}, f32[128,512]{1,0:T(8,128)S(1)}, u32[]{:S(2)}, u32[]{:S(2)}) collective-permute-start(f32[128,512]{1,0:T(8,128)S(1)} %broadcast_select_fusion.8), channel_id=1, source_target_pairs={{0,32},{4,12},{1,33},{5,13},{2,34},{6,14},{3,35},{7,15}} | collective-permute-start | bytes 786440 | tf_op jit(solution)/shard_map/upper_share/ppermute | solution.py:358
  41.9 9.6 %collective-permute-start.15 = (f32[128,512]{1,0:T(8,128)S(1)}, f32[128,512]{1,0:T(8,128)S(1)}, u32[]{:S(2)}, u32[]{:S(2)}) collective-permute-start(f32[128,512]{1,0:T(8,128)S(1)} %add_select_fusion.7), channel_id=1, source_target_pairs={{0,16},{32,48},{64,80},{96,112},{4,68},{12,76},{20,84},{28,92},{1,... | collective-permute-start | bytes 786440 | tf_op jit(solution)/shard_map/upper_share/ppermute | solution.py:358
  43.2 19.5 %collective-permute-start.21 = (f32[256,512]{1,0:T(8,128)S(1)}, f32[256,512]{1,0:T(8,128)S(1)}, u32[]{:S(2)}, u32[]{:S(2)}) collective-permute-start(f32[256,512]{1,0:T(8,128)S(1)} %upper_share.1), channel_id=1, source_target_pairs={{5,7}} | collective-permute-start | bytes 1572872 | tf_op jit(solution)/shard_map/upper_share/ppermute | solution.py:406
  45.3 18.8 %collective-permute-start.20 = (f32[256,512]{1,0:T(8,128)S(1)}, f32[256,512]{1,0:T(8,128)}, u32[]{:S(2)}, u32[]{:S(2)}) collective-permute-start(f32[256,512]{1,0:T(8,128)S(1)} %upper_share.1), channel_id=1, source_target_pairs={{5,4}} | collective-permute-start | bytes 1572872 | tf_op jit(solution)/shard_map/upper_share/ppermute | solution.py:406
  46.8 18.0 %collective-permute-start.19 = (f32[256,512]{1,0:T(8,128)S(1)}, f32[256,512]{1,0:T(8,128)}, u32[]{:S(2)}, u32[]{:S(2)}) collective-permute-start(f32[256,512]{1,0:T(8,128)S(1)} %upper_share.1), channel_id=1, source_target_pairs={{5,6}} | collective-permute-start | bytes 1572872 | tf_op jit(solution)/shard_map/upper_share/ppermute | solution.py:406
  50.3 5.2 %collective-permute-start.14 = (f32[128,512]{1,0:T(8,128)S(1)}, f32[128,512]{1,0:T(8,128)S(1)}, u32[]{:S(2)}, u32[]{:S(2)}) collective-permute-start(f32[128,512]{1,0:T(8,128)S(1)} %add_select_fusion.7), channel_id=1, source_target_pairs={{0,24},{32,56},{64,88},{96,120},{4,100},{12,108},{20,116},{28,124}... | collective-permute-start | bytes 786440 | tf_op jit(solution)/shard_map/upper_share/ppermute | solution.py:358
  51.6 5.7 %collective-permute-start.13 = (f32[128,512]{1,0:T(8,128)S(1)}, f32[128,512]{1,0:T(8,128)}, u32[]{:S(2)}, u32[]{:S(2)}) collective-permute-start(f32[128,512]{1,0:T(8,128)S(1)} %add_select_fusion.7), channel_id=1, source_target_pairs={{0,8},{32,40},{64,72},{96,104},{4,36},{12,44},{20,52},{28,60},{1,9... | collective-permute-start | bytes 786440 | tf_op jit(solution)/shard_map/upper_share/ppermute | solution.py:358
  55.4 13.2 %collective-permute-start.18 = (f32[128,512]{1,0:T(8,128)S(1)}, f32[128,512]{1,0:T(8,128)S(1)}, u32[]{:S(2)}, u32[]{:S(2)}) collective-permute-start(f32[128,512]{1,0:T(8,128)S(1)} %add_select_fusion.8), channel_id=1, source_target_pairs={{0,16},{32,48},{64,80},{96,112},{4,68},{12,76},{20,84},{28,92},{1,... | collective-permute-start | bytes 786440 | tf_op jit(solution)/shard_map/upper_share/ppermute | solution.py:358
  57.3 11.3 %collective-permute-start.17 = (f32[128,512]{1,0:T(8,128)S(1)}, f32[128,512]{1,0:T(8,128)S(1)}, u32[]{:S(2)}, u32[]{:S(2)}) collective-permute-start(f32[128,512]{1,0:T(8,128)S(1)} %add_select_fusion.8), channel_id=1, source_target_pairs={{0,24},{32,56},{64,88},{96,120},{4,100},{12,108},{20,116},{28,124}... | collective-permute-start | bytes 786440 | tf_op jit(solution)/shard_map/upper_share/ppermute | solution.py:358
  62.8 5.8 %collective-permute-start.16 = (f32[128,512]{1,0:T(8,128)S(1)}, f32[128,512]{1,0:T(8,128)S(1)}, u32[]{:S(2)}, u32[]{:S(2)}) collective-permute-start(f32[128,512]{1,0:T(8,128)S(1)} %add_select_fusion.8), channel_id=1, source_target_pairs={{0,8},{32,40},{64,72},{96,104},{4,36},{12,44},{20,52},{28,60},{1,9... | collective-permute-start | bytes 786440 | tf_op jit(solution)/shard_map/upper_share/ppermute | solution.py:358
  64.1 5.0 %collective-permute-start.9 = (f32[2,512,128]{2,1,0:T(8,128)S(1)}, f32[2,512,128]{2,1,0:T(8,128)S(1)}, u32[]{:S(2)}, u32[]{:S(2)}) collective-permute-start(f32[2,512,128]{2,1,0:T(8,128)S(1)} %broadcast_select_fusion.2.lead), channel_id=1, source_target_pairs={{4,7},{5,6},{8,11},{9,10},{12,15},{13,14},{16,19},{17,18},{20,23},... | collective-permute-start | bytes 1572872 | tf_op jit(solution)/shard_map/upper_share/ppermute | solution.py:398
  64.8 4.4 %collective-permute-start.22 = (f32[128,512]{1,0:T(8,128)S(1)}, f32[128,512]{1,0:T(8,128)S(1)}, u32[]{:S(2)}, u32[]{:S(2)}) collective-permute-start(f32[128,512]{1,0:T(8,128)S(1)} %add_select_fusion.6.refs_0_.refs_4_), channel_id=1, source_target_pairs={{0,4},{4,0},{8,12},{12,8},{16,20},{20,16},{24,28},{28,24},{32,36},... | collective-permute-start | bytes 786440 | tf_op jit(solution)/shard_map/upper_share/ppermute | solution.py:383
  68.6 1.9 %copy-start.4 = (f32[2,512,128]{2,1,0:T(8,128)S(1)}, f32[2,512,128]{2,1,0:T(8,128)}, u32[]{:S(2)}) copy-start(f32[2,512,128]{2,1,0:T(8,128)} %copy-done.3) | copy-start | bytes 1572868
  68.7 1.8 %collective-permute-start.23 = (f32[128,512]{1,0:T(8,128)S(1)}, f32[128,512]{1,0:T(8,128)S(1)}, u32[]{:S(2)}, u32[]{:S(2)}) collective-permute-start(f32[128,512]{1,0:T(8,128)S(1)} %add_select_fusion.5.refs_1_.refs_5_), channel_id=1, source_target_pairs={{0,4},{4,0},{8,12},{12,8},{16,20},{20,16},{24,28},{28,24},{32,36},... | collective-permute-start | bytes 786440 | tf_op jit(solution)/shard_map/upper_share/ppermute | solution.py:383
  86.8 5.2 %collective-permute-start.30 = (f32[144,512]{1,0:T(8,128)S(1)}, f32[144,512]{1,0:T(8,128)S(1)}, u32[]{:S(2)}, u32[]{:S(2)}) collective-permute-start(f32[144,512]{1,0:T(8,128)S(1)} %get-tuple-element.53), channel_id=1, source_target_pairs={{4,0},{5,1},{6,2},{7,3}} | collective-permute-start | bytes 884744 | tf_op jit(solution)/shard_map/second_share/ppermute | solution.py:476
  88.1 12.4 %collective-permute-start.24 = (f32[144,512]{1,0:T(8,128)S(1)}, f32[144,512]{1,0:T(8,128)S(1)}, u32[]{:S(2)}, u32[]{:S(2)}) collective-permute-start(f32[144,512]{1,0:T(8,128)S(1)} %get-tuple-element.49), channel_id=1, source_target_pairs={{4,0},{5,1},{6,2},{7,3}} | collective-permute-start | bytes 884744 | tf_op jit(solution)/shard_map/second_share/ppermute | solution.py:476
  92.0 9.8 %collective-permute-start.33 = (f32[144,512]{1,0:T(8,128)S(1)}, f32[144,512]{1,0:T(8,128)S(1)}, u32[]{:S(2)}, u32[]{:S(2)}) collective-permute-start(f32[144,512]{1,0:T(8,128)S(1)} %broadcast_select_fusion.6), channel_id=1, source_target_pairs={{0,64},{4,20},{1,65},{5,21},{2,66},{6,22},{3,67},{7,23}} | collective-permute-start | bytes 884744 | tf_op jit(solution)/shard_map/second_share/ppermute | solution.py:358
  97.2 6.0 %collective-permute-start.32 = (f32[144,512]{1,0:T(8,128)S(1)}, f32[144,512]{1,0:T(8,128)S(1)}, u32[]{:S(2)}, u32[]{:S(2)}) collective-permute-start(f32[144,512]{1,0:T(8,128)S(1)} %broadcast_select_fusion.6), channel_id=1, source_target_pairs={{0,96},{4,28},{1,97},{5,29},{2,98},{6,30},{3,99},{7,31}} | collective-permute-start | bytes 884744 | tf_op jit(solution)/shard_map/second_share/ppermute | solution.py:358
  98.5 6.0 %collective-permute-start.31 = (f32[144,512]{1,0:T(8,128)S(1)}, f32[144,512]{1,0:T(8,128)S(1)}, u32[]{:S(2)}, u32[]{:S(2)}) collective-permute-start(f32[144,512]{1,0:T(8,128)S(1)} %broadcast_select_fusion.6), channel_id=1, source_target_pairs={{0,32},{4,12},{1,33},{5,13},{2,34},{6,14},{3,35},{7,15}} | collective-permute-start | bytes 884744 | tf_op jit(solution)/shard_map/second_share/ppermute | solution.py:358
  99.8 6.2 %collective-permute-start.28 = (f32[2,96,512]{2,1,0:T(8,128)S(1)}, f32[2,96,512]{2,1,0:T(8,128)S(1)}, u32[]{:S(2)}, u32[]{:S(2)}) collective-permute-start(f32[2,96,512]{2,1,0:T(8,128)S(1)} %get-tuple-element.50), channel_id=1, source_target_pairs={{1,2},{5,6},{9,10},{13,14},{17,18},{21,22},{25,26},{29,30},{33,34}... | collective-permute-start | bytes 1179656 | tf_op jit(solution)/shard_map/second_share/ppermute | solution.py:394
  100.6 7.9 %collective-permute-start.27 = (f32[144,512]{1,0:T(8,128)S(1)}, f32[144,512]{1,0:T(8,128)S(1)}, u32[]{:S(2)}, u32[]{:S(2)}) collective-permute-start(f32[144,512]{1,0:T(8,128)S(1)} %broadcast_select_fusion.7), channel_id=1, source_target_pairs={{0,64},{4,20},{1,65},{5,21},{2,66},{6,22},{3,67},{7,23}} | collective-permute-start | bytes 884744 | tf_op jit(solution)/shard_map/second_share/ppermute | solution.py:358
  101.9 8.6 %collective-permute-start.26 = (f32[144,512]{1,0:T(8,128)S(1)}, f32[144,512]{1,0:T(8,128)S(1)}, u32[]{:S(2)}, u32[]{:S(2)}) collective-permute-start(f32[144,512]{1,0:T(8,128)S(1)} %broadcast_select_fusion.7), channel_id=1, source_target_pairs={{0,96},{4,28},{1,97},{5,29},{2,98},{6,30},{3,99},{7,31}} | collective-permute-start | bytes 884744 | tf_op jit(solution)/shard_map/second_share/ppermute | solution.py:358
  103.2 11.6 %collective-permute-start.25 = (f32[144,512]{1,0:T(8,128)S(1)}, f32[144,512]{1,0:T(8,128)S(1)}, u32[]{:S(2)}, u32[]{:S(2)}) collective-permute-start(f32[144,512]{1,0:T(8,128)S(1)} %broadcast_select_fusion.7), channel_id=1, source_target_pairs={{0,32},{4,12},{1,33},{5,13},{2,34},{6,14},{3,35},{7,15}} | collective-permute-start | bytes 884744 | tf_op jit(solution)/shard_map/second_share/ppermute | solution.py:358
  104.6 14.3 %collective-permute-start.36 = (f32[144,512]{1,0:T(8,128)S(1)}, f32[144,512]{1,0:T(8,128)S(1)}, u32[]{:S(2)}, u32[]{:S(2)}) collective-permute-start(f32[144,512]{1,0:T(8,128)S(1)} %add_select_fusion.3), channel_id=1, source_target_pairs={{0,16},{32,48},{64,80},{96,112},{4,68},{12,76},{20,84},{28,92},{1,... | collective-permute-start | bytes 884744 | tf_op jit(solution)/shard_map/second_share/ppermute | solution.py:358
  106.0 14.9 %collective-permute-start.35 = (f32[144,512]{1,0:T(8,128)S(1)}, f32[144,512]{1,0:T(8,128)S(1)}, u32[]{:S(2)}, u32[]{:S(2)}) collective-permute-start(f32[144,512]{1,0:T(8,128)S(1)} %add_select_fusion.3), channel_id=1, source_target_pairs={{0,24},{32,56},{64,88},{96,120},{4,100},{12,108},{20,116},{28,124}... | collective-permute-start | bytes 884744 | tf_op jit(solution)/shard_map/second_share/ppermute | solution.py:358
  108.5 13.8 %collective-permute-start.34 = (f32[144,512]{1,0:T(8,128)S(1)}, f32[144,512]{1,0:T(8,128)}, u32[]{:S(2)}, u32[]{:S(2)}) collective-permute-start(f32[144,512]{1,0:T(8,128)S(1)} %add_select_fusion.3), channel_id=1, source_target_pairs={{0,8},{32,40},{64,72},{96,104},{4,36},{12,44},{20,52},{28,60},{1,9... | collective-permute-start | bytes 884744 | tf_op jit(solution)/shard_map/second_share/ppermute | solution.py:358
  114.9 8.5 %collective-permute-start.39 = (f32[144,512]{1,0:T(8,128)S(1)}, f32[144,512]{1,0:T(8,128)}, u32[]{:S(2)}, u32[]{:S(2)}) collective-permute-start(f32[144,512]{1,0:T(8,128)S(1)} %add_select_fusion.4), channel_id=1, source_target_pairs={{0,16},{32,48},{64,80},{96,112},{4,68},{12,76},{20,84},{28,92},{1,... | collective-permute-start | bytes 884744 | tf_op jit(solution)/shard_map/second_share/ppermute | solution.py:358
  116.9 6.5 %collective-permute-start.38 = (f32[144,512]{1,0:T(8,128)S(1)}, f32[144,512]{1,0:T(8,128)}, u32[]{:S(2)}, u32[]{:S(2)}) collective-permute-start(f32[144,512]{1,0:T(8,128)S(1)} %add_select_fusion.4), channel_id=1, source_target_pairs={{0,24},{32,56},{64,88},{96,120},{4,100},{12,108},{20,116},{28,124}... | collective-permute-start | bytes 884744 | tf_op jit(solution)/shard_map/second_share/ppermute | solution.py:358
  118.9 5.5 %collective-permute-start.37 = (f32[144,512]{1,0:T(8,128)S(1)}, f32[144,512]{1,0:T(8,128)}, u32[]{:S(2)}, u32[]{:S(2)}) collective-permute-start(f32[144,512]{1,0:T(8,128)S(1)} %add_select_fusion.4), channel_id=1, source_target_pairs={{0,8},{32,40},{64,72},{96,104},{4,36},{12,44},{20,52},{28,60},{1,9... | collective-permute-start | bytes 884744 | tf_op jit(solution)/shard_map/second_share/ppermute | solution.py:358
  121.0 11.6 %collective-permute-start.29 = (f32[2,96,512]{2,1,0:T(8,128)S(1)}, f32[2,96,512]{2,1,0:T(8,128)}, u32[]{:S(2)}, u32[]{:S(2)}) collective-permute-start(f32[2,96,512]{2,1,0:T(8,128)S(1)} %broadcast_select_fusion.4), channel_id=1, source_target_pairs={{1,0},{2,3},{5,4},{6,7},{9,8},{10,11},{13,12},{14,15},{17,16},{18,... | collective-permute-start | bytes 1179656 | tf_op jit(solution)/shard_map/second_share/ppermute | solution.py:398
  123.3 10.3 %collective-permute-start.40 = (f32[144,512]{1,0:T(8,128)S(1)}, f32[144,512]{1,0:T(8,128)S(1)}, u32[]{:S(2)}, u32[]{:S(2)}) collective-permute-start(f32[144,512]{1,0:T(8,128)S(1)} %add_select_fusion.2.refs_0_), channel_id=1, source_target_pairs={{0,4},{4,0},{8,12},{12,8},{16,20},{20,16},{24,28},{28,24},{32,36},... | collective-permute-start | bytes 884744 | tf_op jit(solution)/shard_map/second_share/ppermute | solution.py:383
  125.7 7.9 %collective-permute-start.41 = (f32[144,512]{1,0:T(8,128)S(1)}, f32[144,512]{1,0:T(8,128)S(1)}, u32[]{:S(2)}, u32[]{:S(2)}) collective-permute-start(f32[144,512]{1,0:T(8,128)S(1)} %add_select_fusion.1.refs_1_), channel_id=1, source_target_pairs={{0,4},{4,0},{8,12},{12,8},{16,20},{20,16},{24,28},{28,24},{32,36},... | collective-permute-start | bytes 884744 | tf_op jit(solution)/shard_map/second_share/ppermute | solution.py:383

commit v9 on v7

--- a/solution.py
+++ b/solution.py
@@ -128,12 +128,23 @@
     return tasks
 
 
-def upper_kernel(flags, near, corner, own_u, own_v, out_a, out_b):
+def upper_kernel(flags, far_near, far_u, far_v, corner, out_a, out_b, near, own_u, own_v, sems):
+    loads = [
+        pltpu.make_async_copy(far_near.at[0], near, sems.at[0]),
+        pltpu.make_async_copy(far_u, own_u, sems.at[1]),
+        pltpu.make_async_copy(far_v, own_v, sems.at[2]),
+    ]
+    for load in loads:
+        load.start()
     tile, width = own_u.shape[1:]
     weight = 1.0 / (8.0 * tile)
-    far = near[0]
+    low_rank = weight * dot3(corner[0], corner[1], NT)
+    loads[0].wait()
+    far = near[...]
     start = diagonal_inverse(far)
-    parts = series(far + weight * dot3(corner[0], corner[1], NT), start)
+    parts = series(far + low_rank, start)
+    for load in loads[1:]:
+        load.wait()
     lanes = iota((tile, width), 1)
     values = jnp.concatenate([jnp.where(lanes < flags[2 + s], own_u[s], 0.0).T for s in range(2)], axis=0)
     for part in parts[::-1]:
@@ -444,7 +455,11 @@
         got = near + others
         corner = jnp.where(col == row, pack, got)
     with jax.named_scope("first_upper"):
-        up_a, up_b = call(upper_kernel, (payload, payload), flags[0], near_field, corner, own_u, own_v)
+        up_a, up_b = call(
+            upper_kernel, (payload, payload), flags[0], near_field, own_u, own_v, corner,
+            scratch=[pltpu.VMEM(shape, F32) for shape in ((tile, tile), pair, pair)] + [pltpu.SemaphoreType.DMA((3,))],
+            loads=3,
+        )
     with jax.named_scope("upper_share"):
         crossed = lax.ppermute(up_a, "row", [(0, 1)])
         extra = call(wide_kernel, (payload,), flags[0], near_lead, crossed)

time: 135 us -> 134 us (level)
  other arithmetic: 9.53 us -> 7.32 us
  starting transfers between devices: 34.5 us -> 32.7 us
  waiting for transfers between devices: 48.2 us -> 49.8 us
    ppermute x2, starting transfers between devices: 2.59 us -> 4.37 us  [share_row(): one = lax.ppermute(value, ('row', 'col'), pairs_of([(root, right)]))]
    ppermute x6, starting transfers between devices: 8.14 us -> 6.47 us  [share_pivots(): lax.ppermute(value, ('row', 'col'), [(r * COLS + c, r * COLS + (c + k) %...]
    ppermute x2, waiting for transfers between devices: 11.6 us -> 13.1 us  [share_row(): one = lax.ppermute(value, ('row', 'col'), pairs_of([(root, right)]))]
    ppermute x12, starting transfers between devices: 13.4 us -> 11.9 us  [fan_out(): moved = lax.ppermute(value, axis, pairs)]
    select_n x1, other arithmetic: 1.46 us -> 0.1 us  [body(): corner = jnp.where(col == row, pack, got)]
  transfers between devices with their start and end apart: 26 -> 26, of which waited for: 6 -> 6; matrix products, arithmetic and copies ran while one was open for 9% -> 8% of each run, Pallas kernels for 4% -> 4%
where the time goes in v9:
time: 134 us; the launch traced here: 133 us
  waiting for transfers between devices  49.8 us (37%)
  Pallas kernels  37.9 us (28%)
  starting transfers between devices  32.7 us (24%)
  other arithmetic  7.32 us (5%)
  local copies, waits for them, and re-layouts  4.11 us (3%)
    pallas_call x5, Pallas kernels, call(): pl.pallas_call(kernel, out_shape=shapes, in_specs=[pl.BlockSpec(memory_sp...  37.9 us
    ppermute x12, waiting for transfers between devices, fan_out(): moved = lax.ppermute(value, axis, pairs)  33.8 us
    ppermute x2, waiting for transfers between devices, share_row(): one = lax.ppermute(value, ('row', 'col'), pairs_of([(root, right)]))  13.1 us
    ppermute x12, starting transfers between devices, fan_out(): moved = lax.ppermute(value, axis, pairs)  11.9 us
    ppermute x6, starting transfers between devices, share_pivots(): lax.ppermute(value, ('row', 'col'), [(r * COLS + c, r * COLS + (c + k) %...  6.47 us
    ppermute x2, starting transfers between devices, share_planes(): lax.ppermute(final, 'row', [(r, r ^ 1) for r in range(2 * X_COUNT * Z_COU...  5.94 us
    ppermute x2, starting transfers between devices, share_row(): one = lax.ppermute(value, ('row', 'col'), pairs_of([(root, right)]))  4.37 us
    ppermute x2, waiting for transfers between devices, share_planes(): lax.ppermute(final, 'row', [(r, r ^ 1) for r in range(2 * X_COUNT * Z_COU...  2.85 us
  transfers between devices with their start and end apart: 26, of which 6 were waited for; matrix products, arithmetic and copies ran while one was open for 8% of the time, Pallas kernels for 4%

profile of v9, /device:TPU:43, one launch (start us, length us, event | category | flops | bytes accessed | tf_op | source)
XLA Modules:
  0.0 133.2 jit_solution(9652372024416079670)
XLA Ops:
  0.6 1.0 corner_share.1
  1.7 0.7 collective-permute-start
  2.4 0.7 collective-permute-start.2
  3.1 0.7 collective-permute-start.1
  3.8 0.8 constant_dynamic-slice_fusion
  4.6 0.1 copy.10
  4.7 0.5 slice.24
  5.2 1.0 dynamic-slice_reduce_fusion
  6.2 0.8 slice_reduce_fusion
  7.0 0.1 concatenate.7.flags
  7.1 0.7 iota_compare_fusion
  7.7 0.0 collective-permute-done
  7.8 1.3 collective-permute-start.4
  9.1 0.0 collective-permute-done.2
  9.1 0.1 add_select_fusion.4.corner.refs_0_
  9.2 5.4 %first_upper.1 = (f32[256,512]{1,0:T(8,128)S(1)}, f32[256,512]{1,0:T(8,128)S(1)}) custom-call(s32[12]{0:T(128)S(1)} %concatenate.7.flags, f32[2,512,512]{2,1,0:T(8,128)} %far_near.5, f32[2,512,128]{2,1,0:T(8,128)} %bitcast.16, f32[2,512,128]{2,1,0:T(8,128)} %bitcast.19, f32[2,512,128]{2,1,0:T(8,128)S(1)} %add_select_fusion.4.corner.refs_0_), custom_call_target="tpu_custom_call" | custom-call | tf_op jit(solution)/shard_map/first_upper/pallas_call | solution.py:336
  14.6 0.7 collective-permute-start.3
  15.3 7.2 %collective-permute-done.4 = f32[2,512,128]{2,1,0:T(8,128)} collective-permute-done((f32[2,512,128]{2,1,0:T(8,128)S(1)}, f32[2,512,128]{2,1,0:T(8,128)}, u32[]{:S(2)}, u32[]{:S(2)}) %collective-permute-start.4) | collective-permute-done | bytes 524320 | tf_op jit(solution)/shard_map/corner_share/ppermute | solution.py:396
  22.6 1.1 broadcast_select_fusion.3.lead
  23.7 1.0 upper_share.1
  24.7 0.1 broadcast_select_fusion.4
  24.8 0.7 collective-permute-start.7
  25.5 0.7 collective-permute-start.6
  26.2 1.5 %collective-permute-start.5 = (f32[256,512]{1,0:T(8,128)S(1)}, f32[256,512]{1,0:T(8,128)}, u32[]{:S(2)}, u32[]{:S(2)}) collective-permute-start(f32[256,512]{1,0:T(8,128)S(1)} %broadcast_select_fusion.4), channel_id=1, source_target_pairs={{0,32},{4,12},{1,33},{5,13},{2,34},{6,14},{3,35},{7,15}} | collective-permute-start | bytes 1572872 | tf_op jit(solution)/shard_map/upper_share/ppermute | solution.py:359
  27.7 1.5 %collective-permute-start.14 = (f32[256,512]{1,0:T(8,128)S(1)}, f32[256,512]{1,0:T(8,128)}, u32[]{:S(2)}, u32[]{:S(2)}) collective-permute-start(f32[256,512]{1,0:T(8,128)S(1)} %upper_share.1), channel_id=1, source_target_pairs={{5,7}} | collective-permute-start | bytes 1572872 | tf_op jit(solution)/shard_map/upper_share/ppermute | solution.py:408
  29.2 1.5 %collective-permute-start.13 = (f32[256,512]{1,0:T(8,128)S(1)}, f32[256,512]{1,0:T(8,128)}, u32[]{:S(2)}, u32[]{:S(2)}) collective-permute-start(f32[256,512]{1,0:T(8,128)S(1)} %upper_share.1), channel_id=1, source_target_pairs={{5,4}} | collective-permute-start | bytes 1572872 | tf_op jit(solution)/shard_map/upper_share/ppermute | solution.py:408
  30.6 0.0 collective-permute-done.7
  30.6 1.5 %collective-permute-start.12 = (f32[256,512]{1,0:T(8,128)S(1)}, f32[256,512]{1,0:T(8,128)}, u32[]{:S(2)}, u32[]{:S(2)}) collective-permute-start(f32[256,512]{1,0:T(8,128)S(1)} %upper_share.1), channel_id=1, source_target_pairs={{5,6}} | collective-permute-start | bytes 1572872 | tf_op jit(solution)/shard_map/upper_share/ppermute | solution.py:408
  32.1 0.0 collective-permute-done.6
  32.1 0.8 copy-done
  32.9 0.0 collective-permute-done.5
  32.9 1.4 %add_select_fusion.3 = f32[256,512]{1,0:T(8,128)S(1)} fusion(f32[256,512]{1,0:T(8,128)S(1)} %broadcast_select_fusion.4, f32[256,512]{1,0:T(8,128)S(1)} %collective-permute-done.7, f32[256,512]{1,0:T(8,128)} %collective-permute-done.5, f32[256,512]{1,0:T(8,128)} %copy-done, pred[]{:T(512)S(6)} %lt.38), kind=kLoop, calls=%fused_computation.4 | loop fusion | flops 393216 | bytes 2621441 | tf_op jit(solution)/shard_map/upper_share/jit(_where)/select_n | solution.py:373
  34.3 1.5 %collective-permute-start.11 = (f32[256,512]{1,0:T(8,128)S(1)}, f32[256,512]{1,0:T(8,128)}, u32[]{:S(2)}, u32[]{:S(2)}) collective-permute-start(f32[256,512]{1,0:T(8,128)S(1)} %add_select_fusion.3), channel_id=1, source_target_pairs={{0,16},{32,48},{64,80},{96,112},{4,68},{12,76},{20,84},{28,92},{1,... | collective-permute-start | bytes 1572872 | tf_op jit(solution)/shard_map/upper_share/ppermute | solution.py:359
  35.8 1.5 %collective-permute-start.10 = (f32[256,512]{1,0:T(8,128)S(1)}, f32[256,512]{1,0:T(8,128)}, u32[]{:S(2)}, u32[]{:S(2)}) collective-permute-start(f32[256,512]{1,0:T(8,128)S(1)} %add_select_fusion.3), channel_id=1, source_target_pairs={{0,24},{32,56},{64,88},{96,120},{4,100},{12,108},{20,116},{28,124}... | collective-permute-start | bytes 1572872 | tf_op jit(solution)/shard_map/upper_share/ppermute | solution.py:359
  37.3 1.3 collective-permute-start.9
  38.6 1.3 collective-permute-start.8
  40.0 1.5 %add_add_fusion = f32[256,512]{1,0:T(8,128)S(1)} fusion(f32[256,512]{1,0:T(8,128)} %collective-permute-done.12, f32[256,512]{1,0:T(8,128)} %collective-permute-done.13, f32[256,512]{1,0:T(8,128)} %collective-permute-done.14), kind=kLoop, calls=%fused_computation.2 | loop fusion | flops 262144 | bytes 2097152 | tf_op jit(solution)/shard_map/upper_share/add | solution.py:467
  41.5 15.9 %collective-permute-done.9 = f32[256,512]{1,0:T(8,128)} collective-permute-done((f32[256,512]{1,0:T(8,128)S(1)}, f32[256,512]{1,0:T(8,128)}, u32[]{:S(2)}, u32[]{:S(2)}) %collective-permute-start.9) | collective-permute-done | bytes 524320 | tf_op jit(solution)/shard_map/upper_share/ppermute | solution.py:359
  57.4 1.6 %add_select_fusion.2.ours.refs_0_ = f32[256,512]{1,0:T(8,128)S(1)} fusion(f32[256,512]{1,0:T(8,128)S(1)} %add_select_fusion.3, f32[256,512]{1,0:T(8,128)} %collective-permute-done.11, f32[256,512]{1,0:T(8,128)} %collective-permute-done.9, f32[256,512]{1,0:T(8,128)} %collective-permute-done.10, pred[]{:T(512)S(6)} %eq.51), kind=kLoop, calls=%fused_computation.3 | loop fusion | flops 393216 | bytes 2621441 | tf_op jit(solution)/shard_map/upper_share/jit(_where)/select_n | solution.py:384
  59.0 4.0 %collective-permute-start.15 = (f32[256,512]{1,0:T(8,128)S(1)}, f32[256,512]{1,0:T(8,128)S(1)}, u32[]{:S(2)}, u32[]{:S(2)}) collective-permute-start(f32[256,512]{1,0:T(8,128)S(1)} %add_select_fusion.2.ours.refs_0_), channel_id=1, source_target_pairs={{0,4},{4,0},{8,12},{12,8},{16,20},{20,16},{24,28},{28,24},{32,36},... | collective-permute-start | bytes 1572872 | tf_op jit(solution)/shard_map/upper_share/ppermute | solution.py:385
  63.1 0.1 broadcast_select_fusion.2.refs_1_
  63.1 0.1 broadcast_select_fusion.5.lead
  63.2 1.4 %collective-permute-done.15.theirs.refs_1_ = f32[256,512]{1,0:T(8,128)S(1)} collective-permute-done((f32[256,512]{1,0:T(8,128)S(1)}, f32[256,512]{1,0:T(8,128)S(1)}, u32[]{:S(2)}, u32[]{:S(2)}) %collective-permute-start.15) | collective-permute-done | bytes 524320 | tf_op jit(solution)/shard_map/upper_share/ppermute | solution.py:385
  64.6 16.5 %first_update.1 = (f32[2,512,128]{2,1,0:T(8,128)}, f32[2,512,128]{2,1,0:T(8,128)}, f32[2,96,512]{2,1,0:T(8,128)S(1)}, f32[3,96,512]{2,1,0:T(8,128)}, f32[3,96,512]{2,1,0:T(8,128)S(1)}) custom-call(s32[12]{0:T(128)S(1)} %concatenate.7.flags, f32[2,512,128]{2,1,0:T(8,128)} %bitcast.17, f32[2,512,128]{2,1,0:T(8,128)} %bitcast.20, f32[2,512,512]{2,1,0:T(8,128)} %far_near.5, ...), custom_call_target="tpu_custom_call" | custom-call | tf_op jit(solution)/shard_map/first_update/pallas_call | solution.py:336
  81.1 0.7 collective-permute-start.16
  81.8 3.1 %collective-permute-start.20 = (f32[2,96,512]{2,1,0:T(8,128)S(1)}, f32[2,96,512]{2,1,0:T(8,128)S(1)}, u32[]{:S(2)}, u32[]{:S(2)}) collective-permute-start(f32[2,96,512]{2,1,0:T(8,128)S(1)} %get-tuple-element.36), channel_id=1, source_target_pairs={{1,2},{5,6},{9,10},{13,14},{17,18},{21,22},{25,26},{29,30},{33,34}... | collective-permute-start | bytes 1179656 | tf_op jit(solution)/shard_map/second_share/ppermute | solution.py:396
  84.9 0.1 broadcast_select_fusion
  85.0 0.7 collective-permute-start.19
  85.7 0.7 collective-permute-start.18
  86.4 0.7 collective-permute-start.17
  87.1 5.9 %collective-permute-done.20 = f32[2,96,512]{2,1,0:T(8,128)S(1)} collective-permute-done((f32[2,96,512]{2,1,0:T(8,128)S(1)}, f32[2,96,512]{2,1,0:T(8,128)S(1)}, u32[]{:S(2)}, u32[]{:S(2)}) %collective-permute-start.20) | collective-permute-done | bytes 393248 | tf_op jit(solution)/shard_map/second_share/ppermute | solution.py:396
  93.0 0.1 broadcast_select_fusion.6
  93.1 0.3 add_select_fusion.1
  93.4 0.7 collective-permute-start.24
  94.1 0.7 collective-permute-start.23
  94.8 1.3 collective-permute-start.22
  96.1 1.3 collective-permute-start.21
  97.4 17.8 %collective-permute-done.22 = f32[3,96,512]{2,1,0:T(8,128)S(1)} collective-permute-done((f32[3,96,512]{2,1,0:T(8,128)S(1)}, f32[3,96,512]{2,1,0:T(8,128)S(1)}, u32[]{:S(2)}, u32[]{:S(2)}) %collective-permute-start.22) | collective-permute-done | bytes 589856 | tf_op jit(solution)/shard_map/second_share/ppermute | solution.py:359
  115.2 0.3 add_select_fusion.ours
  115.5 1.9 %collective-permute-start.25 = (f32[3,96,512]{2,1,0:T(8,128)S(1)}, f32[3,96,512]{2,1,0:T(8,128)S(1)}, u32[]{:S(2)}, u32[]{:S(2)}) collective-permute-start(f32[3,96,512]{2,1,0:T(8,128)S(1)} %add_select_fusion.ours), channel_id=1, source_target_pairs={{0,4},{4,0},{8,12},{12,8},{16,20},{20,16},{24,28},{28,24},{32,36},... | collective-permute-start | bytes 1769480 | tf_op jit(solution)/shard_map/second_share/ppermute | solution.py:385
  117.4 0.1 concatenate.6.flags
  117.5 0.1 broadcast_select_fusion.7.lead
  117.6 1.5 %collective-permute-done.25.theirs = f32[3,96,512]{2,1,0:T(8,128)S(1)} collective-permute-done((f32[3,96,512]{2,1,0:T(8,128)S(1)}, f32[3,96,512]{2,1,0:T(8,128)S(1)}, u32[]{:S(2)}, u32[]{:S(2)}) %collective-permute-start.25) | collective-permute-done | bytes 589856 | tf_op jit(solution)/shard_map/second_share/ppermute | solution.py:385
  119.0 13.9 %second_update.1 = (f32[2,512,128]{2,1,0:T(8,128)}, f32[2,512,128]{2,1,0:T(8,128)}) custom-call(s32[12]{0:T(128)S(1)} %concatenate.6.flags, f32[2,512,128]{2,1,0:T(8,128)} %get-tuple-element.32.far_u, f32[2,512,128]{2,1,0:T(8,128)} %get-tuple-element.33.far_v, f32[2,512,512]{2,1,0:T(8,128)} %far_near.5, f32[2,512,128]{2,1,0:T(8,128)} %far_sketch.3, ...), custom_call_target="tpu_custom_call" | custom-call | tf_op jit(solution)/shard_map/second_update/pallas_call | solution.py:336
  (19 shorter events, 0.1 us)
Async XLA Ops:
  1.7 6.0 %collective-permute-start = (f32[2,512,128]{2,1,0:T(8,128)S(1)}, f32[2,512,128]{2,1,0:T(8,128)S(1)}, u32[]{:S(2)}, u32[]{:S(2)}) collective-permute-start(f32[2,512,128]{2,1,0:T(8,128)S(1)} %corner_share.1), channel_id=1, source_target_pairs={{0,1},{5,6}} | collective-permute-start | bytes 1572872 | tf_op jit(solution)/shard_map/corner_share/ppermute | solution.py:408
  2.4 6.7 %collective-permute-start.2 = (f32[2,512,128]{2,1,0:T(8,128)S(1)}, f32[2,512,128]{2,1,0:T(8,128)S(1)}, u32[]{:S(2)}, u32[]{:S(2)}) collective-permute-start(f32[2,512,128]{2,1,0:T(8,128)S(1)} %corner_share.1), channel_id=1, source_target_pairs={{0,2},{5,7}} | collective-permute-start | bytes 1572872 | tf_op jit(solution)/shard_map/corner_share/ppermute | solution.py:408
  3.1 6.0 %collective-permute-start.1 = (f32[2,512,128]{2,1,0:T(8,128)S(1)}, f32[2,512,128]{2,1,0:T(8,128)S(1)}, u32[]{:S(2)}, u32[]{:S(2)}) collective-permute-start(f32[2,512,128]{2,1,0:T(8,128)S(1)} %corner_share.1), channel_id=1, source_target_pairs={{0,3},{5,4}} | collective-permute-start | bytes 1572872 | tf_op jit(solution)/shard_map/corner_share/ppermute | solution.py:408
  7.8 14.8 %collective-permute-start.4 = (f32[2,512,128]{2,1,0:T(8,128)S(1)}, f32[2,512,128]{2,1,0:T(8,128)}, u32[]{:S(2)}, u32[]{:S(2)}) collective-permute-start(f32[2,512,128]{2,1,0:T(8,128)S(1)} %broadcast_select_fusion.1), channel_id=1, source_target_pairs={{4,5},{8,9},{12,13},{16,17},{20,21},{24,25},{28,29},{32,33},{36,37... | collective-permute-start | bytes 1572872 | tf_op jit(solution)/shard_map/corner_share/ppermute | solution.py:396
  14.6 9.1 %collective-permute-start.3 = (f32[256,512]{1,0:T(8,128)S(1)}, f32[256,512]{1,0:T(8,128)S(1)}, u32[]{:S(2)}, u32[]{:S(2)}) collective-permute-start(f32[256,512]{1,0:T(8,128)S(1)} %get-tuple-element.24), channel_id=1, source_target_pairs={{0,4},{1,5},{2,6},{3,7}} | collective-permute-start | bytes 1572872 | tf_op jit(solution)/shard_map/upper_share/ppermute | solution.py:464
  24.8 5.8 %collective-permute-start.7 = (f32[256,512]{1,0:T(8,128)S(1)}, f32[256,512]{1,0:T(8,128)S(1)}, u32[]{:S(2)}, u32[]{:S(2)}) collective-permute-start(f32[256,512]{1,0:T(8,128)S(1)} %broadcast_select_fusion.4), channel_id=1, source_target_pairs={{0,64},{4,20},{1,65},{5,21},{2,66},{6,22},{3,67},{7,23}} | collective-permute-start | bytes 1572872 | tf_op jit(solution)/shard_map/upper_share/ppermute | solution.py:359
  25.5 6.6 %collective-permute-start.6 = (f32[256,512]{1,0:T(8,128)S(1)}, f32[256,512]{1,0:T(8,128)S(1)}, u32[]{:S(2)}, u32[]{:S(2)}) collective-permute-start(f32[256,512]{1,0:T(8,128)S(1)} %broadcast_select_fusion.4), channel_id=1, source_target_pairs={{0,96},{4,28},{1,97},{5,29},{2,98},{6,30},{3,99},{7,31}} | collective-permute-start | bytes 1572872 | tf_op jit(solution)/shard_map/upper_share/ppermute | solution.py:359
  26.2 6.7 %collective-permute-start.5 = (f32[256,512]{1,0:T(8,128)S(1)}, f32[256,512]{1,0:T(8,128)}, u32[]{:S(2)}, u32[]{:S(2)}) collective-permute-start(f32[256,512]{1,0:T(8,128)S(1)} %broadcast_select_fusion.4), channel_id=1, source_target_pairs={{0,32},{4,12},{1,33},{5,13},{2,34},{6,14},{3,35},{7,15}} | collective-permute-start | bytes 1572872 | tf_op jit(solution)/shard_map/upper_share/ppermute | solution.py:359
  27.7 9.6 %collective-permute-start.14 = (f32[256,512]{1,0:T(8,128)S(1)}, f32[256,512]{1,0:T(8,128)}, u32[]{:S(2)}, u32[]{:S(2)}) collective-permute-start(f32[256,512]{1,0:T(8,128)S(1)} %upper_share.1), channel_id=1, source_target_pairs={{5,7}} | collective-permute-start | bytes 1572872 | tf_op jit(solution)/shard_map/upper_share/ppermute | solution.py:408
  29.2 9.4 %collective-permute-start.13 = (f32[256,512]{1,0:T(8,128)S(1)}, f32[256,512]{1,0:T(8,128)}, u32[]{:S(2)}, u32[]{:S(2)}) collective-permute-start(f32[256,512]{1,0:T(8,128)S(1)} %upper_share.1), channel_id=1, source_target_pairs={{5,4}} | collective-permute-start | bytes 1572872 | tf_op jit(solution)/shard_map/upper_share/ppermute | solution.py:408
  30.6 9.3 %collective-permute-start.12 = (f32[256,512]{1,0:T(8,128)S(1)}, f32[256,512]{1,0:T(8,128)}, u32[]{:S(2)}, u32[]{:S(2)}) collective-permute-start(f32[256,512]{1,0:T(8,128)S(1)} %upper_share.1), channel_id=1, source_target_pairs={{5,6}} | collective-permute-start | bytes 1572872 | tf_op jit(solution)/shard_map/upper_share/ppermute | solution.py:408
  32.1 0.8 copy-start
  34.3 7.2 %collective-permute-start.11 = (f32[256,512]{1,0:T(8,128)S(1)}, f32[256,512]{1,0:T(8,128)}, u32[]{:S(2)}, u32[]{:S(2)}) collective-permute-start(f32[256,512]{1,0:T(8,128)S(1)} %add_select_fusion.3), channel_id=1, source_target_pairs={{0,16},{32,48},{64,80},{96,112},{4,68},{12,76},{20,84},{28,92},{1,... | collective-permute-start | bytes 1572872 | tf_op jit(solution)/shard_map/upper_share/ppermute | solution.py:359
  35.8 5.7 %collective-permute-start.10 = (f32[256,512]{1,0:T(8,128)S(1)}, f32[256,512]{1,0:T(8,128)}, u32[]{:S(2)}, u32[]{:S(2)}) collective-permute-start(f32[256,512]{1,0:T(8,128)S(1)} %add_select_fusion.3), channel_id=1, source_target_pairs={{0,24},{32,56},{64,88},{96,120},{4,100},{12,108},{20,116},{28,124}... | collective-permute-start | bytes 1572872 | tf_op jit(solution)/shard_map/upper_share/ppermute | solution.py:359
  37.3 20.2 %collective-permute-start.9 = (f32[256,512]{1,0:T(8,128)S(1)}, f32[256,512]{1,0:T(8,128)}, u32[]{:S(2)}, u32[]{:S(2)}) collective-permute-start(f32[256,512]{1,0:T(8,128)S(1)} %add_select_fusion.3), channel_id=1, source_target_pairs={{0,8},{32,40},{64,72},{96,104},{4,36},{12,44},{20,52},{28,60},{1,9... | collective-permute-start | bytes 1572872 | tf_op jit(solution)/shard_map/upper_share/ppermute | solution.py:359
  38.6 24.5 %collective-permute-start.8 = (f32[2,512,128]{2,1,0:T(8,128)S(1)}, f32[2,512,128]{2,1,0:T(8,128)S(1)}, u32[]{:S(2)}, u32[]{:S(2)}) collective-permute-start(f32[2,512,128]{2,1,0:T(8,128)S(1)} %broadcast_select_fusion.3.lead), channel_id=1, source_target_pairs={{4,7},{5,6},{8,11},{9,10},{12,15},{13,14},{16,19},{17,18},{20,23},... | collective-permute-start | bytes 1572872 | tf_op jit(solution)/shard_map/upper_share/ppermute | solution.py:400
  59.0 5.6 %collective-permute-start.15 = (f32[256,512]{1,0:T(8,128)S(1)}, f32[256,512]{1,0:T(8,128)S(1)}, u32[]{:S(2)}, u32[]{:S(2)}) collective-permute-start(f32[256,512]{1,0:T(8,128)S(1)} %add_select_fusion.2.ours.refs_0_), channel_id=1, source_target_pairs={{0,4},{4,0},{8,12},{12,8},{16,20},{20,16},{24,28},{28,24},{32,36},... | collective-permute-start | bytes 1572872 | tf_op jit(solution)/shard_map/upper_share/ppermute | solution.py:385
  81.1 3.8 %collective-permute-start.16 = (f32[3,96,512]{2,1,0:T(8,128)}, f32[3,96,512]{2,1,0:T(8,128)S(1)}, u32[]{:S(2)}, u32[]{:S(2)}) collective-permute-start(f32[3,96,512]{2,1,0:T(8,128)} %get-tuple-element.35), channel_id=1, source_target_pairs={{4,0},{5,1},{6,2},{7,3}} | collective-permute-start | bytes 1769480 | tf_op jit(solution)/shard_map/second_share/ppermute | solution.py:480
  81.8 11.2 %collective-permute-start.20 = (f32[2,96,512]{2,1,0:T(8,128)S(1)}, f32[2,96,512]{2,1,0:T(8,128)S(1)}, u32[]{:S(2)}, u32[]{:S(2)}) collective-permute-start(f32[2,96,512]{2,1,0:T(8,128)S(1)} %get-tuple-element.36), channel_id=1, source_target_pairs={{1,2},{5,6},{9,10},{13,14},{17,18},{21,22},{25,26},{29,30},{33,34}... | collective-permute-start | bytes 1179656 | tf_op jit(solution)/shard_map/second_share/ppermute | solution.py:396
  85.0 8.0 %collective-permute-start.19 = (f32[3,96,512]{2,1,0:T(8,128)S(1)}, f32[3,96,512]{2,1,0:T(8,128)S(1)}, u32[]{:S(2)}, u32[]{:S(2)}) collective-permute-start(f32[3,96,512]{2,1,0:T(8,128)S(1)} %broadcast_select_fusion), channel_id=1, source_target_pairs={{0,64},{4,20},{1,65},{5,21},{2,66},{6,22},{3,67},{7,23}} | collective-permute-start | bytes 1769480 | tf_op jit(solution)/shard_map/second_share/ppermute | solution.py:359
  85.7 7.3 %collective-permute-start.18 = (f32[3,96,512]{2,1,0:T(8,128)S(1)}, f32[3,96,512]{2,1,0:T(8,128)S(1)}, u32[]{:S(2)}, u32[]{:S(2)}) collective-permute-start(f32[3,96,512]{2,1,0:T(8,128)S(1)} %broadcast_select_fusion), channel_id=1, source_target_pairs={{0,96},{4,28},{1,97},{5,29},{2,98},{6,30},{3,99},{7,31}} | collective-permute-start | bytes 1769480 | tf_op jit(solution)/shard_map/second_share/ppermute | solution.py:359
  86.4 6.6 %collective-permute-start.17 = (f32[3,96,512]{2,1,0:T(8,128)S(1)}, f32[3,96,512]{2,1,0:T(8,128)S(1)}, u32[]{:S(2)}, u32[]{:S(2)}) collective-permute-start(f32[3,96,512]{2,1,0:T(8,128)S(1)} %broadcast_select_fusion), channel_id=1, source_target_pairs={{0,32},{4,12},{1,33},{5,13},{2,34},{6,14},{3,35},{7,15}} | collective-permute-start | bytes 1769480 | tf_op jit(solution)/shard_map/second_share/ppermute | solution.py:359
  93.4 4.0 %collective-permute-start.24 = (f32[3,96,512]{2,1,0:T(8,128)S(1)}, f32[3,96,512]{2,1,0:T(8,128)S(1)}, u32[]{:S(2)}, u32[]{:S(2)}) collective-permute-start(f32[3,96,512]{2,1,0:T(8,128)S(1)} %add_select_fusion.1), channel_id=1, source_target_pairs={{0,16},{32,48},{64,80},{96,112},{4,68},{12,76},{20,84},{28,92},{1,... | collective-permute-start | bytes 1769480 | tf_op jit(solution)/shard_map/second_share/ppermute | solution.py:359
  94.1 3.3 %collective-permute-start.23 = (f32[3,96,512]{2,1,0:T(8,128)S(1)}, f32[3,96,512]{2,1,0:T(8,128)S(1)}, u32[]{:S(2)}, u32[]{:S(2)}) collective-permute-start(f32[3,96,512]{2,1,0:T(8,128)S(1)} %add_select_fusion.1), channel_id=1, source_target_pairs={{0,24},{32,56},{64,88},{96,120},{4,100},{12,108},{20,116},{28,124}... | collective-permute-start | bytes 1769480 | tf_op jit(solution)/shard_map/second_share/ppermute | solution.py:359
  94.8 20.5 %collective-permute-start.22 = (f32[3,96,512]{2,1,0:T(8,128)S(1)}, f32[3,96,512]{2,1,0:T(8,128)S(1)}, u32[]{:S(2)}, u32[]{:S(2)}) collective-permute-start(f32[3,96,512]{2,1,0:T(8,128)S(1)} %add_select_fusion.1), channel_id=1, source_target_pairs={{0,8},{32,40},{64,72},{96,104},{4,36},{12,44},{20,52},{28,60},{1,9... | collective-permute-start | bytes 1769480 | tf_op jit(solution)/shard_map/second_share/ppermute | solution.py:359
  96.1 21.4 %collective-permute-start.21 = (f32[2,96,512]{2,1,0:T(8,128)S(1)}, f32[2,96,512]{2,1,0:T(8,128)S(1)}, u32[]{:S(2)}, u32[]{:S(2)}) collective-permute-start(f32[2,96,512]{2,1,0:T(8,128)S(1)} %broadcast_select_fusion.6), channel_id=1, source_target_pairs={{1,0},{2,3},{5,4},{6,7},{9,8},{10,11},{13,12},{14,15},{17,16},{18,... | collective-permute-start | bytes 1179656 | tf_op jit(solution)/shard_map/second_share/ppermute | solution.py:400
  115.5 3.5 %collective-permute-start.25 = (f32[3,96,512]{2,1,0:T(8,128)S(1)}, f32[3,96,512]{2,1,0:T(8,128)S(1)}, u32[]{:S(2)}, u32[]{:S(2)}) collective-permute-start(f32[3,96,512]{2,1,0:T(8,128)S(1)} %add_select_fusion.ours), channel_id=1, source_target_pairs={{0,4},{4,0},{8,12},{12,8},{16,20},{20,16},{24,28},{28,24},{32,36},... | collective-permute-start | bytes 1769480 | tf_op jit(solution)/shard_map/second_share/ppermute | solution.py:385
